TPU v7x, 32 devices: a whole 2x2x4 slice. The times are simulated.
32 devices in a mesh: dom: 8 (over y, x, core), section: 4 (over z).
Axes of the slice: x: 2, y: 2, z: 4, core: 2. Of those that a mesh axis runs over, the one named last changes fastest.
Arguments:
- saved_inputs: bfloat16 [4, 4, 2048, 256], P('section', None, 'dom'), may hold values from -6 to 6
- grad_out: bfloat16 [4, 2048, 256], P(None, 'dom'), may hold values from -6 to 6
- w_first: bfloat16 [4, 512, 256], P('section'), may hold values from -0.25 to 0.25
- w_second: bfloat16 [4, 256, 256], P('section'), may hold values from -0.25 to 0.25
- face_weight: float32 [6, 2048], P(None, 'dom'), may hold values from 0.25 to 1
- neighbours: int32 [6, 2048], P(None, 'dom'), may hold values from 0 to 320, as said below
- send_rows: int32 [2, 256], P(None, 'dom'), may hold values from 0 to 255, as said below
Outputs:
- grad_in: bfloat16 [4, 4, 2048, 256], P('section', None, 'dom')
- grad_first: float32 [4, 512, 256], P('section')
- grad_second: float32 [4, 256, 256], P('section')
Inputs may be any that keep to these rules, and one draw needn't show every extreme that they name: `neighbours`: slots count as: 0 to 31 the halo from below, 32 to 287 the partition's own cells, then 32 halo slots from above, and 320 a zero row for walls. A partition uses its halo slots unevenly; some partition uses all of them on both sides. `send_rows`: within one partition and one side the rows are distinct local row numbers.
All inputs are finite; a program needn't handle non-finite values.
Results may differ from a plain program's by a relative error of at most 0.027.
Values may be sent and summed in bfloat16 or wider, within the bound.
No kernel may reach another device: no remote copies, remote signals or barrier semaphores. Data moves between devices by JAX's collectives and lax.ppermute only.
A program may use at most 64 MiB of HBM per device.

v0:
```python
import jax
import jax.numpy as jnp
from jax import lax
from jax.sharding import PartitionSpec as P


def with_halo(x, sides, width):
    for axis, dim in sides:
        count, length = (lax.axis_size(axis), x.shape[dim])
        up = [(i, (i + 1) % count) for i in range(count - 1)]
        down = [(j, i) for i, j in up]
        last = lax.slice_in_dim(x, length - width, length, axis=dim)
        initial = lax.slice_in_dim(x, 0, width, axis=dim)
        before = lax.ppermute(last, axis, up)
        after = lax.ppermute(initial, axis, down)
        x = jnp.concatenate([before, x, after], axis=dim)
    return x


def from_behind(value, axis, steps):
    count = lax.axis_size(axis)
    initial, last = (max(0, -steps), min(count, count - steps))
    return lax.ppermute(value, axis, [(source, source + steps) for source in range(initial, last)])


def forward_part(x, below, above, nbr, coef, w_one):
    zero = jnp.zeros((x.shape[0], 1, x.shape[2]), x.dtype)
    ext = jnp.concatenate([below, x, above, zero], axis=1)
    rows = jnp.take(ext, nbr, axis=1)
    agg = jnp.sum(rows.astype(jnp.float32) * coef[None, :, :, None], axis=1).astype(jnp.bfloat16)
    joined = jnp.concatenate([x, agg], axis=2)
    z = jnp.einsum("mrj,jd->mrd", joined, w_one, preferred_element_type=jnp.float32)
    act = jax.nn.silu(z).astype(jnp.bfloat16)
    return (joined, z, act)


def backward_part(joined, z, act, g, nbr, coef, w_one, w_two, slots):
    width = g.shape[-1]
    rows = g.shape[1]
    d_act = jnp.einsum("mrd,jd->mrj", g, w_two, preferred_element_type=jnp.float32)
    sig = jax.nn.sigmoid(z)
    dz = (d_act * sig * (1.0 + z * (1.0 - sig))).astype(jnp.bfloat16)
    dw_two = jnp.einsum("mri,mrj->ij", act, g, preferred_element_type=jnp.float32)
    dw_one = jnp.einsum("mri,mrj->ij", joined, dz, preferred_element_type=jnp.float32)
    d_joined = jnp.einsum("mrj,ij->mri", dz, w_one, preferred_element_type=jnp.float32)
    dx = d_joined[..., :width]
    dagg = d_joined[..., width:]
    contrib = dagg[:, None] * coef[None, :, :, None]
    flat = contrib.transpose(1, 2, 0, 3).reshape(-1, g.shape[0], width)
    dext = jax.ops.segment_sum(flat, nbr.reshape(-1), num_segments=rows + 2 * slots + 1)
    dext = dext.transpose(1, 0, 2)
    local = dx + dext[:, slots : slots + rows]
    return (local, dext[:, :slots], dext[:, slots + rows : slots + rows + slots], dw_one, dw_two)


def per_device(saved_inputs, grad_out, w_first, w_second, face_weight, neighbours, send_rows):
    x_all = saved_inputs[0]
    w_one = w_first[0]
    w_two = w_second[0]
    batches = x_all.shape[0]
    slots = send_rows.shape[1]
    sections = lax.axis_size("section")
    position = lax.axis_index("section")
    send_up = jnp.take(x_all, send_rows[0], axis=1)
    send_down = jnp.take(x_all, send_rows[1], axis=1)
    packed = jnp.concatenate([send_down, send_up], axis=1)
    wide = with_halo(packed, (("dom", 1),), slots)
    below_all = wide[:, :slots]
    above_all = wide[:, 3 * slots :]

    def tick(step, carry):
        sent, grad_in, acc_one, acc_two = carry
        received = from_behind(sent, "section", -1)
        batch = step - (sections - 1 - position)
        valid = (batch >= 0) & (batch < batches)
        index = jnp.clip(batch, 0, batches - 1)

        def pick(array):
            return lax.dynamic_slice_in_dim(array, index, 1, 0)

        g = jnp.where(position == sections - 1, pick(grad_out), received)
        joined, z, act = forward_part(
            pick(x_all), pick(below_all), pick(above_all), neighbours, face_weight, w_one
        )
        local, slot_below, slot_above, d_one, d_two = backward_part(
            joined, z, act, g, neighbours, face_weight, w_one, w_two, slots
        )
        edges = jnp.concatenate([slot_below[0], slot_above[0]], axis=0)
        back = with_halo(edges, (("dom", 0),), slots)
        from_lower = back[:slots]
        from_upper = back[3 * slots :]
        total = local[0].at[send_rows[0]].add(from_upper).at[send_rows[1]].add(from_lower)
        g_new = (g[0].astype(jnp.float32) + total).astype(jnp.bfloat16)[None]
        kept = jnp.where(valid, g_new, pick(grad_in))
        grad_in = lax.dynamic_update_slice_in_dim(grad_in, kept, index, 0)
        acc_one = acc_one + jnp.where(valid, d_one, 0.0)
        acc_two = acc_two + jnp.where(valid, d_two, 0.0)
        return (g_new, grad_in, acc_one, acc_two)

    start = (
        jnp.zeros_like(x_all[:1]),
        jnp.zeros_like(x_all),
        jnp.zeros(w_one.shape, jnp.float32),
        jnp.zeros(w_two.shape, jnp.float32),
    )
    sent, grad_in, acc_one, acc_two = lax.fori_loop(0, batches + sections - 1, tick, start)
    sum_one, sum_two = lax.psum((acc_one, acc_two), "dom")
    return (grad_in[None], sum_one[None], sum_two[None])


def solution(mesh):
    return jax.shard_map(
        per_device,
        mesh=mesh,
        in_specs=(
            P("section", None, "dom", None),
            P(None, "dom", None),
            P("section", None, None),
            P("section", None, None),
            P(None, "dom"),
            P(None, "dom"),
            P(None, "dom"),
        ),
        out_specs=(
            P("section", None, "dom", None),
            P("section", None, None),
            P("section", None, None),
        ),
        check_vma=False,
    )
```

profile of v0, /device:TPU:1, one launch (start us, length us, event | category | flops | bytes accessed | tf_op | source)
XLA Modules:
  0.0 348.9 jit_solution(9377116387823567961)
XLA Ops:
  10.2 4.5 %collective-permute-start.3 = (bf16[4,32,256]{2,0,1:T(4,128)(2,1)S(1)}, bf16[4,32,256]{2,0,1:T(4,128)(2,1)S(1)}, u32[]{:S(2)}, u32[]{:S(2)}) collective-permute-start(bf16[4,32,256]{2,0,1:T(4,128)(2,1)S(1)} %select_bitcast_fusion.1), channel_id=1, source_target_pairs={{0,4},{4,8},{8,12},{12,16},{16,20},{20,24},{24,28},{1,5},{5,9},{9,... | collective-permute-start | bytes 196616 | tf_op jit(solution)/shard_map/ppermute | solution.py:14
  15.5 1.9 collective-permute-start.4
  19.0 2.2 collective-permute-done.4
  23.2 251.3 %while.23 = (s32[]{:T(128)}, bf16[1,256,256]{2,1,0:T(8,128)(2,1)}, bf16[4,256,256]{2,1,0:T(8,128)(2,1)}, f32[512,256]{1,0:T(8,128)S(1)}, f32[256,256]{1,0:T(8,12...) while((s32[]{:T(128)}, bf16[1,256,256]{2,1,0:T(8,128)(2,1)}, ...), condition=%wide.wide.region_5.7_spmd.clone, body=%wide.wide.region_0.6_spmd.clone.sunk | while | flops 274368192 | bytes 20593392 | solution.py:106
  26.5 4.8 %gather_fusion = bf16[1536,256]{1,0:T(8,128)(2,1)S(1)} fusion(bf16[321,256]{1,0:T(8,128)(2,1)S(1)} %maximum_bitcast_fusion.12, s32[2048]{0:T(1024)S(1)} %pad_clamp_fusion.5), kind=kCustom, calls=%fused_computation.1.clone.clone.clone.1 | custom fusion | bytes 1579008 | tf_op jit(solution)/shard_map/while/body/eval_jaxpr/jit(_take)/gather | solution.py:29
  37.7 9.1 %scatter_custom_fusion.16 = f32[321,256]{1,0:T(8,128)S(1)} fusion(s32[1536]{0:T(1024)} %get-tuple-element.729, f32[1536,1,256]{2,0,1:T(8,128)S(1)} %bitcast_multiply_fusion.3, f32[]{:T(128)} %constant.126.clone.9..sunk), kind=kCustom, calls=%fused_computation.6.clone.clone.1 | custom fusion | flops 393216 | bytes 1902080 | tf_op jit(solution)/shard_map/while/body/eval_jaxpr/scatter-add | solution.py:50
  47.8 1.9 collective-permute-start.1
  49.8 3.6 %collective-permute-start.2 = (f32[32,256]{1,0:T(8,128)S(1)}, f32[32,256]{1,0:T(8,128)S(1)}, u32[]{:S(2)}, u32[]{:S(2)}) collective-permute-start(f32[32,256]{1,0:T(8,128)S(1)} %get-tuple-element.660), channel_id=1, source_target_pairs={{0,4},{4,8},{8,12},{12,16},{16,20},{20,24},{24,28},{1,5},{5,9},{9,... | collective-permute-start | bytes 98312 | tf_op jit(solution)/shard_map/while/body/eval_jaxpr/ppermute | solution.py:14
  61.8 4.8 %gather_fusion = bf16[1536,256]{1,0:T(8,128)(2,1)S(1)} fusion(bf16[321,256]{1,0:T(8,128)(2,1)S(1)} %maximum_bitcast_fusion.12, s32[2048]{0:T(1024)S(1)} %pad_clamp_fusion.5), kind=kCustom, calls=%fused_computation.1.clone.clone.clone.1 | custom fusion | bytes 1579008 | tf_op jit(solution)/shard_map/while/body/eval_jaxpr/jit(_take)/gather | solution.py:29
  73.0 9.1 %scatter_custom_fusion.16 = f32[321,256]{1,0:T(8,128)S(1)} fusion(s32[1536]{0:T(1024)} %get-tuple-element.729, f32[1536,1,256]{2,0,1:T(8,128)S(1)} %bitcast_multiply_fusion.3, f32[]{:T(128)} %constant.126.clone.9..sunk), kind=kCustom, calls=%fused_computation.6.clone.clone.1 | custom fusion | flops 393216 | bytes 1902080 | tf_op jit(solution)/shard_map/while/body/eval_jaxpr/scatter-add | solution.py:50
  83.2 1.9 collective-permute-start.1
  85.1 3.6 %collective-permute-start.2 = (f32[32,256]{1,0:T(8,128)S(1)}, f32[32,256]{1,0:T(8,128)S(1)}, u32[]{:S(2)}, u32[]{:S(2)}) collective-permute-start(f32[32,256]{1,0:T(8,128)S(1)} %get-tuple-element.660), channel_id=1, source_target_pairs={{0,4},{4,8},{8,12},{12,16},{16,20},{20,24},{24,28},{1,5},{5,9},{9,... | collective-permute-start | bytes 98312 | tf_op jit(solution)/shard_map/while/body/eval_jaxpr/ppermute | solution.py:14
  97.2 4.8 %gather_fusion = bf16[1536,256]{1,0:T(8,128)(2,1)S(1)} fusion(bf16[321,256]{1,0:T(8,128)(2,1)S(1)} %maximum_bitcast_fusion.12, s32[2048]{0:T(1024)S(1)} %pad_clamp_fusion.5), kind=kCustom, calls=%fused_computation.1.clone.clone.clone.1 | custom fusion | bytes 1579008 | tf_op jit(solution)/shard_map/while/body/eval_jaxpr/jit(_take)/gather | solution.py:29
  108.4 9.1 %scatter_custom_fusion.16 = f32[321,256]{1,0:T(8,128)S(1)} fusion(s32[1536]{0:T(1024)} %get-tuple-element.729, f32[1536,1,256]{2,0,1:T(8,128)S(1)} %bitcast_multiply_fusion.3, f32[]{:T(128)} %constant.126.clone.9..sunk), kind=kCustom, calls=%fused_computation.6.clone.clone.1 | custom fusion | flops 393216 | bytes 1902080 | tf_op jit(solution)/shard_map/while/body/eval_jaxpr/scatter-add | solution.py:50
  118.5 1.9 collective-permute-start.1
  120.5 3.6 %collective-permute-start.2 = (f32[32,256]{1,0:T(8,128)S(1)}, f32[32,256]{1,0:T(8,128)S(1)}, u32[]{:S(2)}, u32[]{:S(2)}) collective-permute-start(f32[32,256]{1,0:T(8,128)S(1)} %get-tuple-element.660), channel_id=1, source_target_pairs={{0,4},{4,8},{8,12},{12,16},{16,20},{20,24},{24,28},{1,5},{5,9},{9,... | collective-permute-start | bytes 98312 | tf_op jit(solution)/shard_map/while/body/eval_jaxpr/ppermute | solution.py:14
  132.5 4.8 %gather_fusion = bf16[1536,256]{1,0:T(8,128)(2,1)S(1)} fusion(bf16[321,256]{1,0:T(8,128)(2,1)S(1)} %maximum_bitcast_fusion.12, s32[2048]{0:T(1024)S(1)} %pad_clamp_fusion.5), kind=kCustom, calls=%fused_computation.1.clone.clone.clone.1 | custom fusion | bytes 1579008 | tf_op jit(solution)/shard_map/while/body/eval_jaxpr/jit(_take)/gather | solution.py:29
  143.7 9.1 %scatter_custom_fusion.16 = f32[321,256]{1,0:T(8,128)S(1)} fusion(s32[1536]{0:T(1024)} %get-tuple-element.729, f32[1536,1,256]{2,0,1:T(8,128)S(1)} %bitcast_multiply_fusion.3, f32[]{:T(128)} %constant.126.clone.9..sunk), kind=kCustom, calls=%fused_computation.6.clone.clone.1 | custom fusion | flops 393216 | bytes 1902080 | tf_op jit(solution)/shard_map/while/body/eval_jaxpr/scatter-add | solution.py:50
  153.9 1.9 collective-permute-start.1
  155.8 4.5 %collective-permute-start.2 = (f32[32,256]{1,0:T(8,128)S(1)}, f32[32,256]{1,0:T(8,128)S(1)}, u32[]{:S(2)}, u32[]{:S(2)}) collective-permute-start(f32[32,256]{1,0:T(8,128)S(1)} %get-tuple-element.660), channel_id=1, source_target_pairs={{0,4},{4,8},{8,12},{12,16},{16,20},{20,24},{24,28},{1,5},{5,9},{9,... | collective-permute-start | bytes 98312 | tf_op jit(solution)/shard_map/while/body/eval_jaxpr/ppermute | solution.py:14
  168.7 4.8 %gather_fusion = bf16[1536,256]{1,0:T(8,128)(2,1)S(1)} fusion(bf16[321,256]{1,0:T(8,128)(2,1)S(1)} %maximum_bitcast_fusion.12, s32[2048]{0:T(1024)S(1)} %pad_clamp_fusion.5), kind=kCustom, calls=%fused_computation.1.clone.clone.clone.1 | custom fusion | bytes 1579008 | tf_op jit(solution)/shard_map/while/body/eval_jaxpr/jit(_take)/gather | solution.py:29
  179.9 9.1 %scatter_custom_fusion.16 = f32[321,256]{1,0:T(8,128)S(1)} fusion(s32[1536]{0:T(1024)} %get-tuple-element.729, f32[1536,1,256]{2,0,1:T(8,128)S(1)} %bitcast_multiply_fusion.3, f32[]{:T(128)} %constant.126.clone.9..sunk), kind=kCustom, calls=%fused_computation.6.clone.clone.1 | custom fusion | flops 393216 | bytes 1902080 | tf_op jit(solution)/shard_map/while/body/eval_jaxpr/scatter-add | solution.py:50
  190.1 1.9 collective-permute-start.1
  192.0 4.5 %collective-permute-start.2 = (f32[32,256]{1,0:T(8,128)S(1)}, f32[32,256]{1,0:T(8,128)S(1)}, u32[]{:S(2)}, u32[]{:S(2)}) collective-permute-start(f32[32,256]{1,0:T(8,128)S(1)} %get-tuple-element.660), channel_id=1, source_target_pairs={{0,4},{4,8},{8,12},{12,16},{16,20},{20,24},{24,28},{1,5},{5,9},{9,... | collective-permute-start | bytes 98312 | tf_op jit(solution)/shard_map/while/body/eval_jaxpr/ppermute | solution.py:14
  205.0 4.8 %gather_fusion = bf16[1536,256]{1,0:T(8,128)(2,1)S(1)} fusion(bf16[321,256]{1,0:T(8,128)(2,1)S(1)} %maximum_bitcast_fusion.12, s32[2048]{0:T(1024)S(1)} %pad_clamp_fusion.5), kind=kCustom, calls=%fused_computation.1.clone.clone.clone.1 | custom fusion | bytes 1579008 | tf_op jit(solution)/shard_map/while/body/eval_jaxpr/jit(_take)/gather | solution.py:29
  216.2 9.1 %scatter_custom_fusion.16 = f32[321,256]{1,0:T(8,128)S(1)} fusion(s32[1536]{0:T(1024)} %get-tuple-element.729, f32[1536,1,256]{2,0,1:T(8,128)S(1)} %bitcast_multiply_fusion.3, f32[]{:T(128)} %constant.126.clone.9..sunk), kind=kCustom, calls=%fused_computation.6.clone.clone.1 | custom fusion | flops 393216 | bytes 1902080 | tf_op jit(solution)/shard_map/while/body/eval_jaxpr/scatter-add | solution.py:50
  226.3 1.9 collective-permute-start.1
  228.3 4.5 %collective-permute-start.2 = (f32[32,256]{1,0:T(8,128)S(1)}, f32[32,256]{1,0:T(8,128)S(1)}, u32[]{:S(2)}, u32[]{:S(2)}) collective-permute-start(f32[32,256]{1,0:T(8,128)S(1)} %get-tuple-element.660), channel_id=1, source_target_pairs={{0,4},{4,8},{8,12},{12,16},{16,20},{20,24},{24,28},{1,5},{5,9},{9,... | collective-permute-start | bytes 98312 | tf_op jit(solution)/shard_map/while/body/eval_jaxpr/ppermute | solution.py:14
  241.2 4.8 %gather_fusion = bf16[1536,256]{1,0:T(8,128)(2,1)S(1)} fusion(bf16[321,256]{1,0:T(8,128)(2,1)S(1)} %maximum_bitcast_fusion.12, s32[2048]{0:T(1024)S(1)} %pad_clamp_fusion.5), kind=kCustom, calls=%fused_computation.1.clone.clone.clone.1 | custom fusion | bytes 1579008 | tf_op jit(solution)/shard_map/while/body/eval_jaxpr/jit(_take)/gather | solution.py:29
  252.4 9.1 %scatter_custom_fusion.16 = f32[321,256]{1,0:T(8,128)S(1)} fusion(s32[1536]{0:T(1024)} %get-tuple-element.729, f32[1536,1,256]{2,0,1:T(8,128)S(1)} %bitcast_multiply_fusion.3, f32[]{:T(128)} %constant.126.clone.9..sunk), kind=kCustom, calls=%fused_computation.6.clone.clone.1 | custom fusion | flops 393216 | bytes 1902080 | tf_op jit(solution)/shard_map/while/body/eval_jaxpr/scatter-add | solution.py:50
  264.5 4.9 %collective-permute-start.2 = (f32[32,256]{1,0:T(8,128)S(1)}, f32[32,256]{1,0:T(8,128)S(1)}, u32[]{:S(2)}, u32[]{:S(2)}) collective-permute-start(f32[32,256]{1,0:T(8,128)S(1)} %get-tuple-element.660), channel_id=1, source_target_pairs={{0,4},{4,8},{8,12},{12,16},{16,20},{20,24},{24,28},{1,5},{5,9},{9,... | collective-permute-start | bytes 98312 | tf_op jit(solution)/shard_map/while/body/eval_jaxpr/ppermute | solution.py:14
  275.4 63.1 %all-reduce.3.cloned.1.call-done = (f32[1,512,256]{2,1,0:T(8,128)}, f32[1,256,256]{2,1,0:T(8,128)}) async-done(((f32[1,512,256]{2,1,0:T(8,128)}, f32[1,256,256]{2,1,0:T(8,128)}), (f32[1,512,256]{2,1,0:T(8,128)}, f32[1,256,256]{2,1,0:T(8,128)})) %all-reduce.3.cloned.1.call-update) | async-done | bytes 786448 | tf_op jit(solution)/shard_map/psum | solution.py:107
  (374 shorter events, 122.8 us)
Async XLA Ops:
  7.2 331.3 %all-reduce.3.cloned.1.call-start = ((), (), s32[]{:S(2)}) async-start(), calls=%async_computation | async-start | bytes 1572864 | tf_op jit(solution)/shard_map/psum | solution.py:107
  8.0 15.2 %copy-start = (bf16[1,512,256]{2,1,0:T(8,128)(2,1)S(1)}, bf16[1,512,256]{2,1,0:T(8,128)(2,1)}, u32[]{:S(2)}) copy-start(bf16[1,512,256]{2,1,0:T(8,128)(2,1)} %param.13) | copy-start | bytes 786436
  10.2 8.7 %collective-permute-start.3 = (bf16[4,32,256]{2,0,1:T(4,128)(2,1)S(1)}, bf16[4,32,256]{2,0,1:T(4,128)(2,1)S(1)}, u32[]{:S(2)}, u32[]{:S(2)}) collective-permute-start(bf16[4,32,256]{2,0,1:T(4,128)(2,1)S(1)} %select_bitcast_fusion.1), channel_id=1, source_target_pairs={{0,4},{4,8},{8,12},{12,16},{16,20},{20,24},{24,28},{1,5},{5,9},{9,... | collective-permute-start | bytes 196616 | tf_op jit(solution)/shard_map/ppermute | solution.py:14
  15.5 5.6 %collective-permute-start.4 = (bf16[4,32,256]{2,0,1:T(4,128)(2,1)S(1)}, bf16[4,32,256]{2,0,1:T(4,128)(2,1)S(1)}, u32[]{:S(2)}, u32[]{:S(2)}) collective-permute-start(bf16[4,32,256]{2,0,1:T(4,128)(2,1)S(1)} %select_bitcast_fusion), channel_id=1, source_target_pairs={{4,0},{8,4},{12,8},{16,12},{20,16},{24,20},{28,24},{5,1},{9,5},{13... | collective-permute-start | bytes 196616 | tf_op jit(solution)/shard_map/ppermute | solution.py:15
  23.2 14.2 %copy-start.9 = (f32[1536]{0:T(1024)}, f32[1536]{0:T(1024)S(1)}, u32[]{:S(2)}) copy-start(f32[1536]{0:T(1024)S(1)} %get-tuple-element.730) | copy-start | bytes 18436 | tf_op jit(solution)/shard_map/while
  23.2 10.2 %collective-permute-start = (bf16[1,256,256]{2,1,0:T(8,128)(2,1)}, bf16[1,256,256]{2,1,0:T(8,128)(2,1)S(1)}, u32[]{:S(2)}, u32[]{:S(2)}) collective-permute-start(bf16[1,256,256]{2,1,0:T(8,128)(2,1)} %get-tuple-element.689), channel_id=1, source_target_pairs={{1,0},{2,1},{3,2},{5,4},{6,5},{7,6},{9,8},{10,9},{11,10},{13,12},{... | collective-permute-start | bytes 393224 | tf_op jit(solution)/shard_map/while/body/eval_jaxpr/ppermute | solution.py:23
  47.8 7.2 %collective-permute-start.1 = (f32[32,256]{1,0:T(8,128)S(1)}, f32[32,256]{1,0:T(8,128)S(1)}, u32[]{:S(2)}, u32[]{:S(2)}) collective-permute-start(f32[32,256]{1,0:T(8,128)S(1)} %get-tuple-element.658), channel_id=1, source_target_pairs={{4,0},{8,4},{12,8},{16,12},{20,16},{24,20},{28,24},{5,1},{9,5},{13... | collective-permute-start | bytes 98312 | tf_op jit(solution)/shard_map/while/body/eval_jaxpr/ppermute | solution.py:15
  49.8 6.2 %collective-permute-start.2 = (f32[32,256]{1,0:T(8,128)S(1)}, f32[32,256]{1,0:T(8,128)S(1)}, u32[]{:S(2)}, u32[]{:S(2)}) collective-permute-start(f32[32,256]{1,0:T(8,128)S(1)} %get-tuple-element.660), channel_id=1, source_target_pairs={{0,4},{4,8},{8,12},{12,16},{16,20},{20,24},{24,28},{1,5},{5,9},{9,... | collective-permute-start | bytes 98312 | tf_op jit(solution)/shard_map/while/body/eval_jaxpr/ppermute | solution.py:14
  58.6 14.2 %copy-start.9 = (f32[1536]{0:T(1024)}, f32[1536]{0:T(1024)S(1)}, u32[]{:S(2)}) copy-start(f32[1536]{0:T(1024)S(1)} %get-tuple-element.730) | copy-start | bytes 18436 | tf_op jit(solution)/shard_map/while
  58.6 10.2 %collective-permute-start = (bf16[1,256,256]{2,1,0:T(8,128)(2,1)}, bf16[1,256,256]{2,1,0:T(8,128)(2,1)S(1)}, u32[]{:S(2)}, u32[]{:S(2)}) collective-permute-start(bf16[1,256,256]{2,1,0:T(8,128)(2,1)} %get-tuple-element.689), channel_id=1, source_target_pairs={{1,0},{2,1},{3,2},{5,4},{6,5},{7,6},{9,8},{10,9},{11,10},{13,12},{... | collective-permute-start | bytes 393224 | tf_op jit(solution)/shard_map/while/body/eval_jaxpr/ppermute | solution.py:23
  83.2 7.2 %collective-permute-start.1 = (f32[32,256]{1,0:T(8,128)S(1)}, f32[32,256]{1,0:T(8,128)S(1)}, u32[]{:S(2)}, u32[]{:S(2)}) collective-permute-start(f32[32,256]{1,0:T(8,128)S(1)} %get-tuple-element.658), channel_id=1, source_target_pairs={{4,0},{8,4},{12,8},{16,12},{20,16},{24,20},{28,24},{5,1},{9,5},{13... | collective-permute-start | bytes 98312 | tf_op jit(solution)/shard_map/while/body/eval_jaxpr/ppermute | solution.py:15
  85.1 6.2 %collective-permute-start.2 = (f32[32,256]{1,0:T(8,128)S(1)}, f32[32,256]{1,0:T(8,128)S(1)}, u32[]{:S(2)}, u32[]{:S(2)}) collective-permute-start(f32[32,256]{1,0:T(8,128)S(1)} %get-tuple-element.660), channel_id=1, source_target_pairs={{0,4},{4,8},{8,12},{12,16},{16,20},{20,24},{24,28},{1,5},{5,9},{9,... | collective-permute-start | bytes 98312 | tf_op jit(solution)/shard_map/while/body/eval_jaxpr/ppermute | solution.py:14
  93.9 14.2 %copy-start.9 = (f32[1536]{0:T(1024)}, f32[1536]{0:T(1024)S(1)}, u32[]{:S(2)}) copy-start(f32[1536]{0:T(1024)S(1)} %get-tuple-element.730) | copy-start | bytes 18436 | tf_op jit(solution)/shard_map/while
  93.9 10.2 %collective-permute-start = (bf16[1,256,256]{2,1,0:T(8,128)(2,1)}, bf16[1,256,256]{2,1,0:T(8,128)(2,1)S(1)}, u32[]{:S(2)}, u32[]{:S(2)}) collective-permute-start(bf16[1,256,256]{2,1,0:T(8,128)(2,1)} %get-tuple-element.689), channel_id=1, source_target_pairs={{1,0},{2,1},{3,2},{5,4},{6,5},{7,6},{9,8},{10,9},{11,10},{13,12},{... | collective-permute-start | bytes 393224 | tf_op jit(solution)/shard_map/while/body/eval_jaxpr/ppermute | solution.py:23
  118.5 7.2 %collective-permute-start.1 = (f32[32,256]{1,0:T(8,128)S(1)}, f32[32,256]{1,0:T(8,128)S(1)}, u32[]{:S(2)}, u32[]{:S(2)}) collective-permute-start(f32[32,256]{1,0:T(8,128)S(1)} %get-tuple-element.658), channel_id=1, source_target_pairs={{4,0},{8,4},{12,8},{16,12},{20,16},{24,20},{28,24},{5,1},{9,5},{13... | collective-permute-start | bytes 98312 | tf_op jit(solution)/shard_map/while/body/eval_jaxpr/ppermute | solution.py:15
  120.5 6.2 %collective-permute-start.2 = (f32[32,256]{1,0:T(8,128)S(1)}, f32[32,256]{1,0:T(8,128)S(1)}, u32[]{:S(2)}, u32[]{:S(2)}) collective-permute-start(f32[32,256]{1,0:T(8,128)S(1)} %get-tuple-element.660), channel_id=1, source_target_pairs={{0,4},{4,8},{8,12},{12,16},{16,20},{20,24},{24,28},{1,5},{5,9},{9,... | collective-permute-start | bytes 98312 | tf_op jit(solution)/shard_map/while/body/eval_jaxpr/ppermute | solution.py:14
  129.3 14.2 %copy-start.9 = (f32[1536]{0:T(1024)}, f32[1536]{0:T(1024)S(1)}, u32[]{:S(2)}) copy-start(f32[1536]{0:T(1024)S(1)} %get-tuple-element.730) | copy-start | bytes 18436 | tf_op jit(solution)/shard_map/while
  129.3 10.2 %collective-permute-start = (bf16[1,256,256]{2,1,0:T(8,128)(2,1)}, bf16[1,256,256]{2,1,0:T(8,128)(2,1)S(1)}, u32[]{:S(2)}, u32[]{:S(2)}) collective-permute-start(bf16[1,256,256]{2,1,0:T(8,128)(2,1)} %get-tuple-element.689), channel_id=1, source_target_pairs={{1,0},{2,1},{3,2},{5,4},{6,5},{7,6},{9,8},{10,9},{11,10},{13,12},{... | collective-permute-start | bytes 393224 | tf_op jit(solution)/shard_map/while/body/eval_jaxpr/ppermute | solution.py:23
  153.9 8.1 %collective-permute-start.1 = (f32[32,256]{1,0:T(8,128)S(1)}, f32[32,256]{1,0:T(8,128)S(1)}, u32[]{:S(2)}, u32[]{:S(2)}) collective-permute-start(f32[32,256]{1,0:T(8,128)S(1)} %get-tuple-element.658), channel_id=1, source_target_pairs={{4,0},{8,4},{12,8},{16,12},{20,16},{24,20},{28,24},{5,1},{9,5},{13... | collective-permute-start | bytes 98312 | tf_op jit(solution)/shard_map/while/body/eval_jaxpr/ppermute | solution.py:15
  155.8 7.1 %collective-permute-start.2 = (f32[32,256]{1,0:T(8,128)S(1)}, f32[32,256]{1,0:T(8,128)S(1)}, u32[]{:S(2)}, u32[]{:S(2)}) collective-permute-start(f32[32,256]{1,0:T(8,128)S(1)} %get-tuple-element.660), channel_id=1, source_target_pairs={{0,4},{4,8},{8,12},{12,16},{16,20},{20,24},{24,28},{1,5},{5,9},{9,... | collective-permute-start | bytes 98312 | tf_op jit(solution)/shard_map/while/body/eval_jaxpr/ppermute | solution.py:14
  165.5 14.2 %copy-start.9 = (f32[1536]{0:T(1024)}, f32[1536]{0:T(1024)S(1)}, u32[]{:S(2)}) copy-start(f32[1536]{0:T(1024)S(1)} %get-tuple-element.730) | copy-start | bytes 18436 | tf_op jit(solution)/shard_map/while
  165.5 10.2 %collective-permute-start = (bf16[1,256,256]{2,1,0:T(8,128)(2,1)}, bf16[1,256,256]{2,1,0:T(8,128)(2,1)S(1)}, u32[]{:S(2)}, u32[]{:S(2)}) collective-permute-start(bf16[1,256,256]{2,1,0:T(8,128)(2,1)} %get-tuple-element.689), channel_id=1, source_target_pairs={{1,0},{2,1},{3,2},{5,4},{6,5},{7,6},{9,8},{10,9},{11,10},{13,12},{... | collective-permute-start | bytes 393224 | tf_op jit(solution)/shard_map/while/body/eval_jaxpr/ppermute | solution.py:23
  190.1 8.1 %collective-permute-start.1 = (f32[32,256]{1,0:T(8,128)S(1)}, f32[32,256]{1,0:T(8,128)S(1)}, u32[]{:S(2)}, u32[]{:S(2)}) collective-permute-start(f32[32,256]{1,0:T(8,128)S(1)} %get-tuple-element.658), channel_id=1, source_target_pairs={{4,0},{8,4},{12,8},{16,12},{20,16},{24,20},{28,24},{5,1},{9,5},{13... | collective-permute-start | bytes 98312 | tf_op jit(solution)/shard_map/while/body/eval_jaxpr/ppermute | solution.py:15
  192.0 7.1 %collective-permute-start.2 = (f32[32,256]{1,0:T(8,128)S(1)}, f32[32,256]{1,0:T(8,128)S(1)}, u32[]{:S(2)}, u32[]{:S(2)}) collective-permute-start(f32[32,256]{1,0:T(8,128)S(1)} %get-tuple-element.660), channel_id=1, source_target_pairs={{0,4},{4,8},{8,12},{12,16},{16,20},{20,24},{24,28},{1,5},{5,9},{9,... | collective-permute-start | bytes 98312 | tf_op jit(solution)/shard_map/while/body/eval_jaxpr/ppermute | solution.py:14
  201.7 14.2 %copy-start.9 = (f32[1536]{0:T(1024)}, f32[1536]{0:T(1024)S(1)}, u32[]{:S(2)}) copy-start(f32[1536]{0:T(1024)S(1)} %get-tuple-element.730) | copy-start | bytes 18436 | tf_op jit(solution)/shard_map/while
  201.7 10.2 %collective-permute-start = (bf16[1,256,256]{2,1,0:T(8,128)(2,1)}, bf16[1,256,256]{2,1,0:T(8,128)(2,1)S(1)}, u32[]{:S(2)}, u32[]{:S(2)}) collective-permute-start(bf16[1,256,256]{2,1,0:T(8,128)(2,1)} %get-tuple-element.689), channel_id=1, source_target_pairs={{1,0},{2,1},{3,2},{5,4},{6,5},{7,6},{9,8},{10,9},{11,10},{13,12},{... | collective-permute-start | bytes 393224 | tf_op jit(solution)/shard_map/while/body/eval_jaxpr/ppermute | solution.py:23
  226.3 8.1 %collective-permute-start.1 = (f32[32,256]{1,0:T(8,128)S(1)}, f32[32,256]{1,0:T(8,128)S(1)}, u32[]{:S(2)}, u32[]{:S(2)}) collective-permute-start(f32[32,256]{1,0:T(8,128)S(1)} %get-tuple-element.658), channel_id=1, source_target_pairs={{4,0},{8,4},{12,8},{16,12},{20,16},{24,20},{28,24},{5,1},{9,5},{13... | collective-permute-start | bytes 98312 | tf_op jit(solution)/shard_map/while/body/eval_jaxpr/ppermute | solution.py:15
  228.3 7.1 %collective-permute-start.2 = (f32[32,256]{1,0:T(8,128)S(1)}, f32[32,256]{1,0:T(8,128)S(1)}, u32[]{:S(2)}, u32[]{:S(2)}) collective-permute-start(f32[32,256]{1,0:T(8,128)S(1)} %get-tuple-element.660), channel_id=1, source_target_pairs={{0,4},{4,8},{8,12},{12,16},{16,20},{20,24},{24,28},{1,5},{5,9},{9,... | collective-permute-start | bytes 98312 | tf_op jit(solution)/shard_map/while/body/eval_jaxpr/ppermute | solution.py:14
  238.0 14.2 %copy-start.9 = (f32[1536]{0:T(1024)}, f32[1536]{0:T(1024)S(1)}, u32[]{:S(2)}) copy-start(f32[1536]{0:T(1024)S(1)} %get-tuple-element.730) | copy-start | bytes 18436 | tf_op jit(solution)/shard_map/while
  238.0 10.2 %collective-permute-start = (bf16[1,256,256]{2,1,0:T(8,128)(2,1)}, bf16[1,256,256]{2,1,0:T(8,128)(2,1)S(1)}, u32[]{:S(2)}, u32[]{:S(2)}) collective-permute-start(bf16[1,256,256]{2,1,0:T(8,128)(2,1)} %get-tuple-element.689), channel_id=1, source_target_pairs={{1,0},{2,1},{3,2},{5,4},{6,5},{7,6},{9,8},{10,9},{11,10},{13,12},{... | collective-permute-start | bytes 393224 | tf_op jit(solution)/shard_map/while/body/eval_jaxpr/ppermute | solution.py:23
  262.6 8.5 %collective-permute-start.1 = (f32[32,256]{1,0:T(8,128)S(1)}, f32[32,256]{1,0:T(8,128)S(1)}, u32[]{:S(2)}, u32[]{:S(2)}) collective-permute-start(f32[32,256]{1,0:T(8,128)S(1)} %get-tuple-element.658), channel_id=1, source_target_pairs={{4,0},{8,4},{12,8},{16,12},{20,16},{24,20},{28,24},{5,1},{9,5},{13... | collective-permute-start | bytes 98312 | tf_op jit(solution)/shard_map/while/body/eval_jaxpr/ppermute | solution.py:15
  264.5 7.5 %collective-permute-start.2 = (f32[32,256]{1,0:T(8,128)S(1)}, f32[32,256]{1,0:T(8,128)S(1)}, u32[]{:S(2)}, u32[]{:S(2)}) collective-permute-start(f32[32,256]{1,0:T(8,128)S(1)} %get-tuple-element.660), channel_id=1, source_target_pairs={{0,4},{4,8},{8,12},{12,16},{16,20},{20,24},{24,28},{1,5},{5,9},{9,... | collective-permute-start | bytes 98312 | tf_op jit(solution)/shard_map/while/body/eval_jaxpr/ppermute | solution.py:14
  (73 other events, 402.4 us)
Sparse Core Ops, SparseCore 0:
  275.5 62.9 all-reduce.2
where the time goes:
time: 353 us; the launch traced here: 349 us
  other arithmetic  118 us (33%)
  waiting for transfers between devices  65.3 us (18%)
  starting transfers between devices  58.3 us (17%)
  local copies, waits for them, and re-layouts  56.6 us (16%)
  matrix products  33.5 us (9%)
  between operations  14.1 us (4%)
    scatter-add x7, other arithmetic, backward_part(): jax.ops.segment_sum(flat, nbr.reshape(-1), num_segments=rows + 2 * slots...  63.4 us
    psum x1, waiting for transfers between devices, per_device(): sum_one, sum_two = lax.psum((acc_one, acc_two), 'dom')  63.1 us
    ppermute x8, starting transfers between devices, with_halo(): before = lax.ppermute(last, axis, up)  33.9 us
    gather x7, local copies, waits for them, and re-layouts, forward_part(): rows = jnp.take(ext, nbr, axis=1)  33.3 us
    ppermute x8, starting transfers between devices, with_halo(): after = lax.ppermute(initial, axis, down)  15.4 us
    dot_general x7, matrix products, backward_part(): jnp.einsum('mrd,jd->mrj', g, w_two, preferred_element_type=jnp.float32)  12.8 us
    scatter-add x14, other arithmetic, tick(): local[0].at[send_rows[0]].add(from_upper).at[send_rows[1]].add(from_lower)  12.5 us
    dynamic_update_slice x7, other arithmetic, tick(): grad_in = lax.dynamic_update_slice_in_dim(grad_in, kept, index, 0)  11.5 us
  transfers between devices with their start and end apart: 24, of which 2 were waited for; matrix products, arithmetic and copies ran while one was open for 23% of the time, Pallas kernels for 0%

commit v1 on v0

v1 whole, which is shorter than its diff:
```python
import jax
import jax.numpy as jnp
from jax import lax
from jax.experimental import pallas as pl
from jax.experimental.pallas import tpu as pltpu
from jax.sharding import PartitionSpec as P

F32 = jnp.float32
BF16 = jnp.bfloat16
CHUNKS = 2


def dot(a, b, dims=((1,), (0,))):
    return lax.dot_general(a, b, (dims, ((), ())), preferred_element_type=F32)


def vmem():
    return pl.BlockSpec(memory_space=pltpu.VMEM)


def params():
    return pltpu.CompilerParams(vmem_limit_bytes=48 * 1024 * 1024)


def pack_kernel(x_ref, send_ref, place_ref, up_ref, down_ref):
    batches, rows, _ = x_ref.shape
    slots = send_ref.shape[1]
    row = lax.broadcasted_iota(jnp.int32, (rows, slots), 0)
    up = jnp.where(row == send_ref[0:1, :], 1.0, 0.0)
    down = jnp.where(row == send_ref[1:2, :], 1.0, 0.0)
    place = jnp.concatenate([up, down], axis=1)
    place_ref[...] = place.astype(BF16)
    pick = place.T.astype(BF16)
    for m in range(batches):
        sent = dot(pick, x_ref[m]).astype(BF16)
        up_ref[m] = sent[:slots]
        down_ref[m] = sent[slots:]


def forward_kernel(x_ref, below_ref, above_ref, nbr_ref, coef_ref, w_ref,
                   slope_ref, act_ref, agg_ref, own_ref, halo_ref):
    batches, rows, width = x_ref.shape
    slots = below_ref.shape[1]
    faces = nbr_ref.shape[0]
    slot = lax.broadcasted_iota(jnp.int32, (rows + 2 * slots, rows), 0)
    spread = jnp.zeros((rows + 2 * slots, rows), F32)
    for k in range(faces):
        spread = spread + jnp.where(slot == nbr_ref[k : k + 1, :], coef_ref[k : k + 1, :], 0.0)
    own = spread[slots : slots + rows]
    halo = jnp.concatenate([spread[:slots], spread[slots + rows :]], axis=0)
    own_ref[...] = own.astype(BF16)
    halo_ref[...] = halo.astype(BF16)
    own_t = own.T.astype(BF16)
    halo_t = halo.T.astype(BF16)
    for m in range(batches):
        x = x_ref[m]
        edge = jnp.concatenate([below_ref[m], above_ref[m]], axis=0)
        agg = (dot(own_t, x) + dot(halo_t, edge)).astype(BF16)
        z = dot(x, w_ref[:width]) + dot(agg, w_ref[width:])
        sig = 1.0 / (1.0 + jnp.exp(-z))
        agg_ref[m] = agg
        act_ref[m] = (z * sig).astype(BF16)
        slope_ref[m] = sig * (1.0 + z * (1.0 - sig))


def layer_step(g, first, slope_ref, own_ref, halo_ref, w1_ref, w2_ref, sent, kept, g_buf, dz_buf, sems):
    rows, width = slope_ref.shape[1], slope_ref.shape[2]
    local_ref, below_ref, above_ref = sent
    slots = below_ref.shape[1]
    count = len(g)
    copies = []

    def keep(n, source):
        copy = pltpu.make_async_copy(source, kept[n].at[pl.ds(first, count)], sems.at[n])
        copy.start()
        copies.append(copy)

    for j in range(count):
        g_buf[j] = g[j]
    keep(3, g_buf)
    stacked = jnp.concatenate(g, axis=0) if count > 1 else g[0]
    d_act = dot(stacked, w2_ref[...], ((1,), (1,)))
    dzs = []
    for j in range(count):
        dz = (d_act[j * rows : (j + 1) * rows] * slope_ref[first + j]).astype(BF16)
        dz_buf[j] = dz
        dzs.append(dz)
    keep(4, dz_buf)
    dz = jnp.concatenate(dzs, axis=0) if count > 1 else dzs[0]
    dj = dot(dz, w1_ref[...], ((1,), (1,)))
    for j in range(count):
        part = dj[j * rows : (j + 1) * rows]
        dagg = part[:, width:].astype(BF16)
        local = g[j].astype(F32) + part[:, :width] + dot(own_ref[...], dagg)
        local_ref[j] = local.astype(BF16)
        edge = dot(halo_ref[...], dagg).astype(BF16)
        below_ref[j] = edge[:slots]
        above_ref[j] = edge[slots:]
    for n in range(3):
        keep(n, sent[n])
    for copy in copies:
        copy.wait()


def assemble(local, upper, lower, place):
    edge = jnp.concatenate([upper, lower], axis=0)
    return (local.astype(F32) + dot(place, edge)).astype(BF16)


def make_step_kernel(hop, first, count, fresh):
    def body(hop_ref, *refs):
        inputs, refs = (refs[:1], refs[1:]) if hop == 0 else (refs[:4], refs[4:])
        slope_ref, own_ref, halo_ref, w1_ref, w2_ref = refs[:5]
        refs = refs[5:] if fresh else refs[10:]
        sent, kept, (g_buf, dz_buf, sems) = refs[:3], refs[3:8], refs[8:]

        @pl.when(hop_ref[0] == hop)
        def _():
            if hop == 0:
                g = [inputs[0][first + j] for j in range(count)]
            else:
                loc_ref, upper_ref, lower_ref, place_ref = inputs
                g = [assemble(loc_ref[j], upper_ref[j], lower_ref[j], place_ref[...]) for j in range(count)]
            layer_step(g, first, slope_ref, own_ref, halo_ref, w1_ref, w2_ref, sent, kept, g_buf, dz_buf, sems)

    return body


def weight_kernel(x_ref, agg_ref, act_ref, g_ref, dz_ref, grad_ref):
    batches, rows, width = x_ref.shape
    total = batches * rows
    g = g_ref[...].reshape(total, width)
    dz = dz_ref[...].reshape(total, width)
    over = ((0,), (0,))
    grad_ref[:width] = dot(x_ref[...].reshape(total, width), dz, over)
    grad_ref[width : 2 * width] = dot(agg_ref[...].reshape(total, width), dz, over)
    grad_ref[2 * width :] = dot(act_ref[...].reshape(total, width), g, over)


def finish_kernel(loc_ref, upper_ref, lower_ref, place_ref, out_ref):
    for m in range(loc_ref.shape[0]):
        out_ref[m] = assemble(loc_ref[m], upper_ref[m], lower_ref[m], place_ref[...])


def sum_over_dom(part, count):
    if count & (count - 1) or count < 4:
        return lax.psum(part, "dom")
    me = lax.axis_index("dom")

    def swap(value, mask):
        return lax.ppermute(value, "dom", [(i, i ^ mask) for i in range(count)])

    half = part.shape[0] // 2
    low = me % 2 == 0
    keep = jnp.where(low, part[:half], part[half:])
    give = jnp.where(low, part[half:], part[:half]).astype(BF16)
    acc = keep + swap(give, 1).astype(F32)
    bit = 2
    while bit < count:
        mine = acc.astype(BF16)
        if bit * 2 < count:
            others = [swap(mine, mask) for mask in (bit, 2 * bit, 3 * bit)]
            a, b, c = [other.astype(F32) for other in others]
            acc = (mine.astype(F32) + a) + (b + c)
            bit *= 4
        else:
            acc = mine.astype(F32) + swap(mine, bit).astype(F32)
            bit *= 2
    mine = acc.astype(BF16)
    other = swap(mine, 1)
    first = jnp.where(low, mine, other)
    second = jnp.where(low, other, mine)
    return jnp.concatenate([first, second], axis=0).astype(F32)


def per_device(saved_inputs, grad_out, w_first, w_second, face_weight, neighbours, send_rows):
    x = saved_inputs[0]
    w1 = w_first[0]
    w2 = w_second[0]
    batches, rows, width = x.shape
    slots = send_rows.shape[1]
    sections = lax.axis_size("section")
    doms = lax.axis_size("dom")
    chunks = CHUNKS if batches % CHUNKS == 0 else 1
    count = batches // chunks
    hop_here = (sections - 1 - lax.axis_index("section")).astype(jnp.int32).reshape(1)
    sds = jax.ShapeDtypeStruct

    place, up, down = pl.pallas_call(
        pack_kernel,
        out_shape=(sds((rows, 2 * slots), BF16), sds((batches, slots, width), BF16),
                   sds((batches, slots, width), BF16)),
        compiler_params=params(), name="pack",
    )(x, send_rows)
    rise = [(i, i + 1) for i in range(doms - 1)]
    fall = [(i + 1, i) for i in range(doms - 1)]
    below = lax.ppermute(up, "dom", rise)
    above = lax.ppermute(down, "dom", fall)

    slope, act, agg, own, halo = pl.pallas_call(
        forward_kernel,
        out_shape=(sds((batches, rows, width), F32), sds((batches, rows, width), BF16),
                   sds((batches, rows, width), BF16), sds((rows, rows), BF16), sds((2 * slots, rows), BF16)),
        compiler_params=params(), name="forward",
    )(x, below, above, neighbours, face_weight, w1)

    def move(value, hop, shift):
        source = sections - 1 - hop
        pairs = [(p * sections + source, (p + shift) * sections + source - 1)
                 for p in range(doms) if 0 <= p + shift < doms]
        return lax.ppermute(value, ("dom", "section"), pairs)

    def shapes(n):
        full, edge = sds((n, rows, width), BF16), sds((n, slots, width), BF16)
        return (full, edge, edge)

    any_spec = pl.BlockSpec(memory_space=pl.ANY)
    kept = ()
    received = [None] * chunks
    for hop in range(sections):
        sent = []
        for c in range(chunks):
            inputs = (grad_out,) if hop == 0 else (*received[c], place)
            inputs = (hop_here, *inputs, slope, own, halo, w1, w2)
            outs = pl.pallas_call(
                make_step_kernel(hop, c * count, count, not kept),
                in_specs=[pl.BlockSpec(memory_space=pltpu.SMEM)] + [vmem()] * (len(inputs) - 1)
                + [any_spec] * len(kept),
                out_specs=[vmem()] * 3 + [any_spec] * 5,
                out_shape=shapes(count) + shapes(batches) + (shapes(batches)[0],) * 2,
                scratch_shapes=[pltpu.VMEM((count, rows, width), BF16), pltpu.VMEM((count, rows, width), BF16),
                                pltpu.SemaphoreType.DMA((5,))],
                input_output_aliases={len(inputs) + n: 3 + n for n in range(len(kept))},
                compiler_params=params(), name="step",
            )(*inputs, *kept)
            kept = outs[3:]
            if hop + 1 < sections:
                local, to_below, to_above = outs[:3]
                sent.append((move(local, hop, 0), move(to_below, hop, -1), move(to_above, hop, 1)))
        received = sent
    local, to_below, to_above, g, dz = kept

    grad = pl.pallas_call(
        weight_kernel, out_shape=sds((3 * width, width), F32),
        compiler_params=params(), name="weights",
    )(x, agg, act, g, dz)

    total = sum_over_dom(grad, doms)
    from_upper = lax.ppermute(to_below, "dom", fall)
    from_lower = lax.ppermute(to_above, "dom", rise)
    grad_in = pl.pallas_call(
        finish_kernel, out_shape=sds((batches, rows, width), BF16),
        compiler_params=params(), name="finish",
    )(local, from_upper, from_lower, place)
    return grad_in[None], total[None, : 2 * width], total[None, 2 * width :]


def solution(mesh):
    return jax.shard_map(
        per_device,
        mesh=mesh,
        in_specs=(
            P("section", None, "dom", None),
            P(None, "dom", None),
            P("section", None, None),
            P("section", None, None),
            P(None, "dom"),
            P(None, "dom"),
            P(None, "dom"),
        ),
        out_specs=(
            P("section", None, "dom", None),
            P("section", None, None),
            P("section", None, None),
        ),
        check_vma=False,
    )
```

time: 353 us -> 107 us (0.30)
  other arithmetic: 118 us -> 1.01 us
  local copies, waits for them, and re-layouts: 56.6 us -> 5.19 us
  matrix products: 33.5 us -> 0 us
  starting transfers between devices: 58.3 us -> 31.1 us
  between operations: 14.1 us -> 1.16 us
  Pallas kernels: 0 us -> 11 us
  waiting for transfers between devices: 65.3 us -> 56.6 us
    scatter-add x21 -> x0, other arithmetic: 75.9 us -> none  [the longest x7 63.4 us: backward_part(): jax.ops.segment_sum(flat, nbr.reshape(-1), num_segments=rows + 2 * slots...]
    psum x1 -> x0, waiting for transfers between devices: 63.1 us -> none  [per_device(): sum_one, sum_two = lax.psum((acc_one, acc_two), 'dom')]
    ppermute x23 -> x27, waiting for transfers between devices: 2.21 us -> 56.6 us  [the longest x18 40.9 us: move(): return lax.ppermute(value, ('dom', 'section'), pairs)]
    gather x9 -> x0, local copies, waits for them, and re-layouts: 34.6 us -> none  [the longest x7 33.3 us: forward_part(): rows = jnp.take(ext, nbr, axis=1)]
    dot_general x35 -> x0, matrix products: 33.5 us -> none  [the longest x7 12.8 us: backward_part(): jnp.einsum('mrd,jd->mrj', g, w_two, preferred_element_type=jnp.float32)]
    ppermute x23 -> x27, starting transfers between devices: 58.3 us -> 31.1 us  [the longest x18 15.8 us: move(): return lax.ppermute(value, ('dom', 'section'), pairs)]
    select_n x23 -> x1, other arithmetic: 16.1 us -> 0.03 us  [sum_over_dom(): first = jnp.where(low, mine, other)]
    dynamic_update_slice x7 -> x0, other arithmetic: 11.5 us -> none  [tick(): grad_in = lax.dynamic_update_slice_in_dim(grad_in, kept, index, 0)]
  transfers between devices with their start and end apart: 24 -> 27, of which waited for: 2 -> 7; matrix products, arithmetic and copies ran while one was open for 23% -> 0% of each run, Pallas kernels for 0% -> 5%
where the time goes in v1:
time: 107 us; the launch traced here: 106 us
  waiting for transfers between devices  56.6 us (53%)
  starting transfers between devices  31.1 us (29%)
  Pallas kernels  11 us (10%)
  local copies, waits for them, and re-layouts  5.19 us (5%)
  between operations  1.16 us (1%)
    ppermute x18, waiting for transfers between devices, move(): return lax.ppermute(value, ('dom', 'section'), pairs)  40.9 us
    ppermute x18, starting transfers between devices, move(): return lax.ppermute(value, ('dom', 'section'), pairs)  15.8 us
    ppermute x5, waiting for transfers between devices, swap(): return lax.ppermute(value, 'dom', [(i, i ^ mask) for i in range(count)])  10.7 us
    pallas_call x8, Pallas kernels, per_device(): pl.pallas_call(make_step_kernel(hop, c * count, count, not kept), in_spec...  7.8 us
    ppermute x1, starting transfers between devices, per_device(): below = lax.ppermute(up, 'dom', rise)  4.51 us
    unnamed x26, local copies, waits for them, and re-layouts  4.36 us
    ppermute x1, waiting for transfers between devices, per_device(): above = lax.ppermute(down, 'dom', fall)  3.64 us
    ppermute x1, starting transfers between devices, per_device(): from_lower = lax.ppermute(to_above, 'dom', rise)  3.62 us
  transfers between devices with their start and end apart: 27, of which 7 were waited for; matrix products, arithmetic and copies ran while one was open for 0% of the time, Pallas kernels for 5%

profile of v1, /device:TPU:1, one launch (start us, length us, event | category | flops | bytes accessed | tf_op | source)
XLA Modules:
  0.0 106.0 jit_solution(15992329923502818632)
XLA Ops:
  1.3 1.0 copy-done.2
  2.7 4.5 %collective-permute-start = (bf16[4,32,256]{2,1,0:T(8,128)(2,1)S(1)}, bf16[4,32,256]{2,1,0:T(8,128)(2,1)S(1)}, u32[]{:S(2)}, u32[]{:S(2)}) collective-permute-start(bf16[4,32,256]{2,1,0:T(8,128)(2,1)S(1)} %get-tuple-element.69), channel_id=1, source_target_pairs={{0,4},{4,8},{8,12},{12,16},{16,20},{20,24},{24,28},{1,5},{5,9},{9,... | collective-permute-start | bytes 196616 | tf_op jit(solution)/shard_map/ppermute | solution.py:197
  7.2 1.9 %collective-permute-start.1 = (bf16[4,32,256]{2,1,0:T(8,128)(2,1)S(1)}, bf16[4,32,256]{2,1,0:T(8,128)(2,1)S(1)}, u32[]{:S(2)}, u32[]{:S(2)}) collective-permute-start(bf16[4,32,256]{2,1,0:T(8,128)(2,1)S(1)} %get-tuple-element.70), channel_id=1, source_target_pairs={{4,0},{8,4},{12,8},{16,12},{20,16},{24,20},{28,24},{5,1},{9,5},{13... | collective-permute-start | bytes 196616 | tf_op jit(solution)/shard_map/ppermute | solution.py:198
  9.2 3.6 %collective-permute-done.1.above_ref = bf16[4,32,256]{2,1,0:T(8,128)(2,1)S(1)} collective-permute-done((bf16[4,32,256]{2,1,0:T(8,128)(2,1)S(1)}, bf16[4,32,256]{2,1,0:T(8,128)(2,1)S(1)}, u32[]{:S(2)}, u32[]{:S(2)}) %collective-permute-start.1) | collective-permute-done | bytes 65568 | tf_op jit(solution)/shard_map/ppermute | solution.py:198
  12.8 1.0 copy-done.3
  13.9 1.2 %forward.1 = (f32[4,256,256]{2,1,0:T(8,128)S(1)}, bf16[4,256,256]{2,1,0:T(8,128)(2,1)S(1)}, bf16[4,256,256]{2,1,0:T(8,128)(2,1)S(1)}, bf16[256,256]{1,0:T(8,128)(2,1)S(1)}, bf16[64,256]{1,0:T(8,128)(2,1)S(1)}) custom-call(bf16[4,256,256]{2,1,0:T(8,128)(2,1)S(1)} %bitcast.27, bf16[4,32,256]{2,1,0:T(8,128)(2,1)S(1)} %collective-permute-done.below_ref, ...), custom_call_target="tpu_custom_call" | custom-call | tf_op jit(solution)/shard_map/forward/pallas_call | solution.py:200
  15.0 0.8 copy-done.6
  15.8 0.8 copy-done.8
  17.4 0.7 collective-permute-start.2
  20.9 0.7 collective-permute-start.11
  25.1 0.8 step.12
  25.9 1.3 %collective-permute-start.17 = (bf16[2,256,256]{2,1,0:T(8,128)(2,1)}, bf16[2,256,256]{2,1,0:T(8,128)(2,1)}, u32[]{:S(2)}, u32[]{:S(2)}) collective-permute-start(bf16[2,256,256]{2,1,0:T(8,128)(2,1)} %get-tuple-element.115), channel_id=1, source_target_pairs={{1,0},{5,4},{9,8},{13,12},{17,16},{21,20},{25,24},{29,28}} | collective-permute-start | bytes 786440 | tf_op jit(solution)/shard_map/ppermute | solution.py:211
  27.2 0.8 step.13
  28.0 1.3 %collective-permute-start.14 = (bf16[2,256,256]{2,1,0:T(8,128)(2,1)}, bf16[2,256,256]{2,1,0:T(8,128)(2,1)}, u32[]{:S(2)}, u32[]{:S(2)}) collective-permute-start(bf16[2,256,256]{2,1,0:T(8,128)(2,1)} %get-tuple-element.112), channel_id=1, source_target_pairs={{1,0},{5,4},{9,8},{13,12},{17,16},{21,20},{25,24},{29,28}} | collective-permute-start | bytes 786440 | tf_op jit(solution)/shard_map/ppermute | solution.py:211
  29.3 1.3 %collective-permute-start.18 = (bf16[2,32,256]{2,1,0:T(8,128)(2,1)S(1)}, bf16[2,32,256]{2,1,0:T(8,128)(2,1)S(1)}, u32[]{:S(2)}, u32[]{:S(2)}) collective-permute-start(bf16[2,32,256]{2,1,0:T(8,128)(2,1)S(1)} %get-tuple-element.116), channel_id=1, source_target_pairs={{5,0},{9,4},{13,8},{17,12},{21,16},{25,20},{29,24}} | collective-permute-start | bytes 98312 | tf_op jit(solution)/shard_map/ppermute | solution.py:211
  30.6 1.3 %collective-permute-start.19 = (bf16[2,32,256]{2,1,0:T(8,128)(2,1)S(1)}, bf16[2,32,256]{2,1,0:T(8,128)(2,1)S(1)}, u32[]{:S(2)}, u32[]{:S(2)}) collective-permute-start(bf16[2,32,256]{2,1,0:T(8,128)(2,1)S(1)} %get-tuple-element.117), channel_id=1, source_target_pairs={{1,4},{5,8},{9,12},{13,16},{17,20},{21,24},{25,28}} | collective-permute-start | bytes 98312 | tf_op jit(solution)/shard_map/ppermute | solution.py:211
  31.9 1.3 %collective-permute-start.15 = (bf16[2,32,256]{2,1,0:T(8,128)(2,1)}, bf16[2,32,256]{2,1,0:T(8,128)(2,1)S(1)}, u32[]{:S(2)}, u32[]{:S(2)}) collective-permute-start(bf16[2,32,256]{2,1,0:T(8,128)(2,1)} %get-tuple-element.113), channel_id=1, source_target_pairs={{5,0},{9,4},{13,8},{17,12},{21,16},{25,20},{29,24}} | collective-permute-start | bytes 98312 | tf_op jit(solution)/shard_map/ppermute | solution.py:211
  33.2 39.7 %collective-permute-done.18.refs_1_ = bf16[2,32,256]{2,1,0:T(8,128)(2,1)S(1)} collective-permute-done((bf16[2,32,256]{2,1,0:T(8,128)(2,1)S(1)}, bf16[2,32,256]{2,1,0:T(8,128)(2,1)S(1)}, u32[]{:S(2)}, u32[]{:S(2)}) %collective-permute-start.18) | collective-permute-done | bytes 32800 | tf_op jit(solution)/shard_map/ppermute | solution.py:211
  72.8 1.3 %collective-permute-start.16 = (bf16[2,32,256]{2,1,0:T(8,128)(2,1)}, bf16[2,32,256]{2,1,0:T(8,128)(2,1)S(1)}, u32[]{:S(2)}, u32[]{:S(2)}) collective-permute-start(bf16[2,32,256]{2,1,0:T(8,128)(2,1)} %get-tuple-element.114), channel_id=1, source_target_pairs={{1,4},{5,8},{9,12},{13,16},{17,20},{21,24},{25,28}} | collective-permute-start | bytes 98312 | tf_op jit(solution)/shard_map/ppermute | solution.py:211
  74.2 2.9 %step.14 = (bf16[2,256,256]{2,1,0:T(8,128)(2,1)}, bf16[2,32,256]{2,1,0:T(8,128)(2,1)}, bf16[2,32,256]{2,1,0:T(8,128)(2,1)}, bf16[4,256,256]{2,1,0:T(8,128)(2,1)S...) custom-call(s32[1]{0:T(128)} %bitcast.hop_ref, ...), custom_call_target="tpu_custom_call", output_to_operand_aliasing={{3}: (10, {}), {4}: (11, {}), {5}: (12, {}), {6}: (13, {}),... | custom-call | tf_op jit(solution)/shard_map/step/pallas_call | solution.py:225
  77.1 1.2 %collective-permute-done.16.refs_2_ = bf16[2,32,256]{2,1,0:T(8,128)(2,1)S(1)} collective-permute-done((bf16[2,32,256]{2,1,0:T(8,128)(2,1)}, bf16[2,32,256]{2,1,0:T(8,128)(2,1)S(1)}, u32[]{:S(2)}, u32[]{:S(2)}) %collective-permute-start.16) | collective-permute-done | bytes 32800 | tf_op jit(solution)/shard_map/ppermute | solution.py:211
  78.3 3.1 %step.15 = (bf16[2,256,256]{2,1,0:T(8,128)(2,1)}, bf16[2,32,256]{2,1,0:T(8,128)(2,1)}, bf16[2,32,256]{2,1,0:T(8,128)(2,1)}, bf16[4,256,256]{2,1,0:T(8,128)(2,1)S...) custom-call(s32[1]{0:T(128)} %bitcast.hop_ref, ...), custom_call_target="tpu_custom_call", output_to_operand_aliasing={{3}: (10, {}), {4}: (11, {}), {5}: (12, {}), {6}: (13, {}),... | custom-call | tf_op jit(solution)/shard_map/step/pallas_call | solution.py:225
  82.2 1.4 %collective-permute-done.22 = bf16[384,256]{1,0:T(8,128)(2,1)S(1)} collective-permute-done((bf16[384,256]{1,0:T(8,128)(2,1)S(1)}, bf16[384,256]{1,0:T(8,128)(2,1)S(1)}, u32[]{:S(2)}, u32[]{:S(2)}) %collective-permute-start.22) | collective-permute-done | bytes 196640 | tf_op jit(solution)/shard_map/ppermute | solution.py:151
  83.8 2.4 %collective-permute-start.24 = (bf16[384,256]{1,0:T(8,128)(2,1)S(1)}, bf16[384,256]{1,0:T(8,128)(2,1)S(1)}, u32[]{:S(2)}, u32[]{:S(2)}) collective-permute-start(bf16[384,256]{1,0:T(8,128)(2,1)S(1)} %add_convert_fusion.1), channel_id=1, source_target_pairs={{0,16},{4,20},{8,24},{12,28},{16,0},{20,4},{24,8},{28,12},{1,17},{... | collective-permute-start | bytes 589832 | tf_op jit(solution)/shard_map/ppermute | solution.py:151
  86.4 4.7 %collective-permute-done.25 = bf16[384,256]{1,0:T(8,128)(2,1)S(1)} collective-permute-done((bf16[384,256]{1,0:T(8,128)(2,1)S(1)}, bf16[384,256]{1,0:T(8,128)(2,1)S(1)}, u32[]{:S(2)}, u32[]{:S(2)}) %collective-permute-start.25) | collective-permute-done | bytes 196640 | tf_op jit(solution)/shard_map/ppermute | solution.py:151
  91.1 4.6 %collective-permute-done.24 = bf16[384,256]{1,0:T(8,128)(2,1)S(1)} collective-permute-done((bf16[384,256]{1,0:T(8,128)(2,1)S(1)}, bf16[384,256]{1,0:T(8,128)(2,1)S(1)}, u32[]{:S(2)}, u32[]{:S(2)}) %collective-permute-start.24) | collective-permute-done | bytes 196640 | tf_op jit(solution)/shard_map/ppermute | solution.py:151
  96.4 1.9 %collective-permute-start.20 = (bf16[4,32,256]{2,1,0:T(8,128)(2,1)S(1)}, bf16[4,32,256]{2,1,0:T(8,128)(2,1)S(1)}, u32[]{:S(2)}, u32[]{:S(2)}) collective-permute-start(bf16[4,32,256]{2,1,0:T(8,128)(2,1)S(1)} %get-tuple-element.129), channel_id=1, source_target_pairs={{4,0},{8,4},{12,8},{16,12},{20,16},{24,20},{28,24},{5,1},{9,5},{13... | collective-permute-start | bytes 196616 | tf_op jit(solution)/shard_map/ppermute | solution.py:249
  98.3 3.6 %collective-permute-start.21 = (bf16[4,32,256]{2,1,0:T(8,128)(2,1)S(1)}, bf16[4,32,256]{2,1,0:T(8,128)(2,1)S(1)}, u32[]{:S(2)}, u32[]{:S(2)}) collective-permute-start(bf16[4,32,256]{2,1,0:T(8,128)(2,1)S(1)} %get-tuple-element.130), channel_id=1, source_target_pairs={{0,4},{4,8},{8,12},{12,16},{16,20},{20,24},{24,28},{1,5},{5,9},{9,... | collective-permute-start | bytes 196616 | tf_op jit(solution)/shard_map/ppermute | solution.py:250
  101.9 1.3 %collective-permute-done.21.lower_ref = bf16[4,32,256]{2,1,0:T(8,128)(2,1)S(1)} collective-permute-done((bf16[4,32,256]{2,1,0:T(8,128)(2,1)S(1)}, bf16[4,32,256]{2,1,0:T(8,128)(2,1)S(1)}, u32[]{:S(2)}, u32[]{:S(2)}) %collective-permute-start.21) | collective-permute-done | bytes 65568 | tf_op jit(solution)/shard_map/ppermute | solution.py:250
  103.2 1.1 %finish.1 = bf16[4,256,256]{2,1,0:T(8,128)(2,1)} custom-call(bf16[4,256,256]{2,1,0:T(8,128)(2,1)S(1)} %get-tuple-element.128.loc_ref, bf16[4,32,256]{2,1,0:T(8,128)(2,1)S(1)} %collective-permute-done.20.upper_ref, bf16[4,32,256]{2,1,0:T(8,128)(2,1)S(1)} %collective-permute-done.21.lower_ref, bf16[256,64]{1,0:T(8,128)(2,1)S(1)} %get-tuple-element.82.refs_3_.place_ref), custom_call_target="tpu_custom_call" | custom-call | tf_op jit(solution)/shard_map/finish/pallas_call | solution.py:251
  104.3 0.7 convert_bitcast_fusion
  105.1 0.8 slice_bitcast_fusion
  (67 shorter events, 9.8 us)
Async XLA Ops:
  2.4 10.4 %copy-start = (bf16[1,512,256]{2,1,0:T(8,128)(2,1)S(1)}, bf16[1,512,256]{2,1,0:T(8,128)(2,1)}, u32[]{:S(2)}) copy-start(bf16[1,512,256]{2,1,0:T(8,128)(2,1)} %param.9) | copy-start | bytes 786436
  2.4 10.4 %copy-start.11 = (f32[6,256]{1,0:T(8,128)S(1)}, f32[6,256]{1,0:T(8,128)}, u32[]{:S(2)}) copy-start(f32[6,256]{1,0:T(8,128)} %coef_ref.1) | copy-start | bytes 18436
  2.7 10.1 %copy-start.10 = (s32[6,256]{1,0:T(8,128)S(1)}, s32[6,256]{1,0:T(8,128)}, u32[]{:S(2)}) copy-start(s32[6,256]{1,0:T(8,128)} %nbr_ref.1) | copy-start | bytes 18436
  2.7 6.5 %collective-permute-start = (bf16[4,32,256]{2,1,0:T(8,128)(2,1)S(1)}, bf16[4,32,256]{2,1,0:T(8,128)(2,1)S(1)}, u32[]{:S(2)}, u32[]{:S(2)}) collective-permute-start(bf16[4,32,256]{2,1,0:T(8,128)(2,1)S(1)} %get-tuple-element.69), channel_id=1, source_target_pairs={{0,4},{4,8},{8,12},{12,16},{16,20},{20,24},{24,28},{1,5},{5,9},{9,... | collective-permute-start | bytes 196616 | tf_op jit(solution)/shard_map/ppermute | solution.py:197
  7.2 5.6 %collective-permute-start.1 = (bf16[4,32,256]{2,1,0:T(8,128)(2,1)S(1)}, bf16[4,32,256]{2,1,0:T(8,128)(2,1)S(1)}, u32[]{:S(2)}, u32[]{:S(2)}) collective-permute-start(bf16[4,32,256]{2,1,0:T(8,128)(2,1)S(1)} %get-tuple-element.70), channel_id=1, source_target_pairs={{4,0},{8,4},{12,8},{16,12},{20,16},{24,20},{28,24},{5,1},{9,5},{13... | collective-permute-start | bytes 196616 | tf_op jit(solution)/shard_map/ppermute | solution.py:198
  16.7 4.1 %collective-permute-start.5 = (bf16[2,256,256]{2,1,0:T(8,128)(2,1)S(1)}, bf16[2,256,256]{2,1,0:T(8,128)(2,1)S(1)}, u32[]{:S(2)}, u32[]{:S(2)}) collective-permute-start(bf16[2,256,256]{2,1,0:T(8,128)(2,1)S(1)} %get-tuple-element.83), channel_id=1, source_target_pairs={{3,2},{7,6},{11,10},{15,14},{19,18},{23,22},{27,26},{31,30}} | collective-permute-start | bytes 786440 | tf_op jit(solution)/shard_map/ppermute | solution.py:211
  17.4 4.2 %collective-permute-start.2 = (bf16[2,256,256]{2,1,0:T(8,128)(2,1)S(1)}, bf16[2,256,256]{2,1,0:T(8,128)(2,1)S(1)}, u32[]{:S(2)}, u32[]{:S(2)}) collective-permute-start(bf16[2,256,256]{2,1,0:T(8,128)(2,1)S(1)} %get-tuple-element.79), channel_id=1, source_target_pairs={{3,2},{7,6},{11,10},{15,14},{19,18},{23,22},{27,26},{31,30}} | collective-permute-start | bytes 786440 | tf_op jit(solution)/shard_map/ppermute | solution.py:211
  18.1 2.0 %collective-permute-start.6 = (bf16[2,32,256]{2,1,0:T(8,128)(2,1)S(1)}, bf16[2,32,256]{2,1,0:T(8,128)(2,1)S(1)}, u32[]{:S(2)}, u32[]{:S(2)}) collective-permute-start(bf16[2,32,256]{2,1,0:T(8,128)(2,1)S(1)} %get-tuple-element.84), channel_id=1, source_target_pairs={{7,2},{11,6},{15,10},{19,14},{23,18},{27,22},{31,26}} | collective-permute-start | bytes 98312 | tf_op jit(solution)/shard_map/ppermute | solution.py:211
  18.8 2.0 %collective-permute-start.7 = (bf16[2,32,256]{2,1,0:T(8,128)(2,1)S(1)}, bf16[2,32,256]{2,1,0:T(8,128)(2,1)S(1)}, u32[]{:S(2)}, u32[]{:S(2)}) collective-permute-start(bf16[2,32,256]{2,1,0:T(8,128)(2,1)S(1)} %get-tuple-element.85), channel_id=1, source_target_pairs={{3,6},{7,10},{11,14},{15,18},{19,22},{23,26},{27,30}} | collective-permute-start | bytes 98312 | tf_op jit(solution)/shard_map/ppermute | solution.py:211
  19.4 2.1 %collective-permute-start.3 = (bf16[2,32,256]{2,1,0:T(8,128)(2,1)S(1)}, bf16[2,32,256]{2,1,0:T(8,128)(2,1)S(1)}, u32[]{:S(2)}, u32[]{:S(2)}) collective-permute-start(bf16[2,32,256]{2,1,0:T(8,128)(2,1)S(1)} %get-tuple-element.80), channel_id=1, source_target_pairs={{7,2},{11,6},{15,10},{19,14},{23,18},{27,22},{31,26}} | collective-permute-start | bytes 98312 | tf_op jit(solution)/shard_map/ppermute | solution.py:211
  20.1 1.5 %collective-permute-start.4 = (bf16[2,32,256]{2,1,0:T(8,128)(2,1)S(1)}, bf16[2,32,256]{2,1,0:T(8,128)(2,1)S(1)}, u32[]{:S(2)}, u32[]{:S(2)}) collective-permute-start(bf16[2,32,256]{2,1,0:T(8,128)(2,1)S(1)} %get-tuple-element.81), channel_id=1, source_target_pairs={{3,6},{7,10},{11,14},{15,18},{19,22},{23,26},{27,30}} | collective-permute-start | bytes 98312 | tf_op jit(solution)/shard_map/ppermute | solution.py:211
  20.9 4.2 %collective-permute-start.11 = (bf16[2,256,256]{2,1,0:T(8,128)(2,1)S(1)}, bf16[2,256,256]{2,1,0:T(8,128)(2,1)S(1)}, u32[]{:S(2)}, u32[]{:S(2)}) collective-permute-start(bf16[2,256,256]{2,1,0:T(8,128)(2,1)S(1)} %get-tuple-element.99), channel_id=1, source_target_pairs={{2,1},{6,5},{10,9},{14,13},{18,17},{22,21},{26,25},{30,29}} | collective-permute-start | bytes 786440 | tf_op jit(solution)/shard_map/ppermute | solution.py:211
  21.7 5.5 %collective-permute-start.8 = (bf16[2,256,256]{2,1,0:T(8,128)(2,1)S(1)}, bf16[2,256,256]{2,1,0:T(8,128)(2,1)S(1)}, u32[]{:S(2)}, u32[]{:S(2)}) collective-permute-start(bf16[2,256,256]{2,1,0:T(8,128)(2,1)S(1)} %get-tuple-element.96), channel_id=1, source_target_pairs={{2,1},{6,5},{10,9},{14,13},{18,17},{22,21},{26,25},{30,29}} | collective-permute-start | bytes 786440 | tf_op jit(solution)/shard_map/ppermute | solution.py:211
  22.4 2.0 %collective-permute-start.12 = (bf16[2,32,256]{2,1,0:T(8,128)(2,1)S(1)}, bf16[2,32,256]{2,1,0:T(8,128)(2,1)S(1)}, u32[]{:S(2)}, u32[]{:S(2)}) collective-permute-start(bf16[2,32,256]{2,1,0:T(8,128)(2,1)S(1)} %get-tuple-element.100), channel_id=1, source_target_pairs={{6,1},{10,5},{14,9},{18,13},{22,17},{26,21},{30,25}} | collective-permute-start | bytes 98312 | tf_op jit(solution)/shard_map/ppermute | solution.py:211
  23.0 2.0 %collective-permute-start.13 = (bf16[2,32,256]{2,1,0:T(8,128)(2,1)S(1)}, bf16[2,32,256]{2,1,0:T(8,128)(2,1)S(1)}, u32[]{:S(2)}, u32[]{:S(2)}) collective-permute-start(bf16[2,32,256]{2,1,0:T(8,128)(2,1)S(1)} %get-tuple-element.101), channel_id=1, source_target_pairs={{2,5},{6,9},{10,13},{14,17},{18,21},{22,25},{26,29}} | collective-permute-start | bytes 98312 | tf_op jit(solution)/shard_map/ppermute | solution.py:211
  23.7 3.5 %collective-permute-start.9 = (bf16[2,32,256]{2,1,0:T(8,128)(2,1)S(1)}, bf16[2,32,256]{2,1,0:T(8,128)(2,1)S(1)}, u32[]{:S(2)}, u32[]{:S(2)}) collective-permute-start(bf16[2,32,256]{2,1,0:T(8,128)(2,1)S(1)} %get-tuple-element.97), channel_id=1, source_target_pairs={{6,1},{10,5},{14,9},{18,13},{22,17},{26,21},{30,25}} | collective-permute-start | bytes 98312 | tf_op jit(solution)/shard_map/ppermute | solution.py:211
  24.4 2.8 %collective-permute-start.10 = (bf16[2,32,256]{2,1,0:T(8,128)(2,1)S(1)}, bf16[2,32,256]{2,1,0:T(8,128)(2,1)S(1)}, u32[]{:S(2)}, u32[]{:S(2)}) collective-permute-start(bf16[2,32,256]{2,1,0:T(8,128)(2,1)S(1)} %get-tuple-element.98), channel_id=1, source_target_pairs={{2,5},{6,9},{10,13},{14,17},{18,21},{22,25},{26,29}} | collective-permute-start | bytes 98312 | tf_op jit(solution)/shard_map/ppermute | solution.py:211
  25.9 48.3 %collective-permute-start.17 = (bf16[2,256,256]{2,1,0:T(8,128)(2,1)}, bf16[2,256,256]{2,1,0:T(8,128)(2,1)}, u32[]{:S(2)}, u32[]{:S(2)}) collective-permute-start(bf16[2,256,256]{2,1,0:T(8,128)(2,1)} %get-tuple-element.115), channel_id=1, source_target_pairs={{1,0},{5,4},{9,8},{13,12},{17,16},{21,20},{25,24},{29,28}} | collective-permute-start | bytes 786440 | tf_op jit(solution)/shard_map/ppermute | solution.py:211
  28.0 50.3 %collective-permute-start.14 = (bf16[2,256,256]{2,1,0:T(8,128)(2,1)}, bf16[2,256,256]{2,1,0:T(8,128)(2,1)}, u32[]{:S(2)}, u32[]{:S(2)}) collective-permute-start(bf16[2,256,256]{2,1,0:T(8,128)(2,1)} %get-tuple-element.112), channel_id=1, source_target_pairs={{1,0},{5,4},{9,8},{13,12},{17,16},{21,20},{25,24},{29,28}} | collective-permute-start | bytes 786440 | tf_op jit(solution)/shard_map/ppermute | solution.py:211
  29.3 43.6 %collective-permute-start.18 = (bf16[2,32,256]{2,1,0:T(8,128)(2,1)S(1)}, bf16[2,32,256]{2,1,0:T(8,128)(2,1)S(1)}, u32[]{:S(2)}, u32[]{:S(2)}) collective-permute-start(bf16[2,32,256]{2,1,0:T(8,128)(2,1)S(1)} %get-tuple-element.116), channel_id=1, source_target_pairs={{5,0},{9,4},{13,8},{17,12},{21,16},{25,20},{29,24}} | collective-permute-start | bytes 98312 | tf_op jit(solution)/shard_map/ppermute | solution.py:211
  30.6 43.6 %collective-permute-start.19 = (bf16[2,32,256]{2,1,0:T(8,128)(2,1)S(1)}, bf16[2,32,256]{2,1,0:T(8,128)(2,1)S(1)}, u32[]{:S(2)}, u32[]{:S(2)}) collective-permute-start(bf16[2,32,256]{2,1,0:T(8,128)(2,1)S(1)} %get-tuple-element.117), channel_id=1, source_target_pairs={{1,4},{5,8},{9,12},{13,16},{17,20},{21,24},{25,28}} | collective-permute-start | bytes 98312 | tf_op jit(solution)/shard_map/ppermute | solution.py:211
  31.9 45.2 %collective-permute-start.15 = (bf16[2,32,256]{2,1,0:T(8,128)(2,1)}, bf16[2,32,256]{2,1,0:T(8,128)(2,1)S(1)}, u32[]{:S(2)}, u32[]{:S(2)}) collective-permute-start(bf16[2,32,256]{2,1,0:T(8,128)(2,1)} %get-tuple-element.113), channel_id=1, source_target_pairs={{5,0},{9,4},{13,8},{17,12},{21,16},{25,20},{29,24}} | collective-permute-start | bytes 98312 | tf_op jit(solution)/shard_map/ppermute | solution.py:211
  72.8 5.5 %collective-permute-start.16 = (bf16[2,32,256]{2,1,0:T(8,128)(2,1)}, bf16[2,32,256]{2,1,0:T(8,128)(2,1)S(1)}, u32[]{:S(2)}, u32[]{:S(2)}) collective-permute-start(bf16[2,32,256]{2,1,0:T(8,128)(2,1)} %get-tuple-element.114), channel_id=1, source_target_pairs={{1,4},{5,8},{9,12},{13,16},{17,20},{21,24},{25,28}} | collective-permute-start | bytes 98312 | tf_op jit(solution)/shard_map/ppermute | solution.py:211
  78.3 3.1 %copy-start.7 = (bf16[4,256,256]{2,1,0:T(8,128)(2,1)S(1)}, bf16[4,256,256]{2,1,0:T(8,128)(2,1)}, u32[]{:S(2)}) copy-start(bf16[4,256,256]{2,1,0:T(8,128)(2,1)} %copy-done.6) | copy-start | bytes 1572868
  78.3 3.1 %copy-start.9 = (bf16[4,256,256]{2,1,0:T(8,128)(2,1)S(1)}, bf16[4,256,256]{2,1,0:T(8,128)(2,1)}, u32[]{:S(2)}) copy-start(bf16[4,256,256]{2,1,0:T(8,128)(2,1)} %copy-done.8) | copy-start | bytes 1572868
  82.1 1.5 %collective-permute-start.22 = (bf16[384,256]{1,0:T(8,128)(2,1)S(1)}, bf16[384,256]{1,0:T(8,128)(2,1)S(1)}, u32[]{:S(2)}, u32[]{:S(2)}) collective-permute-start(bf16[384,256]{1,0:T(8,128)(2,1)S(1)} %select_convert_fusion), channel_id=1, source_target_pairs={{0,4},{4,0},{8,12},{12,8},{16,20},{20,16},{24,28},{28,24},{1,5},{5... | collective-permute-start | bytes 589832 | tf_op jit(solution)/shard_map/ppermute | solution.py:151
  83.7 7.4 %collective-permute-start.25 = (bf16[384,256]{1,0:T(8,128)(2,1)S(1)}, bf16[384,256]{1,0:T(8,128)(2,1)S(1)}, u32[]{:S(2)}, u32[]{:S(2)}) collective-permute-start(bf16[384,256]{1,0:T(8,128)(2,1)S(1)} %add_convert_fusion.1), channel_id=1, source_target_pairs={{0,24},{4,28},{8,16},{12,20},{16,8},{20,12},{24,0},{28,4},{1,25},{... | collective-permute-start | bytes 589832 | tf_op jit(solution)/shard_map/ppermute | solution.py:151
  83.8 11.9 %collective-permute-start.24 = (bf16[384,256]{1,0:T(8,128)(2,1)S(1)}, bf16[384,256]{1,0:T(8,128)(2,1)S(1)}, u32[]{:S(2)}, u32[]{:S(2)}) collective-permute-start(bf16[384,256]{1,0:T(8,128)(2,1)S(1)} %add_convert_fusion.1), channel_id=1, source_target_pairs={{0,16},{4,20},{8,24},{12,28},{16,0},{20,4},{24,8},{28,12},{1,17},{... | collective-permute-start | bytes 589832 | tf_op jit(solution)/shard_map/ppermute | solution.py:151
  86.1 9.6 %collective-permute-start.23 = (bf16[384,256]{1,0:T(8,128)(2,1)S(1)}, bf16[384,256]{1,0:T(8,128)(2,1)S(1)}, u32[]{:S(2)}, u32[]{:S(2)}) collective-permute-start(bf16[384,256]{1,0:T(8,128)(2,1)S(1)} %add_convert_fusion.1), channel_id=1, source_target_pairs={{0,8},{4,12},{8,0},{12,4},{16,24},{20,28},{24,16},{28,20},{1,9},{5... | collective-permute-start | bytes 589832 | tf_op jit(solution)/shard_map/ppermute | solution.py:151
  95.8 8.5 %collective-permute-start.26 = (bf16[384,256]{1,0:T(8,128)(2,1)S(1)}, bf16[384,256]{1,0:T(8,128)(2,1)S(1)}, u32[]{:S(2)}, u32[]{:S(2)}) collective-permute-start(bf16[384,256]{1,0:T(8,128)(2,1)S(1)} %add_convert_fusion), channel_id=1, source_target_pairs={{0,4},{4,0},{8,12},{12,8},{16,20},{20,16},{24,28},{28,24},{1,5},{5... | collective-permute-start | bytes 589832 | tf_op jit(solution)/shard_map/ppermute | solution.py:151
  96.4 5.6 %collective-permute-start.20 = (bf16[4,32,256]{2,1,0:T(8,128)(2,1)S(1)}, bf16[4,32,256]{2,1,0:T(8,128)(2,1)S(1)}, u32[]{:S(2)}, u32[]{:S(2)}) collective-permute-start(bf16[4,32,256]{2,1,0:T(8,128)(2,1)S(1)} %get-tuple-element.129), channel_id=1, source_target_pairs={{4,0},{8,4},{12,8},{16,12},{20,16},{24,20},{28,24},{5,1},{9,5},{13... | collective-permute-start | bytes 196616 | tf_op jit(solution)/shard_map/ppermute | solution.py:249
  98.3 4.9 %collective-permute-start.21 = (bf16[4,32,256]{2,1,0:T(8,128)(2,1)S(1)}, bf16[4,32,256]{2,1,0:T(8,128)(2,1)S(1)}, u32[]{:S(2)}, u32[]{:S(2)}) collective-permute-start(bf16[4,32,256]{2,1,0:T(8,128)(2,1)S(1)} %get-tuple-element.130), channel_id=1, source_target_pairs={{0,4},{4,8},{8,12},{12,16},{16,20},{20,24},{24,28},{1,5},{5,9},{9,... | collective-permute-start | bytes 196616 | tf_op jit(solution)/shard_map/ppermute | solution.py:250
  (8 other events, 13.0 us)

commit v2 on v1

--- a/solution.py
+++ b/solution.py
@@ -8,6 +8,7 @@
 F32 = jnp.float32
 BF16 = jnp.bfloat16
 CHUNKS = 2
+STEP_FLOPS = 10**11
 
 
 def dot(a, b, dims=((1,), (0,))):
@@ -19,7 +20,7 @@
 
 
 def params():
-    return pltpu.CompilerParams(vmem_limit_bytes=48 * 1024 * 1024)
+    return pltpu.CompilerParams(vmem_limit_bytes=16 * 1024 * 1024)
 
 
 def pack_kernel(x_ref, send_ref, place_ref, up_ref, down_ref):
@@ -231,6 +232,7 @@
                 scratch_shapes=[pltpu.VMEM((count, rows, width), BF16), pltpu.VMEM((count, rows, width), BF16),
                                 pltpu.SemaphoreType.DMA((5,))],
                 input_output_aliases={len(inputs) + n: 3 + n for n in range(len(kept))},
+                cost_estimate=pl.CostEstimate(flops=STEP_FLOPS, bytes_accessed=1 << 20, transcendentals=0),
                 compiler_params=params(), name="step",
             )(*inputs, *kept)
             kept = outs[3:]

time: 107 us -> 90 us (0.84)
  the two profiles are of different devices: /device:TPU:1 before, /device:TPU:4 now
where the time goes in v2:
time: 90 us; the launch traced here: 89.4 us
  waiting for transfers between devices  44.6 us (50%)
  starting transfers between devices  31.7 us (35%)
  Pallas kernels  7.48 us (8%)
  local copies, waits for them, and re-layouts  3.51 us (4%)
  between operations  1.13 us (1%)
  other arithmetic  1.01 us (1%)
    ppermute x18, waiting for transfers between devices, move(): return lax.ppermute(value, ('dom', 'section'), pairs)  28 us
    ppermute x18, starting transfers between devices, move(): return lax.ppermute(value, ('dom', 'section'), pairs)  15.8 us
    ppermute x5, waiting for transfers between devices, swap(): return lax.ppermute(value, 'dom', [(i, i ^ mask) for i in range(count)])  10.2 us
    ppermute x1, waiting for transfers between devices, per_device(): from_lower = lax.ppermute(to_above, 'dom', rise)  4.54 us
    ppermute x1, starting transfers between devices, per_device(): above = lax.ppermute(down, 'dom', fall)  4.54 us
    pallas_call x8, Pallas kernels, per_device(): pl.pallas_call(make_step_kernel(hop, c * count, count, not kept), in_spec...  4.32 us
    ppermute x1, starting transfers between devices, per_device(): from_upper = lax.ppermute(to_below, 'dom', fall)  3.81 us
    ppermute x5, starting transfers between devices, swap(): return lax.ppermute(value, 'dom', [(i, i ^ mask) for i in range(count)])  3.77 us
  transfers between devices with their start and end apart: 27, of which 10 were waited for; matrix products, arithmetic and copies ran while one was open for 0% of the time, Pallas kernels for 4%

profile of v2, /device:TPU:4, one launch (start us, length us, event | category | flops | bytes accessed | tf_op | source)
XLA Modules:
  0.0 89.4 jit_solution(8845065122082286941)
XLA Ops:
  1.3 1.0 %copy-done = bf16[1,4,256,256]{3,2,1,0:T(8,128)(2,1)S(1)} copy-done((bf16[1,4,256,256]{3,2,1,0:T(8,128)(2,1)S(1)}, bf16[1,4,256,256]{3,2,1,0:T(8,128)(2,1)}, u32[]{:S(2)}) %copy-start) | copy-done | bytes 524312
  2.7 1.9 %collective-permute-start = (bf16[4,32,256]{2,1,0:T(8,128)(2,1)S(1)}, bf16[4,32,256]{2,1,0:T(8,128)(2,1)S(1)}, u32[]{:S(2)}, u32[]{:S(2)}) collective-permute-start(bf16[4,32,256]{2,1,0:T(8,128)(2,1)S(1)} %get-tuple-element.69), channel_id=1, source_target_pairs={{0,4},{4,8},{8,12},{12,16},{16,20},{20,24},{24,28},{1,5},{5,9},{9,... | collective-permute-start | bytes 196616 | tf_op jit(solution)/shard_map/ppermute | solution.py:198
  4.6 4.5 %collective-permute-start.1 = (bf16[4,32,256]{2,1,0:T(8,128)(2,1)S(1)}, bf16[4,32,256]{2,1,0:T(8,128)(2,1)S(1)}, u32[]{:S(2)}, u32[]{:S(2)}) collective-permute-start(bf16[4,32,256]{2,1,0:T(8,128)(2,1)S(1)} %get-tuple-element.70), channel_id=1, source_target_pairs={{4,0},{8,4},{12,8},{16,12},{20,16},{24,20},{28,24},{5,1},{9,5},{13... | collective-permute-start | bytes 196616 | tf_op jit(solution)/shard_map/ppermute | solution.py:199
  9.2 1.8 %collective-permute-done.1.above_ref = bf16[4,32,256]{2,1,0:T(8,128)(2,1)S(1)} collective-permute-done((bf16[4,32,256]{2,1,0:T(8,128)(2,1)S(1)}, bf16[4,32,256]{2,1,0:T(8,128)(2,1)S(1)}, u32[]{:S(2)}, u32[]{:S(2)}) %collective-permute-start.1) | collective-permute-done | bytes 65568 | tf_op jit(solution)/shard_map/ppermute | solution.py:199
  11.1 0.9 %copy-done.2 = bf16[1,512,256]{2,1,0:T(8,128)(2,1)S(1)} copy-done((bf16[1,512,256]{2,1,0:T(8,128)(2,1)S(1)}, bf16[1,512,256]{2,1,0:T(8,128)(2,1)}, u32[]{:S(2)}) %copy-start.2) | copy-done | bytes 262168
  12.0 1.2 %forward.1 = (f32[4,256,256]{2,1,0:T(8,128)S(1)}, bf16[4,256,256]{2,1,0:T(8,128)(2,1)S(1)}, bf16[4,256,256]{2,1,0:T(8,128)(2,1)S(1)}, bf16[256,256]{1,0:T(8,128)(2,1)S(1)}, bf16[64,256]{1,0:T(8,128)(2,1)S(1)}) custom-call(bf16[4,256,256]{2,1,0:T(8,128)(2,1)S(1)} %bitcast.10, bf16[4,32,256]{2,1,0:T(8,128)(2,1)S(1)} %collective-permute-done.below_ref, ...), custom_call_target="tpu_custom_call" | custom-call | tf_op jit(solution)/shard_map/forward/pallas_call | solution.py:201
  14.6 0.7 collective-permute-start.5
  16.7 0.7 collective-permute-start.2
  18.8 0.7 collective-permute-start.11
  21.0 0.7 collective-permute-start.8
  21.7 1.3 %collective-permute-start.18 = (bf16[2,32,256]{2,1,0:T(8,128)(2,1)S(1)}, bf16[2,32,256]{2,1,0:T(8,128)(2,1)S(1)}, u32[]{:S(2)}, u32[]{:S(2)}) collective-permute-start(bf16[2,32,256]{2,1,0:T(8,128)(2,1)S(1)} %get-tuple-element.116), channel_id=1, source_target_pairs={{5,0},{9,4},{13,8},{17,12},{21,16},{25,20},{29,24}} | collective-permute-start | bytes 98312 | tf_op jit(solution)/shard_map/ppermute | solution.py:212
  23.0 1.3 %collective-permute-start.19 = (bf16[2,32,256]{2,1,0:T(8,128)(2,1)S(1)}, bf16[2,32,256]{2,1,0:T(8,128)(2,1)S(1)}, u32[]{:S(2)}, u32[]{:S(2)}) collective-permute-start(bf16[2,32,256]{2,1,0:T(8,128)(2,1)S(1)} %get-tuple-element.117), channel_id=1, source_target_pairs={{1,4},{5,8},{9,12},{13,16},{17,20},{21,24},{25,28}} | collective-permute-start | bytes 98312 | tf_op jit(solution)/shard_map/ppermute | solution.py:212
  24.4 1.3 %collective-permute-start.17 = (bf16[2,256,256]{2,1,0:T(8,128)(2,1)S(1)}, bf16[2,256,256]{2,1,0:T(8,128)(2,1)S(1)}, u32[]{:S(2)}, u32[]{:S(2)}) collective-permute-start(bf16[2,256,256]{2,1,0:T(8,128)(2,1)S(1)} %get-tuple-element.115), channel_id=1, source_target_pairs={{1,0},{5,4},{9,8},{13,12},{17,16},{21,20},{25,24},{29,28}} | collective-permute-start | bytes 786440 | tf_op jit(solution)/shard_map/ppermute | solution.py:212
  25.8 1.3 %collective-permute-start.15 = (bf16[2,32,256]{2,1,0:T(8,128)(2,1)S(1)}, bf16[2,32,256]{2,1,0:T(8,128)(2,1)S(1)}, u32[]{:S(2)}, u32[]{:S(2)}) collective-permute-start(bf16[2,32,256]{2,1,0:T(8,128)(2,1)S(1)} %get-tuple-element.113), channel_id=1, source_target_pairs={{5,0},{9,4},{13,8},{17,12},{21,16},{25,20},{29,24}} | collective-permute-start | bytes 98312 | tf_op jit(solution)/shard_map/ppermute | solution.py:212
  27.1 1.3 %collective-permute-start.16 = (bf16[2,32,256]{2,1,0:T(8,128)(2,1)S(1)}, bf16[2,32,256]{2,1,0:T(8,128)(2,1)S(1)}, u32[]{:S(2)}, u32[]{:S(2)}) collective-permute-start(bf16[2,32,256]{2,1,0:T(8,128)(2,1)S(1)} %get-tuple-element.114), channel_id=1, source_target_pairs={{1,4},{5,8},{9,12},{13,16},{17,20},{21,24},{25,28}} | collective-permute-start | bytes 98312 | tf_op jit(solution)/shard_map/ppermute | solution.py:212
  28.4 13.5 %collective-permute-done.18.refs_1_ = bf16[2,32,256]{2,1,0:T(8,128)(2,1)S(1)} collective-permute-done((bf16[2,32,256]{2,1,0:T(8,128)(2,1)S(1)}, bf16[2,32,256]{2,1,0:T(8,128)(2,1)S(1)}, u32[]{:S(2)}, u32[]{:S(2)}) %collective-permute-start.18) | collective-permute-done | bytes 32800 | tf_op jit(solution)/shard_map/ppermute | solution.py:212
  41.9 1.3 %collective-permute-start.14 = (bf16[2,256,256]{2,1,0:T(8,128)(2,1)S(1)}, bf16[2,256,256]{2,1,0:T(8,128)(2,1)S(1)}, u32[]{:S(2)}, u32[]{:S(2)}) collective-permute-start(bf16[2,256,256]{2,1,0:T(8,128)(2,1)S(1)} %get-tuple-element.112), channel_id=1, source_target_pairs={{1,0},{5,4},{9,8},{13,12},{17,16},{21,20},{25,24},{29,28}} | collective-permute-start | bytes 786440 | tf_op jit(solution)/shard_map/ppermute | solution.py:212
  43.2 4.6 %collective-permute-done.19.refs_2_ = bf16[2,32,256]{2,1,0:T(8,128)(2,1)S(1)} collective-permute-done((bf16[2,32,256]{2,1,0:T(8,128)(2,1)S(1)}, bf16[2,32,256]{2,1,0:T(8,128)(2,1)S(1)}, u32[]{:S(2)}, u32[]{:S(2)}) %collective-permute-start.19) | collective-permute-done | bytes 32800 | tf_op jit(solution)/shard_map/ppermute | solution.py:212
  47.7 5.5 %collective-permute-done.17.refs_0_ = bf16[2,256,256]{2,1,0:T(8,128)(2,1)S(1)} collective-permute-done((bf16[2,256,256]{2,1,0:T(8,128)(2,1)S(1)}, bf16[2,256,256]{2,1,0:T(8,128)(2,1)S(1)}, u32[]{:S(2)}, u32[]{:S(2)}) %collective-permute-start.17) | collective-permute-done | bytes 262176 | tf_op jit(solution)/shard_map/ppermute | solution.py:212
  53.3 2.0 %step.14 = (bf16[2,256,256]{2,1,0:T(8,128)(2,1)}, bf16[2,32,256]{2,1,0:T(8,128)(2,1)}, bf16[2,32,256]{2,1,0:T(8,128)(2,1)}, bf16[4,256,256]{2,1,0:T(8,128)(2,1)S...) custom-call(s32[1]{0:T(128)} %bitcast.hop_ref, ...), custom_call_target="tpu_custom_call", output_to_operand_aliasing={{3}: (10, {}), {4}: (11, {}), {5}: (12, {}), {6}: (13, {}),... | custom-call | flops 99999997952 | bytes 1048576 | tf_op jit(solution)/shard_map/step/pallas_call | solution.py:226
  55.5 4.1 %collective-permute-done.14.refs_0_ = bf16[2,256,256]{2,1,0:T(8,128)(2,1)S(1)} collective-permute-done((bf16[2,256,256]{2,1,0:T(8,128)(2,1)S(1)}, bf16[2,256,256]{2,1,0:T(8,128)(2,1)S(1)}, u32[]{:S(2)}, u32[]{:S(2)}) %collective-permute-start.14) | collective-permute-done | bytes 262176 | tf_op jit(solution)/shard_map/ppermute | solution.py:212
  59.6 2.0 %step.15 = (bf16[2,256,256]{2,1,0:T(8,128)(2,1)}, bf16[2,32,256]{2,1,0:T(8,128)(2,1)}, bf16[2,32,256]{2,1,0:T(8,128)(2,1)}, bf16[4,256,256]{2,1,0:T(8,128)(2,1)S...) custom-call(s32[1]{0:T(128)} %bitcast.hop_ref, ...), custom_call_target="tpu_custom_call", output_to_operand_aliasing={{3}: (10, {}), {4}: (11, {}), {5}: (12, {}), {6}: (13, {}),... | custom-call | flops 99999997952 | bytes 1048576 | tf_op jit(solution)/shard_map/step/pallas_call | solution.py:226
  62.3 1.4 %collective-permute-done.22 = bf16[384,256]{1,0:T(8,128)(2,1)S(1)} collective-permute-done((bf16[384,256]{1,0:T(8,128)(2,1)S(1)}, bf16[384,256]{1,0:T(8,128)(2,1)S(1)}, u32[]{:S(2)}, u32[]{:S(2)}) %collective-permute-start.22) | collective-permute-done | bytes 196640 | tf_op jit(solution)/shard_map/ppermute | solution.py:152
  63.8 3.0 %collective-permute-start.25 = (bf16[384,256]{1,0:T(8,128)(2,1)S(1)}, bf16[384,256]{1,0:T(8,128)(2,1)S(1)}, u32[]{:S(2)}, u32[]{:S(2)}) collective-permute-start(bf16[384,256]{1,0:T(8,128)(2,1)S(1)} %add_convert_fusion.1), channel_id=1, source_target_pairs={{0,24},{4,28},{8,16},{12,20},{16,8},{20,12},{24,0},{28,4},{1,25},{... | collective-permute-start | bytes 589832 | tf_op jit(solution)/shard_map/ppermute | solution.py:152
  67.5 5.1 %collective-permute-done.25 = bf16[384,256]{1,0:T(8,128)(2,1)S(1)} collective-permute-done((bf16[384,256]{1,0:T(8,128)(2,1)S(1)}, bf16[384,256]{1,0:T(8,128)(2,1)S(1)}, u32[]{:S(2)}, u32[]{:S(2)}) %collective-permute-start.25) | collective-permute-done | bytes 196640 | tf_op jit(solution)/shard_map/ppermute | solution.py:152
  72.6 3.7 %collective-permute-done.24 = bf16[384,256]{1,0:T(8,128)(2,1)S(1)} collective-permute-done((bf16[384,256]{1,0:T(8,128)(2,1)S(1)}, bf16[384,256]{1,0:T(8,128)(2,1)S(1)}, u32[]{:S(2)}, u32[]{:S(2)}) %collective-permute-start.24) | collective-permute-done | bytes 196640 | tf_op jit(solution)/shard_map/ppermute | solution.py:152
  76.4 3.8 %collective-permute-start.20 = (bf16[4,32,256]{2,1,0:T(8,128)(2,1)S(1)}, bf16[4,32,256]{2,1,0:T(8,128)(2,1)S(1)}, u32[]{:S(2)}, u32[]{:S(2)}) collective-permute-start(bf16[4,32,256]{2,1,0:T(8,128)(2,1)S(1)} %get-tuple-element.129), channel_id=1, source_target_pairs={{4,0},{8,4},{12,8},{16,12},{20,16},{24,20},{28,24},{5,1},{9,5},{13... | collective-permute-start | bytes 196616 | tf_op jit(solution)/shard_map/ppermute | solution.py:251
  80.2 1.9 %collective-permute-start.21 = (bf16[4,32,256]{2,1,0:T(8,128)(2,1)S(1)}, bf16[4,32,256]{2,1,0:T(8,128)(2,1)S(1)}, u32[]{:S(2)}, u32[]{:S(2)}) collective-permute-start(bf16[4,32,256]{2,1,0:T(8,128)(2,1)S(1)} %get-tuple-element.130), channel_id=1, source_target_pairs={{0,4},{4,8},{8,12},{12,16},{16,20},{20,24},{24,28},{1,5},{5,9},{9,... | collective-permute-start | bytes 196616 | tf_op jit(solution)/shard_map/ppermute | solution.py:252
  82.2 4.5 %collective-permute-done.21.lower_ref = bf16[4,32,256]{2,1,0:T(8,128)(2,1)S(1)} collective-permute-done((bf16[4,32,256]{2,1,0:T(8,128)(2,1)S(1)}, bf16[4,32,256]{2,1,0:T(8,128)(2,1)S(1)}, u32[]{:S(2)}, u32[]{:S(2)}) %collective-permute-start.21) | collective-permute-done | bytes 65568 | tf_op jit(solution)/shard_map/ppermute | solution.py:252
  86.7 1.1 %finish.1 = bf16[4,256,256]{2,1,0:T(8,128)(2,1)} custom-call(bf16[4,256,256]{2,1,0:T(8,128)(2,1)S(1)} %get-tuple-element.128.loc_ref, bf16[4,32,256]{2,1,0:T(8,128)(2,1)S(1)} %collective-permute-done.20.upper_ref, bf16[4,32,256]{2,1,0:T(8,128)(2,1)S(1)} %collective-permute-done.21.lower_ref, bf16[256,64]{1,0:T(8,128)(2,1)S(1)} %get-tuple-element.82.refs_3_.place_ref), custom_call_target="tpu_custom_call" | custom-call | tf_op jit(solution)/shard_map/finish/pallas_call | solution.py:253
  87.8 0.7 convert_bitcast_fusion
  88.6 0.8 slice_bitcast_fusion
  (59 shorter events, 8.7 us)
Async XLA Ops:
  2.4 8.7 %copy-start.1 = (bf16[1,4,256,256]{3,2,1,0:T(8,128)(2,1)S(1)}, bf16[1,4,256,256]{3,2,1,0:T(8,128)(2,1)}, u32[]{:S(2)}) copy-start(bf16[1,4,256,256]{3,2,1,0:T(8,128)(2,1)} %param.7) | copy-start | bytes 1572868
  2.7 6.5 %collective-permute-start = (bf16[4,32,256]{2,1,0:T(8,128)(2,1)S(1)}, bf16[4,32,256]{2,1,0:T(8,128)(2,1)S(1)}, u32[]{:S(2)}, u32[]{:S(2)}) collective-permute-start(bf16[4,32,256]{2,1,0:T(8,128)(2,1)S(1)} %get-tuple-element.69), channel_id=1, source_target_pairs={{0,4},{4,8},{8,12},{12,16},{16,20},{20,24},{24,28},{1,5},{5,9},{9,... | collective-permute-start | bytes 196616 | tf_op jit(solution)/shard_map/ppermute | solution.py:198
  4.6 6.4 %collective-permute-start.1 = (bf16[4,32,256]{2,1,0:T(8,128)(2,1)S(1)}, bf16[4,32,256]{2,1,0:T(8,128)(2,1)S(1)}, u32[]{:S(2)}, u32[]{:S(2)}) collective-permute-start(bf16[4,32,256]{2,1,0:T(8,128)(2,1)S(1)} %get-tuple-element.70), channel_id=1, source_target_pairs={{4,0},{8,4},{12,8},{16,12},{20,16},{24,20},{28,24},{5,1},{9,5},{13... | collective-permute-start | bytes 196616 | tf_op jit(solution)/shard_map/ppermute | solution.py:199
  9.2 1.9 %copy-start.5 = (f32[6,256]{1,0:T(8,128)S(1)}, f32[6,256]{1,0:T(8,128)}, u32[]{:S(2)}) copy-start(f32[6,256]{1,0:T(8,128)} %coef_ref.1) | copy-start | bytes 18436
  9.2 1.9 %copy-start.4 = (s32[6,256]{1,0:T(8,128)S(1)}, s32[6,256]{1,0:T(8,128)}, u32[]{:S(2)}) copy-start(s32[6,256]{1,0:T(8,128)} %nbr_ref.1) | copy-start | bytes 18436
  12.0 1.2 %copy-start.7 = (bf16[4,256,256]{2,1,0:T(8,128)(2,1)S(1)}, bf16[4,256,256]{2,1,0:T(8,128)(2,1)}, u32[]{:S(2)}) copy-start(bf16[4,256,256]{2,1,0:T(8,128)(2,1)} %refs_0_.3) | copy-start | bytes 1572868
  12.0 1.2 %copy-start.8 = (bf16[1,256,256]{2,1,0:T(8,128)(2,1)S(1)}, bf16[1,256,256]{2,1,0:T(8,128)(2,1)}, u32[]{:S(2)}) copy-start(bf16[1,256,256]{2,1,0:T(8,128)(2,1)} %param.10) | copy-start | bytes 393220
  13.3 3.4 %collective-permute-start.6 = (bf16[2,32,256]{2,1,0:T(8,128)(2,1)S(1)}, bf16[2,32,256]{2,1,0:T(8,128)(2,1)S(1)}, u32[]{:S(2)}, u32[]{:S(2)}) collective-permute-start(bf16[2,32,256]{2,1,0:T(8,128)(2,1)S(1)} %get-tuple-element.84), channel_id=1, source_target_pairs={{7,2},{11,6},{15,10},{19,14},{23,18},{27,22},{31,26}} | collective-permute-start | bytes 98312 | tf_op jit(solution)/shard_map/ppermute | solution.py:212
  13.9 3.5 %collective-permute-start.7 = (bf16[2,32,256]{2,1,0:T(8,128)(2,1)S(1)}, bf16[2,32,256]{2,1,0:T(8,128)(2,1)S(1)}, u32[]{:S(2)}, u32[]{:S(2)}) collective-permute-start(bf16[2,32,256]{2,1,0:T(8,128)(2,1)S(1)} %get-tuple-element.85), channel_id=1, source_target_pairs={{3,6},{7,10},{11,14},{15,18},{19,22},{23,26},{27,30}} | collective-permute-start | bytes 98312 | tf_op jit(solution)/shard_map/ppermute | solution.py:212
  14.6 2.8 %collective-permute-start.5 = (bf16[2,256,256]{2,1,0:T(8,128)(2,1)S(1)}, bf16[2,256,256]{2,1,0:T(8,128)(2,1)S(1)}, u32[]{:S(2)}, u32[]{:S(2)}) collective-permute-start(bf16[2,256,256]{2,1,0:T(8,128)(2,1)S(1)} %get-tuple-element.83), channel_id=1, source_target_pairs={{3,2},{7,6},{11,10},{15,14},{19,18},{23,22},{27,26},{31,30}} | collective-permute-start | bytes 786440 | tf_op jit(solution)/shard_map/ppermute | solution.py:212
  15.4 3.5 %collective-permute-start.3 = (bf16[2,32,256]{2,1,0:T(8,128)(2,1)S(1)}, bf16[2,32,256]{2,1,0:T(8,128)(2,1)S(1)}, u32[]{:S(2)}, u32[]{:S(2)}) collective-permute-start(bf16[2,32,256]{2,1,0:T(8,128)(2,1)S(1)} %get-tuple-element.80), channel_id=1, source_target_pairs={{7,2},{11,6},{15,10},{19,14},{23,18},{27,22},{31,26}} | collective-permute-start | bytes 98312 | tf_op jit(solution)/shard_map/ppermute | solution.py:212
  16.0 3.5 %collective-permute-start.4 = (bf16[2,32,256]{2,1,0:T(8,128)(2,1)S(1)}, bf16[2,32,256]{2,1,0:T(8,128)(2,1)S(1)}, u32[]{:S(2)}, u32[]{:S(2)}) collective-permute-start(bf16[2,32,256]{2,1,0:T(8,128)(2,1)S(1)} %get-tuple-element.81), channel_id=1, source_target_pairs={{3,6},{7,10},{11,14},{15,18},{19,22},{23,26},{27,30}} | collective-permute-start | bytes 98312 | tf_op jit(solution)/shard_map/ppermute | solution.py:212
  16.7 2.8 %collective-permute-start.2 = (bf16[2,256,256]{2,1,0:T(8,128)(2,1)S(1)}, bf16[2,256,256]{2,1,0:T(8,128)(2,1)S(1)}, u32[]{:S(2)}, u32[]{:S(2)}) collective-permute-start(bf16[2,256,256]{2,1,0:T(8,128)(2,1)S(1)} %get-tuple-element.79), channel_id=1, source_target_pairs={{3,2},{7,6},{11,10},{15,14},{19,18},{23,22},{27,26},{31,30}} | collective-permute-start | bytes 786440 | tf_op jit(solution)/shard_map/ppermute | solution.py:212
  17.5 3.5 %collective-permute-start.12 = (bf16[2,32,256]{2,1,0:T(8,128)(2,1)S(1)}, bf16[2,32,256]{2,1,0:T(8,128)(2,1)S(1)}, u32[]{:S(2)}, u32[]{:S(2)}) collective-permute-start(bf16[2,32,256]{2,1,0:T(8,128)(2,1)S(1)} %get-tuple-element.100), channel_id=1, source_target_pairs={{6,1},{10,5},{14,9},{18,13},{22,17},{26,21},{30,25}} | collective-permute-start | bytes 98312 | tf_op jit(solution)/shard_map/ppermute | solution.py:212
  18.2 3.5 %collective-permute-start.13 = (bf16[2,32,256]{2,1,0:T(8,128)(2,1)S(1)}, bf16[2,32,256]{2,1,0:T(8,128)(2,1)S(1)}, u32[]{:S(2)}, u32[]{:S(2)}) collective-permute-start(bf16[2,32,256]{2,1,0:T(8,128)(2,1)S(1)} %get-tuple-element.101), channel_id=1, source_target_pairs={{2,5},{6,9},{10,13},{14,17},{18,21},{22,25},{26,29}} | collective-permute-start | bytes 98312 | tf_op jit(solution)/shard_map/ppermute | solution.py:212
  18.8 2.8 %collective-permute-start.11 = (bf16[2,256,256]{2,1,0:T(8,128)(2,1)S(1)}, bf16[2,256,256]{2,1,0:T(8,128)(2,1)S(1)}, u32[]{:S(2)}, u32[]{:S(2)}) collective-permute-start(bf16[2,256,256]{2,1,0:T(8,128)(2,1)S(1)} %get-tuple-element.99), channel_id=1, source_target_pairs={{2,1},{6,5},{10,9},{14,13},{18,17},{22,21},{26,25},{30,29}} | collective-permute-start | bytes 786440 | tf_op jit(solution)/shard_map/ppermute | solution.py:212
  19.6 4.7 %collective-permute-start.9 = (bf16[2,32,256]{2,1,0:T(8,128)(2,1)S(1)}, bf16[2,32,256]{2,1,0:T(8,128)(2,1)S(1)}, u32[]{:S(2)}, u32[]{:S(2)}) collective-permute-start(bf16[2,32,256]{2,1,0:T(8,128)(2,1)S(1)} %get-tuple-element.97), channel_id=1, source_target_pairs={{6,1},{10,5},{14,9},{18,13},{22,17},{26,21},{30,25}} | collective-permute-start | bytes 98312 | tf_op jit(solution)/shard_map/ppermute | solution.py:212
  20.3 5.4 %collective-permute-start.10 = (bf16[2,32,256]{2,1,0:T(8,128)(2,1)S(1)}, bf16[2,32,256]{2,1,0:T(8,128)(2,1)S(1)}, u32[]{:S(2)}, u32[]{:S(2)}) collective-permute-start(bf16[2,32,256]{2,1,0:T(8,128)(2,1)S(1)} %get-tuple-element.98), channel_id=1, source_target_pairs={{2,5},{6,9},{10,13},{14,17},{18,21},{22,25},{26,29}} | collective-permute-start | bytes 98312 | tf_op jit(solution)/shard_map/ppermute | solution.py:212
  21.0 4.7 %collective-permute-start.8 = (bf16[2,256,256]{2,1,0:T(8,128)(2,1)S(1)}, bf16[2,256,256]{2,1,0:T(8,128)(2,1)S(1)}, u32[]{:S(2)}, u32[]{:S(2)}) collective-permute-start(bf16[2,256,256]{2,1,0:T(8,128)(2,1)S(1)} %get-tuple-element.96), channel_id=1, source_target_pairs={{2,1},{6,5},{10,9},{14,13},{18,17},{22,21},{26,25},{30,29}} | collective-permute-start | bytes 786440 | tf_op jit(solution)/shard_map/ppermute | solution.py:212
  21.7 20.1 %collective-permute-start.18 = (bf16[2,32,256]{2,1,0:T(8,128)(2,1)S(1)}, bf16[2,32,256]{2,1,0:T(8,128)(2,1)S(1)}, u32[]{:S(2)}, u32[]{:S(2)}) collective-permute-start(bf16[2,32,256]{2,1,0:T(8,128)(2,1)S(1)} %get-tuple-element.116), channel_id=1, source_target_pairs={{5,0},{9,4},{13,8},{17,12},{21,16},{25,20},{29,24}} | collective-permute-start | bytes 98312 | tf_op jit(solution)/shard_map/ppermute | solution.py:212
  23.0 24.7 %collective-permute-start.19 = (bf16[2,32,256]{2,1,0:T(8,128)(2,1)S(1)}, bf16[2,32,256]{2,1,0:T(8,128)(2,1)S(1)}, u32[]{:S(2)}, u32[]{:S(2)}) collective-permute-start(bf16[2,32,256]{2,1,0:T(8,128)(2,1)S(1)} %get-tuple-element.117), channel_id=1, source_target_pairs={{1,4},{5,8},{9,12},{13,16},{17,20},{21,24},{25,28}} | collective-permute-start | bytes 98312 | tf_op jit(solution)/shard_map/ppermute | solution.py:212
  24.4 28.9 %collective-permute-start.17 = (bf16[2,256,256]{2,1,0:T(8,128)(2,1)S(1)}, bf16[2,256,256]{2,1,0:T(8,128)(2,1)S(1)}, u32[]{:S(2)}, u32[]{:S(2)}) collective-permute-start(bf16[2,256,256]{2,1,0:T(8,128)(2,1)S(1)} %get-tuple-element.115), channel_id=1, source_target_pairs={{1,0},{5,4},{9,8},{13,12},{17,16},{21,20},{25,24},{29,28}} | collective-permute-start | bytes 786440 | tf_op jit(solution)/shard_map/ppermute | solution.py:212
  25.8 29.5 %collective-permute-start.15 = (bf16[2,32,256]{2,1,0:T(8,128)(2,1)S(1)}, bf16[2,32,256]{2,1,0:T(8,128)(2,1)S(1)}, u32[]{:S(2)}, u32[]{:S(2)}) collective-permute-start(bf16[2,32,256]{2,1,0:T(8,128)(2,1)S(1)} %get-tuple-element.113), channel_id=1, source_target_pairs={{5,0},{9,4},{13,8},{17,12},{21,16},{25,20},{29,24}} | collective-permute-start | bytes 98312 | tf_op jit(solution)/shard_map/ppermute | solution.py:212
  27.1 28.5 %collective-permute-start.16 = (bf16[2,32,256]{2,1,0:T(8,128)(2,1)S(1)}, bf16[2,32,256]{2,1,0:T(8,128)(2,1)S(1)}, u32[]{:S(2)}, u32[]{:S(2)}) collective-permute-start(bf16[2,32,256]{2,1,0:T(8,128)(2,1)S(1)} %get-tuple-element.114), channel_id=1, source_target_pairs={{1,4},{5,8},{9,12},{13,16},{17,20},{21,24},{25,28}} | collective-permute-start | bytes 98312 | tf_op jit(solution)/shard_map/ppermute | solution.py:212
  41.9 17.7 %collective-permute-start.14 = (bf16[2,256,256]{2,1,0:T(8,128)(2,1)S(1)}, bf16[2,256,256]{2,1,0:T(8,128)(2,1)S(1)}, u32[]{:S(2)}, u32[]{:S(2)}) collective-permute-start(bf16[2,256,256]{2,1,0:T(8,128)(2,1)S(1)} %get-tuple-element.112), channel_id=1, source_target_pairs={{1,0},{5,4},{9,8},{13,12},{17,16},{21,20},{25,24},{29,28}} | collective-permute-start | bytes 786440 | tf_op jit(solution)/shard_map/ppermute | solution.py:212
  62.3 1.5 %collective-permute-start.22 = (bf16[384,256]{1,0:T(8,128)(2,1)S(1)}, bf16[384,256]{1,0:T(8,128)(2,1)S(1)}, u32[]{:S(2)}, u32[]{:S(2)}) collective-permute-start(bf16[384,256]{1,0:T(8,128)(2,1)S(1)} %select_convert_fusion), channel_id=1, source_target_pairs={{0,4},{4,0},{8,12},{12,8},{16,20},{20,16},{24,28},{28,24},{1,5},{5... | collective-permute-start | bytes 589832 | tf_op jit(solution)/shard_map/ppermute | solution.py:152
  63.8 8.7 %collective-permute-start.25 = (bf16[384,256]{1,0:T(8,128)(2,1)S(1)}, bf16[384,256]{1,0:T(8,128)(2,1)S(1)}, u32[]{:S(2)}, u32[]{:S(2)}) collective-permute-start(bf16[384,256]{1,0:T(8,128)(2,1)S(1)} %add_convert_fusion.1), channel_id=1, source_target_pairs={{0,24},{4,28},{8,16},{12,20},{16,8},{20,12},{24,0},{28,4},{1,25},{... | collective-permute-start | bytes 589832 | tf_op jit(solution)/shard_map/ppermute | solution.py:152
  66.8 9.4 %collective-permute-start.24 = (bf16[384,256]{1,0:T(8,128)(2,1)S(1)}, bf16[384,256]{1,0:T(8,128)(2,1)S(1)}, u32[]{:S(2)}, u32[]{:S(2)}) collective-permute-start(bf16[384,256]{1,0:T(8,128)(2,1)S(1)} %add_convert_fusion.1), channel_id=1, source_target_pairs={{0,16},{4,20},{8,24},{12,28},{16,0},{20,4},{24,8},{28,12},{1,17},{... | collective-permute-start | bytes 589832 | tf_op jit(solution)/shard_map/ppermute | solution.py:152
  66.8 9.4 %collective-permute-start.23 = (bf16[384,256]{1,0:T(8,128)(2,1)S(1)}, bf16[384,256]{1,0:T(8,128)(2,1)S(1)}, u32[]{:S(2)}, u32[]{:S(2)}) collective-permute-start(bf16[384,256]{1,0:T(8,128)(2,1)S(1)} %add_convert_fusion.1), channel_id=1, source_target_pairs={{0,8},{4,12},{8,0},{12,4},{16,24},{20,28},{24,16},{28,20},{1,9},{5... | collective-permute-start | bytes 589832 | tf_op jit(solution)/shard_map/ppermute | solution.py:152
  76.3 11.5 %collective-permute-start.26 = (bf16[384,256]{1,0:T(8,128)(2,1)S(1)}, bf16[384,256]{1,0:T(8,128)(2,1)S(1)}, u32[]{:S(2)}, u32[]{:S(2)}) collective-permute-start(bf16[384,256]{1,0:T(8,128)(2,1)S(1)} %add_convert_fusion), channel_id=1, source_target_pairs={{0,4},{4,0},{8,12},{12,8},{16,20},{20,16},{24,28},{28,24},{1,5},{5... | collective-permute-start | bytes 589832 | tf_op jit(solution)/shard_map/ppermute | solution.py:152
  76.4 5.8 %collective-permute-start.20 = (bf16[4,32,256]{2,1,0:T(8,128)(2,1)S(1)}, bf16[4,32,256]{2,1,0:T(8,128)(2,1)S(1)}, u32[]{:S(2)}, u32[]{:S(2)}) collective-permute-start(bf16[4,32,256]{2,1,0:T(8,128)(2,1)S(1)} %get-tuple-element.129), channel_id=1, source_target_pairs={{4,0},{8,4},{12,8},{16,12},{20,16},{24,20},{28,24},{5,1},{9,5},{13... | collective-permute-start | bytes 196616 | tf_op jit(solution)/shard_map/ppermute | solution.py:251
  80.2 6.5 %collective-permute-start.21 = (bf16[4,32,256]{2,1,0:T(8,128)(2,1)S(1)}, bf16[4,32,256]{2,1,0:T(8,128)(2,1)S(1)}, u32[]{:S(2)}, u32[]{:S(2)}) collective-permute-start(bf16[4,32,256]{2,1,0:T(8,128)(2,1)S(1)} %get-tuple-element.130), channel_id=1, source_target_pairs={{0,4},{4,8},{8,12},{12,16},{16,20},{20,24},{24,28},{1,5},{5,9},{9,... | collective-permute-start | bytes 196616 | tf_op jit(solution)/shard_map/ppermute | solution.py:252
  (4 other events, 3.8 us)

commit v3 on v2

--- a/solution.py
+++ b/solution.py
@@ -23,39 +23,55 @@
     return pltpu.CompilerParams(vmem_limit_bytes=16 * 1024 * 1024)
 
 
-def pack_kernel(x_ref, send_ref, place_ref, up_ref, down_ref):
+def load_kernel(odd_ref, x_hbm, g_hbm, w1_hbm, w2_hbm, nbr_hbm, coef_hbm, send_hbm,
+                x_ref, g_ref, w1_ref, w2_ref, nbr_ref, coef_ref, place_ref, near_ref, far_ref, send_ref, sems):
+    sources = (send_hbm, x_hbm, nbr_hbm, coef_hbm, w1_hbm, w2_hbm, g_hbm)
+    targets = (send_ref, x_ref, nbr_ref, coef_ref, w1_ref, w2_ref, g_ref)
+    copies = [pltpu.make_async_copy(source, target, sems.at[n])
+              for n, (source, target) in enumerate(zip(sources, targets))]
+    for copy in copies:
+        copy.start()
     batches, rows, _ = x_ref.shape
     slots = send_ref.shape[1]
     row = lax.broadcasted_iota(jnp.int32, (rows, slots), 0)
+    copies[0].wait()
     up = jnp.where(row == send_ref[0:1, :], 1.0, 0.0)
     down = jnp.where(row == send_ref[1:2, :], 1.0, 0.0)
     place = jnp.concatenate([up, down], axis=1)
     place_ref[...] = place.astype(BF16)
     pick = place.T.astype(BF16)
+    copies[1].wait()
+    odd = odd_ref[0] == 1
     for m in range(batches):
-        sent = dot(pick, x_ref[m]).astype(BF16)
-        up_ref[m] = sent[:slots]
-        down_ref[m] = sent[slots:]
-
-
-def forward_kernel(x_ref, below_ref, above_ref, nbr_ref, coef_ref, w_ref,
+        sent = dot(pick, x_ref[m])
+        up, down = sent[:slots], sent[slots:]
+        near_ref[m] = jnp.where(odd, down, up).astype(BF16)
+        far_ref[m] = jnp.where(odd, up, down).astype(BF16)
+    for copy in copies[2:]:
+        copy.wait()
+
+
+def forward_kernel(odd_ref, x_ref, near_ref, far_ref, nbr_ref, coef_ref, w_ref,
                    slope_ref, act_ref, agg_ref, own_ref, halo_ref):
     batches, rows, width = x_ref.shape
-    slots = below_ref.shape[1]
+    slots = near_ref.shape[1]
     faces = nbr_ref.shape[0]
     slot = lax.broadcasted_iota(jnp.int32, (rows + 2 * slots, rows), 0)
     spread = jnp.zeros((rows + 2 * slots, rows), F32)
     for k in range(faces):
         spread = spread + jnp.where(slot == nbr_ref[k : k + 1, :], coef_ref[k : k + 1, :], 0.0)
     own = spread[slots : slots + rows]
-    halo = jnp.concatenate([spread[:slots], spread[slots + rows :]], axis=0)
+    lower, upper = spread[:slots], spread[slots + rows :]
+    halo_ref[...] = jnp.concatenate([lower, upper], axis=0).astype(BF16)
     own_ref[...] = own.astype(BF16)
-    halo_ref[...] = halo.astype(BF16)
     own_t = own.T.astype(BF16)
-    halo_t = halo.T.astype(BF16)
+    odd = odd_ref[0] == 1
+    near = jnp.where(odd, lower, upper)
+    far = jnp.where(odd, upper, lower)
+    halo_t = jnp.concatenate([near, far], axis=0).T.astype(BF16)
     for m in range(batches):
         x = x_ref[m]
-        edge = jnp.concatenate([below_ref[m], above_ref[m]], axis=0)
+        edge = jnp.concatenate([near_ref[m], far_ref[m]], axis=0)
         agg = (dot(own_t, x) + dot(halo_t, edge)).astype(BF16)
         z = dot(x, w_ref[:width]) + dot(agg, w_ref[width:])
         sig = 1.0 / (1.0 + jnp.exp(-z))
@@ -127,7 +143,8 @@
     return body
 
 
-def weight_kernel(x_ref, agg_ref, act_ref, g_ref, dz_ref, grad_ref):
+def weight_kernel(odd_ref, x_ref, agg_ref, act_ref, g_ref, dz_ref, to_below_ref, to_above_ref,
+                  keep_ref, give_ref, near_ref, far_ref, grad_ref):
     batches, rows, width = x_ref.shape
     total = batches * rows
     g = g_ref[...].reshape(total, width)
@@ -136,42 +153,42 @@
     grad_ref[:width] = dot(x_ref[...].reshape(total, width), dz, over)
     grad_ref[width : 2 * width] = dot(agg_ref[...].reshape(total, width), dz, over)
     grad_ref[2 * width :] = dot(act_ref[...].reshape(total, width), g, over)
-
-
-def finish_kernel(loc_ref, upper_ref, lower_ref, place_ref, out_ref):
+    half = keep_ref.shape[0]
+    odd = odd_ref[0]
+    keep_ref[...] = grad_ref[pl.ds(pl.multiple_of(odd * half, half), half)]
+    give_ref[...] = grad_ref[pl.ds(pl.multiple_of((1 - odd) * half, half), half)].astype(BF16)
+    below, above = to_below_ref[...], to_above_ref[...]
+    near_ref[...] = jnp.where(odd == 1, below, above)
+    far_ref[...] = jnp.where(odd == 1, above, below)
+
+
+def total_kernel(*refs):
+    parts, out_ref = refs[:-3], refs[-1]
+    values = [part[...].astype(F32) for part in parts]
+    while len(values) > 1:
+        values = [values[n] + values[n + 1] for n in range(0, len(values), 2)]
+    out_ref[...] = values[0].astype(BF16)
+
+
+def split_kernel(odd_ref, mine_ref, other_ref, first_ref, second_ref):
+    half = mine_ref.shape[0]
+    size = first_ref.shape[0]
+    odd = odd_ref[0] == 1
+    mine, other = mine_ref[...].astype(F32), other_ref[...].astype(F32)
+    low = jnp.where(odd, other, mine)
+    high = jnp.where(odd, mine, other)
+    first_ref[:half] = low
+    first_ref[half:] = high[: size - half]
+    second_ref[...] = high[size - half :]
+
+
+def finish_kernel(odd_ref, loc_ref, near_ref, far_ref, place_ref, out_ref):
+    odd = odd_ref[0] == 1
     for m in range(loc_ref.shape[0]):
-        out_ref[m] = assemble(loc_ref[m], upper_ref[m], lower_ref[m], place_ref[...])
-
-
-def sum_over_dom(part, count):
-    if count & (count - 1) or count < 4:
-        return lax.psum(part, "dom")
-    me = lax.axis_index("dom")
-
-    def swap(value, mask):
-        return lax.ppermute(value, "dom", [(i, i ^ mask) for i in range(count)])
-
-    half = part.shape[0] // 2
-    low = me % 2 == 0
-    keep = jnp.where(low, part[:half], part[half:])
-    give = jnp.where(low, part[half:], part[:half]).astype(BF16)
-    acc = keep + swap(give, 1).astype(F32)
-    bit = 2
-    while bit < count:
-        mine = acc.astype(BF16)
-        if bit * 2 < count:
-            others = [swap(mine, mask) for mask in (bit, 2 * bit, 3 * bit)]
-            a, b, c = [other.astype(F32) for other in others]
-            acc = (mine.astype(F32) + a) + (b + c)
-            bit *= 4
-        else:
-            acc = mine.astype(F32) + swap(mine, bit).astype(F32)
-            bit *= 2
-    mine = acc.astype(BF16)
-    other = swap(mine, 1)
-    first = jnp.where(low, mine, other)
-    second = jnp.where(low, other, mine)
-    return jnp.concatenate([first, second], axis=0).astype(F32)
+        near, far = near_ref[m], far_ref[m]
+        upper = jnp.where(odd, far, near)
+        lower = jnp.where(odd, near, far)
+        out_ref[m] = assemble(loc_ref[m], upper, lower, place_ref[...])
 
 
 def per_device(saved_inputs, grad_out, w_first, w_second, face_weight, neighbours, send_rows):
@@ -185,25 +202,46 @@
     chunks = CHUNKS if batches % CHUNKS == 0 else 1
     count = batches // chunks
     hop_here = (sections - 1 - lax.axis_index("section")).astype(jnp.int32).reshape(1)
+    odd = (lax.axis_index("dom") % 2).astype(jnp.int32).reshape(1)
     sds = jax.ShapeDtypeStruct
-
-    place, up, down = pl.pallas_call(
-        pack_kernel,
-        out_shape=(sds((rows, 2 * slots), BF16), sds((batches, slots, width), BF16),
-                   sds((batches, slots, width), BF16)),
-        compiler_params=params(), name="pack",
-    )(x, send_rows)
-    rise = [(i, i + 1) for i in range(doms - 1)]
-    fall = [(i + 1, i) for i in range(doms - 1)]
-    below = lax.ppermute(up, "dom", rise)
-    above = lax.ppermute(down, "dom", fall)
-
-    slope, act, agg, own, halo = pl.pallas_call(
+    smem = pl.BlockSpec(memory_space=pltpu.SMEM)
+    any_spec = pl.BlockSpec(memory_space=pl.ANY)
+    hbm_spec = pl.BlockSpec(memory_space=pltpu.HBM)
+
+    def like(value):
+        return sds(value.shape, value.dtype)
+
+    def call(body, outs, *args, scratch=(), name):
+        return pl.pallas_call(
+            body, in_specs=[smem] + [vmem()] * (len(args) - 1), out_specs=[vmem()] * len(outs), out_shape=outs,
+            scratch_shapes=scratch, compiler_params=params(), name=name,
+        )(*args)
+
+    near_pairs = [(p, p ^ 1) for p in range(doms)]
+    far_pairs = [(p, p + 1 if p % 2 else p - 1) for p in range(1, doms - 1)]
+
+    def exchange(near, far):
+        return lax.ppermute(near, "dom", near_pairs), lax.ppermute(far, "dom", far_pairs)
+
+    edge_shape = sds((batches, slots, width), BF16)
+    x, grad_out, w1, w2, neighbours, face_weight, place, near, far = pl.pallas_call(
+        load_kernel,
+        in_specs=[smem] + [hbm_spec] * 7,
+        out_specs=[vmem()] * 9,
+        out_shape=(like(x), like(grad_out), like(w1), like(w2), like(neighbours), like(face_weight),
+                   sds((rows, 2 * slots), BF16), edge_shape, edge_shape),
+        scratch_shapes=[pltpu.VMEM(send_rows.shape, send_rows.dtype), pltpu.SemaphoreType.DMA((7,))],
+        compiler_params=params(), name="load",
+    )(odd, *[pltpu.with_memory_space_constraint(value, pltpu.HBM)
+             for value in (x, grad_out, w1, w2, neighbours, face_weight, send_rows)])
+    near, far = exchange(near, far)
+
+    full_shape = sds((batches, rows, width), BF16)
+    slope, act, agg, own, halo = call(
         forward_kernel,
-        out_shape=(sds((batches, rows, width), F32), sds((batches, rows, width), BF16),
-                   sds((batches, rows, width), BF16), sds((rows, rows), BF16), sds((2 * slots, rows), BF16)),
-        compiler_params=params(), name="forward",
-    )(x, below, above, neighbours, face_weight, w1)
+        (sds((batches, rows, width), F32), full_shape, full_shape, sds((rows, rows), BF16),
+         sds((2 * slots, rows), BF16)),
+        odd, x, near, far, neighbours, face_weight, w1, name="forward")
 
     def move(value, hop, shift):
         source = sections - 1 - hop
@@ -215,7 +253,6 @@
         full, edge = sds((n, rows, width), BF16), sds((n, slots, width), BF16)
         return (full, edge, edge)
 
-    any_spec = pl.BlockSpec(memory_space=pl.ANY)
     kept = ()
     received = [None] * chunks
     for hop in range(sections):
@@ -242,19 +279,31 @@
         received = sent
     local, to_below, to_above, g, dz = kept
 
-    grad = pl.pallas_call(
-        weight_kernel, out_shape=sds((3 * width, width), F32),
-        compiler_params=params(), name="weights",
-    )(x, agg, act, g, dz)
-
-    total = sum_over_dom(grad, doms)
-    from_upper = lax.ppermute(to_below, "dom", fall)
-    from_lower = lax.ppermute(to_above, "dom", rise)
-    grad_in = pl.pallas_call(
-        finish_kernel, out_shape=sds((batches, rows, width), BF16),
-        compiler_params=params(), name="finish",
-    )(local, from_upper, from_lower, place)
-    return grad_in[None], total[None, : 2 * width], total[None, 2 * width :]
+    half = sds((3 * width // 2, width), BF16)
+    keep, give, near, far = call(
+        weight_kernel, (sds(half.shape, F32), half, edge_shape, edge_shape),
+        odd, x, agg, act, g, dz, to_below, to_above,
+        scratch=[pltpu.VMEM((3 * width, width), F32)], name="weights")
+
+    def swap(value, mask):
+        return lax.ppermute(value, "dom", [(i, i ^ mask) for i in range(doms)])
+
+    mine = (keep + swap(give, 1).astype(F32)).astype(BF16)
+    near, far = exchange(near, far)
+    bit = 2
+    while bit < doms:
+        masks = (bit, 2 * bit, 3 * bit) if bit * 2 < doms else (bit,)
+        parts = [mine] + [swap(mine, mask) for mask in masks]
+        mine = pl.pallas_call(
+            total_kernel, in_specs=[vmem()] * len(parts) + [any_spec] * 2, out_specs=vmem(), out_shape=half,
+            compiler_params=params(), name="total",
+        )(*parts, near, far)
+        bit *= len(parts)
+    other = swap(mine, 1)
+    (grad_in,) = call(finish_kernel, (full_shape,), odd, local, near, far, place, name="finish")
+    first, second = call(
+        split_kernel, (sds((2 * width, width), F32), sds((width, width), F32)), odd, mine, other, name="split")
+    return grad_in[None], first[None], second[None]
 
 
 def solution(mesh):

time: 90 us -> 78.4 us (0.87)
  the two profiles are of different devices: /device:TPU:4 before, /device:TPU:1 now
where the time goes in v3:
time: 78.4 us; the launch traced here: 77.6 us
  waiting for transfers between devices  37.4 us (48%)
  starting transfers between devices  29.4 us (38%)
  Pallas kernels  9.7 us (12%)
  between operations  1.05 us (1%)
    ppermute x18, waiting for transfers between devices, move(): return lax.ppermute(value, ('dom', 'section'), pairs)  28.9 us
    ppermute x18, starting transfers between devices, move(): return lax.ppermute(value, ('dom', 'section'), pairs)  15.8 us
    ppermute x2, starting transfers between devices, exchange(): lax.ppermute(far, 'dom', far_pairs)  7.99 us
    ppermute x2, waiting for transfers between devices, exchange(): lax.ppermute(far, 'dom', far_pairs)  7.08 us
    ppermute x5, starting transfers between devices, swap(): return lax.ppermute(value, 'dom', [(i, i ^ mask) for i in range(doms)])  4.57 us
    pallas_call x8, Pallas kernels, per_device(): pl.pallas_call(make_step_kernel(hop, c * count, count, not kept), in_spec...  4.32 us
    pallas_call x4, Pallas kernels, call(): pl.pallas_call(body, in_specs=[smem] + [vmem()] * (len(args) - 1), out_sp...  3.85 us
  transfers between devices with their start and end apart: 27, of which 8 were waited for; matrix products, arithmetic and copies ran while one was open for 0% of the time, Pallas kernels for 4%

profile of v3, /device:TPU:1, one launch (start us, length us, event | category | flops | bytes accessed | tf_op | source)
XLA Modules:
  0.0 77.6 jit_solution(14121430662344771322)
XLA Ops:
  0.6 1.4 %load.1 = (bf16[4,256,256]{2,1,0:T(8,128)(2,1)S(1)}, bf16[4,256,256]{2,1,0:T(8,128)(2,1)S(1)}, bf16[512,256]{1,0:T(8,128)(2,1)S(1)}, bf16[256,256]{1,0:T(8,128)(...) custom-call(s32[1]{0:T(128)} %bitcast.odd_ref, ...), custom_call_target="tpu_custom_call" | custom-call | tf_op jit(solution)/shard_map/load/pallas_call | solution.py:227
  2.2 4.5 %collective-permute-start.1 = (bf16[4,32,256]{2,1,0:T(8,128)(2,1)S(1)}, bf16[4,32,256]{2,1,0:T(8,128)(2,1)S(1)}, u32[]{:S(2)}, u32[]{:S(2)}) collective-permute-start(bf16[4,32,256]{2,1,0:T(8,128)(2,1)S(1)} %get-tuple-element.84), channel_id=1, source_target_pairs={{4,8},{8,4},{12,16},{16,12},{20,24},{24,20},{5,9},{9,5},{13,17},{1... | collective-permute-start | bytes 196616 | tf_op jit(solution)/shard_map/ppermute | solution.py:224
  6.7 1.9 %collective-permute-done.1.far_ref = bf16[4,32,256]{2,1,0:T(8,128)(2,1)S(1)} collective-permute-done((bf16[4,32,256]{2,1,0:T(8,128)(2,1)S(1)}, bf16[4,32,256]{2,1,0:T(8,128)(2,1)S(1)}, u32[]{:S(2)}, u32[]{:S(2)}) %collective-permute-start.1) | collective-permute-done | bytes 65568 | tf_op jit(solution)/shard_map/ppermute | solution.py:224
  8.6 1.2 %forward.1 = (f32[4,256,256]{2,1,0:T(8,128)S(1)}, bf16[4,256,256]{2,1,0:T(8,128)(2,1)S(1)}, bf16[4,256,256]{2,1,0:T(8,128)(2,1)S(1)}, bf16[256,256]{1,0:T(8,128)(2,1)S(1)}, bf16[64,256]{1,0:T(8,128)(2,1)S(1)}) custom-call(s32[1]{0:T(128)} %bitcast.odd_ref, bf16[4,256,256]{2,1,0:T(8,128)(2,1)S(1)} %get-tuple-element.82.x_ref, ...), custom_call_target="tpu_custom_call" | custom-call | tf_op jit(solution)/shard_map/forward/pallas_call | solution.py:215
  9.8 0.7 collective-permute-start.6
  10.5 0.7 collective-permute-start.7
  11.2 0.7 collective-permute-start.5
  11.9 0.7 collective-permute-start.3
  12.6 0.7 collective-permute-start.4
  13.3 0.7 collective-permute-start.2
  15.4 0.7 collective-permute-start.11
  17.6 0.7 collective-permute-start.8
  18.3 1.3 %collective-permute-start.18 = (bf16[2,32,256]{2,1,0:T(8,128)(2,1)S(1)}, bf16[2,32,256]{2,1,0:T(8,128)(2,1)S(1)}, u32[]{:S(2)}, u32[]{:S(2)}) collective-permute-start(bf16[2,32,256]{2,1,0:T(8,128)(2,1)S(1)} %get-tuple-element.134), channel_id=1, source_target_pairs={{5,0},{9,4},{13,8},{17,12},{21,16},{25,20},{29,24}} | collective-permute-start | bytes 98312 | tf_op jit(solution)/shard_map/ppermute | solution.py:250
  19.6 1.3 %collective-permute-start.19 = (bf16[2,32,256]{2,1,0:T(8,128)(2,1)S(1)}, bf16[2,32,256]{2,1,0:T(8,128)(2,1)S(1)}, u32[]{:S(2)}, u32[]{:S(2)}) collective-permute-start(bf16[2,32,256]{2,1,0:T(8,128)(2,1)S(1)} %get-tuple-element.135), channel_id=1, source_target_pairs={{1,4},{5,8},{9,12},{13,16},{17,20},{21,24},{25,28}} | collective-permute-start | bytes 98312 | tf_op jit(solution)/shard_map/ppermute | solution.py:250
  20.9 1.3 %collective-permute-start.17 = (bf16[2,256,256]{2,1,0:T(8,128)(2,1)S(1)}, bf16[2,256,256]{2,1,0:T(8,128)(2,1)S(1)}, u32[]{:S(2)}, u32[]{:S(2)}) collective-permute-start(bf16[2,256,256]{2,1,0:T(8,128)(2,1)S(1)} %get-tuple-element.133), channel_id=1, source_target_pairs={{1,0},{5,4},{9,8},{13,12},{17,16},{21,20},{25,24},{29,28}} | collective-permute-start | bytes 786440 | tf_op jit(solution)/shard_map/ppermute | solution.py:250
  22.3 1.3 %collective-permute-start.15 = (bf16[2,32,256]{2,1,0:T(8,128)(2,1)S(1)}, bf16[2,32,256]{2,1,0:T(8,128)(2,1)S(1)}, u32[]{:S(2)}, u32[]{:S(2)}) collective-permute-start(bf16[2,32,256]{2,1,0:T(8,128)(2,1)S(1)} %get-tuple-element.131), channel_id=1, source_target_pairs={{5,0},{9,4},{13,8},{17,12},{21,16},{25,20},{29,24}} | collective-permute-start | bytes 98312 | tf_op jit(solution)/shard_map/ppermute | solution.py:250
  23.6 1.3 %collective-permute-start.16 = (bf16[2,32,256]{2,1,0:T(8,128)(2,1)S(1)}, bf16[2,32,256]{2,1,0:T(8,128)(2,1)S(1)}, u32[]{:S(2)}, u32[]{:S(2)}) collective-permute-start(bf16[2,32,256]{2,1,0:T(8,128)(2,1)S(1)} %get-tuple-element.132), channel_id=1, source_target_pairs={{1,4},{5,8},{9,12},{13,16},{17,20},{21,24},{25,28}} | collective-permute-start | bytes 98312 | tf_op jit(solution)/shard_map/ppermute | solution.py:250
  24.9 19.8 %collective-permute-done.18.refs_1_ = bf16[2,32,256]{2,1,0:T(8,128)(2,1)S(1)} collective-permute-done((bf16[2,32,256]{2,1,0:T(8,128)(2,1)S(1)}, bf16[2,32,256]{2,1,0:T(8,128)(2,1)S(1)}, u32[]{:S(2)}, u32[]{:S(2)}) %collective-permute-start.18) | collective-permute-done | bytes 32800 | tf_op jit(solution)/shard_map/ppermute | solution.py:250
  44.8 1.3 %collective-permute-start.14 = (bf16[2,256,256]{2,1,0:T(8,128)(2,1)S(1)}, bf16[2,256,256]{2,1,0:T(8,128)(2,1)S(1)}, u32[]{:S(2)}, u32[]{:S(2)}) collective-permute-start(bf16[2,256,256]{2,1,0:T(8,128)(2,1)S(1)} %get-tuple-element.130), channel_id=1, source_target_pairs={{1,0},{5,4},{9,8},{13,12},{17,16},{21,20},{25,24},{29,28}} | collective-permute-start | bytes 786440 | tf_op jit(solution)/shard_map/ppermute | solution.py:250
  46.1 4.0 %collective-permute-done.17.refs_0_ = bf16[2,256,256]{2,1,0:T(8,128)(2,1)S(1)} collective-permute-done((bf16[2,256,256]{2,1,0:T(8,128)(2,1)S(1)}, bf16[2,256,256]{2,1,0:T(8,128)(2,1)S(1)}, u32[]{:S(2)}, u32[]{:S(2)}) %collective-permute-start.17) | collective-permute-done | bytes 262176 | tf_op jit(solution)/shard_map/ppermute | solution.py:250
  50.0 2.0 %step.14 = (bf16[2,256,256]{2,1,0:T(8,128)(2,1)}, bf16[2,32,256]{2,1,0:T(8,128)(2,1)}, bf16[2,32,256]{2,1,0:T(8,128)(2,1)}, bf16[4,256,256]{2,1,0:T(8,128)(2,1)S...) custom-call(s32[1]{0:T(128)} %bitcast.1.hop_ref, ...), custom_call_target="tpu_custom_call", output_to_operand_aliasing={{3}: (10, {}), {4}: (11, {}), {5}: (12, {}), {6}: (13, {}),... | custom-call | flops 99999997952 | bytes 1048576 | tf_op jit(solution)/shard_map/step/pallas_call | solution.py:263
  52.0 1.1 %collective-permute-done.15.refs_1_ = bf16[2,32,256]{2,1,0:T(8,128)(2,1)S(1)} collective-permute-done((bf16[2,32,256]{2,1,0:T(8,128)(2,1)S(1)}, bf16[2,32,256]{2,1,0:T(8,128)(2,1)S(1)}, u32[]{:S(2)}, u32[]{:S(2)}) %collective-permute-start.15) | collective-permute-done | bytes 32800 | tf_op jit(solution)/shard_map/ppermute | solution.py:250
  53.1 4.0 %collective-permute-done.14.refs_0_ = bf16[2,256,256]{2,1,0:T(8,128)(2,1)S(1)} collective-permute-done((bf16[2,256,256]{2,1,0:T(8,128)(2,1)S(1)}, bf16[2,256,256]{2,1,0:T(8,128)(2,1)S(1)}, u32[]{:S(2)}, u32[]{:S(2)}) %collective-permute-start.14) | collective-permute-done | bytes 262176 | tf_op jit(solution)/shard_map/ppermute | solution.py:250
  57.1 2.0 %step.15 = (bf16[2,256,256]{2,1,0:T(8,128)(2,1)}, bf16[2,32,256]{2,1,0:T(8,128)(2,1)}, bf16[2,32,256]{2,1,0:T(8,128)(2,1)}, bf16[4,256,256]{2,1,0:T(8,128)(2,1)S...) custom-call(s32[1]{0:T(128)} %bitcast.1.hop_ref, ...), custom_call_target="tpu_custom_call", output_to_operand_aliasing={{3}: (10, {}), {4}: (11, {}), {5}: (12, {}), {6}: (13, {}),... | custom-call | flops 99999997952 | bytes 1048576 | tf_op jit(solution)/shard_map/step/pallas_call | solution.py:263
  59.1 0.7 weights.1
  60.2 1.1 %collective-permute-done.22 = bf16[384,256]{1,0:T(8,128)(2,1)S(1)} collective-permute-done((bf16[384,256]{1,0:T(8,128)(2,1)S(1)}, bf16[384,256]{1,0:T(8,128)(2,1)S(1)}, u32[]{:S(2)}, u32[]{:S(2)}) %collective-permute-start.22) | collective-permute-done | bytes 196640 | tf_op jit(solution)/shard_map/ppermute | solution.py:289
  61.4 4.0 %collective-permute-start.24 = (bf16[384,256]{1,0:T(8,128)(2,1)S(1)}, bf16[384,256]{1,0:T(8,128)(2,1)S(1)}, u32[]{:S(2)}, u32[]{:S(2)}) collective-permute-start(bf16[384,256]{1,0:T(8,128)(2,1)S(1)} %add_convert_fusion.refs_0_), channel_id=1, source_target_pairs={{0,16},{4,20},{8,24},{12,28},{16,0},{20,4},{24,8},{28,12},{1,17},{... | collective-permute-start | bytes 589832 | tf_op jit(solution)/shard_map/ppermute | solution.py:289
  65.4 0.9 %collective-permute-start.20 = (bf16[4,32,256]{2,1,0:T(8,128)(2,1)S(1)}, bf16[4,32,256]{2,1,0:T(8,128)(2,1)S(1)}, u32[]{:S(2)}, u32[]{:S(2)}) collective-permute-start(bf16[4,32,256]{2,1,0:T(8,128)(2,1)S(1)} %get-tuple-element.153), channel_id=1, source_target_pairs={{0,4},{4,0},{8,12},{12,8},{16,20},{20,16},{24,28},{28,24},{1,5},{5... | collective-permute-start | bytes 196616 | tf_op jit(solution)/shard_map/ppermute | solution.py:224
  66.3 3.5 %collective-permute-start.21 = (bf16[4,32,256]{2,1,0:T(8,128)(2,1)S(1)}, bf16[4,32,256]{2,1,0:T(8,128)(2,1)S(1)}, u32[]{:S(2)}, u32[]{:S(2)}) collective-permute-start(bf16[4,32,256]{2,1,0:T(8,128)(2,1)S(1)} %get-tuple-element.154), channel_id=1, source_target_pairs={{4,8},{8,4},{12,16},{16,12},{20,24},{24,20},{5,9},{9,5},{13,17},{1... | collective-permute-start | bytes 196616 | tf_op jit(solution)/shard_map/ppermute | solution.py:224
  69.9 5.2 %collective-permute-done.21.far_ref.refs_5_ = bf16[4,32,256]{2,1,0:T(8,128)(2,1)S(1)} collective-permute-done((bf16[4,32,256]{2,1,0:T(8,128)(2,1)S(1)}, bf16[4,32,256]{2,1,0:T(8,128)(2,1)S(1)}, u32[]{:S(2)}, u32[]{:S(2)}) %collective-permute-start.21) | collective-permute-done | bytes 65568 | tf_op jit(solution)/shard_map/ppermute | solution.py:224
  75.2 1.1 %finish.1 = bf16[4,256,256]{2,1,0:T(8,128)(2,1)} custom-call(s32[1]{0:T(128)} %bitcast.odd_ref, bf16[4,256,256]{2,1,0:T(8,128)(2,1)S(1)} %get-tuple-element.146.loc_ref, bf16[4,32,256]{2,1,0:T(8,128)(2,1)S(1)} %collective-permute-done.20.near_ref.refs_4_, bf16[4,32,256]{2,1,0:T(8,128)(2,1)S(1)} %collective-permute-done.21.far_ref.refs_5_, ...), custom_call_target="tpu_custom_call" | custom-call | tf_op jit(solution)/shard_map/finish/pallas_call | solution.py:215
  76.7 0.9 %split.1 = (f32[512,256]{1,0:T(8,128)}, f32[256,256]{1,0:T(8,128)}) custom-call(s32[1]{0:T(128)} %bitcast.odd_ref, bf16[384,256]{1,0:T(8,128)(2,1)S(1)} %total.1.mine_ref, bf16[384,256]{1,0:T(8,128)(2,1)S(1)} %collective-permute-done.26.other_ref), custom_call_target="tpu_custom_call" | custom-call | tf_op jit(solution)/shard_map/split/pallas_call | solution.py:215
  (37 shorter events, 4.3 us)
Async XLA Ops:
  2.1 4.6 %collective-permute-start = (bf16[4,32,256]{2,1,0:T(8,128)(2,1)S(1)}, bf16[4,32,256]{2,1,0:T(8,128)(2,1)S(1)}, u32[]{:S(2)}, u32[]{:S(2)}) collective-permute-start(bf16[4,32,256]{2,1,0:T(8,128)(2,1)S(1)} %get-tuple-element.83), channel_id=1, source_target_pairs={{0,4},{4,0},{8,12},{12,8},{16,20},{20,16},{24,28},{28,24},{1,5},{5... | collective-permute-start | bytes 196616 | tf_op jit(solution)/shard_map/ppermute | solution.py:224
  2.2 6.4 %collective-permute-start.1 = (bf16[4,32,256]{2,1,0:T(8,128)(2,1)S(1)}, bf16[4,32,256]{2,1,0:T(8,128)(2,1)S(1)}, u32[]{:S(2)}, u32[]{:S(2)}) collective-permute-start(bf16[4,32,256]{2,1,0:T(8,128)(2,1)S(1)} %get-tuple-element.84), channel_id=1, source_target_pairs={{4,8},{8,4},{12,16},{16,12},{20,24},{24,20},{5,9},{9,5},{13,17},{1... | collective-permute-start | bytes 196616 | tf_op jit(solution)/shard_map/ppermute | solution.py:224
  9.8 3.4 %collective-permute-start.6 = (bf16[2,32,256]{2,1,0:T(8,128)(2,1)S(1)}, bf16[2,32,256]{2,1,0:T(8,128)(2,1)S(1)}, u32[]{:S(2)}, u32[]{:S(2)}) collective-permute-start(bf16[2,32,256]{2,1,0:T(8,128)(2,1)S(1)} %get-tuple-element.102), channel_id=1, source_target_pairs={{7,2},{11,6},{15,10},{19,14},{23,18},{27,22},{31,26}} | collective-permute-start | bytes 98312 | tf_op jit(solution)/shard_map/ppermute | solution.py:250
  10.5 3.5 %collective-permute-start.7 = (bf16[2,32,256]{2,1,0:T(8,128)(2,1)S(1)}, bf16[2,32,256]{2,1,0:T(8,128)(2,1)S(1)}, u32[]{:S(2)}, u32[]{:S(2)}) collective-permute-start(bf16[2,32,256]{2,1,0:T(8,128)(2,1)S(1)} %get-tuple-element.103), channel_id=1, source_target_pairs={{3,6},{7,10},{11,14},{15,18},{19,22},{23,26},{27,30}} | collective-permute-start | bytes 98312 | tf_op jit(solution)/shard_map/ppermute | solution.py:250
  11.2 2.8 %collective-permute-start.5 = (bf16[2,256,256]{2,1,0:T(8,128)(2,1)S(1)}, bf16[2,256,256]{2,1,0:T(8,128)(2,1)S(1)}, u32[]{:S(2)}, u32[]{:S(2)}) collective-permute-start(bf16[2,256,256]{2,1,0:T(8,128)(2,1)S(1)} %get-tuple-element.101), channel_id=1, source_target_pairs={{3,2},{7,6},{11,10},{15,14},{19,18},{23,22},{27,26},{31,30}} | collective-permute-start | bytes 786440 | tf_op jit(solution)/shard_map/ppermute | solution.py:250
  11.9 3.5 %collective-permute-start.3 = (bf16[2,32,256]{2,1,0:T(8,128)(2,1)S(1)}, bf16[2,32,256]{2,1,0:T(8,128)(2,1)S(1)}, u32[]{:S(2)}, u32[]{:S(2)}) collective-permute-start(bf16[2,32,256]{2,1,0:T(8,128)(2,1)S(1)} %get-tuple-element.98), channel_id=1, source_target_pairs={{7,2},{11,6},{15,10},{19,14},{23,18},{27,22},{31,26}} | collective-permute-start | bytes 98312 | tf_op jit(solution)/shard_map/ppermute | solution.py:250
  12.6 3.5 %collective-permute-start.4 = (bf16[2,32,256]{2,1,0:T(8,128)(2,1)S(1)}, bf16[2,32,256]{2,1,0:T(8,128)(2,1)S(1)}, u32[]{:S(2)}, u32[]{:S(2)}) collective-permute-start(bf16[2,32,256]{2,1,0:T(8,128)(2,1)S(1)} %get-tuple-element.99), channel_id=1, source_target_pairs={{3,6},{7,10},{11,14},{15,18},{19,22},{23,26},{27,30}} | collective-permute-start | bytes 98312 | tf_op jit(solution)/shard_map/ppermute | solution.py:250
  13.3 2.8 %collective-permute-start.2 = (bf16[2,256,256]{2,1,0:T(8,128)(2,1)S(1)}, bf16[2,256,256]{2,1,0:T(8,128)(2,1)S(1)}, u32[]{:S(2)}, u32[]{:S(2)}) collective-permute-start(bf16[2,256,256]{2,1,0:T(8,128)(2,1)S(1)} %get-tuple-element.97), channel_id=1, source_target_pairs={{3,2},{7,6},{11,10},{15,14},{19,18},{23,22},{27,26},{31,30}} | collective-permute-start | bytes 786440 | tf_op jit(solution)/shard_map/ppermute | solution.py:250
  14.1 3.5 %collective-permute-start.12 = (bf16[2,32,256]{2,1,0:T(8,128)(2,1)S(1)}, bf16[2,32,256]{2,1,0:T(8,128)(2,1)S(1)}, u32[]{:S(2)}, u32[]{:S(2)}) collective-permute-start(bf16[2,32,256]{2,1,0:T(8,128)(2,1)S(1)} %get-tuple-element.118), channel_id=1, source_target_pairs={{6,1},{10,5},{14,9},{18,13},{22,17},{26,21},{30,25}} | collective-permute-start | bytes 98312 | tf_op jit(solution)/shard_map/ppermute | solution.py:250
  14.7 3.5 %collective-permute-start.13 = (bf16[2,32,256]{2,1,0:T(8,128)(2,1)S(1)}, bf16[2,32,256]{2,1,0:T(8,128)(2,1)S(1)}, u32[]{:S(2)}, u32[]{:S(2)}) collective-permute-start(bf16[2,32,256]{2,1,0:T(8,128)(2,1)S(1)} %get-tuple-element.119), channel_id=1, source_target_pairs={{2,5},{6,9},{10,13},{14,17},{18,21},{22,25},{26,29}} | collective-permute-start | bytes 98312 | tf_op jit(solution)/shard_map/ppermute | solution.py:250
  15.4 2.8 %collective-permute-start.11 = (bf16[2,256,256]{2,1,0:T(8,128)(2,1)S(1)}, bf16[2,256,256]{2,1,0:T(8,128)(2,1)S(1)}, u32[]{:S(2)}, u32[]{:S(2)}) collective-permute-start(bf16[2,256,256]{2,1,0:T(8,128)(2,1)S(1)} %get-tuple-element.117), channel_id=1, source_target_pairs={{2,1},{6,5},{10,9},{14,13},{18,17},{22,21},{26,25},{30,29}} | collective-permute-start | bytes 786440 | tf_op jit(solution)/shard_map/ppermute | solution.py:250
  16.2 4.7 %collective-permute-start.9 = (bf16[2,32,256]{2,1,0:T(8,128)(2,1)S(1)}, bf16[2,32,256]{2,1,0:T(8,128)(2,1)S(1)}, u32[]{:S(2)}, u32[]{:S(2)}) collective-permute-start(bf16[2,32,256]{2,1,0:T(8,128)(2,1)S(1)} %get-tuple-element.115), channel_id=1, source_target_pairs={{6,1},{10,5},{14,9},{18,13},{22,17},{26,21},{30,25}} | collective-permute-start | bytes 98312 | tf_op jit(solution)/shard_map/ppermute | solution.py:250
  16.9 5.4 %collective-permute-start.10 = (bf16[2,32,256]{2,1,0:T(8,128)(2,1)S(1)}, bf16[2,32,256]{2,1,0:T(8,128)(2,1)S(1)}, u32[]{:S(2)}, u32[]{:S(2)}) collective-permute-start(bf16[2,32,256]{2,1,0:T(8,128)(2,1)S(1)} %get-tuple-element.116), channel_id=1, source_target_pairs={{2,5},{6,9},{10,13},{14,17},{18,21},{22,25},{26,29}} | collective-permute-start | bytes 98312 | tf_op jit(solution)/shard_map/ppermute | solution.py:250
  17.6 4.7 %collective-permute-start.8 = (bf16[2,256,256]{2,1,0:T(8,128)(2,1)S(1)}, bf16[2,256,256]{2,1,0:T(8,128)(2,1)S(1)}, u32[]{:S(2)}, u32[]{:S(2)}) collective-permute-start(bf16[2,256,256]{2,1,0:T(8,128)(2,1)S(1)} %get-tuple-element.114), channel_id=1, source_target_pairs={{2,1},{6,5},{10,9},{14,13},{18,17},{22,21},{26,25},{30,29}} | collective-permute-start | bytes 786440 | tf_op jit(solution)/shard_map/ppermute | solution.py:250
  18.3 26.5 %collective-permute-start.18 = (bf16[2,32,256]{2,1,0:T(8,128)(2,1)S(1)}, bf16[2,32,256]{2,1,0:T(8,128)(2,1)S(1)}, u32[]{:S(2)}, u32[]{:S(2)}) collective-permute-start(bf16[2,32,256]{2,1,0:T(8,128)(2,1)S(1)} %get-tuple-element.134), channel_id=1, source_target_pairs={{5,0},{9,4},{13,8},{17,12},{21,16},{25,20},{29,24}} | collective-permute-start | bytes 98312 | tf_op jit(solution)/shard_map/ppermute | solution.py:250
  19.6 26.4 %collective-permute-start.19 = (bf16[2,32,256]{2,1,0:T(8,128)(2,1)S(1)}, bf16[2,32,256]{2,1,0:T(8,128)(2,1)S(1)}, u32[]{:S(2)}, u32[]{:S(2)}) collective-permute-start(bf16[2,32,256]{2,1,0:T(8,128)(2,1)S(1)} %get-tuple-element.135), channel_id=1, source_target_pairs={{1,4},{5,8},{9,12},{13,16},{17,20},{21,24},{25,28}} | collective-permute-start | bytes 98312 | tf_op jit(solution)/shard_map/ppermute | solution.py:250
  20.9 29.1 %collective-permute-start.17 = (bf16[2,256,256]{2,1,0:T(8,128)(2,1)S(1)}, bf16[2,256,256]{2,1,0:T(8,128)(2,1)S(1)}, u32[]{:S(2)}, u32[]{:S(2)}) collective-permute-start(bf16[2,256,256]{2,1,0:T(8,128)(2,1)S(1)} %get-tuple-element.133), channel_id=1, source_target_pairs={{1,0},{5,4},{9,8},{13,12},{17,16},{21,20},{25,24},{29,28}} | collective-permute-start | bytes 786440 | tf_op jit(solution)/shard_map/ppermute | solution.py:250
  22.3 30.8 %collective-permute-start.15 = (bf16[2,32,256]{2,1,0:T(8,128)(2,1)S(1)}, bf16[2,32,256]{2,1,0:T(8,128)(2,1)S(1)}, u32[]{:S(2)}, u32[]{:S(2)}) collective-permute-start(bf16[2,32,256]{2,1,0:T(8,128)(2,1)S(1)} %get-tuple-element.131), channel_id=1, source_target_pairs={{5,0},{9,4},{13,8},{17,12},{21,16},{25,20},{29,24}} | collective-permute-start | bytes 98312 | tf_op jit(solution)/shard_map/ppermute | solution.py:250
  23.6 29.5 %collective-permute-start.16 = (bf16[2,32,256]{2,1,0:T(8,128)(2,1)S(1)}, bf16[2,32,256]{2,1,0:T(8,128)(2,1)S(1)}, u32[]{:S(2)}, u32[]{:S(2)}) collective-permute-start(bf16[2,32,256]{2,1,0:T(8,128)(2,1)S(1)} %get-tuple-element.132), channel_id=1, source_target_pairs={{1,4},{5,8},{9,12},{13,16},{17,20},{21,24},{25,28}} | collective-permute-start | bytes 98312 | tf_op jit(solution)/shard_map/ppermute | solution.py:250
  44.8 12.3 %collective-permute-start.14 = (bf16[2,256,256]{2,1,0:T(8,128)(2,1)S(1)}, bf16[2,256,256]{2,1,0:T(8,128)(2,1)S(1)}, u32[]{:S(2)}, u32[]{:S(2)}) collective-permute-start(bf16[2,256,256]{2,1,0:T(8,128)(2,1)S(1)} %get-tuple-element.130), channel_id=1, source_target_pairs={{1,0},{5,4},{9,8},{13,12},{17,16},{21,20},{25,24},{29,28}} | collective-permute-start | bytes 786440 | tf_op jit(solution)/shard_map/ppermute | solution.py:250
  59.8 1.5 %collective-permute-start.22 = (bf16[384,256]{1,0:T(8,128)(2,1)S(1)}, bf16[384,256]{1,0:T(8,128)(2,1)S(1)}, u32[]{:S(2)}, u32[]{:S(2)}) collective-permute-start(bf16[384,256]{1,0:T(8,128)(2,1)S(1)} %get-tuple-element.156), channel_id=1, source_target_pairs={{0,4},{4,0},{8,12},{12,8},{16,20},{20,16},{24,28},{28,24},{1,5},{5... | collective-permute-start | bytes 589832 | tf_op jit(solution)/shard_map/ppermute | solution.py:289
  61.4 13.7 %collective-permute-start.25 = (bf16[384,256]{1,0:T(8,128)(2,1)S(1)}, bf16[384,256]{1,0:T(8,128)(2,1)S(1)}, u32[]{:S(2)}, u32[]{:S(2)}) collective-permute-start(bf16[384,256]{1,0:T(8,128)(2,1)S(1)} %add_convert_fusion.refs_0_), channel_id=1, source_target_pairs={{0,24},{4,28},{8,16},{12,20},{16,8},{20,12},{24,0},{28,4},{1,25},{... | collective-permute-start | bytes 589832 | tf_op jit(solution)/shard_map/ppermute | solution.py:289
  61.4 13.6 %collective-permute-start.24 = (bf16[384,256]{1,0:T(8,128)(2,1)S(1)}, bf16[384,256]{1,0:T(8,128)(2,1)S(1)}, u32[]{:S(2)}, u32[]{:S(2)}) collective-permute-start(bf16[384,256]{1,0:T(8,128)(2,1)S(1)} %add_convert_fusion.refs_0_), channel_id=1, source_target_pairs={{0,16},{4,20},{8,24},{12,28},{16,0},{20,4},{24,8},{28,12},{1,17},{... | collective-permute-start | bytes 589832 | tf_op jit(solution)/shard_map/ppermute | solution.py:289
  65.4 9.7 %collective-permute-start.23 = (bf16[384,256]{1,0:T(8,128)(2,1)S(1)}, bf16[384,256]{1,0:T(8,128)(2,1)S(1)}, u32[]{:S(2)}, u32[]{:S(2)}) collective-permute-start(bf16[384,256]{1,0:T(8,128)(2,1)S(1)} %add_convert_fusion.refs_0_), channel_id=1, source_target_pairs={{0,8},{4,12},{8,0},{12,4},{16,24},{20,28},{24,16},{28,20},{1,9},{5... | collective-permute-start | bytes 589832 | tf_op jit(solution)/shard_map/ppermute | solution.py:289
  65.4 4.5 %collective-permute-start.20 = (bf16[4,32,256]{2,1,0:T(8,128)(2,1)S(1)}, bf16[4,32,256]{2,1,0:T(8,128)(2,1)S(1)}, u32[]{:S(2)}, u32[]{:S(2)}) collective-permute-start(bf16[4,32,256]{2,1,0:T(8,128)(2,1)S(1)} %get-tuple-element.153), channel_id=1, source_target_pairs={{0,4},{4,0},{8,12},{12,8},{16,20},{20,16},{24,28},{28,24},{1,5},{5... | collective-permute-start | bytes 196616 | tf_op jit(solution)/shard_map/ppermute | solution.py:224
  66.3 8.7 %collective-permute-start.21 = (bf16[4,32,256]{2,1,0:T(8,128)(2,1)S(1)}, bf16[4,32,256]{2,1,0:T(8,128)(2,1)S(1)}, u32[]{:S(2)}, u32[]{:S(2)}) collective-permute-start(bf16[4,32,256]{2,1,0:T(8,128)(2,1)S(1)} %get-tuple-element.154), channel_id=1, source_target_pairs={{4,8},{8,4},{12,16},{16,12},{20,24},{24,20},{5,9},{9,5},{13,17},{1... | collective-permute-start | bytes 196616 | tf_op jit(solution)/shard_map/ppermute | solution.py:224
  75.2 1.5 %collective-permute-start.26 = (bf16[384,256]{1,0:T(8,128)(2,1)S(1)}, bf16[384,256]{1,0:T(8,128)(2,1)S(1)}, u32[]{:S(2)}, u32[]{:S(2)}) collective-permute-start(bf16[384,256]{1,0:T(8,128)(2,1)S(1)} %total.1.mine_ref), channel_id=1, source_target_pairs={{0,4},{4,0},{8,12},{12,8},{16,20},{20,16},{24,28},{28,24},{1,5},{5... | collective-permute-start | bytes 589832 | tf_op jit(solution)/shard_map/ppermute | solution.py:289

commit v4 on v3

--- a/solution.py
+++ b/solution.py
@@ -8,7 +8,8 @@
 F32 = jnp.float32
 BF16 = jnp.bfloat16
 CHUNKS = 2
-STEP_FLOPS = 10**11
+STEP_FLOPS = 2700 * 10**6
+LAST_FLOPS = 2754 * 10**6
 
 
 def dot(a, b, dims=((1,), (0,))):
@@ -87,22 +88,22 @@
     count = len(g)
     copies = []
 
-    def keep(n, source):
-        copy = pltpu.make_async_copy(source, kept[n].at[pl.ds(first, count)], sems.at[n])
+    def keep(n, source, j):
+        copy = pltpu.make_async_copy(source.at[j], kept[n].at[first + j], sems.at[n, j])
         copy.start()
         copies.append(copy)
 
     for j in range(count):
         g_buf[j] = g[j]
-    keep(3, g_buf)
+        keep(3, g_buf, j)
     stacked = jnp.concatenate(g, axis=0) if count > 1 else g[0]
     d_act = dot(stacked, w2_ref[...], ((1,), (1,)))
     dzs = []
     for j in range(count):
         dz = (d_act[j * rows : (j + 1) * rows] * slope_ref[first + j]).astype(BF16)
         dz_buf[j] = dz
+        keep(4, dz_buf, j)
         dzs.append(dz)
-    keep(4, dz_buf)
     dz = jnp.concatenate(dzs, axis=0) if count > 1 else dzs[0]
     dj = dot(dz, w1_ref[...], ((1,), (1,)))
     for j in range(count):
@@ -110,11 +111,12 @@
         dagg = part[:, width:].astype(BF16)
         local = g[j].astype(F32) + part[:, :width] + dot(own_ref[...], dagg)
         local_ref[j] = local.astype(BF16)
+        keep(0, local_ref, j)
         edge = dot(halo_ref[...], dagg).astype(BF16)
         below_ref[j] = edge[:slots]
         above_ref[j] = edge[slots:]
-    for n in range(3):
-        keep(n, sent[n])
+        keep(1, below_ref, j)
+        keep(2, above_ref, j)
     for copy in copies:
         copy.wait()
 
@@ -124,12 +126,15 @@
     return (local.astype(F32) + dot(place, edge)).astype(BF16)
 
 
-def make_step_kernel(hop, first, count, fresh):
+def make_step_kernel(hop, first, count, fresh, last):
     def body(hop_ref, *refs):
         inputs, refs = (refs[:1], refs[1:]) if hop == 0 else (refs[:4], refs[4:])
         slope_ref, own_ref, halo_ref, w1_ref, w2_ref = refs[:5]
         refs = refs[5:] if fresh else refs[10:]
-        sent, kept, (g_buf, dz_buf, sems) = refs[:3], refs[3:8], refs[8:]
+        if last:
+            kept, g_buf, dz_buf, sems, *sent = refs[:5], *refs[5:]
+        else:
+            sent, kept, (g_buf, dz_buf, sems) = refs[:3], refs[3:8], refs[8:]
 
         @pl.when(hop_ref[0] == hop)
         def _():
@@ -144,7 +149,7 @@
 
 
 def weight_kernel(odd_ref, x_ref, agg_ref, act_ref, g_ref, dz_ref, to_below_ref, to_above_ref,
-                  keep_ref, give_ref, near_ref, far_ref, grad_ref):
+                  keep_ref, give_ref, far_ref, grad_ref):
     batches, rows, width = x_ref.shape
     total = batches * rows
     g = g_ref[...].reshape(total, width)
@@ -156,18 +161,20 @@
     half = keep_ref.shape[0]
     odd = odd_ref[0]
     keep_ref[...] = grad_ref[pl.ds(pl.multiple_of(odd * half, half), half)]
-    give_ref[...] = grad_ref[pl.ds(pl.multiple_of((1 - odd) * half, half), half)].astype(BF16)
+    give_ref[:half] = grad_ref[pl.ds(pl.multiple_of((1 - odd) * half, half), half)].astype(BF16)
     below, above = to_below_ref[...], to_above_ref[...]
-    near_ref[...] = jnp.where(odd == 1, below, above)
+    give_ref[half:] = jnp.where(odd == 1, below, above).reshape(give_ref.shape[0] - half, width)
     far_ref[...] = jnp.where(odd == 1, above, below)
 
 
-def total_kernel(*refs):
-    parts, out_ref = refs[:-3], refs[-1]
-    values = [part[...].astype(F32) for part in parts]
-    while len(values) > 1:
-        values = [values[n] + values[n + 1] for n in range(0, len(values), 2)]
-    out_ref[...] = values[0].astype(BF16)
+def add(a, b):
+    return (a.astype(F32) + b.astype(F32)).astype(BF16)
+
+
+def join_kernel(p_ref, p_other_ref, q_ref, q_other_ref, far_ref, out_ref):
+    quarter = p_ref.shape[0]
+    out_ref[:quarter] = add(p_ref[...], p_other_ref[...])
+    out_ref[quarter:] = add(q_ref[...], q_other_ref[...])
 
 
 def split_kernel(odd_ref, mine_ref, other_ref, first_ref, second_ref):
@@ -182,10 +189,12 @@
     second_ref[...] = high[size - half :]
 
 
-def finish_kernel(odd_ref, loc_ref, near_ref, far_ref, place_ref, out_ref):
+def finish_kernel(odd_ref, loc_ref, came_ref, far_ref, place_ref, out_ref):
     odd = odd_ref[0] == 1
-    for m in range(loc_ref.shape[0]):
-        near, far = near_ref[m], far_ref[m]
+    batches, slots = far_ref.shape[:2]
+    start = came_ref.shape[0] - batches * slots
+    for m in range(batches):
+        near, far = came_ref[start + m * slots : start + (m + 1) * slots], far_ref[m]
         upper = jnp.where(odd, far, near)
         lower = jnp.where(odd, near, far)
         out_ref[m] = assemble(loc_ref[m], upper, lower, place_ref[...])
@@ -260,47 +269,58 @@
         for c in range(chunks):
             inputs = (grad_out,) if hop == 0 else (*received[c], place)
             inputs = (hop_here, *inputs, slope, own, halo, w1, w2)
+            last = hop + 1 == sections
+            sends = () if last else shapes(count)
+            buffers = [pltpu.VMEM((count, rows, width), BF16)] * 2 + [pltpu.SemaphoreType.DMA((5, count))]
+            if last:
+                buffers += [pltpu.VMEM(shape.shape, shape.dtype) for shape in shapes(count)]
             outs = pl.pallas_call(
-                make_step_kernel(hop, c * count, count, not kept),
-                in_specs=[pl.BlockSpec(memory_space=pltpu.SMEM)] + [vmem()] * (len(inputs) - 1)
-                + [any_spec] * len(kept),
-                out_specs=[vmem()] * 3 + [any_spec] * 5,
-                out_shape=shapes(count) + shapes(batches) + (shapes(batches)[0],) * 2,
-                scratch_shapes=[pltpu.VMEM((count, rows, width), BF16), pltpu.VMEM((count, rows, width), BF16),
-                                pltpu.SemaphoreType.DMA((5,))],
-                input_output_aliases={len(inputs) + n: 3 + n for n in range(len(kept))},
-                cost_estimate=pl.CostEstimate(flops=STEP_FLOPS, bytes_accessed=1 << 20, transcendentals=0),
+                make_step_kernel(hop, c * count, count, not kept, last),
+                in_specs=[smem] + [vmem()] * (len(inputs) - 1) + [any_spec] * len(kept),
+                out_specs=[vmem()] * len(sends) + [any_spec] * 5,
+                out_shape=sends + shapes(batches) + (shapes(batches)[0],) * 2,
+                scratch_shapes=buffers,
+                input_output_aliases={len(inputs) + n: len(sends) + n for n in range(len(kept))},
+                cost_estimate=pl.CostEstimate(flops=LAST_FLOPS if last else STEP_FLOPS, bytes_accessed=1 << 20, transcendentals=0),
                 compiler_params=params(), name="step",
             )(*inputs, *kept)
-            kept = outs[3:]
-            if hop + 1 < sections:
+            kept = outs[len(sends):]
+            if not last:
                 local, to_below, to_above = outs[:3]
                 sent.append((move(local, hop, 0), move(to_below, hop, -1), move(to_above, hop, 1)))
         received = sent
     local, to_below, to_above, g, dz = kept
 
-    half = sds((3 * width // 2, width), BF16)
-    keep, give, near, far = call(
-        weight_kernel, (sds(half.shape, F32), half, edge_shape, edge_shape),
+    half = 3 * width // 2
+    keep, give, far = call(
+        weight_kernel,
+        (sds((half, width), F32), sds((half + batches * slots, width), BF16), edge_shape),
         odd, x, agg, act, g, dz, to_below, to_above,
         scratch=[pltpu.VMEM((3 * width, width), F32)], name="weights")
 
     def swap(value, mask):
         return lax.ppermute(value, "dom", [(i, i ^ mask) for i in range(doms)])
 
-    mine = (keep + swap(give, 1).astype(F32)).astype(BF16)
-    near, far = exchange(near, far)
+    came = swap(give, 1)
+    far = lax.ppermute(far, "dom", far_pairs)
+    p = add(keep[: half // 2], came[: half // 2])
+    q = add(keep[half // 2 :], came[half // 2 : half])
     bit = 2
     while bit < doms:
-        masks = (bit, 2 * bit, 3 * bit) if bit * 2 < doms else (bit,)
-        parts = [mine] + [swap(mine, mask) for mask in masks]
-        mine = pl.pallas_call(
-            total_kernel, in_specs=[vmem()] * len(parts) + [any_spec] * 2, out_specs=vmem(), out_shape=half,
-            compiler_params=params(), name="total",
-        )(*parts, near, far)
-        bit *= len(parts)
+        if bit * 2 < doms:
+            p, q = add(p, swap(p, bit)), add(q, swap(q, 2 * bit))
+            p_other, q_other = swap(p, 2 * bit), swap(q, bit)
+        else:
+            p_other, q_other = swap(p, bit), swap(q, bit)
+        bit *= 4
+        if bit < doms:
+            p, q = add(p, p_other), add(q, q_other)
+    mine = pl.pallas_call(
+        join_kernel, in_specs=[vmem()] * 4 + [any_spec], out_specs=vmem(), out_shape=sds((half, width), BF16),
+        compiler_params=params(), name="join",
+    )(p, p_other, q, q_other, far)
     other = swap(mine, 1)
-    (grad_in,) = call(finish_kernel, (full_shape,), odd, local, near, far, place, name="finish")
+    (grad_in,) = call(finish_kernel, (full_shape,), odd, local, came, far, place, name="finish")
     first, second = call(
         split_kernel, (sds((2 * width, width), F32), sds((width, width), F32)), odd, mine, other, name="split")
     return grad_in[None], first[None], second[None]

time: 78.4 us -> 81.1 us (1.034)
  waiting for transfers between devices: 37.4 us -> 40.5 us
  starting transfers between devices: 29.4 us -> 27.6 us
  Pallas kernels: 9.7 us -> 11.4 us
    ppermute x2 -> x1, waiting for transfers between devices: 7.08 us -> 1.92 us  [exchange(): lax.ppermute(far, 'dom', far_pairs)]
    ppermute x0 -> x1, starting transfers between devices: none -> 4.8 us  [per_device(): far = lax.ppermute(far, 'dom', far_pairs)]
    ppermute x5 -> x6, waiting for transfers between devices: 1.43 us -> 5.04 us  [swap(): return lax.ppermute(value, 'dom', [(i, i ^ mask) for i in range(doms)])]
    ppermute x2 -> x1, starting transfers between devices: 7.99 us -> 4.47 us  [exchange(): lax.ppermute(far, 'dom', far_pairs)]
    ppermute x18, waiting for transfers between devices: 28.9 us -> 31.4 us  [move(): return lax.ppermute(value, ('dom', 'section'), pairs)]
    ppermute x0 -> x1, waiting for transfers between devices: none -> 2.14 us  [per_device(): far = lax.ppermute(far, 'dom', far_pairs)]
    ppermute x5 -> x6, starting transfers between devices: 4.57 us -> 2.48 us  [swap(): return lax.ppermute(value, 'dom', [(i, i ^ mask) for i in range(doms)])]
    pallas_call x9, Pallas kernels: 4.42 us -> 6.1 us  [the longest x8 6.05 us: per_device(): pl.pallas_call(make_step_kernel(hop, c * count, count, not kept, last), i...]
  transfers between devices with their start and end apart: 27 -> 27, of which waited for: 8 -> 7; matrix products, arithmetic and copies ran while one was open for 0% -> 0% of each run, Pallas kernels for 4% -> 5%
where the time goes in v4:
time: 81.1 us; the launch traced here: 80.6 us
  waiting for transfers between devices  40.5 us (50%)
  starting transfers between devices  27.6 us (34%)
  Pallas kernels  11.4 us (14%)
  between operations  1.05 us (1%)
    ppermute x18, waiting for transfers between devices, move(): return lax.ppermute(value, ('dom', 'section'), pairs)  31.4 us
    ppermute x18, starting transfers between devices, move(): return lax.ppermute(value, ('dom', 'section'), pairs)  15.8 us
    pallas_call x8, Pallas kernels, per_device(): pl.pallas_call(make_step_kernel(hop, c * count, count, not kept, last), i...  6.05 us
    ppermute x6, waiting for transfers between devices, swap(): return lax.ppermute(value, 'dom', [(i, i ^ mask) for i in range(doms)])  5.04 us
    ppermute x1, starting transfers between devices, per_device(): far = lax.ppermute(far, 'dom', far_pairs)  4.8 us
    ppermute x1, starting transfers between devices, exchange(): lax.ppermute(far, 'dom', far_pairs)  4.47 us
    pallas_call x4, Pallas kernels, call(): pl.pallas_call(body, in_specs=[smem] + [vmem()] * (len(args) - 1), out_sp...  3.85 us
    ppermute x6, starting transfers between devices, swap(): return lax.ppermute(value, 'dom', [(i, i ^ mask) for i in range(doms)])  2.48 us
  transfers between devices with their start and end apart: 27, of which 7 were waited for; matrix products, arithmetic and copies ran while one was open for 0% of the time, Pallas kernels for 5%

profile of v4, /device:TPU:1, one launch (start us, length us, event | category | flops | bytes accessed | tf_op | source)
XLA Modules:
  0.0 80.6 jit_solution(7216020421818581848)
XLA Ops:
  0.6 1.4 %load.1 = (bf16[4,256,256]{2,1,0:T(8,128)(2,1)S(1)}, bf16[4,256,256]{2,1,0:T(8,128)(2,1)S(1)}, bf16[512,256]{1,0:T(8,128)(2,1)S(1)}, bf16[256,256]{1,0:T(8,128)(...) custom-call(s32[1]{0:T(128)} %bitcast.odd_ref, ...), custom_call_target="tpu_custom_call" | custom-call | tf_op jit(solution)/shard_map/load/pallas_call | solution.py:236
  2.2 4.5 %collective-permute-start.1 = (bf16[4,32,256]{2,1,0:T(8,128)(2,1)S(1)}, bf16[4,32,256]{2,1,0:T(8,128)(2,1)S(1)}, u32[]{:S(2)}, u32[]{:S(2)}) collective-permute-start(bf16[4,32,256]{2,1,0:T(8,128)(2,1)S(1)} %get-tuple-element.83), channel_id=1, source_target_pairs={{4,8},{8,4},{12,16},{16,12},{20,24},{24,20},{5,9},{9,5},{13,17},{1... | collective-permute-start | bytes 196616 | tf_op jit(solution)/shard_map/ppermute | solution.py:233
  6.7 1.9 %collective-permute-done.1.far_ref = bf16[4,32,256]{2,1,0:T(8,128)(2,1)S(1)} collective-permute-done((bf16[4,32,256]{2,1,0:T(8,128)(2,1)S(1)}, bf16[4,32,256]{2,1,0:T(8,128)(2,1)S(1)}, u32[]{:S(2)}, u32[]{:S(2)}) %collective-permute-start.1) | collective-permute-done | bytes 65568 | tf_op jit(solution)/shard_map/ppermute | solution.py:233
  8.6 1.2 %forward.1 = (f32[4,256,256]{2,1,0:T(8,128)S(1)}, bf16[4,256,256]{2,1,0:T(8,128)(2,1)S(1)}, bf16[4,256,256]{2,1,0:T(8,128)(2,1)S(1)}, bf16[256,256]{1,0:T(8,128)(2,1)S(1)}, bf16[64,256]{1,0:T(8,128)(2,1)S(1)}) custom-call(s32[1]{0:T(128)} %bitcast.odd_ref, bf16[4,256,256]{2,1,0:T(8,128)(2,1)S(1)} %get-tuple-element.81.x_ref, ...), custom_call_target="tpu_custom_call" | custom-call | tf_op jit(solution)/shard_map/forward/pallas_call | solution.py:224
  9.9 0.7 collective-permute-start.5
  10.6 0.7 collective-permute-start.6
  11.2 0.7 collective-permute-start.7
  12.0 0.7 collective-permute-start.2
  12.7 0.7 collective-permute-start.3
  13.4 0.7 collective-permute-start.4
  14.2 0.7 collective-permute-start.11
  14.9 0.7 collective-permute-start.12
  16.4 0.7 collective-permute-start.8
  18.6 1.3 %collective-permute-start.17 = (bf16[2,256,256]{2,1,0:T(8,128)(2,1)S(1)}, bf16[2,256,256]{2,1,0:T(8,128)(2,1)S(1)}, u32[]{:S(2)}, u32[]{:S(2)}) collective-permute-start(bf16[2,256,256]{2,1,0:T(8,128)(2,1)S(1)} %get-tuple-element.132), channel_id=1, source_target_pairs={{1,0},{5,4},{9,8},{13,12},{17,16},{21,20},{25,24},{29,28}} | collective-permute-start | bytes 786440 | tf_op jit(solution)/shard_map/ppermute | solution.py:259
  19.9 1.3 %collective-permute-start.18 = (bf16[2,32,256]{2,1,0:T(8,128)(2,1)S(1)}, bf16[2,32,256]{2,1,0:T(8,128)(2,1)S(1)}, u32[]{:S(2)}, u32[]{:S(2)}) collective-permute-start(bf16[2,32,256]{2,1,0:T(8,128)(2,1)S(1)} %get-tuple-element.133), channel_id=1, source_target_pairs={{5,0},{9,4},{13,8},{17,12},{21,16},{25,20},{29,24}} | collective-permute-start | bytes 98312 | tf_op jit(solution)/shard_map/ppermute | solution.py:259
  21.2 1.3 %collective-permute-start.19 = (bf16[2,32,256]{2,1,0:T(8,128)(2,1)S(1)}, bf16[2,32,256]{2,1,0:T(8,128)(2,1)S(1)}, u32[]{:S(2)}, u32[]{:S(2)}) collective-permute-start(bf16[2,32,256]{2,1,0:T(8,128)(2,1)S(1)} %get-tuple-element.134), channel_id=1, source_target_pairs={{1,4},{5,8},{9,12},{13,16},{17,20},{21,24},{25,28}} | collective-permute-start | bytes 98312 | tf_op jit(solution)/shard_map/ppermute | solution.py:259
  22.6 1.3 %collective-permute-start.14 = (bf16[2,256,256]{2,1,0:T(8,128)(2,1)S(1)}, bf16[2,256,256]{2,1,0:T(8,128)(2,1)S(1)}, u32[]{:S(2)}, u32[]{:S(2)}) collective-permute-start(bf16[2,256,256]{2,1,0:T(8,128)(2,1)S(1)} %get-tuple-element.129), channel_id=1, source_target_pairs={{1,0},{5,4},{9,8},{13,12},{17,16},{21,20},{25,24},{29,28}} | collective-permute-start | bytes 786440 | tf_op jit(solution)/shard_map/ppermute | solution.py:259
  23.9 1.3 %collective-permute-start.15 = (bf16[2,32,256]{2,1,0:T(8,128)(2,1)S(1)}, bf16[2,32,256]{2,1,0:T(8,128)(2,1)S(1)}, u32[]{:S(2)}, u32[]{:S(2)}) collective-permute-start(bf16[2,32,256]{2,1,0:T(8,128)(2,1)S(1)} %get-tuple-element.130), channel_id=1, source_target_pairs={{5,0},{9,4},{13,8},{17,12},{21,16},{25,20},{29,24}} | collective-permute-start | bytes 98312 | tf_op jit(solution)/shard_map/ppermute | solution.py:259
  25.2 28.3 %collective-permute-done.18.refs_1_ = bf16[2,32,256]{2,1,0:T(8,128)(2,1)S(1)} collective-permute-done((bf16[2,32,256]{2,1,0:T(8,128)(2,1)S(1)}, bf16[2,32,256]{2,1,0:T(8,128)(2,1)S(1)}, u32[]{:S(2)}, u32[]{:S(2)}) %collective-permute-start.18) | collective-permute-done | bytes 32800 | tf_op jit(solution)/shard_map/ppermute | solution.py:259
  53.5 1.3 %collective-permute-start.16 = (bf16[2,32,256]{2,1,0:T(8,128)(2,1)S(1)}, bf16[2,32,256]{2,1,0:T(8,128)(2,1)S(1)}, u32[]{:S(2)}, u32[]{:S(2)}) collective-permute-start(bf16[2,32,256]{2,1,0:T(8,128)(2,1)S(1)} %get-tuple-element.131), channel_id=1, source_target_pairs={{1,4},{5,8},{9,12},{13,16},{17,20},{21,24},{25,28}} | collective-permute-start | bytes 98312 | tf_op jit(solution)/shard_map/ppermute | solution.py:259
  54.8 2.7 %step.14 = (bf16[4,256,256]{2,1,0:T(8,128)(2,1)S(1)}, bf16[4,32,256]{2,1,0:T(8,128)(2,1)S(1)}, bf16[4,32,256]{2,1,0:T(8,128)(2,1)S(1)}, bf16[4,256,256]{2,1,0:T(8,128)(2,1)S(1)}, bf16[4,256,256]{2,1,0:T(8,128)(2,1)S(1)}) custom-call(s32[1]{0:T(128)} %bitcast.1.hop_ref, ...), custom_call_target="tpu_custom_call", output_to_operand_aliasing={{0}: (10, {}), {1}: (11, {}), {2}: (12, {}), {3}: (13, {}),... | custom-call | flops 2753999872 | bytes 1048576 | tf_op jit(solution)/shard_map/step/pallas_call | solution.py:277
  57.6 3.0 %collective-permute-done.15.refs_1_ = bf16[2,32,256]{2,1,0:T(8,128)(2,1)S(1)} collective-permute-done((bf16[2,32,256]{2,1,0:T(8,128)(2,1)S(1)}, bf16[2,32,256]{2,1,0:T(8,128)(2,1)S(1)}, u32[]{:S(2)}, u32[]{:S(2)}) %collective-permute-start.15) | collective-permute-done | bytes 32800 | tf_op jit(solution)/shard_map/ppermute | solution.py:259
  60.6 2.7 %step.15 = (bf16[4,256,256]{2,1,0:T(8,128)(2,1)S(1)}, bf16[4,32,256]{2,1,0:T(8,128)(2,1)S(1)}, bf16[4,32,256]{2,1,0:T(8,128)(2,1)S(1)}, bf16[4,256,256]{2,1,0:T(8,128)(2,1)S(1)}, bf16[4,256,256]{2,1,0:T(8,128)(2,1)S(1)}) custom-call(s32[1]{0:T(128)} %bitcast.1.hop_ref, ...), custom_call_target="tpu_custom_call", output_to_operand_aliasing={{0}: (10, {}), {1}: (11, {}), {2}: (12, {}), {3}: (13, {}),... | custom-call | flops 2753999872 | bytes 1048576 | tf_op jit(solution)/shard_map/step/pallas_call | solution.py:277
  63.3 0.7 weights.1
  64.0 1.5 %collective-permute-done.20.came_ref = bf16[512,256]{1,0:T(8,128)(2,1)S(1)} collective-permute-done((bf16[512,256]{1,0:T(8,128)(2,1)S(1)}, bf16[512,256]{1,0:T(8,128)(2,1)S(1)}, u32[]{:S(2)}, u32[]{:S(2)}) %collective-permute-start.20) | collective-permute-done | bytes 262176 | tf_op jit(solution)/shard_map/ppermute | solution.py:302
  65.6 1.2 %collective-permute-start.24 = (bf16[192,256]{1,0:T(8,128)(2,1)S(1)}, bf16[192,256]{1,0:T(8,128)(2,1)S(1)}, u32[]{:S(2)}, u32[]{:S(2)}) collective-permute-start(bf16[192,256]{1,0:T(8,128)(2,1)S(1)} %get-tuple-element.157), channel_id=1, source_target_pairs={{0,16},{4,20},{8,24},{12,28},{16,0},{20,4},{24,8},{28,12},{1,17},{... | collective-permute-start | bytes 294920 | tf_op jit(solution)/shard_map/ppermute | solution.py:302
  66.8 3.2 %collective-permute-done.24 = bf16[192,256]{1,0:T(8,128)(2,1)S(1)} collective-permute-done((bf16[192,256]{1,0:T(8,128)(2,1)S(1)}, bf16[192,256]{1,0:T(8,128)(2,1)S(1)}, u32[]{:S(2)}, u32[]{:S(2)}) %collective-permute-start.24) | collective-permute-done | bytes 98336 | tf_op jit(solution)/shard_map/ppermute | solution.py:302
  70.0 0.7 collective-permute-start.25
  71.2 4.8 %collective-permute-start.21 = (bf16[4,32,256]{2,1,0:T(8,128)(2,1)S(1)}, bf16[4,32,256]{2,1,0:T(8,128)(2,1)S(1)}, u32[]{:S(2)}, u32[]{:S(2)}) collective-permute-start(bf16[4,32,256]{2,1,0:T(8,128)(2,1)S(1)} %get-tuple-element.153), channel_id=1, source_target_pairs={{4,8},{8,4},{12,16},{16,12},{20,24},{24,20},{5,9},{9,5},{13,17},{1... | collective-permute-start | bytes 196616 | tf_op jit(solution)/shard_map/ppermute | solution.py:305
  76.0 2.1 %collective-permute-done.21.far_ref = bf16[4,32,256]{2,1,0:T(8,128)(2,1)S(1)} collective-permute-done((bf16[4,32,256]{2,1,0:T(8,128)(2,1)S(1)}, bf16[4,32,256]{2,1,0:T(8,128)(2,1)S(1)}, u32[]{:S(2)}, u32[]{:S(2)}) %collective-permute-start.21) | collective-permute-done | bytes 65568 | tf_op jit(solution)/shard_map/ppermute | solution.py:305
  78.3 1.1 %finish.1 = bf16[4,256,256]{2,1,0:T(8,128)(2,1)} custom-call(s32[1]{0:T(128)} %bitcast.odd_ref, bf16[4,256,256]{2,1,0:T(8,128)(2,1)S(1)} %get-tuple-element.145.loc_ref, bf16[512,256]{1,0:T(8,128)(2,1)S(1)} %collective-permute-done.20.came_ref, bf16[4,32,256]{2,1,0:T(8,128)(2,1)S(1)} %collective-permute-done.21.far_ref, ...), custom_call_target="tpu_custom_call" | custom-call | tf_op jit(solution)/shard_map/finish/pallas_call | solution.py:224
  79.7 0.9 %split.1 = (f32[512,256]{1,0:T(8,128)}, f32[256,256]{1,0:T(8,128)}) custom-call(s32[1]{0:T(128)} %bitcast.odd_ref, bf16[384,256]{1,0:T(8,128)(2,1)S(1)} %join.1.mine_ref, bf16[384,256]{1,0:T(8,128)(2,1)S(1)} %collective-permute-done.26.other_ref), custom_call_target="tpu_custom_call" | custom-call | tf_op jit(solution)/shard_map/split/pallas_call | solution.py:224
  (39 shorter events, 3.9 us)
Async XLA Ops:
  2.1 4.6 %collective-permute-start = (bf16[4,32,256]{2,1,0:T(8,128)(2,1)S(1)}, bf16[4,32,256]{2,1,0:T(8,128)(2,1)S(1)}, u32[]{:S(2)}, u32[]{:S(2)}) collective-permute-start(bf16[4,32,256]{2,1,0:T(8,128)(2,1)S(1)} %get-tuple-element.82), channel_id=1, source_target_pairs={{0,4},{4,0},{8,12},{12,8},{16,20},{20,16},{24,28},{28,24},{1,5},{5... | collective-permute-start | bytes 196616 | tf_op jit(solution)/shard_map/ppermute | solution.py:233
  2.2 6.4 %collective-permute-start.1 = (bf16[4,32,256]{2,1,0:T(8,128)(2,1)S(1)}, bf16[4,32,256]{2,1,0:T(8,128)(2,1)S(1)}, u32[]{:S(2)}, u32[]{:S(2)}) collective-permute-start(bf16[4,32,256]{2,1,0:T(8,128)(2,1)S(1)} %get-tuple-element.83), channel_id=1, source_target_pairs={{4,8},{8,4},{12,16},{16,12},{20,24},{24,20},{5,9},{9,5},{13,17},{1... | collective-permute-start | bytes 196616 | tf_op jit(solution)/shard_map/ppermute | solution.py:233
  9.9 4.2 %collective-permute-start.5 = (bf16[2,256,256]{2,1,0:T(8,128)(2,1)S(1)}, bf16[2,256,256]{2,1,0:T(8,128)(2,1)S(1)}, u32[]{:S(2)}, u32[]{:S(2)}) collective-permute-start(bf16[2,256,256]{2,1,0:T(8,128)(2,1)S(1)} %get-tuple-element.100), channel_id=1, source_target_pairs={{3,2},{7,6},{11,10},{15,14},{19,18},{23,22},{27,26},{31,30}} | collective-permute-start | bytes 786440 | tf_op jit(solution)/shard_map/ppermute | solution.py:259
  10.6 2.8 %collective-permute-start.6 = (bf16[2,32,256]{2,1,0:T(8,128)(2,1)S(1)}, bf16[2,32,256]{2,1,0:T(8,128)(2,1)S(1)}, u32[]{:S(2)}, u32[]{:S(2)}) collective-permute-start(bf16[2,32,256]{2,1,0:T(8,128)(2,1)S(1)} %get-tuple-element.101), channel_id=1, source_target_pairs={{7,2},{11,6},{15,10},{19,14},{23,18},{27,22},{31,26}} | collective-permute-start | bytes 98312 | tf_op jit(solution)/shard_map/ppermute | solution.py:259
  11.2 2.8 %collective-permute-start.7 = (bf16[2,32,256]{2,1,0:T(8,128)(2,1)S(1)}, bf16[2,32,256]{2,1,0:T(8,128)(2,1)S(1)}, u32[]{:S(2)}, u32[]{:S(2)}) collective-permute-start(bf16[2,32,256]{2,1,0:T(8,128)(2,1)S(1)} %get-tuple-element.102), channel_id=1, source_target_pairs={{3,6},{7,10},{11,14},{15,18},{19,22},{23,26},{27,30}} | collective-permute-start | bytes 98312 | tf_op jit(solution)/shard_map/ppermute | solution.py:259
  12.0 4.2 %collective-permute-start.2 = (bf16[2,256,256]{2,1,0:T(8,128)(2,1)S(1)}, bf16[2,256,256]{2,1,0:T(8,128)(2,1)S(1)}, u32[]{:S(2)}, u32[]{:S(2)}) collective-permute-start(bf16[2,256,256]{2,1,0:T(8,128)(2,1)S(1)} %get-tuple-element.96), channel_id=1, source_target_pairs={{3,2},{7,6},{11,10},{15,14},{19,18},{23,22},{27,26},{31,30}} | collective-permute-start | bytes 786440 | tf_op jit(solution)/shard_map/ppermute | solution.py:259
  12.7 2.8 %collective-permute-start.3 = (bf16[2,32,256]{2,1,0:T(8,128)(2,1)S(1)}, bf16[2,32,256]{2,1,0:T(8,128)(2,1)S(1)}, u32[]{:S(2)}, u32[]{:S(2)}) collective-permute-start(bf16[2,32,256]{2,1,0:T(8,128)(2,1)S(1)} %get-tuple-element.97), channel_id=1, source_target_pairs={{7,2},{11,6},{15,10},{19,14},{23,18},{27,22},{31,26}} | collective-permute-start | bytes 98312 | tf_op jit(solution)/shard_map/ppermute | solution.py:259
  13.4 2.8 %collective-permute-start.4 = (bf16[2,32,256]{2,1,0:T(8,128)(2,1)S(1)}, bf16[2,32,256]{2,1,0:T(8,128)(2,1)S(1)}, u32[]{:S(2)}, u32[]{:S(2)}) collective-permute-start(bf16[2,32,256]{2,1,0:T(8,128)(2,1)S(1)} %get-tuple-element.98), channel_id=1, source_target_pairs={{3,6},{7,10},{11,14},{15,18},{19,22},{23,26},{27,30}} | collective-permute-start | bytes 98312 | tf_op jit(solution)/shard_map/ppermute | solution.py:259
  14.2 4.2 %collective-permute-start.11 = (bf16[2,256,256]{2,1,0:T(8,128)(2,1)S(1)}, bf16[2,256,256]{2,1,0:T(8,128)(2,1)S(1)}, u32[]{:S(2)}, u32[]{:S(2)}) collective-permute-start(bf16[2,256,256]{2,1,0:T(8,128)(2,1)S(1)} %get-tuple-element.116), channel_id=1, source_target_pairs={{2,1},{6,5},{10,9},{14,13},{18,17},{22,21},{26,25},{30,29}} | collective-permute-start | bytes 786440 | tf_op jit(solution)/shard_map/ppermute | solution.py:259
  14.9 2.8 %collective-permute-start.12 = (bf16[2,32,256]{2,1,0:T(8,128)(2,1)S(1)}, bf16[2,32,256]{2,1,0:T(8,128)(2,1)S(1)}, u32[]{:S(2)}, u32[]{:S(2)}) collective-permute-start(bf16[2,32,256]{2,1,0:T(8,128)(2,1)S(1)} %get-tuple-element.117), channel_id=1, source_target_pairs={{6,1},{10,5},{14,9},{18,13},{22,17},{26,21},{30,25}} | collective-permute-start | bytes 98312 | tf_op jit(solution)/shard_map/ppermute | solution.py:259
  15.6 2.8 %collective-permute-start.13 = (bf16[2,32,256]{2,1,0:T(8,128)(2,1)S(1)}, bf16[2,32,256]{2,1,0:T(8,128)(2,1)S(1)}, u32[]{:S(2)}, u32[]{:S(2)}) collective-permute-start(bf16[2,32,256]{2,1,0:T(8,128)(2,1)S(1)} %get-tuple-element.118), channel_id=1, source_target_pairs={{2,5},{6,9},{10,13},{14,17},{18,21},{22,25},{26,29}} | collective-permute-start | bytes 98312 | tf_op jit(solution)/shard_map/ppermute | solution.py:259
  16.4 6.1 %collective-permute-start.8 = (bf16[2,256,256]{2,1,0:T(8,128)(2,1)S(1)}, bf16[2,256,256]{2,1,0:T(8,128)(2,1)S(1)}, u32[]{:S(2)}, u32[]{:S(2)}) collective-permute-start(bf16[2,256,256]{2,1,0:T(8,128)(2,1)S(1)} %get-tuple-element.113), channel_id=1, source_target_pairs={{2,1},{6,5},{10,9},{14,13},{18,17},{22,21},{26,25},{30,29}} | collective-permute-start | bytes 786440 | tf_op jit(solution)/shard_map/ppermute | solution.py:259
  17.1 4.1 %collective-permute-start.9 = (bf16[2,32,256]{2,1,0:T(8,128)(2,1)S(1)}, bf16[2,32,256]{2,1,0:T(8,128)(2,1)S(1)}, u32[]{:S(2)}, u32[]{:S(2)}) collective-permute-start(bf16[2,32,256]{2,1,0:T(8,128)(2,1)S(1)} %get-tuple-element.114), channel_id=1, source_target_pairs={{6,1},{10,5},{14,9},{18,13},{22,17},{26,21},{30,25}} | collective-permute-start | bytes 98312 | tf_op jit(solution)/shard_map/ppermute | solution.py:259
  17.7 4.7 %collective-permute-start.10 = (bf16[2,32,256]{2,1,0:T(8,128)(2,1)S(1)}, bf16[2,32,256]{2,1,0:T(8,128)(2,1)S(1)}, u32[]{:S(2)}, u32[]{:S(2)}) collective-permute-start(bf16[2,32,256]{2,1,0:T(8,128)(2,1)S(1)} %get-tuple-element.115), channel_id=1, source_target_pairs={{2,5},{6,9},{10,13},{14,17},{18,21},{22,25},{26,29}} | collective-permute-start | bytes 98312 | tf_op jit(solution)/shard_map/ppermute | solution.py:259
  18.6 36.3 %collective-permute-start.17 = (bf16[2,256,256]{2,1,0:T(8,128)(2,1)S(1)}, bf16[2,256,256]{2,1,0:T(8,128)(2,1)S(1)}, u32[]{:S(2)}, u32[]{:S(2)}) collective-permute-start(bf16[2,256,256]{2,1,0:T(8,128)(2,1)S(1)} %get-tuple-element.132), channel_id=1, source_target_pairs={{1,0},{5,4},{9,8},{13,12},{17,16},{21,20},{25,24},{29,28}} | collective-permute-start | bytes 786440 | tf_op jit(solution)/shard_map/ppermute | solution.py:259
  19.9 33.7 %collective-permute-start.18 = (bf16[2,32,256]{2,1,0:T(8,128)(2,1)S(1)}, bf16[2,32,256]{2,1,0:T(8,128)(2,1)S(1)}, u32[]{:S(2)}, u32[]{:S(2)}) collective-permute-start(bf16[2,32,256]{2,1,0:T(8,128)(2,1)S(1)} %get-tuple-element.133), channel_id=1, source_target_pairs={{5,0},{9,4},{13,8},{17,12},{21,16},{25,20},{29,24}} | collective-permute-start | bytes 98312 | tf_op jit(solution)/shard_map/ppermute | solution.py:259
  21.2 33.7 %collective-permute-start.19 = (bf16[2,32,256]{2,1,0:T(8,128)(2,1)S(1)}, bf16[2,32,256]{2,1,0:T(8,128)(2,1)S(1)}, u32[]{:S(2)}, u32[]{:S(2)}) collective-permute-start(bf16[2,32,256]{2,1,0:T(8,128)(2,1)S(1)} %get-tuple-element.134), channel_id=1, source_target_pairs={{1,4},{5,8},{9,12},{13,16},{17,20},{21,24},{25,28}} | collective-permute-start | bytes 98312 | tf_op jit(solution)/shard_map/ppermute | solution.py:259
  22.6 38.0 %collective-permute-start.14 = (bf16[2,256,256]{2,1,0:T(8,128)(2,1)S(1)}, bf16[2,256,256]{2,1,0:T(8,128)(2,1)S(1)}, u32[]{:S(2)}, u32[]{:S(2)}) collective-permute-start(bf16[2,256,256]{2,1,0:T(8,128)(2,1)S(1)} %get-tuple-element.129), channel_id=1, source_target_pairs={{1,0},{5,4},{9,8},{13,12},{17,16},{21,20},{25,24},{29,28}} | collective-permute-start | bytes 786440 | tf_op jit(solution)/shard_map/ppermute | solution.py:259
  23.9 36.7 %collective-permute-start.15 = (bf16[2,32,256]{2,1,0:T(8,128)(2,1)S(1)}, bf16[2,32,256]{2,1,0:T(8,128)(2,1)S(1)}, u32[]{:S(2)}, u32[]{:S(2)}) collective-permute-start(bf16[2,32,256]{2,1,0:T(8,128)(2,1)S(1)} %get-tuple-element.130), channel_id=1, source_target_pairs={{5,0},{9,4},{13,8},{17,12},{21,16},{25,20},{29,24}} | collective-permute-start | bytes 98312 | tf_op jit(solution)/shard_map/ppermute | solution.py:259
  53.5 7.0 %collective-permute-start.16 = (bf16[2,32,256]{2,1,0:T(8,128)(2,1)S(1)}, bf16[2,32,256]{2,1,0:T(8,128)(2,1)S(1)}, u32[]{:S(2)}, u32[]{:S(2)}) collective-permute-start(bf16[2,32,256]{2,1,0:T(8,128)(2,1)S(1)} %get-tuple-element.131), channel_id=1, source_target_pairs={{1,4},{5,8},{9,12},{13,16},{17,20},{21,24},{25,28}} | collective-permute-start | bytes 98312 | tf_op jit(solution)/shard_map/ppermute | solution.py:259
  64.0 1.6 %collective-permute-start.20 = (bf16[512,256]{1,0:T(8,128)(2,1)S(1)}, bf16[512,256]{1,0:T(8,128)(2,1)S(1)}, u32[]{:S(2)}, u32[]{:S(2)}) collective-permute-start(bf16[512,256]{1,0:T(8,128)(2,1)S(1)} %get-tuple-element.152), channel_id=1, source_target_pairs={{0,4},{4,0},{8,12},{12,8},{16,20},{20,16},{24,28},{28,24},{1,5},{5... | collective-permute-start | bytes 786440 | tf_op jit(solution)/shard_map/ppermute | solution.py:302
  65.6 4.3 %collective-permute-start.24 = (bf16[192,256]{1,0:T(8,128)(2,1)S(1)}, bf16[192,256]{1,0:T(8,128)(2,1)S(1)}, u32[]{:S(2)}, u32[]{:S(2)}) collective-permute-start(bf16[192,256]{1,0:T(8,128)(2,1)S(1)} %get-tuple-element.157), channel_id=1, source_target_pairs={{0,16},{4,20},{8,24},{12,28},{16,0},{20,4},{24,8},{28,12},{1,17},{... | collective-permute-start | bytes 294920 | tf_op jit(solution)/shard_map/ppermute | solution.py:302
  66.8 3.9 %collective-permute-start.22 = (bf16[192,256]{1,0:T(8,128)(2,1)S(1)}, bf16[192,256]{1,0:T(8,128)(2,1)S(1)}, u32[]{:S(2)}, u32[]{:S(2)}) collective-permute-start(bf16[192,256]{1,0:T(8,128)(2,1)S(1)} %get-tuple-element.158), channel_id=1, source_target_pairs={{0,8},{4,12},{8,0},{12,4},{16,24},{20,28},{24,16},{28,20},{1,9},{5... | collective-permute-start | bytes 294920 | tf_op jit(solution)/shard_map/ppermute | solution.py:302
  70.0 8.2 %collective-permute-start.25 = (bf16[192,256]{1,0:T(8,128)(2,1)S(1)}, bf16[192,256]{1,0:T(8,128)(2,1)S(1)}, u32[]{:S(2)}, u32[]{:S(2)}) collective-permute-start(bf16[192,256]{1,0:T(8,128)(2,1)S(1)} %add_convert_fusion.q_ref), channel_id=1, source_target_pairs={{0,8},{4,12},{8,0},{12,4},{16,24},{20,28},{24,16},{28,20},{1,9},{5... | collective-permute-start | bytes 294920 | tf_op jit(solution)/shard_map/ppermute | solution.py:302
  70.7 7.4 %collective-permute-start.23 = (bf16[192,256]{1,0:T(8,128)(2,1)S(1)}, bf16[192,256]{1,0:T(8,128)(2,1)S(1)}, u32[]{:S(2)}, u32[]{:S(2)}) collective-permute-start(bf16[192,256]{1,0:T(8,128)(2,1)S(1)} %add_convert_fusion.2.p_ref), channel_id=1, source_target_pairs={{0,16},{4,20},{8,24},{12,28},{16,0},{20,4},{24,8},{28,12},{1,17},{... | collective-permute-start | bytes 294920 | tf_op jit(solution)/shard_map/ppermute | solution.py:302
  71.2 7.0 %collective-permute-start.21 = (bf16[4,32,256]{2,1,0:T(8,128)(2,1)S(1)}, bf16[4,32,256]{2,1,0:T(8,128)(2,1)S(1)}, u32[]{:S(2)}, u32[]{:S(2)}) collective-permute-start(bf16[4,32,256]{2,1,0:T(8,128)(2,1)S(1)} %get-tuple-element.153), channel_id=1, source_target_pairs={{4,8},{8,4},{12,16},{16,12},{20,24},{24,20},{5,9},{9,5},{13,17},{1... | collective-permute-start | bytes 196616 | tf_op jit(solution)/shard_map/ppermute | solution.py:305
  78.2 1.5 %collective-permute-start.26 = (bf16[384,256]{1,0:T(8,128)(2,1)S(1)}, bf16[384,256]{1,0:T(8,128)(2,1)S(1)}, u32[]{:S(2)}, u32[]{:S(2)}) collective-permute-start(bf16[384,256]{1,0:T(8,128)(2,1)S(1)} %join.1.mine_ref), channel_id=1, source_target_pairs={{0,4},{4,0},{8,12},{12,8},{16,20},{20,16},{24,28},{28,24},{1,5},{5... | collective-permute-start | bytes 589832 | tf_op jit(solution)/shard_map/ppermute | solution.py:302

commit v5 on v3

v5 whole, which is shorter than its diff:
```python
import jax
import jax.numpy as jnp
from jax import lax
from jax.experimental import pallas as pl
from jax.experimental.pallas import tpu as pltpu
from jax.sharding import PartitionSpec as P

F32 = jnp.float32
BF16 = jnp.bfloat16
CHUNKS = 2
STEP_FLOPS = 10**11


def dot(a, b, dims=((1,), (0,))):
    return lax.dot_general(a, b, (dims, ((), ())), preferred_element_type=F32)


def vmem():
    return pl.BlockSpec(memory_space=pltpu.VMEM)


def params():
    return pltpu.CompilerParams(vmem_limit_bytes=16 * 1024 * 1024)


def load_kernel(odd_ref, x_hbm, g_hbm, w1_hbm, w2_hbm, nbr_hbm, coef_hbm, send_hbm,
                x_ref, g_ref, w1_ref, w2_ref, nbr_ref, coef_ref, place_ref, near_ref, far_ref, send_ref, sems):
    sources = (send_hbm, x_hbm, nbr_hbm, coef_hbm, w1_hbm, w2_hbm, g_hbm)
    targets = (send_ref, x_ref, nbr_ref, coef_ref, w1_ref, w2_ref, g_ref)
    copies = [pltpu.make_async_copy(source, target, sems.at[n])
              for n, (source, target) in enumerate(zip(sources, targets))]
    for copy in copies:
        copy.start()
    batches, rows, _ = x_ref.shape
    slots = send_ref.shape[1]
    row = lax.broadcasted_iota(jnp.int32, (rows, slots), 0)
    copies[0].wait()
    up = jnp.where(row == send_ref[0:1, :], 1.0, 0.0)
    down = jnp.where(row == send_ref[1:2, :], 1.0, 0.0)
    place = jnp.concatenate([up, down], axis=1)
    place_ref[...] = place.astype(BF16)
    pick = place.T.astype(BF16)
    copies[1].wait()
    odd = odd_ref[0] == 1
    for m in range(batches):
        sent = dot(pick, x_ref[m])
        up, down = sent[:slots], sent[slots:]
        near_ref[m] = jnp.where(odd, down, up).astype(BF16)
        far_ref[m] = jnp.where(odd, up, down).astype(BF16)
    for copy in copies[2:]:
        copy.wait()


def inner_kernel(x_ref, nbr_ref, coef_ref, w_ref, base_ref, inner_ref, own_ref, halo_ref):
    batches, rows, width = x_ref.shape
    slots = halo_ref.shape[0] // 2
    faces = nbr_ref.shape[0]
    slot = lax.broadcasted_iota(jnp.int32, (rows + 2 * slots, rows), 0)
    spread = jnp.zeros((rows + 2 * slots, rows), F32)
    for k in range(faces):
        spread = spread + jnp.where(slot == nbr_ref[k : k + 1, :], coef_ref[k : k + 1, :], 0.0)
    own = spread[slots : slots + rows]
    halo_ref[...] = jnp.concatenate([spread[:slots], spread[slots + rows :]], axis=0).astype(BF16)
    own_ref[...] = own.astype(BF16)
    own_t = own.T.astype(BF16)
    for m in range(batches):
        x = x_ref[m]
        inner_ref[m] = dot(own_t, x)
        base_ref[m] = dot(x, w_ref[:width])


def forward_kernel(odd_ref, base_ref, inner_ref, near_ref, far_ref, halo_ref, w_ref, slope_ref, act_ref, agg_ref):
    batches, rows, width = base_ref.shape
    slots = near_ref.shape[1]
    odd = odd_ref[0] == 1
    lower, upper = halo_ref[:slots].astype(F32), halo_ref[slots:].astype(F32)
    near = jnp.where(odd, lower, upper)
    far = jnp.where(odd, upper, lower)
    halo_t = jnp.concatenate([near, far], axis=0).T.astype(BF16)
    for m in range(batches):
        edge = jnp.concatenate([near_ref[m], far_ref[m]], axis=0)
        agg = (inner_ref[m] + dot(halo_t, edge)).astype(BF16)
        z = base_ref[m] + dot(agg, w_ref[width:])
        sig = 1.0 / (1.0 + jnp.exp(-z))
        agg_ref[m] = agg
        act_ref[m] = (z * sig).astype(BF16)
        slope_ref[m] = sig * (1.0 + z * (1.0 - sig))


def assemble(local, upper, lower, place):
    edge = jnp.concatenate([upper, lower], axis=0)
    return (local.astype(F32) + dot(place, edge)).astype(BF16)


def make_step_kernel(hop, first, count):
    def body(hop_ref, *refs):
        *inputs, slope_ref, own_ref, halo_ref, w1_ref, w2_ref, local_ref, below_ref, above_ref, g_ref, dz_ref = refs

        @pl.when(hop_ref[0] == hop)
        def _():
            rows, width = slope_ref.shape[1:]
            slots = below_ref.shape[1]
            if hop == 0:
                g = [inputs[0][first + j] for j in range(count)]
            else:
                loc_ref, upper_ref, lower_ref, place_ref = inputs
                g = [assemble(loc_ref[j], upper_ref[j], lower_ref[j], place_ref[...]) for j in range(count)]
            d_act = dot(jnp.concatenate(g, axis=0), w2_ref[...], ((1,), (1,)))
            dz = [(d_act[j * rows : (j + 1) * rows] * slope_ref[first + j]).astype(BF16) for j in range(count)]
            dj = dot(jnp.concatenate(dz, axis=0), w1_ref[...], ((1,), (1,)))
            for j in range(count):
                part = dj[j * rows : (j + 1) * rows]
                dagg = part[:, width:].astype(BF16)
                local = g[j].astype(F32) + part[:, :width] + dot(own_ref[...], dagg)
                local_ref[j] = local.astype(BF16)
                edge = dot(halo_ref[...], dagg).astype(BF16)
                below_ref[j] = edge[:slots]
                above_ref[j] = edge[slots:]
                g_ref[j] = g[j]
                dz_ref[j] = dz[j]

    return body


def make_weight_kernel(hops, chunks):
    def body(hop_ref, odd_ref, x_ref, agg_ref, act_ref, *refs):
        here = [refs[4 * c : 4 * c + 4] for c in range(chunks)]
        pieces = refs[4 * chunks :]
        local_ref, keep_ref, give_ref, far_ref, grad_ref, below_ref, above_ref, g_ref, dz_ref, sems = refs[-10:]
        targets = (local_ref, below_ref, above_ref, g_ref, dz_ref)
        batches, rows, width = x_ref.shape
        count = batches // chunks

        def copies(hop):
            return [pltpu.make_async_copy(pieces[(hop * chunks + c) * 5 + n],
                                          targets[n].at[pl.ds(c * count, count)], sems.at[n, c])
                    for n in range(5) for c in range(chunks)]

        def gradients(parts):
            over = ((0,), (0,))
            for n, source in enumerate((x_ref, agg_ref, act_ref)):
                total = 0.0
                for first, size, g, dz in parts:
                    left = source[first : first + size].reshape(size * rows, width)
                    right = (g if n == 2 else dz)[...].reshape(size * rows, width)
                    total = total + dot(left, right, over)
                grad_ref[n * width : (n + 1) * width] = total

        for hop in range(hops - 1):
            @pl.when(hop_ref[0] == hop)
            def _():
                for copy in copies(hop):
                    copy.start()

        @pl.when(hop_ref[0] == hops - 1)
        def _():
            gradients([(c * count, count, g, dz) for c, (g, dz, _, _) in enumerate(here)])
            for c, (_, _, below, above) in enumerate(here):
                below_ref[c * count : (c + 1) * count] = below[...]
                above_ref[c * count : (c + 1) * count] = above[...]

        if hops > 1:
            @pl.when(hop_ref[0] != hops - 1)
            def _():
                for copy in copies(0):
                    copy.wait()
                gradients([(0, batches, g_ref, dz_ref)])

        half = keep_ref.shape[0]
        odd = odd_ref[0]
        keep_ref[...] = grad_ref[pl.ds(pl.multiple_of(odd * half, half), half)]
        give_ref[:half] = grad_ref[pl.ds(pl.multiple_of((1 - odd) * half, half), half)].astype(BF16)
        below, above = below_ref[...], above_ref[...]
        give_ref[half:] = jnp.where(odd == 1, below, above).reshape(give_ref.shape[0] - half, width)
        far_ref[...] = jnp.where(odd == 1, above, below)

    return body


def add(a, b):
    return (a.astype(F32) + b.astype(F32)).astype(BF16)


def add_kernel(p_ref, p_other_ref, q_ref, q_other_ref, far_ref, p_out_ref, q_out_ref):
    p_out_ref[...] = add(p_ref[...], p_other_ref[...])
    q_out_ref[...] = add(q_ref[...], q_other_ref[...])


def split_kernel(odd_ref, mine_ref, other_ref, first_ref, second_ref):
    half = mine_ref.shape[0]
    size = first_ref.shape[0]
    odd = odd_ref[0] == 1
    mine, other = mine_ref[...].astype(F32), other_ref[...].astype(F32)
    low = jnp.where(odd, other, mine)
    high = jnp.where(odd, mine, other)
    first_ref[:half] = low
    first_ref[half:] = high[: size - half]
    second_ref[...] = high[size - half :]


def make_finish_kernel(last):
    def body(hop_ref, odd_ref, came_ref, far_ref, place_ref, loc_ref, *refs):
        here, out_ref = refs[:-1], refs[-1]
        odd = odd_ref[0] == 1
        batches, slots = far_ref.shape[:2]
        count = batches // len(here)
        start = came_ref.shape[0] - batches * slots

        def write(local):
            for m in range(batches):
                near, far = came_ref[start + m * slots : start + (m + 1) * slots], far_ref[m]
                upper = jnp.where(odd, far, near)
                lower = jnp.where(odd, near, far)
                out_ref[m] = assemble(local(m), upper, lower, place_ref[...])

        @pl.when(hop_ref[0] == last)
        def _():
            write(lambda m: here[m // count][m % count])

        @pl.when(hop_ref[0] != last)
        def _():
            write(lambda m: loc_ref[m])

    return body


def per_device(saved_inputs, grad_out, w_first, w_second, face_weight, neighbours, send_rows):
    x = saved_inputs[0]
    w1 = w_first[0]
    w2 = w_second[0]
    batches, rows, width = x.shape
    slots = send_rows.shape[1]
    sections = lax.axis_size("section")
    doms = lax.axis_size("dom")
    chunks = CHUNKS if batches % CHUNKS == 0 else 1
    count = batches // chunks
    hop_here = (sections - 1 - lax.axis_index("section")).astype(jnp.int32).reshape(1)
    odd = (lax.axis_index("dom") % 2).astype(jnp.int32).reshape(1)
    sds = jax.ShapeDtypeStruct
    smem = pl.BlockSpec(memory_space=pltpu.SMEM)
    any_spec = pl.BlockSpec(memory_space=pl.ANY)
    hbm_spec = pl.BlockSpec(memory_space=pltpu.HBM)

    def like(value):
        return sds(value.shape, value.dtype)

    def call(body, outs, *args, scratch=(), name):
        return pl.pallas_call(
            body, in_specs=[smem] + [vmem()] * (len(args) - 1), out_specs=[vmem()] * len(outs), out_shape=outs,
            scratch_shapes=scratch, compiler_params=params(), name=name,
        )(*args)

    near_pairs = [(p, p ^ 1) for p in range(doms)]
    far_pairs = [(p, p + 1 if p % 2 else p - 1) for p in range(1, doms - 1)]

    edge_shape = sds((batches, slots, width), BF16)
    x, grad_out, w1, w2, neighbours, face_weight, place, near, far = pl.pallas_call(
        load_kernel,
        in_specs=[smem] + [hbm_spec] * 7,
        out_specs=[vmem()] * 9,
        out_shape=(like(x), like(grad_out), like(w1), like(w2), like(neighbours), like(face_weight),
                   sds((rows, 2 * slots), BF16), edge_shape, edge_shape),
        scratch_shapes=[pltpu.VMEM(send_rows.shape, send_rows.dtype), pltpu.SemaphoreType.DMA((7,))],
        compiler_params=params(), name="load",
    )(odd, *[pltpu.with_memory_space_constraint(value, pltpu.HBM)
             for value in (x, grad_out, w1, w2, neighbours, face_weight, send_rows)])
    near, far = lax.ppermute(near, "dom", near_pairs), lax.ppermute(far, "dom", far_pairs)

    full_shape = sds((batches, rows, width), BF16)
    wide_shape = sds((batches, rows, width), F32)
    base, inner, own, halo = pl.pallas_call(
        inner_kernel, in_specs=[vmem()] * 4, out_specs=[vmem()] * 4,
        out_shape=(wide_shape, wide_shape, sds((rows, rows), BF16), sds((2 * slots, rows), BF16)),
        compiler_params=params(), name="inner",
    )(x, neighbours, face_weight, w1)
    slope, act, agg = call(
        forward_kernel, (wide_shape, full_shape, full_shape), odd, base, inner, near, far, halo, w1, name="forward")

    def move(value, hop, shift):
        source = sections - 1 - hop
        pairs = [(p * sections + source, (p + shift) * sections + source - 1)
                 for p in range(doms) if 0 <= p + shift < doms]
        return lax.ppermute(value, ("dom", "section"), pairs)

    piece, piece_edge = sds((count, rows, width), BF16), sds((count, slots, width), BF16)
    pieces = []
    received = [None] * chunks
    for hop in range(sections):
        sent = []
        for c in range(chunks):
            inputs = (grad_out,) if hop == 0 else (*received[c], place)
            inputs = (hop_here, *inputs, slope, own, halo, w1, w2)
            local, to_below, to_above, g, dz = pl.pallas_call(
                make_step_kernel(hop, c * count, count),
                in_specs=[smem] + [vmem()] * (len(inputs) - 1), out_specs=[vmem()] * 5,
                out_shape=(piece, piece_edge, piece_edge, piece, piece),
                cost_estimate=pl.CostEstimate(flops=STEP_FLOPS, bytes_accessed=1 << 20, transcendentals=0),
                compiler_params=params(), name="step",
            )(*inputs)
            pieces.append((local, to_below, to_above, g, dz))
            if hop + 1 < sections:
                sent.append((move(local, hop, 0), move(to_below, hop, -1), move(to_above, hop, 1)))
        received = sent

    half = 3 * width // 2
    here = [outs[n] for outs in pieces[-chunks:] for n in (3, 4, 1, 2)]
    others = [value for outs in pieces[:-chunks] for value in outs]
    local, keep, give, far = pl.pallas_call(
        make_weight_kernel(sections, chunks),
        in_specs=[smem] * 2 + [vmem()] * (3 + len(here)) + [any_spec] * len(others),
        out_specs=[vmem()] * 4,
        out_shape=(full_shape, sds((half, width), F32), sds((half + batches * slots, width), BF16), edge_shape),
        scratch_shapes=[pltpu.VMEM((3 * width, width), F32), pltpu.VMEM(edge_shape.shape, BF16),
                        pltpu.VMEM(edge_shape.shape, BF16), pltpu.VMEM(full_shape.shape, BF16),
                        pltpu.VMEM(full_shape.shape, BF16), pltpu.SemaphoreType.DMA((5, chunks))],
        compiler_params=params(), name="weights",
    )(hop_here, odd, x, agg, act, *here, *others)

    def swap(value, mask):
        return lax.ppermute(value, "dom", [(i, i ^ mask) for i in range(doms)])

    came = swap(give, 1)
    far = lax.ppermute(far, "dom", far_pairs)
    p = add(keep[: half // 2], came[: half // 2])
    q = add(keep[half // 2 :], came[half // 2 : half])
    bit = 2
    while bit < doms:
        if bit * 2 < doms:
            p, q = pl.pallas_call(
                add_kernel, in_specs=[vmem()] * 4 + [any_spec], out_specs=[vmem()] * 2,
                out_shape=(sds(p.shape, BF16), sds(q.shape, BF16)), compiler_params=params(), name="add",
            )(p, swap(p, bit), q, swap(q, 2 * bit), far)
            p, q = add(p, swap(p, 2 * bit)), add(q, swap(q, bit))
        else:
            p, q = add(p, swap(p, bit)), add(q, swap(q, bit))
        bit *= 4
    mine = jnp.concatenate([p, q], axis=0)
    other = swap(mine, 1)
    grad_in = pl.pallas_call(
        make_finish_kernel(sections - 1), in_specs=[smem] * 2 + [vmem()] * (4 + chunks), out_specs=vmem(),
        out_shape=full_shape, compiler_params=params(), name="finish",
    )(hop_here, odd, came, far, place, local, *[outs[0] for outs in pieces[-chunks:]])
    first, second = call(
        split_kernel, (sds((2 * width, width), F32), sds((width, width), F32)), odd, mine, other, name="split")
    return grad_in[None], first[None], second[None]


def solution(mesh):
    return jax.shard_map(
        per_device,
        mesh=mesh,
        in_specs=(
            P("section", None, "dom", None),
            P(None, "dom", None),
            P("section", None, None),
            P("section", None, None),
            P(None, "dom"),
            P(None, "dom"),
            P(None, "dom"),
        ),
        out_specs=(
            P("section", None, "dom", None),
            P("section", None, None),
            P("section", None, None),
        ),
        check_vma=False,
    )
```

time: 78.4 us -> 79.6 us (1.015)
  Pallas kernels: 9.7 us -> 7.29 us
  starting transfers between devices: 29.4 us -> 31.5 us
    ppermute x5 -> x6, starting transfers between devices: 4.57 us -> 8.38 us  [swap(): return lax.ppermute(value, 'dom', [(i, i ^ mask) for i in range(doms)])]
    ppermute x4 -> x3, waiting for transfers between devices: 7.09 us -> 4.05 us  [the longest x1 2.77 us: per_device(): far = lax.ppermute(far, 'dom', far_pairs)]
    ppermute x5 -> x6, waiting for transfers between devices: 1.43 us -> 4.44 us  [swap(): return lax.ppermute(value, 'dom', [(i, i ^ mask) for i in range(doms)])]
    pallas_call x4 -> x2, Pallas kernels: 3.85 us -> 1.74 us  [call(): pl.pallas_call(body, in_specs=[smem] + [vmem()] * (len(args) - 1), out_sp...]
    ppermute x4 -> x3, starting transfers between devices: 9.05 us -> 7.39 us  [the longest x1 4.47 us: per_device(): lax.ppermute(far, 'dom', far_pairs)]
    pallas_call x9 -> x12, Pallas kernels: 4.42 us -> 4.12 us  [the longest x8 1.59 us: per_device(): pl.pallas_call(make_step_kernel(hop, c * count, count), in_specs=[smem] +...]
  transfers between devices with their start and end apart: 27 -> 27, of which waited for: 8 -> 9; matrix products, arithmetic and copies ran while one was open for 0% -> 0% of each run, Pallas kernels for 4% -> 3%
where the time goes in v5:
time: 79.6 us; the launch traced here: 78.8 us
  waiting for transfers between devices  37.6 us (47%)
  starting transfers between devices  31.5 us (40%)
  Pallas kernels  7.29 us (9%)
  between operations  1.47 us (2%)
    ppermute x18, waiting for transfers between devices, move(): return lax.ppermute(value, ('dom', 'section'), pairs)  29.1 us
    ppermute x18, starting transfers between devices, move(): return lax.ppermute(value, ('dom', 'section'), pairs)  15.8 us
    ppermute x6, starting transfers between devices, swap(): return lax.ppermute(value, 'dom', [(i, i ^ mask) for i in range(doms)])  8.38 us
    ppermute x1, starting transfers between devices, per_device(): lax.ppermute(far, 'dom', far_pairs)  4.47 us
    ppermute x6, waiting for transfers between devices, swap(): return lax.ppermute(value, 'dom', [(i, i ^ mask) for i in range(doms)])  4.44 us
    ppermute x1, starting transfers between devices, per_device(): far = lax.ppermute(far, 'dom', far_pairs)  2.8 us
    ppermute x1, waiting for transfers between devices, per_device(): far = lax.ppermute(far, 'dom', far_pairs)  2.77 us
    pallas_call x2, Pallas kernels, call(): pl.pallas_call(body, in_specs=[smem] + [vmem()] * (len(args) - 1), out_sp...  1.74 us
  transfers between devices with their start and end apart: 27, of which 9 were waited for; matrix products, arithmetic and copies ran while one was open for 0% of the time, Pallas kernels for 3%

profile of v5, /device:TPU:1, one launch (start us, length us, event | category | flops | bytes accessed | tf_op | source)
XLA Modules:
  0.0 78.8 jit_solution(11337838280248240685)
XLA Ops:
  0.6 1.4 %load.1 = (bf16[4,256,256]{2,1,0:T(8,128)(2,1)S(1)}, bf16[4,256,256]{2,1,0:T(8,128)(2,1)S(1)}, bf16[512,256]{1,0:T(8,128)(2,1)S(1)}, bf16[256,256]{1,0:T(8,128)(...) custom-call(s32[1]{0:T(128)} %bitcast.1.odd_ref, ...), custom_call_target="tpu_custom_call" | custom-call | tf_op jit(solution)/shard_map/load/pallas_call | solution.py:257
  2.2 4.5 %collective-permute-start.1 = (bf16[4,32,256]{2,1,0:T(8,128)(2,1)S(1)}, bf16[4,32,256]{2,1,0:T(8,128)(2,1)S(1)}, u32[]{:S(2)}, u32[]{:S(2)}) collective-permute-start(bf16[4,32,256]{2,1,0:T(8,128)(2,1)S(1)} %get-tuple-element.74), channel_id=1, source_target_pairs={{4,8},{8,4},{12,16},{16,12},{20,24},{24,20},{5,9},{9,5},{13,17},{1... | collective-permute-start | bytes 196616 | tf_op jit(solution)/shard_map/ppermute | solution.py:267
  7.3 1.3 %collective-permute-done.1.far_ref = bf16[4,32,256]{2,1,0:T(8,128)(2,1)S(1)} collective-permute-done((bf16[4,32,256]{2,1,0:T(8,128)(2,1)S(1)}, bf16[4,32,256]{2,1,0:T(8,128)(2,1)S(1)}, u32[]{:S(2)}, u32[]{:S(2)}) %collective-permute-start.1) | collective-permute-done | bytes 65568 | tf_op jit(solution)/shard_map/ppermute | solution.py:267
  8.6 0.8 %forward.1 = (f32[4,256,256]{2,1,0:T(8,128)S(1)}, bf16[4,256,256]{2,1,0:T(8,128)(2,1)S(1)}, bf16[4,256,256]{2,1,0:T(8,128)(2,1)S(1)}) custom-call(s32[1]{0:T(128)} %bitcast.1.odd_ref, f32[4,256,256]{2,1,0:T(8,128)S(1)} %get-tuple-element.71.base_ref, f32[4,256,256]{2,1,0:T(8,128)S(1)} %get-tuple-element.72.inner_ref, ...), custom_call_target="tpu_custom_call" | custom-call | tf_op jit(solution)/shard_map/forward/pallas_call | solution.py:248
  10.8 0.7 collective-permute-start.2
  12.9 0.7 collective-permute-start.11
  15.1 0.7 collective-permute-start.5
  17.2 0.7 collective-permute-start.14
  18.0 1.3 %collective-permute-start.9 = (bf16[2,32,256]{2,1,0:T(8,128)(2,1)S(1)}, bf16[2,32,256]{2,1,0:T(8,128)(2,1)S(1)}, u32[]{:S(2)}, u32[]{:S(2)}) collective-permute-start(bf16[2,32,256]{2,1,0:T(8,128)(2,1)S(1)} %get-tuple-element.90.refs_29_), channel_id=1, source_target_pairs={{5,0},{9,4},{13,8},{17,12},{21,16},{25,20},{29,24}} | collective-permute-start | bytes 98312 | tf_op jit(solution)/shard_map/ppermute | solution.py:283
  19.3 1.3 %collective-permute-start.10 = (bf16[2,32,256]{2,1,0:T(8,128)(2,1)S(1)}, bf16[2,32,256]{2,1,0:T(8,128)(2,1)S(1)}, u32[]{:S(2)}, u32[]{:S(2)}) collective-permute-start(bf16[2,32,256]{2,1,0:T(8,128)(2,1)S(1)} %get-tuple-element.91.refs_30_), channel_id=1, source_target_pairs={{1,4},{5,8},{9,12},{13,16},{17,20},{21,24},{25,28}} | collective-permute-start | bytes 98312 | tf_op jit(solution)/shard_map/ppermute | solution.py:283
  20.6 1.3 %collective-permute-start.8 = (bf16[2,256,256]{2,1,0:T(8,128)(2,1)S(1)}, bf16[2,256,256]{2,1,0:T(8,128)(2,1)S(1)}, u32[]{:S(2)}, u32[]{:S(2)}) collective-permute-start(bf16[2,256,256]{2,1,0:T(8,128)(2,1)S(1)} %get-tuple-element.89.refs_28_), channel_id=1, source_target_pairs={{1,0},{5,4},{9,8},{13,12},{17,16},{21,20},{25,24},{29,28}} | collective-permute-start | bytes 786440 | tf_op jit(solution)/shard_map/ppermute | solution.py:283
  22.0 1.3 %collective-permute-start.18 = (bf16[2,32,256]{2,1,0:T(8,128)(2,1)S(1)}, bf16[2,32,256]{2,1,0:T(8,128)(2,1)S(1)}, u32[]{:S(2)}, u32[]{:S(2)}) collective-permute-start(bf16[2,32,256]{2,1,0:T(8,128)(2,1)S(1)} %get-tuple-element.103.refs_34_), channel_id=1, source_target_pairs={{5,0},{9,4},{13,8},{17,12},{21,16},{25,20},{29,24}} | collective-permute-start | bytes 98312 | tf_op jit(solution)/shard_map/ppermute | solution.py:283
  23.3 1.3 %collective-permute-start.19 = (bf16[2,32,256]{2,1,0:T(8,128)(2,1)S(1)}, bf16[2,32,256]{2,1,0:T(8,128)(2,1)S(1)}, u32[]{:S(2)}, u32[]{:S(2)}) collective-permute-start(bf16[2,32,256]{2,1,0:T(8,128)(2,1)S(1)} %get-tuple-element.104.refs_35_), channel_id=1, source_target_pairs={{1,4},{5,8},{9,12},{13,16},{17,20},{21,24},{25,28}} | collective-permute-start | bytes 98312 | tf_op jit(solution)/shard_map/ppermute | solution.py:283
  24.6 18.9 %collective-permute-done.9.refs_1_ = bf16[2,32,256]{2,1,0:T(8,128)(2,1)S(1)} collective-permute-done((bf16[2,32,256]{2,1,0:T(8,128)(2,1)S(1)}, bf16[2,32,256]{2,1,0:T(8,128)(2,1)S(1)}, u32[]{:S(2)}, u32[]{:S(2)}) %collective-permute-start.9) | collective-permute-done | bytes 32800 | tf_op jit(solution)/shard_map/ppermute | solution.py:283
  43.5 1.3 %collective-permute-start.17 = (bf16[2,256,256]{2,1,0:T(8,128)(2,1)S(1)}, bf16[2,256,256]{2,1,0:T(8,128)(2,1)S(1)}, u32[]{:S(2)}, u32[]{:S(2)}) collective-permute-start(bf16[2,256,256]{2,1,0:T(8,128)(2,1)S(1)} %get-tuple-element.102.refs_33_), channel_id=1, source_target_pairs={{1,0},{5,4},{9,8},{13,12},{17,16},{21,20},{25,24},{29,28}} | collective-permute-start | bytes 786440 | tf_op jit(solution)/shard_map/ppermute | solution.py:283
  44.8 4.0 %collective-permute-done.8.refs_0_ = bf16[2,256,256]{2,1,0:T(8,128)(2,1)S(1)} collective-permute-done((bf16[2,256,256]{2,1,0:T(8,128)(2,1)S(1)}, bf16[2,256,256]{2,1,0:T(8,128)(2,1)S(1)}, u32[]{:S(2)}, u32[]{:S(2)}) %collective-permute-start.8) | collective-permute-done | bytes 262176 | tf_op jit(solution)/shard_map/ppermute | solution.py:283
  48.8 0.8 step.11
  49.6 2.2 %collective-permute-done.18.refs_1_ = bf16[2,32,256]{2,1,0:T(8,128)(2,1)S(1)} collective-permute-done((bf16[2,32,256]{2,1,0:T(8,128)(2,1)S(1)}, bf16[2,32,256]{2,1,0:T(8,128)(2,1)S(1)}, u32[]{:S(2)}, u32[]{:S(2)}) %collective-permute-start.18) | collective-permute-done | bytes 32800 | tf_op jit(solution)/shard_map/ppermute | solution.py:283
  51.8 4.0 %collective-permute-done.17.refs_0_ = bf16[2,256,256]{2,1,0:T(8,128)(2,1)S(1)} collective-permute-done((bf16[2,256,256]{2,1,0:T(8,128)(2,1)S(1)}, bf16[2,256,256]{2,1,0:T(8,128)(2,1)S(1)}, u32[]{:S(2)}, u32[]{:S(2)}) %collective-permute-start.17) | collective-permute-done | bytes 262176 | tf_op jit(solution)/shard_map/ppermute | solution.py:283
  55.9 0.8 step.15
  57.4 0.8 weights.1
  58.6 1.2 %collective-permute-done.20.came_ref = bf16[512,256]{1,0:T(8,128)(2,1)S(1)} collective-permute-done((bf16[512,256]{1,0:T(8,128)(2,1)S(1)}, bf16[512,256]{1,0:T(8,128)(2,1)S(1)}, u32[]{:S(2)}, u32[]{:S(2)}) %collective-permute-start.20) | collective-permute-done | bytes 262176 | tf_op jit(solution)/shard_map/ppermute | solution.py:320
  59.9 1.6 %collective-permute-start.23 = (bf16[192,256]{1,0:T(8,128)(2,1)S(1)}, bf16[192,256]{1,0:T(8,128)(2,1)S(1)}, u32[]{:S(2)}, u32[]{:S(2)}) collective-permute-start(bf16[192,256]{1,0:T(8,128)(2,1)S(1)} %get-tuple-element.131.q_ref), channel_id=1, source_target_pairs={{0,16},{4,20},{8,24},{12,28},{16,0},{20,4},{24,8},{28,12},{1,17},{... | collective-permute-start | bytes 294920 | tf_op jit(solution)/shard_map/ppermute | solution.py:320
  61.5 1.4 %collective-permute-start.22 = (bf16[192,256]{1,0:T(8,128)(2,1)S(1)}, bf16[192,256]{1,0:T(8,128)(2,1)S(1)}, u32[]{:S(2)}, u32[]{:S(2)}) collective-permute-start(bf16[192,256]{1,0:T(8,128)(2,1)S(1)} %get-tuple-element.132.p_ref), channel_id=1, source_target_pairs={{0,8},{4,12},{8,0},{12,4},{16,24},{20,28},{24,16},{28,20},{1,9},{5... | collective-permute-start | bytes 294920 | tf_op jit(solution)/shard_map/ppermute | solution.py:320
  62.8 2.8 %collective-permute-start.21 = (bf16[4,32,256]{2,1,0:T(8,128)(2,1)S(1)}, bf16[4,32,256]{2,1,0:T(8,128)(2,1)S(1)}, u32[]{:S(2)}, u32[]{:S(2)}) collective-permute-start(bf16[4,32,256]{2,1,0:T(8,128)(2,1)S(1)} %get-tuple-element.122), channel_id=1, source_target_pairs={{4,8},{8,4},{12,16},{16,12},{20,24},{24,20},{5,9},{9,5},{13,17},{1... | collective-permute-start | bytes 196616 | tf_op jit(solution)/shard_map/ppermute | solution.py:323
  65.6 2.8 %collective-permute-done.21.far_ref = bf16[4,32,256]{2,1,0:T(8,128)(2,1)S(1)} collective-permute-done((bf16[4,32,256]{2,1,0:T(8,128)(2,1)S(1)}, bf16[4,32,256]{2,1,0:T(8,128)(2,1)S(1)}, u32[]{:S(2)}, u32[]{:S(2)}) %collective-permute-start.21) | collective-permute-done | bytes 65568 | tf_op jit(solution)/shard_map/ppermute | solution.py:323
  68.5 1.5 %collective-permute-start.24 = (bf16[192,256]{1,0:T(8,128)(2,1)S(1)}, bf16[192,256]{1,0:T(8,128)(2,1)S(1)}, u32[]{:S(2)}, u32[]{:S(2)}) collective-permute-start(bf16[192,256]{1,0:T(8,128)(2,1)S(1)} %get-tuple-element.127), channel_id=1, source_target_pairs={{0,16},{4,20},{8,24},{12,28},{16,0},{20,4},{24,8},{28,12},{1,17},{... | collective-permute-start | bytes 294920 | tf_op jit(solution)/shard_map/ppermute | solution.py:320
  70.4 1.6 %collective-permute-done.24 = bf16[192,256]{1,0:T(8,128)(2,1)S(1)} collective-permute-done((bf16[192,256]{1,0:T(8,128)(2,1)S(1)}, bf16[192,256]{1,0:T(8,128)(2,1)S(1)}, u32[]{:S(2)}, u32[]{:S(2)}) %collective-permute-start.24) | collective-permute-done | bytes 98336 | tf_op jit(solution)/shard_map/ppermute | solution.py:320
  72.0 1.7 %collective-permute-done.25 = bf16[192,256]{1,0:T(8,128)(2,1)S(1)} collective-permute-done((bf16[192,256]{1,0:T(8,128)(2,1)S(1)}, bf16[192,256]{1,0:T(8,128)(2,1)S(1)}, u32[]{:S(2)}, u32[]{:S(2)}) %collective-permute-start.25) | collective-permute-done | bytes 98336 | tf_op jit(solution)/shard_map/ppermute | solution.py:320
  73.7 3.0 %collective-permute-start.26 = (bf16[384,256]{1,0:T(8,128)(2,1)S(1)}, bf16[384,256]{1,0:T(8,128)(2,1)S(1)}, u32[]{:S(2)}, u32[]{:S(2)}) collective-permute-start(bf16[384,256]{1,0:T(8,128)(2,1)S(1)} %pad_maximum_fusion.mine_ref), channel_id=1, source_target_pairs={{0,4},{4,0},{8,12},{12,8},{16,20},{20,16},{24,28},{28,24},{1,5},{5... | collective-permute-start | bytes 589832 | tf_op jit(solution)/shard_map/ppermute | solution.py:320
  76.8 1.1 %finish.1 = bf16[4,256,256]{2,1,0:T(8,128)(2,1)} custom-call(s32[1]{0:T(128)} %bitcast.hop_ref, s32[1]{0:T(128)} %bitcast.1.odd_ref, bf16[512,256]{1,0:T(8,128)(2,1)S(1)} %collective-permute-done.20.came_ref, bf16[4,32,256]{2,1,0:T(8,128)(2,1)S(1)} %collective-permute-done.21.far_ref, bf16[256,64]{1,0:T(8,128)(2,1)S(1)} %get-tuple-element.85.refs_3_.place_ref, ...), custom_call_target="tpu_custom_call" | custom-call | tf_op jit(solution)/shard_map/finish/pallas_call | solution.py:339
  77.8 0.9 %split.1 = (f32[512,256]{1,0:T(8,128)}, f32[256,256]{1,0:T(8,128)}) custom-call(s32[1]{0:T(128)} %bitcast.1.odd_ref, bf16[384,256]{1,0:T(8,128)(2,1)S(1)} %pad_maximum_fusion.mine_ref, bf16[384,256]{1,0:T(8,128)(2,1)S(1)} %collective-permute-done.26.other_ref), custom_call_target="tpu_custom_call" | custom-call | tf_op jit(solution)/shard_map/split/pallas_call | solution.py:248
  (101 shorter events, 8.0 us)
Async XLA Ops:
  2.1 5.2 %collective-permute-start = (bf16[4,32,256]{2,1,0:T(8,128)(2,1)S(1)}, bf16[4,32,256]{2,1,0:T(8,128)(2,1)S(1)}, u32[]{:S(2)}, u32[]{:S(2)}) collective-permute-start(bf16[4,32,256]{2,1,0:T(8,128)(2,1)S(1)} %get-tuple-element.73), channel_id=1, source_target_pairs={{0,4},{4,0},{8,12},{12,8},{16,20},{20,16},{24,28},{28,24},{1,5},{5... | collective-permute-start | bytes 196616 | tf_op jit(solution)/shard_map/ppermute | solution.py:267
  2.2 6.4 %collective-permute-start.1 = (bf16[4,32,256]{2,1,0:T(8,128)(2,1)S(1)}, bf16[4,32,256]{2,1,0:T(8,128)(2,1)S(1)}, u32[]{:S(2)}, u32[]{:S(2)}) collective-permute-start(bf16[4,32,256]{2,1,0:T(8,128)(2,1)S(1)} %get-tuple-element.74), channel_id=1, source_target_pairs={{4,8},{8,4},{12,16},{16,12},{20,24},{24,20},{5,9},{9,5},{13,17},{1... | collective-permute-start | bytes 196616 | tf_op jit(solution)/shard_map/ppermute | solution.py:267
  9.5 3.5 %collective-permute-start.3 = (bf16[2,32,256]{2,1,0:T(8,128)(2,1)S(1)}, bf16[2,32,256]{2,1,0:T(8,128)(2,1)S(1)}, u32[]{:S(2)}, u32[]{:S(2)}) collective-permute-start(bf16[2,32,256]{2,1,0:T(8,128)(2,1)S(1)} %get-tuple-element.83.refs_9_), channel_id=1, source_target_pairs={{7,2},{11,6},{15,10},{19,14},{23,18},{27,22},{31,26}} | collective-permute-start | bytes 98312 | tf_op jit(solution)/shard_map/ppermute | solution.py:283
  10.1 3.5 %collective-permute-start.4 = (bf16[2,32,256]{2,1,0:T(8,128)(2,1)S(1)}, bf16[2,32,256]{2,1,0:T(8,128)(2,1)S(1)}, u32[]{:S(2)}, u32[]{:S(2)}) collective-permute-start(bf16[2,32,256]{2,1,0:T(8,128)(2,1)S(1)} %get-tuple-element.84.refs_10_), channel_id=1, source_target_pairs={{3,6},{7,10},{11,14},{15,18},{19,22},{23,26},{27,30}} | collective-permute-start | bytes 98312 | tf_op jit(solution)/shard_map/ppermute | solution.py:283
  10.8 2.8 %collective-permute-start.2 = (bf16[2,256,256]{2,1,0:T(8,128)(2,1)S(1)}, bf16[2,256,256]{2,1,0:T(8,128)(2,1)S(1)}, u32[]{:S(2)}, u32[]{:S(2)}) collective-permute-start(bf16[2,256,256]{2,1,0:T(8,128)(2,1)S(1)} %get-tuple-element.82.refs_8_), channel_id=1, source_target_pairs={{3,2},{7,6},{11,10},{15,14},{19,18},{23,22},{27,26},{31,30}} | collective-permute-start | bytes 786440 | tf_op jit(solution)/shard_map/ppermute | solution.py:283
  11.6 3.5 %collective-permute-start.12 = (bf16[2,32,256]{2,1,0:T(8,128)(2,1)S(1)}, bf16[2,32,256]{2,1,0:T(8,128)(2,1)S(1)}, u32[]{:S(2)}, u32[]{:S(2)}) collective-permute-start(bf16[2,32,256]{2,1,0:T(8,128)(2,1)S(1)} %get-tuple-element.97.refs_14_), channel_id=1, source_target_pairs={{7,2},{11,6},{15,10},{19,14},{23,18},{27,22},{31,26}} | collective-permute-start | bytes 98312 | tf_op jit(solution)/shard_map/ppermute | solution.py:283
  12.3 3.5 %collective-permute-start.13 = (bf16[2,32,256]{2,1,0:T(8,128)(2,1)S(1)}, bf16[2,32,256]{2,1,0:T(8,128)(2,1)S(1)}, u32[]{:S(2)}, u32[]{:S(2)}) collective-permute-start(bf16[2,32,256]{2,1,0:T(8,128)(2,1)S(1)} %get-tuple-element.98.refs_15_), channel_id=1, source_target_pairs={{3,6},{7,10},{11,14},{15,18},{19,22},{23,26},{27,30}} | collective-permute-start | bytes 98312 | tf_op jit(solution)/shard_map/ppermute | solution.py:283
  12.9 2.8 %collective-permute-start.11 = (bf16[2,256,256]{2,1,0:T(8,128)(2,1)S(1)}, bf16[2,256,256]{2,1,0:T(8,128)(2,1)S(1)}, u32[]{:S(2)}, u32[]{:S(2)}) collective-permute-start(bf16[2,256,256]{2,1,0:T(8,128)(2,1)S(1)} %get-tuple-element.96.refs_13_), channel_id=1, source_target_pairs={{3,2},{7,6},{11,10},{15,14},{19,18},{23,22},{27,26},{31,30}} | collective-permute-start | bytes 786440 | tf_op jit(solution)/shard_map/ppermute | solution.py:283
  13.7 3.5 %collective-permute-start.6 = (bf16[2,32,256]{2,1,0:T(8,128)(2,1)S(1)}, bf16[2,32,256]{2,1,0:T(8,128)(2,1)S(1)}, u32[]{:S(2)}, u32[]{:S(2)}) collective-permute-start(bf16[2,32,256]{2,1,0:T(8,128)(2,1)S(1)} %get-tuple-element.87.refs_19_), channel_id=1, source_target_pairs={{6,1},{10,5},{14,9},{18,13},{22,17},{26,21},{30,25}} | collective-permute-start | bytes 98312 | tf_op jit(solution)/shard_map/ppermute | solution.py:283
  14.4 3.5 %collective-permute-start.7 = (bf16[2,32,256]{2,1,0:T(8,128)(2,1)S(1)}, bf16[2,32,256]{2,1,0:T(8,128)(2,1)S(1)}, u32[]{:S(2)}, u32[]{:S(2)}) collective-permute-start(bf16[2,32,256]{2,1,0:T(8,128)(2,1)S(1)} %get-tuple-element.88.refs_20_), channel_id=1, source_target_pairs={{2,5},{6,9},{10,13},{14,17},{18,21},{22,25},{26,29}} | collective-permute-start | bytes 98312 | tf_op jit(solution)/shard_map/ppermute | solution.py:283
  15.1 2.8 %collective-permute-start.5 = (bf16[2,256,256]{2,1,0:T(8,128)(2,1)S(1)}, bf16[2,256,256]{2,1,0:T(8,128)(2,1)S(1)}, u32[]{:S(2)}, u32[]{:S(2)}) collective-permute-start(bf16[2,256,256]{2,1,0:T(8,128)(2,1)S(1)} %get-tuple-element.86.refs_18_), channel_id=1, source_target_pairs={{2,1},{6,5},{10,9},{14,13},{18,17},{22,21},{26,25},{30,29}} | collective-permute-start | bytes 786440 | tf_op jit(solution)/shard_map/ppermute | solution.py:283
  15.9 4.7 %collective-permute-start.15 = (bf16[2,32,256]{2,1,0:T(8,128)(2,1)S(1)}, bf16[2,32,256]{2,1,0:T(8,128)(2,1)S(1)}, u32[]{:S(2)}, u32[]{:S(2)}) collective-permute-start(bf16[2,32,256]{2,1,0:T(8,128)(2,1)S(1)} %get-tuple-element.100.refs_24_), channel_id=1, source_target_pairs={{6,1},{10,5},{14,9},{18,13},{22,17},{26,21},{30,25}} | collective-permute-start | bytes 98312 | tf_op jit(solution)/shard_map/ppermute | solution.py:283
  16.5 5.4 %collective-permute-start.16 = (bf16[2,32,256]{2,1,0:T(8,128)(2,1)S(1)}, bf16[2,32,256]{2,1,0:T(8,128)(2,1)S(1)}, u32[]{:S(2)}, u32[]{:S(2)}) collective-permute-start(bf16[2,32,256]{2,1,0:T(8,128)(2,1)S(1)} %get-tuple-element.101.refs_25_), channel_id=1, source_target_pairs={{2,5},{6,9},{10,13},{14,17},{18,21},{22,25},{26,29}} | collective-permute-start | bytes 98312 | tf_op jit(solution)/shard_map/ppermute | solution.py:283
  17.2 4.7 %collective-permute-start.14 = (bf16[2,256,256]{2,1,0:T(8,128)(2,1)S(1)}, bf16[2,256,256]{2,1,0:T(8,128)(2,1)S(1)}, u32[]{:S(2)}, u32[]{:S(2)}) collective-permute-start(bf16[2,256,256]{2,1,0:T(8,128)(2,1)S(1)} %get-tuple-element.99.refs_23_), channel_id=1, source_target_pairs={{2,1},{6,5},{10,9},{14,13},{18,17},{22,21},{26,25},{30,29}} | collective-permute-start | bytes 786440 | tf_op jit(solution)/shard_map/ppermute | solution.py:283
  18.0 25.5 %collective-permute-start.9 = (bf16[2,32,256]{2,1,0:T(8,128)(2,1)S(1)}, bf16[2,32,256]{2,1,0:T(8,128)(2,1)S(1)}, u32[]{:S(2)}, u32[]{:S(2)}) collective-permute-start(bf16[2,32,256]{2,1,0:T(8,128)(2,1)S(1)} %get-tuple-element.90.refs_29_), channel_id=1, source_target_pairs={{5,0},{9,4},{13,8},{17,12},{21,16},{25,20},{29,24}} | collective-permute-start | bytes 98312 | tf_op jit(solution)/shard_map/ppermute | solution.py:283
  19.3 25.5 %collective-permute-start.10 = (bf16[2,32,256]{2,1,0:T(8,128)(2,1)S(1)}, bf16[2,32,256]{2,1,0:T(8,128)(2,1)S(1)}, u32[]{:S(2)}, u32[]{:S(2)}) collective-permute-start(bf16[2,32,256]{2,1,0:T(8,128)(2,1)S(1)} %get-tuple-element.91.refs_30_), channel_id=1, source_target_pairs={{1,4},{5,8},{9,12},{13,16},{17,20},{21,24},{25,28}} | collective-permute-start | bytes 98312 | tf_op jit(solution)/shard_map/ppermute | solution.py:283
  20.6 28.2 %collective-permute-start.8 = (bf16[2,256,256]{2,1,0:T(8,128)(2,1)S(1)}, bf16[2,256,256]{2,1,0:T(8,128)(2,1)S(1)}, u32[]{:S(2)}, u32[]{:S(2)}) collective-permute-start(bf16[2,256,256]{2,1,0:T(8,128)(2,1)S(1)} %get-tuple-element.89.refs_28_), channel_id=1, source_target_pairs={{1,0},{5,4},{9,8},{13,12},{17,16},{21,20},{25,24},{29,28}} | collective-permute-start | bytes 786440 | tf_op jit(solution)/shard_map/ppermute | solution.py:283
  22.0 29.8 %collective-permute-start.18 = (bf16[2,32,256]{2,1,0:T(8,128)(2,1)S(1)}, bf16[2,32,256]{2,1,0:T(8,128)(2,1)S(1)}, u32[]{:S(2)}, u32[]{:S(2)}) collective-permute-start(bf16[2,32,256]{2,1,0:T(8,128)(2,1)S(1)} %get-tuple-element.103.refs_34_), channel_id=1, source_target_pairs={{5,0},{9,4},{13,8},{17,12},{21,16},{25,20},{29,24}} | collective-permute-start | bytes 98312 | tf_op jit(solution)/shard_map/ppermute | solution.py:283
  23.3 28.5 %collective-permute-start.19 = (bf16[2,32,256]{2,1,0:T(8,128)(2,1)S(1)}, bf16[2,32,256]{2,1,0:T(8,128)(2,1)S(1)}, u32[]{:S(2)}, u32[]{:S(2)}) collective-permute-start(bf16[2,32,256]{2,1,0:T(8,128)(2,1)S(1)} %get-tuple-element.104.refs_35_), channel_id=1, source_target_pairs={{1,4},{5,8},{9,12},{13,16},{17,20},{21,24},{25,28}} | collective-permute-start | bytes 98312 | tf_op jit(solution)/shard_map/ppermute | solution.py:283
  43.5 12.3 %collective-permute-start.17 = (bf16[2,256,256]{2,1,0:T(8,128)(2,1)S(1)}, bf16[2,256,256]{2,1,0:T(8,128)(2,1)S(1)}, u32[]{:S(2)}, u32[]{:S(2)}) collective-permute-start(bf16[2,256,256]{2,1,0:T(8,128)(2,1)S(1)} %get-tuple-element.102.refs_33_), channel_id=1, source_target_pairs={{1,0},{5,4},{9,8},{13,12},{17,16},{21,20},{25,24},{29,28}} | collective-permute-start | bytes 786440 | tf_op jit(solution)/shard_map/ppermute | solution.py:283
  49.6 7.1 %copy-start.1 = (bf16[2,256,256]{2,1,0:T(8,128)(2,1)S(1)}, bf16[2,256,256]{2,1,0:T(8,128)(2,1)}, u32[]{:S(2)}) copy-start(bf16[2,256,256]{2,1,0:T(8,128)(2,1)} %copy-done) | copy-start | bytes 786436
  49.6 7.1 %copy-start.3 = (bf16[2,256,256]{2,1,0:T(8,128)(2,1)S(1)}, bf16[2,256,256]{2,1,0:T(8,128)(2,1)}, u32[]{:S(2)}) copy-start(bf16[2,256,256]{2,1,0:T(8,128)(2,1)} %copy-done.2) | copy-start | bytes 786436
  49.6 7.1 %copy-start.5 = (bf16[2,256,256]{2,1,0:T(8,128)(2,1)S(1)}, bf16[2,256,256]{2,1,0:T(8,128)(2,1)}, u32[]{:S(2)}) copy-start(bf16[2,256,256]{2,1,0:T(8,128)(2,1)} %copy-done.4) | copy-start | bytes 786436
  49.6 7.1 %copy-start.7 = (bf16[2,256,256]{2,1,0:T(8,128)(2,1)S(1)}, bf16[2,256,256]{2,1,0:T(8,128)(2,1)}, u32[]{:S(2)}) copy-start(bf16[2,256,256]{2,1,0:T(8,128)(2,1)} %copy-done.6) | copy-start | bytes 786436
  49.6 7.1 %copy-start.9 = (bf16[2,256,256]{2,1,0:T(8,128)(2,1)S(1)}, bf16[2,256,256]{2,1,0:T(8,128)(2,1)}, u32[]{:S(2)}) copy-start(bf16[2,256,256]{2,1,0:T(8,128)(2,1)} %copy-done.8) | copy-start | bytes 786436
  58.2 1.6 %collective-permute-start.20 = (bf16[512,256]{1,0:T(8,128)(2,1)S(1)}, bf16[512,256]{1,0:T(8,128)(2,1)S(1)}, u32[]{:S(2)}, u32[]{:S(2)}) collective-permute-start(bf16[512,256]{1,0:T(8,128)(2,1)S(1)} %get-tuple-element.121), channel_id=1, source_target_pairs={{0,4},{4,0},{8,12},{12,8},{16,20},{20,16},{24,28},{28,24},{1,5},{5... | collective-permute-start | bytes 786440 | tf_op jit(solution)/shard_map/ppermute | solution.py:320
  59.9 8.6 %collective-permute-start.23 = (bf16[192,256]{1,0:T(8,128)(2,1)S(1)}, bf16[192,256]{1,0:T(8,128)(2,1)S(1)}, u32[]{:S(2)}, u32[]{:S(2)}) collective-permute-start(bf16[192,256]{1,0:T(8,128)(2,1)S(1)} %get-tuple-element.131.q_ref), channel_id=1, source_target_pairs={{0,16},{4,20},{8,24},{12,28},{16,0},{20,4},{24,8},{28,12},{1,17},{... | collective-permute-start | bytes 294920 | tf_op jit(solution)/shard_map/ppermute | solution.py:320
  61.5 7.0 %collective-permute-start.22 = (bf16[192,256]{1,0:T(8,128)(2,1)S(1)}, bf16[192,256]{1,0:T(8,128)(2,1)S(1)}, u32[]{:S(2)}, u32[]{:S(2)}) collective-permute-start(bf16[192,256]{1,0:T(8,128)(2,1)S(1)} %get-tuple-element.132.p_ref), channel_id=1, source_target_pairs={{0,8},{4,12},{8,0},{12,4},{16,24},{20,28},{24,16},{28,20},{1,9},{5... | collective-permute-start | bytes 294920 | tf_op jit(solution)/shard_map/ppermute | solution.py:320
  62.8 5.6 %collective-permute-start.21 = (bf16[4,32,256]{2,1,0:T(8,128)(2,1)S(1)}, bf16[4,32,256]{2,1,0:T(8,128)(2,1)S(1)}, u32[]{:S(2)}, u32[]{:S(2)}) collective-permute-start(bf16[4,32,256]{2,1,0:T(8,128)(2,1)S(1)} %get-tuple-element.122), channel_id=1, source_target_pairs={{4,8},{8,4},{12,16},{16,12},{20,24},{24,20},{5,9},{9,5},{13,17},{1... | collective-permute-start | bytes 196616 | tf_op jit(solution)/shard_map/ppermute | solution.py:323
  68.5 3.5 %collective-permute-start.24 = (bf16[192,256]{1,0:T(8,128)(2,1)S(1)}, bf16[192,256]{1,0:T(8,128)(2,1)S(1)}, u32[]{:S(2)}, u32[]{:S(2)}) collective-permute-start(bf16[192,256]{1,0:T(8,128)(2,1)S(1)} %get-tuple-element.127), channel_id=1, source_target_pairs={{0,16},{4,20},{8,24},{12,28},{16,0},{20,4},{24,8},{28,12},{1,17},{... | collective-permute-start | bytes 294920 | tf_op jit(solution)/shard_map/ppermute | solution.py:320
  69.9 3.8 %collective-permute-start.25 = (bf16[192,256]{1,0:T(8,128)(2,1)S(1)}, bf16[192,256]{1,0:T(8,128)(2,1)S(1)}, u32[]{:S(2)}, u32[]{:S(2)}) collective-permute-start(bf16[192,256]{1,0:T(8,128)(2,1)S(1)} %get-tuple-element.128), channel_id=1, source_target_pairs={{0,8},{4,12},{8,0},{12,4},{16,24},{20,28},{24,16},{28,20},{1,9},{5... | collective-permute-start | bytes 294920 | tf_op jit(solution)/shard_map/ppermute | solution.py:320
  73.7 4.1 %collective-permute-start.26 = (bf16[384,256]{1,0:T(8,128)(2,1)S(1)}, bf16[384,256]{1,0:T(8,128)(2,1)S(1)}, u32[]{:S(2)}, u32[]{:S(2)}) collective-permute-start(bf16[384,256]{1,0:T(8,128)(2,1)S(1)} %pad_maximum_fusion.mine_ref), channel_id=1, source_target_pairs={{0,4},{4,0},{8,12},{12,8},{16,20},{20,16},{24,28},{28,24},{1,5},{5... | collective-permute-start | bytes 589832 | tf_op jit(solution)/shard_map/ppermute | solution.py:320
  (25 other events, 46.2 us)

commit v6 on v5

v6 whole, which is shorter than its diff:
```python
import jax
import jax.numpy as jnp
from jax import lax
from jax.experimental import pallas as pl
from jax.experimental.pallas import tpu as pltpu
from jax.sharding import PartitionSpec as P

F32 = jnp.float32
BF16 = jnp.bfloat16
CHUNKS = 2
STEP_FLOPS = 10**11


def dot(a, b, dims=((1,), (0,))):
    return lax.dot_general(a, b, (dims, ((), ())), preferred_element_type=F32)


def hop_of(info_ref):
    return info_ref[0] >> 2


def odd_of(info_ref):
    return (info_ref[0] >> 1) & 1


def end_of(info_ref):
    return info_ref[0] & 1


def vmem():
    return pl.BlockSpec(memory_space=pltpu.VMEM)


def params():
    return pltpu.CompilerParams(vmem_limit_bytes=16 * 1024 * 1024)


def load_kernel(info_ref, x_hbm, g_hbm, w1_hbm, w2_hbm, nbr_hbm, coef_hbm, send_hbm,
                x_ref, g_ref, w1_ref, w2_ref, nbr_ref, coef_ref, place_ref, near_ref, far_ref, send_ref, sems):
    sources = (send_hbm, x_hbm, nbr_hbm, coef_hbm, w1_hbm, w2_hbm, g_hbm)
    targets = (send_ref, x_ref, nbr_ref, coef_ref, w1_ref, w2_ref, g_ref)
    copies = [pltpu.make_async_copy(source, target, sems.at[n])
              for n, (source, target) in enumerate(zip(sources, targets))]
    for copy in copies:
        copy.start()
    batches, rows, _ = x_ref.shape
    slots = send_ref.shape[1]
    row = lax.broadcasted_iota(jnp.int32, (rows, slots), 0)
    copies[0].wait()
    up = jnp.where(row == send_ref[0:1, :], 1.0, 0.0)
    down = jnp.where(row == send_ref[1:2, :], 1.0, 0.0)
    place = jnp.concatenate([up, down], axis=1)
    place_ref[...] = place.astype(BF16)
    pick = place.T.astype(BF16)
    copies[1].wait()
    odd = odd_of(info_ref) == 1
    for m in range(batches):
        sent = dot(pick, x_ref[m])
        up, down = sent[:slots], sent[slots:]
        near_ref[m] = jnp.where(odd, down, up).astype(BF16)
        far_ref[m] = jnp.where(odd, up, down).astype(BF16)
    for copy in copies[2:]:
        copy.wait()


def inner_kernel(x_ref, nbr_ref, coef_ref, w_ref, base_ref, inner_ref, own_ref, halo_ref):
    batches, rows, width = x_ref.shape
    slots = halo_ref.shape[0] // 2
    faces = nbr_ref.shape[0]
    slot = lax.broadcasted_iota(jnp.int32, (rows + 2 * slots, rows), 0)
    spread = jnp.zeros((rows + 2 * slots, rows), F32)
    for k in range(faces):
        spread = spread + jnp.where(slot == nbr_ref[k : k + 1, :], coef_ref[k : k + 1, :], 0.0)
    own = spread[slots : slots + rows]
    halo_ref[...] = jnp.concatenate([spread[:slots], spread[slots + rows :]], axis=0).astype(BF16)
    own_ref[...] = own.astype(BF16)
    own_t = own.T.astype(BF16)
    for m in range(batches):
        x = x_ref[m]
        inner_ref[m] = dot(own_t, x)
        base_ref[m] = dot(x, w_ref[:width])


def forward_kernel(info_ref, base_ref, inner_ref, near_ref, far_ref, halo_ref, w_ref, slope_ref, act_ref, agg_ref):
    batches, rows, width = base_ref.shape
    slots = near_ref.shape[1]
    odd = odd_of(info_ref) == 1
    lower, upper = halo_ref[:slots].astype(F32), halo_ref[slots:].astype(F32)
    near = jnp.where(odd, lower, upper)
    far = jnp.where(end_of(info_ref) == 1, 0.0, jnp.where(odd, upper, lower))
    halo_t = jnp.concatenate([near, far], axis=0).T.astype(BF16)
    for m in range(batches):
        edge = jnp.concatenate([near_ref[m], far_ref[m]], axis=0)
        agg = (inner_ref[m] + dot(halo_t, edge)).astype(BF16)
        z = base_ref[m] + dot(agg, w_ref[width:])
        sig = 1.0 / (1.0 + jnp.exp(-z))
        agg_ref[m] = agg
        act_ref[m] = (z * sig).astype(BF16)
        slope_ref[m] = sig * (1.0 + z * (1.0 - sig))


def assemble(local, upper, lower, place):
    edge = jnp.concatenate([upper, lower], axis=0)
    return (local.astype(F32) + dot(place, edge)).astype(BF16)


def step(g, first, slope_ref, own_ref, halo_ref, w1_ref, w2_ref, local_ref, below_ref, above_ref, g_ref, dz_ref):
    rows, width = slope_ref.shape[1:]
    slots = halo_ref.shape[0] // 2
    count = len(g)
    d_act = dot(jnp.concatenate(g, axis=0), w2_ref[...], ((1,), (1,)))
    dz = [(d_act[j * rows : (j + 1) * rows] * slope_ref[first + j]).astype(BF16) for j in range(count)]
    dj = dot(jnp.concatenate(dz, axis=0), w1_ref[...], ((1,), (1,)))
    for j in range(count):
        part = dj[j * rows : (j + 1) * rows]
        dagg = part[:, width:].astype(BF16)
        local = g[j].astype(F32) + part[:, :width] + dot(own_ref[...], dagg)
        local_ref[j] = local.astype(BF16)
        edge = dot(halo_ref[...], dagg).astype(BF16)
        below_ref[j] = edge[:slots]
        above_ref[j] = edge[slots:]
        g_ref[j] = g[j]
        dz_ref[j] = dz[j]


def start_values(hop, first, count, inputs):
    if hop == 0:
        return [inputs[0][first + j] for j in range(count)]
    loc_ref, upper_ref, lower_ref, place_ref = inputs
    return [assemble(loc_ref[j], upper_ref[j], lower_ref[j], place_ref[...]) for j in range(count)]


def make_step_kernel(hop, first, count):
    def body(info_ref, *refs):
        inputs, arrays = refs[:-10], refs[-10:]

        @pl.when(hop_of(info_ref) == hop)
        def _():
            step(start_values(hop, first, count, inputs), first, *arrays)

    return body


def make_last_kernel(hop, first, count, earlier):
    def body(info_ref, *refs):
        (local_ref, g_ref, dz_ref, near_ref, far_ref, below_ref, above_ref) = refs[-7:]
        kept_below, kept_above = refs[-9:-7]
        edges = refs[-9 - 2 * earlier : -9]
        arrays = refs[-14 - 2 * earlier : -9 - 2 * earlier]
        inputs = refs[: -14 - 2 * earlier]
        odd = odd_of(info_ref) == 1

        def sort(below, above, where):
            near_ref[where] = jnp.where(odd, below, above)
            far_ref[where] = jnp.where(odd, above, below)

        @pl.when(hop_of(info_ref) == hop)
        def _():
            step(start_values(hop, first, count, inputs), first, *arrays,
                 local_ref, below_ref, above_ref, g_ref, dz_ref)
            for c in range(earlier):
                sort(edges[2 * c][...], edges[2 * c + 1][...], slice(c * count, (c + 1) * count))
            sort(below_ref[...], above_ref[...], slice(first, first + count))

        @pl.when(hop_of(info_ref) != hop)
        def _():
            sort(kept_below[...], kept_above[...], slice(0, first + count))

    return body


def gradients(sources, parts, out_ref, start=None):
    width = out_ref.shape[1]
    for n, source in enumerate(sources):
        total = 0.0 if start is None else start[n * width : (n + 1) * width]
        for first, size, g, dz in parts:
            rows = source.shape[1]
            left = source[first : first + size].reshape(size * rows, width)
            right = (g if n == 2 else dz)[...].reshape(size * rows, width)
            total = total + dot(left, right, ((0,), (0,)))
        out_ref[n * width : (n + 1) * width] = total


def make_partial_kernel(hops, chunks):
    def body(info_ref, x_ref, agg_ref, act_ref, *refs):
        part_ref, local_ref, below_ref, above_ref, g_ref, dz_ref, sems = refs[-7:]
        here = [refs[2 * c : 2 * c + 2] for c in range(chunks - 1)]
        pieces = refs[2 * chunks - 2 : -7]
        targets = (local_ref, below_ref, above_ref, g_ref, dz_ref)
        batches = x_ref.shape[0]
        count = batches // chunks

        def copies(hop):
            return [pltpu.make_async_copy(pieces[(hop * chunks + c) * 5 + n],
                                          targets[n].at[pl.ds(c * count, count)], sems.at[n, c])
                    for n in range(5) for c in range(chunks)]

        for hop in range(hops - 1):
            @pl.when(hop_of(info_ref) == hop)
            def _():
                for copy in copies(hop):
                    copy.start()

        if chunks > 1:
            @pl.when(hop_of(info_ref) == hops - 1)
            def _():
                parts = [(c * count, count, g, dz) for c, (g, dz) in enumerate(here)]
                gradients((x_ref, agg_ref, act_ref), parts, part_ref)
        else:
            @pl.when(hop_of(info_ref) == hops - 1)
            def _():
                part_ref[...] = jnp.zeros_like(part_ref)

        if hops > 1:
            @pl.when(hop_of(info_ref) != hops - 1)
            def _():
                for copy in copies(0):
                    copy.wait()
                gradients((x_ref, agg_ref, act_ref), [(0, batches, g_ref, dz_ref)], part_ref)

    return body


def make_weight_kernel(last, first, count):
    def body(info_ref, x_ref, agg_ref, act_ref, part_ref, g_ref, dz_ref, near_ref, keep_ref, give_ref, grad_ref):
        width = part_ref.shape[1]
        half = keep_ref.shape[0]
        odd = odd_of(info_ref)

        @pl.when(hop_of(info_ref) == last)
        def _():
            gradients((x_ref, agg_ref, act_ref), [(first, count, g_ref, dz_ref)], grad_ref, part_ref)

        @pl.when(hop_of(info_ref) != last)
        def _():
            grad_ref[...] = part_ref[...]

        keep_ref[...] = grad_ref[pl.ds(pl.multiple_of(odd * half, half), half)]
        give_ref[:half] = grad_ref[pl.ds(pl.multiple_of((1 - odd) * half, half), half)].astype(BF16)
        give_ref[half:] = near_ref[...].reshape(give_ref.shape[0] - half, width)

    return body


def add(a, b):
    return (a.astype(F32) + b.astype(F32)).astype(BF16)


def take_kernel(keep_ref, came_ref, far_ref, p_ref, q_ref):
    quarter = p_ref.shape[0]
    p_ref[...] = add(keep_ref[:quarter], came_ref[:quarter])
    q_ref[...] = add(keep_ref[quarter:], came_ref[quarter : 2 * quarter])


def split_kernel(info_ref, mine_ref, other_ref, first_ref, second_ref):
    half = mine_ref.shape[0]
    size = first_ref.shape[0]
    odd = odd_of(info_ref) == 1
    mine, other = mine_ref[...].astype(F32), other_ref[...].astype(F32)
    low = jnp.where(odd, other, mine)
    high = jnp.where(odd, mine, other)
    first_ref[:half] = low
    first_ref[half:] = high[: size - half]
    second_ref[...] = high[size - half :]


def make_finish_kernel(last):
    def body(info_ref, came_ref, far_ref, place_ref, loc_ref, *refs):
        here, out_ref = refs[:-1], refs[-1]
        odd, end = odd_of(info_ref) == 1, end_of(info_ref) == 1
        batches, slots = far_ref.shape[:2]
        count = batches // len(here)
        start = came_ref.shape[0] - batches * slots

        def write(local):
            for m in range(batches):
                near = came_ref[start + m * slots : start + (m + 1) * slots]
                far = jnp.where(end, jnp.zeros_like(far_ref[m]), far_ref[m])
                upper = jnp.where(odd, far, near)
                lower = jnp.where(odd, near, far)
                out_ref[m] = assemble(local(m), upper, lower, place_ref[...])

        @pl.when(hop_of(info_ref) == last)
        def _():
            write(lambda m: here[m // count][m % count])

        @pl.when(hop_of(info_ref) != last)
        def _():
            write(lambda m: loc_ref[m])

    return body


def per_device(saved_inputs, grad_out, w_first, w_second, face_weight, neighbours, send_rows):
    x = saved_inputs[0]
    w1 = w_first[0]
    w2 = w_second[0]
    batches, rows, width = x.shape
    slots = send_rows.shape[1]
    sections = lax.axis_size("section")
    doms = lax.axis_size("dom")
    chunks = CHUNKS if batches % CHUNKS == 0 else 1
    count = batches // chunks
    dom = lax.axis_index("dom")
    hop_here = sections - 1 - lax.axis_index("section")
    end = ((dom == 0) | (dom == doms - 1)).astype(jnp.int32)
    info = (4 * hop_here + 2 * (dom % 2) + end).astype(jnp.int32).reshape(1)
    sds = jax.ShapeDtypeStruct
    smem = pl.BlockSpec(memory_space=pltpu.SMEM)
    any_spec = pl.BlockSpec(memory_space=pl.ANY)
    hbm_spec = pl.BlockSpec(memory_space=pltpu.HBM)

    def like(value):
        return sds(value.shape, value.dtype)

    def call(body, outs, *args, scratch=(), name):
        return pl.pallas_call(
            body, in_specs=[smem] + [vmem()] * (len(args) - 1), out_specs=[vmem()] * len(outs), out_shape=outs,
            scratch_shapes=scratch, compiler_params=params(), name=name,
        )(*args)

    near_pairs = [(p, p ^ 1) for p in range(doms)]
    far_pairs = [(p, (p + 1 if p % 2 else p - 1) % doms) for p in range(doms)]

    edge_shape = sds((batches, slots, width), BF16)
    x, grad_out, w1, w2, neighbours, face_weight, place, near, far = pl.pallas_call(
        load_kernel,
        in_specs=[smem] + [hbm_spec] * 7,
        out_specs=[vmem()] * 9,
        out_shape=(like(x), like(grad_out), like(w1), like(w2), like(neighbours), like(face_weight),
                   sds((rows, 2 * slots), BF16), edge_shape, edge_shape),
        scratch_shapes=[pltpu.VMEM(send_rows.shape, send_rows.dtype), pltpu.SemaphoreType.DMA((7,))],
        compiler_params=params(), name="load",
    )(info, *[pltpu.with_memory_space_constraint(value, pltpu.HBM)
             for value in (x, grad_out, w1, w2, neighbours, face_weight, send_rows)])
    near, far = lax.ppermute(near, "dom", near_pairs), lax.ppermute(far, "dom", far_pairs)

    full_shape = sds((batches, rows, width), BF16)
    wide_shape = sds((batches, rows, width), F32)
    base, inner, own, halo = pl.pallas_call(
        inner_kernel, in_specs=[vmem()] * 4, out_specs=[vmem()] * 4,
        out_shape=(wide_shape, wide_shape, sds((rows, rows), BF16), sds((2 * slots, rows), BF16)),
        compiler_params=params(), name="inner",
    )(x, neighbours, face_weight, w1)
    slope, act, agg = call(
        forward_kernel, (wide_shape, full_shape, full_shape), info, base, inner, near, far, halo, w1, name="forward")

    def move(value, hop, shift):
        source = sections - 1 - hop
        pairs = [(p * sections + source, (p + shift) * sections + source - 1)
                 for p in range(doms) if 0 <= p + shift < doms]
        return lax.ppermute(value, ("dom", "section"), pairs)

    piece, piece_edge = sds((count, rows, width), BF16), sds((count, slots, width), BF16)
    estimate = pl.CostEstimate(flops=STEP_FLOPS, bytes_accessed=1 << 20, transcendentals=0)
    pieces = []
    received = [None] * chunks
    weights = (slope, own, halo, w1, w2)
    for hop in range(sections):
        sent = []
        for c in range(chunks):
            inputs = (grad_out,) if hop == 0 else (*received[c], place)
            if hop + 1 == sections and c + 1 == chunks:
                break
            local, to_below, to_above, g, dz = pl.pallas_call(
                make_step_kernel(hop, c * count, count),
                in_specs=[smem] + [vmem()] * (len(inputs) + 5), out_specs=[vmem()] * 5,
                out_shape=(piece, piece_edge, piece_edge, piece, piece),
                cost_estimate=estimate, compiler_params=params(), name="step",
            )(info, *inputs, *weights)
            pieces.append((local, to_below, to_above, g, dz))
            if hop + 1 < sections:
                sent.append((move(local, hop, 0), move(to_below, hop, -1), move(to_above, hop, 1)))
        received = sent if sent else received

    early = chunks - 1
    here, others = pieces[len(pieces) - early :], pieces[: len(pieces) - early]
    last = sections - 1
    part, local, kept_below, kept_above = pl.pallas_call(
        make_partial_kernel(sections, chunks),
        in_specs=[smem] + [vmem()] * (3 + 2 * early) + [any_spec] * (5 * len(others)),
        out_specs=[vmem()] * 4,
        out_shape=(sds((3 * width, width), F32), full_shape, edge_shape, edge_shape),
        scratch_shapes=[pltpu.VMEM(full_shape.shape, BF16)] * 2 + [pltpu.SemaphoreType.DMA((5, chunks))],
        compiler_params=params(), name="partial",
    )(info, x, agg, act, *[value for outs in here for value in outs[3:]],
      *[value for outs in others for value in outs])
    edges = [value for outs in here for value in outs[1:3]]
    local_last, g, dz, near, far = pl.pallas_call(
        make_last_kernel(last, early * count, count, early),
        in_specs=[smem] + [vmem()] * (len(inputs) + 7 + 2 * early), out_specs=[vmem()] * 5,
        out_shape=(piece, piece, piece, edge_shape, edge_shape),
        scratch_shapes=[pltpu.VMEM(piece_edge.shape, BF16)] * 2,
        cost_estimate=estimate, compiler_params=params(), name="step_last",
    )(info, *inputs, *weights, *edges, kept_below, kept_above)
    far = lax.ppermute(far, "dom", far_pairs)
    half = 3 * width // 2
    keep, give = pl.pallas_call(
        make_weight_kernel(last, early * count, count), in_specs=[smem] + [vmem()] * 7, out_specs=[vmem()] * 2,
        out_shape=(sds((half, width), F32), sds((half + batches * slots, width), BF16)),
        scratch_shapes=[pltpu.VMEM((3 * width, width), F32)],
        cost_estimate=estimate, compiler_params=params(), name="weights",
    )(info, x, agg, act, part, g, dz, near)

    def swap(value, mask):
        return lax.ppermute(value, "dom", [(i, i ^ mask) for i in range(doms)])

    came = swap(give, 1)
    quarter = sds((half // 2, width), BF16)
    p, q = pl.pallas_call(
        take_kernel, in_specs=[vmem()] * 2 + [any_spec], out_specs=[vmem()] * 2, out_shape=(quarter, quarter),
        compiler_params=params(), name="take",
    )(keep, came, far)
    bit = 2
    while bit < doms:
        if bit * 2 < doms:
            p, q = add(p, swap(p, bit)), add(q, swap(q, 2 * bit))
            p, q = add(p, swap(p, 2 * bit)), add(q, swap(q, bit))
        else:
            p, q = add(p, swap(p, bit)), add(q, swap(q, bit))
        bit *= 4
    mine = jnp.concatenate([p, q], axis=0)
    other = swap(mine, 1)
    grad_in = pl.pallas_call(
        make_finish_kernel(last), in_specs=[smem] + [vmem()] * (4 + chunks), out_specs=vmem(),
        out_shape=full_shape, compiler_params=params(), name="finish",
    )(info, came, far, place, local, *[outs[0] for outs in here], local_last)
    first, second = call(
        split_kernel, (sds((2 * width, width), F32), sds((width, width), F32)), info, mine, other, name="split")
    return grad_in[None], first[None], second[None]


def solution(mesh):
    return jax.shard_map(
        per_device,
        mesh=mesh,
        in_specs=(
            P("section", None, "dom", None),
            P(None, "dom", None),
            P("section", None, None),
            P("section", None, None),
            P(None, "dom"),
            P(None, "dom"),
            P(None, "dom"),
        ),
        out_specs=(
            P("section", None, "dom", None),
            P("section", None, None),
            P("section", None, None),
        ),
        check_vma=False,
    )
```

time: 79.6 us -> 76 us (0.955)
  starting transfers between devices: 31.5 us -> 25.3 us
  waiting for transfers between devices: 37.6 us -> 40.1 us
    ppermute x6, starting transfers between devices: 8.38 us -> 4.16 us  [swap(): return lax.ppermute(value, 'dom', [(i, i ^ mask) for i in range(doms)])]
    ppermute x6, waiting for transfers between devices: 4.44 us -> 8.48 us  [swap(): return lax.ppermute(value, 'dom', [(i, i ^ mask) for i in range(doms)])]
    ppermute x1, starting transfers between devices: 4.47 us -> 2.62 us  [per_device(): lax.ppermute(far, 'dom', far_pairs)]
    pallas_call x3 -> x5, Pallas kernels: 1.89 us -> 2.94 us  [the longest x1 1.07 us: per_device(): pl.pallas_call(make_finish_kernel(last), in_specs=[smem] + [vmem()] * (4...]
    pallas_call x8 -> x7, Pallas kernels: 1.59 us -> 0.84 us  [per_device(): pl.pallas_call(make_step_kernel(hop, c * count, count), in_specs=[smem] +...]
  transfers between devices with their start and end apart: 27 -> 27, of which waited for: 9 -> 10; matrix products, arithmetic and copies ran while one was open for 0% -> 0% of each run, Pallas kernels for 3% -> 4%
where the time goes in v6:
time: 76 us; the launch traced here: 75.3 us
  waiting for transfers between devices  40.1 us (53%)
  starting transfers between devices  25.3 us (33%)
  Pallas kernels  7.58 us (10%)
  between operations  1.27 us (2%)
  local copies, waits for them, and re-layouts  0.86 us (1%)
    ppermute x18, waiting for transfers between devices, move(): return lax.ppermute(value, ('dom', 'section'), pairs)  28.4 us
    ppermute x18, starting transfers between devices, move(): return lax.ppermute(value, ('dom', 'section'), pairs)  15.9 us
    ppermute x6, waiting for transfers between devices, swap(): return lax.ppermute(value, 'dom', [(i, i ^ mask) for i in range(doms)])  8.48 us
    ppermute x6, starting transfers between devices, swap(): return lax.ppermute(value, 'dom', [(i, i ^ mask) for i in range(doms)])  4.16 us
    ppermute x1, starting transfers between devices, per_device(): lax.ppermute(far, 'dom', far_pairs)  2.62 us
    ppermute x1, starting transfers between devices, per_device(): far = lax.ppermute(far, 'dom', far_pairs)  2.54 us
    ppermute x1, waiting for transfers between devices, per_device(): far = lax.ppermute(far, 'dom', far_pairs)  2.43 us
    pallas_call x2, Pallas kernels, call(): pl.pallas_call(body, in_specs=[smem] + [vmem()] * (len(args) - 1), out_sp...  1.74 us
  transfers between devices with their start and end apart: 27, of which 10 were waited for; matrix products, arithmetic and copies ran while one was open for 0% of the time, Pallas kernels for 4%

profile of v6, /device:TPU:1, one launch (start us, length us, event | category | flops | bytes accessed | tf_op | source)
XLA Modules:
  0.0 75.3 jit_solution(4729189261087040552)
XLA Ops:
  0.7 1.4 %load.1 = (bf16[4,256,256]{2,1,0:T(8,128)(2,1)S(1)}, bf16[4,256,256]{2,1,0:T(8,128)(2,1)S(1)}, bf16[512,256]{1,0:T(8,128)(2,1)S(1)}, bf16[256,256]{1,0:T(8,128)(...) custom-call(s32[1]{0:T(128)} %bitcast.info_ref, ...), custom_call_target="tpu_custom_call" | custom-call | tf_op jit(solution)/shard_map/load/pallas_call | solution.py:326
  2.2 2.6 %collective-permute-start.1 = (bf16[4,32,256]{2,1,0:T(8,128)(2,1)S(1)}, bf16[4,32,256]{2,1,0:T(8,128)(2,1)S(1)}, u32[]{:S(2)}, u32[]{:S(2)}) collective-permute-start(bf16[4,32,256]{2,1,0:T(8,128)(2,1)S(1)} %get-tuple-element.76), channel_id=1, source_target_pairs={{0,28},{4,8},{8,4},{12,16},{16,12},{20,24},{24,20},{28,0},{1,29},{... | collective-permute-start | bytes 196616 | tf_op jit(solution)/shard_map/ppermute | solution.py:336
  5.5 0.8 %copy-done = bf16[4,256,256]{2,1,0:T(8,128)(2,1)} copy-done((bf16[4,256,256]{2,1,0:T(8,128)(2,1)}, bf16[4,256,256]{2,1,0:T(8,128)(2,1)S(1)}, u32[]{:S(2)}) %copy-start) | copy-done | bytes 524312
  6.3 0.8 %collective-permute-done.1.far_ref = bf16[4,32,256]{2,1,0:T(8,128)(2,1)S(1)} collective-permute-done((bf16[4,32,256]{2,1,0:T(8,128)(2,1)S(1)}, bf16[4,32,256]{2,1,0:T(8,128)(2,1)S(1)}, u32[]{:S(2)}, u32[]{:S(2)}) %collective-permute-start.1) | collective-permute-done | bytes 65568 | tf_op jit(solution)/shard_map/ppermute | solution.py:336
  7.1 0.8 %forward.1 = (f32[4,256,256]{2,1,0:T(8,128)S(1)}, bf16[4,256,256]{2,1,0:T(8,128)(2,1)S(1)}, bf16[4,256,256]{2,1,0:T(8,128)(2,1)S(1)}) custom-call(s32[1]{0:T(128)} %bitcast.info_ref, f32[4,256,256]{2,1,0:T(8,128)S(1)} %get-tuple-element.73.base_ref, f32[4,256,256]{2,1,0:T(8,128)S(1)} %get-tuple-element.74.inner_ref, ...), custom_call_target="tpu_custom_call" | custom-call | tf_op jit(solution)/shard_map/forward/pallas_call | solution.py:317
  7.9 0.7 collective-permute-start.3
  9.3 0.7 collective-permute-start.2
  11.4 0.7 collective-permute-start.11
  13.5 0.7 collective-permute-start.5
  15.6 0.7 collective-permute-start.14
  16.4 1.3 %collective-permute-start.9 = (bf16[2,32,256]{2,1,0:T(8,128)(2,1)S(1)}, bf16[2,32,256]{2,1,0:T(8,128)(2,1)S(1)}, u32[]{:S(2)}, u32[]{:S(2)}) collective-permute-start(bf16[2,32,256]{2,1,0:T(8,128)(2,1)S(1)} %get-tuple-element.92.refs_23_), channel_id=1, source_target_pairs={{5,0},{9,4},{13,8},{17,12},{21,16},{25,20},{29,24}} | collective-permute-start | bytes 98312 | tf_op jit(solution)/shard_map/ppermute | solution.py:352
  17.7 1.3 %collective-permute-start.10 = (bf16[2,32,256]{2,1,0:T(8,128)(2,1)S(1)}, bf16[2,32,256]{2,1,0:T(8,128)(2,1)S(1)}, u32[]{:S(2)}, u32[]{:S(2)}) collective-permute-start(bf16[2,32,256]{2,1,0:T(8,128)(2,1)S(1)} %get-tuple-element.93.refs_24_), channel_id=1, source_target_pairs={{1,4},{5,8},{9,12},{13,16},{17,20},{21,24},{25,28}} | collective-permute-start | bytes 98312 | tf_op jit(solution)/shard_map/ppermute | solution.py:352
  19.0 1.3 %collective-permute-start.8 = (bf16[2,256,256]{2,1,0:T(8,128)(2,1)S(1)}, bf16[2,256,256]{2,1,0:T(8,128)(2,1)S(1)}, u32[]{:S(2)}, u32[]{:S(2)}) collective-permute-start(bf16[2,256,256]{2,1,0:T(8,128)(2,1)S(1)} %get-tuple-element.91.refs_22_), channel_id=1, source_target_pairs={{1,0},{5,4},{9,8},{13,12},{17,16},{21,20},{25,24},{29,28}} | collective-permute-start | bytes 786440 | tf_op jit(solution)/shard_map/ppermute | solution.py:352
  20.3 1.3 %collective-permute-start.18 = (bf16[2,32,256]{2,1,0:T(8,128)(2,1)S(1)}, bf16[2,32,256]{2,1,0:T(8,128)(2,1)S(1)}, u32[]{:S(2)}, u32[]{:S(2)}) collective-permute-start(bf16[2,32,256]{2,1,0:T(8,128)(2,1)S(1)} %get-tuple-element.113.refs_28_), channel_id=1, source_target_pairs={{5,0},{9,4},{13,8},{17,12},{21,16},{25,20},{29,24}} | collective-permute-start | bytes 98312 | tf_op jit(solution)/shard_map/ppermute | solution.py:352
  21.6 1.3 %collective-permute-start.19 = (bf16[2,32,256]{2,1,0:T(8,128)(2,1)S(1)}, bf16[2,32,256]{2,1,0:T(8,128)(2,1)S(1)}, u32[]{:S(2)}, u32[]{:S(2)}) collective-permute-start(bf16[2,32,256]{2,1,0:T(8,128)(2,1)S(1)} %get-tuple-element.114.refs_29_), channel_id=1, source_target_pairs={{1,4},{5,8},{9,12},{13,16},{17,20},{21,24},{25,28}} | collective-permute-start | bytes 98312 | tf_op jit(solution)/shard_map/ppermute | solution.py:352
  22.9 18.6 %collective-permute-done.9.refs_1_ = bf16[2,32,256]{2,1,0:T(8,128)(2,1)S(1)} collective-permute-done((bf16[2,32,256]{2,1,0:T(8,128)(2,1)S(1)}, bf16[2,32,256]{2,1,0:T(8,128)(2,1)S(1)}, u32[]{:S(2)}, u32[]{:S(2)}) %collective-permute-start.9) | collective-permute-done | bytes 32800 | tf_op jit(solution)/shard_map/ppermute | solution.py:352
  41.6 1.4 %collective-permute-start.17 = (bf16[2,256,256]{2,1,0:T(8,128)(2,1)S(1)}, bf16[2,256,256]{2,1,0:T(8,128)(2,1)S(1)}, u32[]{:S(2)}, u32[]{:S(2)}) collective-permute-start(bf16[2,256,256]{2,1,0:T(8,128)(2,1)S(1)} %get-tuple-element.112.refs_27_), channel_id=1, source_target_pairs={{1,0},{5,4},{9,8},{13,12},{17,16},{21,20},{25,24},{29,28}} | collective-permute-start | bytes 786440 | tf_op jit(solution)/shard_map/ppermute | solution.py:352
  43.0 3.1 %collective-permute-done.8.refs_0_ = bf16[2,256,256]{2,1,0:T(8,128)(2,1)S(1)} collective-permute-done((bf16[2,256,256]{2,1,0:T(8,128)(2,1)S(1)}, bf16[2,256,256]{2,1,0:T(8,128)(2,1)S(1)}, u32[]{:S(2)}, u32[]{:S(2)}) %collective-permute-start.8) | collective-permute-done | bytes 262176 | tf_op jit(solution)/shard_map/ppermute | solution.py:352
  46.2 0.8 %step.10 = (bf16[2,256,256]{2,1,0:T(8,128)(2,1)S(1)}, bf16[2,32,256]{2,1,0:T(8,128)(2,1)S(1)}, bf16[2,32,256]{2,1,0:T(8,128)(2,1)S(1)}, bf16[2,256,256]{2,1,0:T(8,128)(2,1)S(1)}, bf16[2,256,256]{2,1,0:T(8,128)(2,1)S(1)}) custom-call(s32[1]{0:T(128)} %bitcast.info_ref, bf16[2,256,256]{2,1,0:T(8,128)(2,1)S(1)} %collective-permute-done.8.refs_0_, ...), custom_call_target="tpu_custom_call" | custom-call | flops 99999997952 | bytes 1048576 | tf_op jit(solution)/shard_map/step/pallas_call | solution.py:365
  47.6 2.4 %collective-permute-done.18.refs_1_ = bf16[2,32,256]{2,1,0:T(8,128)(2,1)S(1)} collective-permute-done((bf16[2,32,256]{2,1,0:T(8,128)(2,1)S(1)}, bf16[2,32,256]{2,1,0:T(8,128)(2,1)S(1)}, u32[]{:S(2)}, u32[]{:S(2)}) %collective-permute-start.18) | collective-permute-done | bytes 32800 | tf_op jit(solution)/shard_map/ppermute | solution.py:352
  50.0 4.1 %collective-permute-done.17.refs_0_ = bf16[2,256,256]{2,1,0:T(8,128)(2,1)S(1)} collective-permute-done((bf16[2,256,256]{2,1,0:T(8,128)(2,1)S(1)}, bf16[2,256,256]{2,1,0:T(8,128)(2,1)S(1)}, u32[]{:S(2)}, u32[]{:S(2)}) %collective-permute-start.17) | collective-permute-done | bytes 262176 | tf_op jit(solution)/shard_map/ppermute | solution.py:352
  54.2 0.8 %step_last.1 = (bf16[2,256,256]{2,1,0:T(8,128)(2,1)S(1)}, bf16[2,256,256]{2,1,0:T(8,128)(2,1)S(1)}, bf16[2,256,256]{2,1,0:T(8,128)(2,1)S(1)}, bf16[4,32,256]{2,1,0:T(8,128)(2,1)S(1)}, bf16[4,32,256]{2,1,0:T(8,128)(2,1)S(1)}) custom-call(s32[1]{0:T(128)} %bitcast.info_ref, bf16[2,256,256]{2,1,0:T(8,128)(2,1)S(1)} %collective-permute-done.17.refs_0_, ...), custom_call_target="tpu_custom_call" | custom-call | flops 99999997952 | bytes 1048576 | tf_op jit(solution)/shard_map/step_last/pallas_call | solution.py:389
  55.9 2.5 %collective-permute-start.21 = (bf16[4,32,256]{2,1,0:T(8,128)(2,1)S(1)}, bf16[4,32,256]{2,1,0:T(8,128)(2,1)S(1)}, u32[]{:S(2)}, u32[]{:S(2)}) collective-permute-start(bf16[4,32,256]{2,1,0:T(8,128)(2,1)S(1)} %get-tuple-element.126), channel_id=1, source_target_pairs={{0,28},{4,8},{8,4},{12,16},{16,12},{20,24},{24,20},{28,0},{1,29},{... | collective-permute-start | bytes 196616 | tf_op jit(solution)/shard_map/ppermute | solution.py:396
  58.4 2.4 %collective-permute-done.21.far_ref = bf16[4,32,256]{2,1,0:T(8,128)(2,1)S(1)} collective-permute-done((bf16[4,32,256]{2,1,0:T(8,128)(2,1)S(1)}, bf16[4,32,256]{2,1,0:T(8,128)(2,1)S(1)}, u32[]{:S(2)}, u32[]{:S(2)}) %collective-permute-start.21) | collective-permute-done | bytes 65568 | tf_op jit(solution)/shard_map/ppermute | solution.py:396
  60.9 2.3 %collective-permute-start.22 = (bf16[192,256]{1,0:T(8,128)(2,1)S(1)}, bf16[192,256]{1,0:T(8,128)(2,1)S(1)}, u32[]{:S(2)}, u32[]{:S(2)}) collective-permute-start(bf16[192,256]{1,0:T(8,128)(2,1)S(1)} %get-tuple-element.131), channel_id=1, source_target_pairs={{0,8},{4,12},{8,0},{12,4},{16,24},{20,28},{24,16},{28,20},{1,9},{5... | collective-permute-start | bytes 294920 | tf_op jit(solution)/shard_map/ppermute | solution.py:406
  63.2 2.8 %collective-permute-done.22 = bf16[192,256]{1,0:T(8,128)(2,1)S(1)} collective-permute-done((bf16[192,256]{1,0:T(8,128)(2,1)S(1)}, bf16[192,256]{1,0:T(8,128)(2,1)S(1)}, u32[]{:S(2)}, u32[]{:S(2)}) %collective-permute-start.22) | collective-permute-done | bytes 98336 | tf_op jit(solution)/shard_map/ppermute | solution.py:406
  66.1 1.7 %collective-permute-done.24 = bf16[192,256]{1,0:T(8,128)(2,1)S(1)} collective-permute-done((bf16[192,256]{1,0:T(8,128)(2,1)S(1)}, bf16[192,256]{1,0:T(8,128)(2,1)S(1)}, u32[]{:S(2)}, u32[]{:S(2)}) %collective-permute-start.24) | collective-permute-done | bytes 98336 | tf_op jit(solution)/shard_map/ppermute | solution.py:406
  67.9 2.7 %collective-permute-done.23 = bf16[192,256]{1,0:T(8,128)(2,1)S(1)} collective-permute-done((bf16[192,256]{1,0:T(8,128)(2,1)S(1)}, bf16[192,256]{1,0:T(8,128)(2,1)S(1)}, u32[]{:S(2)}, u32[]{:S(2)}) %collective-permute-start.23) | collective-permute-done | bytes 98336 | tf_op jit(solution)/shard_map/ppermute | solution.py:406
  70.6 1.3 %collective-permute-done.25 = bf16[192,256]{1,0:T(8,128)(2,1)S(1)} collective-permute-done((bf16[192,256]{1,0:T(8,128)(2,1)S(1)}, bf16[192,256]{1,0:T(8,128)(2,1)S(1)}, u32[]{:S(2)}, u32[]{:S(2)}) %collective-permute-start.25) | collective-permute-done | bytes 98336 | tf_op jit(solution)/shard_map/ppermute | solution.py:406
  72.0 1.3 %collective-permute-start.26 = (bf16[384,256]{1,0:T(8,128)(2,1)S(1)}, bf16[384,256]{1,0:T(8,128)(2,1)S(1)}, u32[]{:S(2)}, u32[]{:S(2)}) collective-permute-start(bf16[384,256]{1,0:T(8,128)(2,1)S(1)} %pad_maximum_fusion.mine_ref), channel_id=1, source_target_pairs={{0,4},{4,0},{8,12},{12,8},{16,20},{20,16},{24,28},{28,24},{1,5},{5... | collective-permute-start | bytes 589832 | tf_op jit(solution)/shard_map/ppermute | solution.py:406
  73.3 1.1 %finish.1 = bf16[4,256,256]{2,1,0:T(8,128)(2,1)} custom-call(s32[1]{0:T(128)} %bitcast.info_ref, bf16[512,256]{1,0:T(8,128)(2,1)S(1)} %collective-permute-done.20.came_ref, bf16[4,32,256]{2,1,0:T(8,128)(2,1)S(1)} %collective-permute-done.21.far_ref, bf16[256,64]{1,0:T(8,128)(2,1)S(1)} %get-tuple-element.87.refs_3_.place_ref, ...), custom_call_target="tpu_custom_call" | custom-call | tf_op jit(solution)/shard_map/finish/pallas_call | solution.py:424
  74.3 0.9 %split.1 = (f32[512,256]{1,0:T(8,128)}, f32[256,256]{1,0:T(8,128)}) custom-call(s32[1]{0:T(128)} %bitcast.info_ref, bf16[384,256]{1,0:T(8,128)(2,1)S(1)} %pad_maximum_fusion.mine_ref, bf16[384,256]{1,0:T(8,128)(2,1)S(1)} %collective-permute-done.26.other_ref), custom_call_target="tpu_custom_call" | custom-call | tf_op jit(solution)/shard_map/split/pallas_call | solution.py:317
  (79 shorter events, 7.4 us)
Async XLA Ops:
  2.1 4.2 %collective-permute-start = (bf16[4,32,256]{2,1,0:T(8,128)(2,1)S(1)}, bf16[4,32,256]{2,1,0:T(8,128)(2,1)S(1)}, u32[]{:S(2)}, u32[]{:S(2)}) collective-permute-start(bf16[4,32,256]{2,1,0:T(8,128)(2,1)S(1)} %get-tuple-element.75), channel_id=1, source_target_pairs={{0,4},{4,0},{8,12},{12,8},{16,20},{20,16},{24,28},{28,24},{1,5},{5... | collective-permute-start | bytes 196616 | tf_op jit(solution)/shard_map/ppermute | solution.py:336
  2.2 4.9 %collective-permute-start.1 = (bf16[4,32,256]{2,1,0:T(8,128)(2,1)S(1)}, bf16[4,32,256]{2,1,0:T(8,128)(2,1)S(1)}, u32[]{:S(2)}, u32[]{:S(2)}) collective-permute-start(bf16[4,32,256]{2,1,0:T(8,128)(2,1)S(1)} %get-tuple-element.76), channel_id=1, source_target_pairs={{0,28},{4,8},{8,4},{12,16},{16,12},{20,24},{24,20},{28,0},{1,29},{... | collective-permute-start | bytes 196616 | tf_op jit(solution)/shard_map/ppermute | solution.py:336
  7.9 3.4 %collective-permute-start.3 = (bf16[2,32,256]{2,1,0:T(8,128)(2,1)S(1)}, bf16[2,32,256]{2,1,0:T(8,128)(2,1)S(1)}, u32[]{:S(2)}, u32[]{:S(2)}) collective-permute-start(bf16[2,32,256]{2,1,0:T(8,128)(2,1)S(1)} %get-tuple-element.85.refs_3_), channel_id=1, source_target_pairs={{7,2},{11,6},{15,10},{19,14},{23,18},{27,22},{31,26}} | collective-permute-start | bytes 98312 | tf_op jit(solution)/shard_map/ppermute | solution.py:352
  8.6 3.4 %collective-permute-start.4 = (bf16[2,32,256]{2,1,0:T(8,128)(2,1)S(1)}, bf16[2,32,256]{2,1,0:T(8,128)(2,1)S(1)}, u32[]{:S(2)}, u32[]{:S(2)}) collective-permute-start(bf16[2,32,256]{2,1,0:T(8,128)(2,1)S(1)} %get-tuple-element.86.refs_4_), channel_id=1, source_target_pairs={{3,6},{7,10},{11,14},{15,18},{19,22},{23,26},{27,30}} | collective-permute-start | bytes 98312 | tf_op jit(solution)/shard_map/ppermute | solution.py:352
  9.3 2.8 %collective-permute-start.2 = (bf16[2,256,256]{2,1,0:T(8,128)(2,1)S(1)}, bf16[2,256,256]{2,1,0:T(8,128)(2,1)S(1)}, u32[]{:S(2)}, u32[]{:S(2)}) collective-permute-start(bf16[2,256,256]{2,1,0:T(8,128)(2,1)S(1)} %get-tuple-element.84.refs_2_), channel_id=1, source_target_pairs={{3,2},{7,6},{11,10},{15,14},{19,18},{23,22},{27,26},{31,30}} | collective-permute-start | bytes 786440 | tf_op jit(solution)/shard_map/ppermute | solution.py:352
  10.0 3.5 %collective-permute-start.12 = (bf16[2,32,256]{2,1,0:T(8,128)(2,1)S(1)}, bf16[2,32,256]{2,1,0:T(8,128)(2,1)S(1)}, u32[]{:S(2)}, u32[]{:S(2)}) collective-permute-start(bf16[2,32,256]{2,1,0:T(8,128)(2,1)S(1)} %get-tuple-element.99.refs_8_), channel_id=1, source_target_pairs={{7,2},{11,6},{15,10},{19,14},{23,18},{27,22},{31,26}} | collective-permute-start | bytes 98312 | tf_op jit(solution)/shard_map/ppermute | solution.py:352
  10.7 3.5 %collective-permute-start.13 = (bf16[2,32,256]{2,1,0:T(8,128)(2,1)S(1)}, bf16[2,32,256]{2,1,0:T(8,128)(2,1)S(1)}, u32[]{:S(2)}, u32[]{:S(2)}) collective-permute-start(bf16[2,32,256]{2,1,0:T(8,128)(2,1)S(1)} %get-tuple-element.100.refs_9_), channel_id=1, source_target_pairs={{3,6},{7,10},{11,14},{15,18},{19,22},{23,26},{27,30}} | collective-permute-start | bytes 98312 | tf_op jit(solution)/shard_map/ppermute | solution.py:352
  11.4 2.8 %collective-permute-start.11 = (bf16[2,256,256]{2,1,0:T(8,128)(2,1)S(1)}, bf16[2,256,256]{2,1,0:T(8,128)(2,1)S(1)}, u32[]{:S(2)}, u32[]{:S(2)}) collective-permute-start(bf16[2,256,256]{2,1,0:T(8,128)(2,1)S(1)} %get-tuple-element.98.refs_7_), channel_id=1, source_target_pairs={{3,2},{7,6},{11,10},{15,14},{19,18},{23,22},{27,26},{31,30}} | collective-permute-start | bytes 786440 | tf_op jit(solution)/shard_map/ppermute | solution.py:352
  12.1 3.5 %collective-permute-start.6 = (bf16[2,32,256]{2,1,0:T(8,128)(2,1)S(1)}, bf16[2,32,256]{2,1,0:T(8,128)(2,1)S(1)}, u32[]{:S(2)}, u32[]{:S(2)}) collective-permute-start(bf16[2,32,256]{2,1,0:T(8,128)(2,1)S(1)} %get-tuple-element.89.refs_13_), channel_id=1, source_target_pairs={{6,1},{10,5},{14,9},{18,13},{22,17},{26,21},{30,25}} | collective-permute-start | bytes 98312 | tf_op jit(solution)/shard_map/ppermute | solution.py:352
  12.8 3.5 %collective-permute-start.7 = (bf16[2,32,256]{2,1,0:T(8,128)(2,1)S(1)}, bf16[2,32,256]{2,1,0:T(8,128)(2,1)S(1)}, u32[]{:S(2)}, u32[]{:S(2)}) collective-permute-start(bf16[2,32,256]{2,1,0:T(8,128)(2,1)S(1)} %get-tuple-element.90.refs_14_), channel_id=1, source_target_pairs={{2,5},{6,9},{10,13},{14,17},{18,21},{22,25},{26,29}} | collective-permute-start | bytes 98312 | tf_op jit(solution)/shard_map/ppermute | solution.py:352
  13.5 2.8 %collective-permute-start.5 = (bf16[2,256,256]{2,1,0:T(8,128)(2,1)S(1)}, bf16[2,256,256]{2,1,0:T(8,128)(2,1)S(1)}, u32[]{:S(2)}, u32[]{:S(2)}) collective-permute-start(bf16[2,256,256]{2,1,0:T(8,128)(2,1)S(1)} %get-tuple-element.88.refs_12_), channel_id=1, source_target_pairs={{2,1},{6,5},{10,9},{14,13},{18,17},{22,21},{26,25},{30,29}} | collective-permute-start | bytes 786440 | tf_op jit(solution)/shard_map/ppermute | solution.py:352
  14.3 4.7 %collective-permute-start.15 = (bf16[2,32,256]{2,1,0:T(8,128)(2,1)S(1)}, bf16[2,32,256]{2,1,0:T(8,128)(2,1)S(1)}, u32[]{:S(2)}, u32[]{:S(2)}) collective-permute-start(bf16[2,32,256]{2,1,0:T(8,128)(2,1)S(1)} %get-tuple-element.106.refs_18_), channel_id=1, source_target_pairs={{6,1},{10,5},{14,9},{18,13},{22,17},{26,21},{30,25}} | collective-permute-start | bytes 98312 | tf_op jit(solution)/shard_map/ppermute | solution.py:352
  14.9 5.3 %collective-permute-start.16 = (bf16[2,32,256]{2,1,0:T(8,128)(2,1)S(1)}, bf16[2,32,256]{2,1,0:T(8,128)(2,1)S(1)}, u32[]{:S(2)}, u32[]{:S(2)}) collective-permute-start(bf16[2,32,256]{2,1,0:T(8,128)(2,1)S(1)} %get-tuple-element.107.refs_19_), channel_id=1, source_target_pairs={{2,5},{6,9},{10,13},{14,17},{18,21},{22,25},{26,29}} | collective-permute-start | bytes 98312 | tf_op jit(solution)/shard_map/ppermute | solution.py:352
  15.6 4.7 %collective-permute-start.14 = (bf16[2,256,256]{2,1,0:T(8,128)(2,1)S(1)}, bf16[2,256,256]{2,1,0:T(8,128)(2,1)S(1)}, u32[]{:S(2)}, u32[]{:S(2)}) collective-permute-start(bf16[2,256,256]{2,1,0:T(8,128)(2,1)S(1)} %get-tuple-element.105.refs_17_), channel_id=1, source_target_pairs={{2,1},{6,5},{10,9},{14,13},{18,17},{22,21},{26,25},{30,29}} | collective-permute-start | bytes 786440 | tf_op jit(solution)/shard_map/ppermute | solution.py:352
  16.4 25.2 %collective-permute-start.9 = (bf16[2,32,256]{2,1,0:T(8,128)(2,1)S(1)}, bf16[2,32,256]{2,1,0:T(8,128)(2,1)S(1)}, u32[]{:S(2)}, u32[]{:S(2)}) collective-permute-start(bf16[2,32,256]{2,1,0:T(8,128)(2,1)S(1)} %get-tuple-element.92.refs_23_), channel_id=1, source_target_pairs={{5,0},{9,4},{13,8},{17,12},{21,16},{25,20},{29,24}} | collective-permute-start | bytes 98312 | tf_op jit(solution)/shard_map/ppermute | solution.py:352
  17.7 25.3 %collective-permute-start.10 = (bf16[2,32,256]{2,1,0:T(8,128)(2,1)S(1)}, bf16[2,32,256]{2,1,0:T(8,128)(2,1)S(1)}, u32[]{:S(2)}, u32[]{:S(2)}) collective-permute-start(bf16[2,32,256]{2,1,0:T(8,128)(2,1)S(1)} %get-tuple-element.93.refs_24_), channel_id=1, source_target_pairs={{1,4},{5,8},{9,12},{13,16},{17,20},{21,24},{25,28}} | collective-permute-start | bytes 98312 | tf_op jit(solution)/shard_map/ppermute | solution.py:352
  19.0 27.2 %collective-permute-start.8 = (bf16[2,256,256]{2,1,0:T(8,128)(2,1)S(1)}, bf16[2,256,256]{2,1,0:T(8,128)(2,1)S(1)}, u32[]{:S(2)}, u32[]{:S(2)}) collective-permute-start(bf16[2,256,256]{2,1,0:T(8,128)(2,1)S(1)} %get-tuple-element.91.refs_22_), channel_id=1, source_target_pairs={{1,0},{5,4},{9,8},{13,12},{17,16},{21,20},{25,24},{29,28}} | collective-permute-start | bytes 786440 | tf_op jit(solution)/shard_map/ppermute | solution.py:352
  20.3 29.7 %collective-permute-start.18 = (bf16[2,32,256]{2,1,0:T(8,128)(2,1)S(1)}, bf16[2,32,256]{2,1,0:T(8,128)(2,1)S(1)}, u32[]{:S(2)}, u32[]{:S(2)}) collective-permute-start(bf16[2,32,256]{2,1,0:T(8,128)(2,1)S(1)} %get-tuple-element.113.refs_28_), channel_id=1, source_target_pairs={{5,0},{9,4},{13,8},{17,12},{21,16},{25,20},{29,24}} | collective-permute-start | bytes 98312 | tf_op jit(solution)/shard_map/ppermute | solution.py:352
  21.6 28.4 %collective-permute-start.19 = (bf16[2,32,256]{2,1,0:T(8,128)(2,1)S(1)}, bf16[2,32,256]{2,1,0:T(8,128)(2,1)S(1)}, u32[]{:S(2)}, u32[]{:S(2)}) collective-permute-start(bf16[2,32,256]{2,1,0:T(8,128)(2,1)S(1)} %get-tuple-element.114.refs_29_), channel_id=1, source_target_pairs={{1,4},{5,8},{9,12},{13,16},{17,20},{21,24},{25,28}} | collective-permute-start | bytes 98312 | tf_op jit(solution)/shard_map/ppermute | solution.py:352
  41.5 5.4 %copy-start.1 = (bf16[4,256,256]{2,1,0:T(8,128)(2,1)S(1)}, bf16[4,256,256]{2,1,0:T(8,128)(2,1)}, u32[]{:S(2)}) copy-start(bf16[4,256,256]{2,1,0:T(8,128)(2,1)} %copy-done) | copy-start | bytes 1572868
  41.5 5.4 %copy-start.3 = (bf16[2,256,256]{2,1,0:T(8,128)(2,1)S(1)}, bf16[2,256,256]{2,1,0:T(8,128)(2,1)}, u32[]{:S(2)}) copy-start(bf16[2,256,256]{2,1,0:T(8,128)(2,1)} %copy-done.2) | copy-start | bytes 786436
  41.5 5.4 %copy-start.5 = (bf16[2,256,256]{2,1,0:T(8,128)(2,1)S(1)}, bf16[2,256,256]{2,1,0:T(8,128)(2,1)}, u32[]{:S(2)}) copy-start(bf16[2,256,256]{2,1,0:T(8,128)(2,1)} %copy-done.4) | copy-start | bytes 786436
  41.5 5.4 %copy-start.7 = (bf16[2,256,256]{2,1,0:T(8,128)(2,1)S(1)}, bf16[2,256,256]{2,1,0:T(8,128)(2,1)}, u32[]{:S(2)}) copy-start(bf16[2,256,256]{2,1,0:T(8,128)(2,1)} %copy-done.6) | copy-start | bytes 786436
  41.5 5.4 %copy-start.9 = (bf16[2,256,256]{2,1,0:T(8,128)(2,1)S(1)}, bf16[2,256,256]{2,1,0:T(8,128)(2,1)}, u32[]{:S(2)}) copy-start(bf16[2,256,256]{2,1,0:T(8,128)(2,1)} %copy-done.8) | copy-start | bytes 786436
  41.6 12.6 %collective-permute-start.17 = (bf16[2,256,256]{2,1,0:T(8,128)(2,1)S(1)}, bf16[2,256,256]{2,1,0:T(8,128)(2,1)S(1)}, u32[]{:S(2)}, u32[]{:S(2)}) collective-permute-start(bf16[2,256,256]{2,1,0:T(8,128)(2,1)S(1)} %get-tuple-element.112.refs_27_), channel_id=1, source_target_pairs={{1,0},{5,4},{9,8},{13,12},{17,16},{21,20},{25,24},{29,28}} | collective-permute-start | bytes 786440 | tf_op jit(solution)/shard_map/ppermute | solution.py:352
  55.4 5.4 %collective-permute-start.20 = (bf16[512,256]{1,0:T(8,128)(2,1)S(1)}, bf16[512,256]{1,0:T(8,128)(2,1)S(1)}, u32[]{:S(2)}, u32[]{:S(2)}) collective-permute-start(bf16[512,256]{1,0:T(8,128)(2,1)S(1)} %get-tuple-element.125), channel_id=1, source_target_pairs={{0,4},{4,0},{8,12},{12,8},{16,20},{20,16},{24,28},{28,24},{1,5},{5... | collective-permute-start | bytes 786440 | tf_op jit(solution)/shard_map/ppermute | solution.py:406
  55.9 5.0 %collective-permute-start.21 = (bf16[4,32,256]{2,1,0:T(8,128)(2,1)S(1)}, bf16[4,32,256]{2,1,0:T(8,128)(2,1)S(1)}, u32[]{:S(2)}, u32[]{:S(2)}) collective-permute-start(bf16[4,32,256]{2,1,0:T(8,128)(2,1)S(1)} %get-tuple-element.126), channel_id=1, source_target_pairs={{0,28},{4,8},{8,4},{12,16},{16,12},{20,24},{24,20},{28,0},{1,29},{... | collective-permute-start | bytes 196616 | tf_op jit(solution)/shard_map/ppermute | solution.py:396
  60.9 5.1 %collective-permute-start.22 = (bf16[192,256]{1,0:T(8,128)(2,1)S(1)}, bf16[192,256]{1,0:T(8,128)(2,1)S(1)}, u32[]{:S(2)}, u32[]{:S(2)}) collective-permute-start(bf16[192,256]{1,0:T(8,128)(2,1)S(1)} %get-tuple-element.131), channel_id=1, source_target_pairs={{0,8},{4,12},{8,0},{12,4},{16,24},{20,28},{24,16},{28,20},{1,9},{5... | collective-permute-start | bytes 294920 | tf_op jit(solution)/shard_map/ppermute | solution.py:406
  63.2 4.7 %collective-permute-start.24 = (bf16[192,256]{1,0:T(8,128)(2,1)S(1)}, bf16[192,256]{1,0:T(8,128)(2,1)S(1)}, u32[]{:S(2)}, u32[]{:S(2)}) collective-permute-start(bf16[192,256]{1,0:T(8,128)(2,1)S(1)} %get-tuple-element.132), channel_id=1, source_target_pairs={{0,16},{4,20},{8,24},{12,28},{16,0},{20,4},{24,8},{28,12},{1,17},{... | collective-permute-start | bytes 294920 | tf_op jit(solution)/shard_map/ppermute | solution.py:406
  66.0 4.6 %collective-permute-start.23 = (bf16[192,256]{1,0:T(8,128)(2,1)S(1)}, bf16[192,256]{1,0:T(8,128)(2,1)S(1)}, u32[]{:S(2)}, u32[]{:S(2)}) collective-permute-start(bf16[192,256]{1,0:T(8,128)(2,1)S(1)} %add_convert_fusion.3), channel_id=1, source_target_pairs={{0,16},{4,20},{8,24},{12,28},{16,0},{20,4},{24,8},{28,12},{1,17},{... | collective-permute-start | bytes 294920 | tf_op jit(solution)/shard_map/ppermute | solution.py:406
  67.9 4.0 %collective-permute-start.25 = (bf16[192,256]{1,0:T(8,128)(2,1)S(1)}, bf16[192,256]{1,0:T(8,128)(2,1)S(1)}, u32[]{:S(2)}, u32[]{:S(2)}) collective-permute-start(bf16[192,256]{1,0:T(8,128)(2,1)S(1)} %add_convert_fusion.1), channel_id=1, source_target_pairs={{0,8},{4,12},{8,0},{12,4},{16,24},{20,28},{24,16},{28,20},{1,9},{5... | collective-permute-start | bytes 294920 | tf_op jit(solution)/shard_map/ppermute | solution.py:406
  72.0 2.4 %collective-permute-start.26 = (bf16[384,256]{1,0:T(8,128)(2,1)S(1)}, bf16[384,256]{1,0:T(8,128)(2,1)S(1)}, u32[]{:S(2)}, u32[]{:S(2)}) collective-permute-start(bf16[384,256]{1,0:T(8,128)(2,1)S(1)} %pad_maximum_fusion.mine_ref), channel_id=1, source_target_pairs={{0,4},{4,0},{8,12},{12,8},{16,20},{20,16},{24,28},{28,24},{1,5},{5... | collective-permute-start | bytes 589832 | tf_op jit(solution)/shard_map/ppermute | solution.py:406
  (13 other events, 21.0 us)

commit v7 on v6

--- a/solution.py
+++ b/solution.py
@@ -1,3 +1,5 @@
+import functools
+
 import jax
 import jax.numpy as jnp
 from jax import lax
@@ -16,7 +18,11 @@
 
 
 def hop_of(info_ref):
-    return info_ref[0] >> 2
+    return info_ref[0] >> 3
+
+
+def direct_of(info_ref):
+    return (info_ref[0] >> 2) & 1
 
 
 def odd_of(info_ref):
@@ -222,7 +228,7 @@
 
 
 def make_weight_kernel(last, first, count):
-    def body(info_ref, x_ref, agg_ref, act_ref, part_ref, g_ref, dz_ref, near_ref, keep_ref, give_ref, grad_ref):
+    def body(info_ref, x_ref, agg_ref, act_ref, part_ref, g_ref, dz_ref, near_ref, far_ref, keep_ref, give_ref, grad_ref):
         width = part_ref.shape[1]
         half = keep_ref.shape[0]
         odd = odd_of(info_ref)
@@ -237,7 +243,10 @@
 
         keep_ref[...] = grad_ref[pl.ds(pl.multiple_of(odd * half, half), half)]
         give_ref[:half] = grad_ref[pl.ds(pl.multiple_of((1 - odd) * half, half), half)].astype(BF16)
-        give_ref[half:] = near_ref[...].reshape(give_ref.shape[0] - half, width)
+        size = near_ref.shape[0] * near_ref.shape[1]
+        give_ref[half : half + size] = near_ref[...].reshape(size, width)
+        if give_ref.shape[0] > half + size:
+            give_ref[half + size :] = far_ref[...].reshape(size, width)
 
     return body
 
@@ -247,9 +256,23 @@
 
 
 def take_kernel(keep_ref, came_ref, far_ref, p_ref, q_ref):
-    quarter = p_ref.shape[0]
-    p_ref[...] = add(keep_ref[:quarter], came_ref[:quarter])
+    quarter = q_ref.shape[0]
+    p_ref[:quarter] = add(keep_ref[:quarter], came_ref[:quarter])
     q_ref[...] = add(keep_ref[quarter:], came_ref[quarter : 2 * quarter])
+    extra = p_ref.shape[0] - quarter
+    if extra:
+        p_ref[quarter:] = came_ref[came_ref.shape[0] - extra :]
+
+
+def forward_sum_kernel(p_ref, other_ref, out_ref, *, quarter):
+    out_ref[:quarter] = add(p_ref[:quarter], other_ref[:quarter])
+    out_ref[quarter:] = other_ref[quarter:]
+
+
+def join_kernel(p_ref, p_other_ref, q_ref, q_other_ref, out_ref):
+    quarter = q_ref.shape[0]
+    out_ref[:quarter] = add(p_ref[:quarter], p_other_ref[:quarter])
+    out_ref[quarter:] = add(q_ref[...], q_other_ref[...])
 
 
 def split_kernel(info_ref, mine_ref, other_ref, first_ref, second_ref):
@@ -264,18 +287,24 @@
     second_ref[...] = high[size - half :]
 
 
-def make_finish_kernel(last):
-    def body(info_ref, came_ref, far_ref, place_ref, loc_ref, *refs):
-        here, out_ref = refs[:-1], refs[-1]
+def make_finish_kernel(last, half, slots, relay):
+    def body(info_ref, came_ref, place_ref, loc_ref, *refs):
+        here, halos, out_ref = refs[: -2 - relay], refs[-2 - relay : -1], refs[-1]
         odd, end = odd_of(info_ref) == 1, end_of(info_ref) == 1
-        batches, slots = far_ref.shape[:2]
+        batches = loc_ref.shape[0]
         count = batches // len(here)
-        start = came_ref.shape[0] - batches * slots
+
+        def far_of(m):
+            if not relay:
+                return halos[0][m]
+            first, second = [halo[halo.shape[0] - (batches - m) * slots :][:slots] for halo in halos]
+            return jnp.where(direct_of(info_ref) == 1, first, second)
 
         def write(local):
             for m in range(batches):
-                near = came_ref[start + m * slots : start + (m + 1) * slots]
-                far = jnp.where(end, jnp.zeros_like(far_ref[m]), far_ref[m])
+                near = came_ref[half + m * slots : half + (m + 1) * slots]
+                far = far_of(m)
+                far = jnp.where(end, jnp.zeros_like(far), far)
                 upper = jnp.where(odd, far, near)
                 lower = jnp.where(odd, near, far)
                 out_ref[m] = assemble(local(m), upper, lower, place_ref[...])
@@ -304,7 +333,8 @@
     dom = lax.axis_index("dom")
     hop_here = sections - 1 - lax.axis_index("section")
     end = ((dom == 0) | (dom == doms - 1)).astype(jnp.int32)
-    info = (4 * hop_here + 2 * (dom % 2) + end).astype(jnp.int32).reshape(1)
+    direct = ((dom + 1) % 4 >= 2).astype(jnp.int32)
+    info = (8 * hop_here + 4 * direct + 2 * (dom % 2) + end).astype(jnp.int32).reshape(1)
     sds = jax.ShapeDtypeStruct
     smem = pl.BlockSpec(memory_space=pltpu.SMEM)
     any_spec = pl.BlockSpec(memory_space=pl.ANY)
@@ -393,38 +423,59 @@
         scratch_shapes=[pltpu.VMEM(piece_edge.shape, BF16)] * 2,
         cost_estimate=estimate, compiler_params=params(), name="step_last",
     )(info, *inputs, *weights, *edges, kept_below, kept_above)
-    far = lax.ppermute(far, "dom", far_pairs)
+    relay = doms == 8
     half = 3 * width // 2
+    size = batches * slots
     keep, give = pl.pallas_call(
-        make_weight_kernel(last, early * count, count), in_specs=[smem] + [vmem()] * 7, out_specs=[vmem()] * 2,
-        out_shape=(sds((half, width), F32), sds((half + batches * slots, width), BF16)),
+        make_weight_kernel(last, early * count, count), in_specs=[smem] + [vmem()] * 8, out_specs=[vmem()] * 2,
+        out_shape=(sds((half, width), F32), sds((half + (1 + relay) * size, width), BF16)),
         scratch_shapes=[pltpu.VMEM((3 * width, width), F32)],
         cost_estimate=estimate, compiler_params=params(), name="weights",
-    )(info, x, agg, act, part, g, dz, near)
+    )(info, x, agg, act, part, g, dz, near, far)
+    if not relay:
+        far = lax.ppermute(far, "dom", far_pairs)
 
     def swap(value, mask):
         return lax.ppermute(value, "dom", [(i, i ^ mask) for i in range(doms)])
 
     came = swap(give, 1)
     quarter = sds((half // 2, width), BF16)
+    longer = sds((half // 2 + relay * size, width), BF16)
     p, q = pl.pallas_call(
-        take_kernel, in_specs=[vmem()] * 2 + [any_spec], out_specs=[vmem()] * 2, out_shape=(quarter, quarter),
+        take_kernel, in_specs=[vmem()] * 2 + [any_spec], out_specs=[vmem()] * 2, out_shape=(longer, quarter),
         compiler_params=params(), name="take",
     )(keep, came, far)
+    halos = [] if relay else [far]
     bit = 2
     while bit < doms:
         if bit * 2 < doms:
-            p, q = add(p, swap(p, bit)), add(q, swap(q, 2 * bit))
-            p, q = add(p, swap(p, 2 * bit)), add(q, swap(q, bit))
+            p_other, q_other = swap(p, bit), swap(q, 2 * bit)
+            if relay:
+                halos.append(p_other)
+                p = pl.pallas_call(
+                    functools.partial(forward_sum_kernel, quarter=half // 2), in_specs=[vmem()] * 2, out_specs=vmem(),
+                    out_shape=longer, compiler_params=params(), name="forward_sum",
+                )(p, p_other)
+            else:
+                p = add(p, p_other)
+            q = add(q, q_other)
+            p_other, q_other = swap(p, 2 * bit), swap(q, bit)
+            if relay:
+                halos.append(p_other)
         else:
-            p, q = add(p, swap(p, bit)), add(q, swap(q, bit))
+            p_other, q_other = swap(p, bit), swap(q, bit)
         bit *= 4
-    mine = jnp.concatenate([p, q], axis=0)
+        if bit < doms:
+            p, q = add(p, p_other), add(q, q_other)
+    mine = pl.pallas_call(
+        join_kernel, in_specs=[vmem()] * 4, out_specs=vmem(), out_shape=sds((half, width), BF16),
+        compiler_params=params(), name="join",
+    )(p, p_other, q, q_other)
     other = swap(mine, 1)
     grad_in = pl.pallas_call(
-        make_finish_kernel(last), in_specs=[smem] + [vmem()] * (4 + chunks), out_specs=vmem(),
-        out_shape=full_shape, compiler_params=params(), name="finish",
-    )(info, came, far, place, local, *[outs[0] for outs in here], local_last)
+        make_finish_kernel(last, half, slots, relay), in_specs=[smem] + [vmem()] * (3 + chunks + len(halos)),
+        out_specs=vmem(), out_shape=full_shape, compiler_params=params(), name="finish",
+    )(info, came, place, local, *[outs[0] for outs in here], local_last, *halos)
     first, second = call(
         split_kernel, (sds((2 * width, width), F32), sds((width, width), F32)), info, mine, other, name="split")
     return grad_in[None], first[None], second[None]

time: 76 us -> 73.7 us (0.970)
  waiting for transfers between devices: 40.1 us -> 38.3 us
    ppermute x1 -> x0, starting transfers between devices: 2.54 us -> none  [per_device(): far = lax.ppermute(far, 'dom', far_pairs)]
    ppermute x1 -> x0, waiting for transfers between devices: 2.43 us -> none  [per_device(): far = lax.ppermute(far, 'dom', far_pairs)]
    ppermute x6, starting transfers between devices: 4.16 us -> 6.23 us  [swap(): return lax.ppermute(value, 'dom', [(i, i ^ mask) for i in range(doms)])]
  transfers between devices with their start and end apart: 27 -> 26, of which waited for: 10 -> 9; matrix products, arithmetic and copies ran while one was open for 0% -> 0% of each run, Pallas kernels for 4% -> 4%
where the time goes in v7:
time: 73.7 us; the launch traced here: 73 us
  waiting for transfers between devices  38.3 us (52%)
  starting transfers between devices  24.9 us (34%)
  Pallas kernels  7.66 us (10%)
  between operations  1.25 us (2%)
  local copies, waits for them, and re-layouts  0.86 us (1%)
    ppermute x18, waiting for transfers between devices, move(): return lax.ppermute(value, ('dom', 'section'), pairs)  28.4 us
    ppermute x18, starting transfers between devices, move(): return lax.ppermute(value, ('dom', 'section'), pairs)  15.9 us
    ppermute x6, waiting for transfers between devices, swap(): return lax.ppermute(value, 'dom', [(i, i ^ mask) for i in range(doms)])  9.09 us
    ppermute x6, starting transfers between devices, swap(): return lax.ppermute(value, 'dom', [(i, i ^ mask) for i in range(doms)])  6.23 us
    ppermute x1, starting transfers between devices, per_device(): lax.ppermute(far, 'dom', far_pairs)  2.62 us
    pallas_call x2, Pallas kernels, call(): pl.pallas_call(body, in_specs=[smem] + [vmem()] * (len(args) - 1), out_sp...  1.74 us
  transfers between devices with their start and end apart: 26, of which 9 were waited for; matrix products, arithmetic and copies ran while one was open for 0% of the time, Pallas kernels for 4%

profile of v7, /device:TPU:1, one launch (start us, length us, event | category | flops | bytes accessed | tf_op | source)
XLA Modules:
  0.0 73.0 jit_solution(15086271481425722371)
XLA Ops:
  0.7 1.4 %load.1 = (bf16[4,256,256]{2,1,0:T(8,128)(2,1)S(1)}, bf16[4,256,256]{2,1,0:T(8,128)(2,1)S(1)}, bf16[512,256]{1,0:T(8,128)(2,1)S(1)}, bf16[256,256]{1,0:T(8,128)(...) custom-call(s32[1]{0:T(128)} %bitcast.info_ref, ...), custom_call_target="tpu_custom_call" | custom-call | tf_op jit(solution)/shard_map/load/pallas_call | solution.py:356
  2.2 2.6 %collective-permute-start.1 = (bf16[4,32,256]{2,1,0:T(8,128)(2,1)S(1)}, bf16[4,32,256]{2,1,0:T(8,128)(2,1)S(1)}, u32[]{:S(2)}, u32[]{:S(2)}) collective-permute-start(bf16[4,32,256]{2,1,0:T(8,128)(2,1)S(1)} %get-tuple-element.76), channel_id=1, source_target_pairs={{0,28},{4,8},{8,4},{12,16},{16,12},{20,24},{24,20},{28,0},{1,29},{... | collective-permute-start | bytes 196616 | tf_op jit(solution)/shard_map/ppermute | solution.py:366
  5.5 0.8 %copy-done = bf16[4,256,256]{2,1,0:T(8,128)(2,1)} copy-done((bf16[4,256,256]{2,1,0:T(8,128)(2,1)}, bf16[4,256,256]{2,1,0:T(8,128)(2,1)S(1)}, u32[]{:S(2)}) %copy-start) | copy-done | bytes 524312
  6.3 0.8 %collective-permute-done.1.far_ref = bf16[4,32,256]{2,1,0:T(8,128)(2,1)S(1)} collective-permute-done((bf16[4,32,256]{2,1,0:T(8,128)(2,1)S(1)}, bf16[4,32,256]{2,1,0:T(8,128)(2,1)S(1)}, u32[]{:S(2)}, u32[]{:S(2)}) %collective-permute-start.1) | collective-permute-done | bytes 65568 | tf_op jit(solution)/shard_map/ppermute | solution.py:366
  7.1 0.8 %forward.1 = (f32[4,256,256]{2,1,0:T(8,128)S(1)}, bf16[4,256,256]{2,1,0:T(8,128)(2,1)S(1)}, bf16[4,256,256]{2,1,0:T(8,128)(2,1)S(1)}) custom-call(s32[1]{0:T(128)} %bitcast.info_ref, f32[4,256,256]{2,1,0:T(8,128)S(1)} %get-tuple-element.73.base_ref, f32[4,256,256]{2,1,0:T(8,128)S(1)} %get-tuple-element.74.inner_ref, ...), custom_call_target="tpu_custom_call" | custom-call | tf_op jit(solution)/shard_map/forward/pallas_call | solution.py:347
  7.9 0.7 collective-permute-start.3
  9.3 0.7 collective-permute-start.2
  10.7 0.7 collective-permute-start.13
  11.4 0.7 collective-permute-start.11
  13.5 0.7 collective-permute-start.5
  15.6 0.7 collective-permute-start.14
  16.4 1.3 %collective-permute-start.9 = (bf16[2,32,256]{2,1,0:T(8,128)(2,1)S(1)}, bf16[2,32,256]{2,1,0:T(8,128)(2,1)S(1)}, u32[]{:S(2)}, u32[]{:S(2)}) collective-permute-start(bf16[2,32,256]{2,1,0:T(8,128)(2,1)S(1)} %get-tuple-element.92.refs_23_), channel_id=1, source_target_pairs={{5,0},{9,4},{13,8},{17,12},{21,16},{25,20},{29,24}} | collective-permute-start | bytes 98312 | tf_op jit(solution)/shard_map/ppermute | solution.py:382
  17.7 1.3 %collective-permute-start.10 = (bf16[2,32,256]{2,1,0:T(8,128)(2,1)S(1)}, bf16[2,32,256]{2,1,0:T(8,128)(2,1)S(1)}, u32[]{:S(2)}, u32[]{:S(2)}) collective-permute-start(bf16[2,32,256]{2,1,0:T(8,128)(2,1)S(1)} %get-tuple-element.93.refs_24_), channel_id=1, source_target_pairs={{1,4},{5,8},{9,12},{13,16},{17,20},{21,24},{25,28}} | collective-permute-start | bytes 98312 | tf_op jit(solution)/shard_map/ppermute | solution.py:382
  19.0 1.3 %collective-permute-start.8 = (bf16[2,256,256]{2,1,0:T(8,128)(2,1)S(1)}, bf16[2,256,256]{2,1,0:T(8,128)(2,1)S(1)}, u32[]{:S(2)}, u32[]{:S(2)}) collective-permute-start(bf16[2,256,256]{2,1,0:T(8,128)(2,1)S(1)} %get-tuple-element.91.refs_22_), channel_id=1, source_target_pairs={{1,0},{5,4},{9,8},{13,12},{17,16},{21,20},{25,24},{29,28}} | collective-permute-start | bytes 786440 | tf_op jit(solution)/shard_map/ppermute | solution.py:382
  20.3 1.3 %collective-permute-start.18 = (bf16[2,32,256]{2,1,0:T(8,128)(2,1)S(1)}, bf16[2,32,256]{2,1,0:T(8,128)(2,1)S(1)}, u32[]{:S(2)}, u32[]{:S(2)}) collective-permute-start(bf16[2,32,256]{2,1,0:T(8,128)(2,1)S(1)} %get-tuple-element.113.refs_28_), channel_id=1, source_target_pairs={{5,0},{9,4},{13,8},{17,12},{21,16},{25,20},{29,24}} | collective-permute-start | bytes 98312 | tf_op jit(solution)/shard_map/ppermute | solution.py:382
  21.6 1.3 %collective-permute-start.19 = (bf16[2,32,256]{2,1,0:T(8,128)(2,1)S(1)}, bf16[2,32,256]{2,1,0:T(8,128)(2,1)S(1)}, u32[]{:S(2)}, u32[]{:S(2)}) collective-permute-start(bf16[2,32,256]{2,1,0:T(8,128)(2,1)S(1)} %get-tuple-element.114.refs_29_), channel_id=1, source_target_pairs={{1,4},{5,8},{9,12},{13,16},{17,20},{21,24},{25,28}} | collective-permute-start | bytes 98312 | tf_op jit(solution)/shard_map/ppermute | solution.py:382
  22.9 18.6 %collective-permute-done.9.refs_1_ = bf16[2,32,256]{2,1,0:T(8,128)(2,1)S(1)} collective-permute-done((bf16[2,32,256]{2,1,0:T(8,128)(2,1)S(1)}, bf16[2,32,256]{2,1,0:T(8,128)(2,1)S(1)}, u32[]{:S(2)}, u32[]{:S(2)}) %collective-permute-start.9) | collective-permute-done | bytes 32800 | tf_op jit(solution)/shard_map/ppermute | solution.py:382
  41.6 1.4 %collective-permute-start.17 = (bf16[2,256,256]{2,1,0:T(8,128)(2,1)S(1)}, bf16[2,256,256]{2,1,0:T(8,128)(2,1)S(1)}, u32[]{:S(2)}, u32[]{:S(2)}) collective-permute-start(bf16[2,256,256]{2,1,0:T(8,128)(2,1)S(1)} %get-tuple-element.112.refs_27_), channel_id=1, source_target_pairs={{1,0},{5,4},{9,8},{13,12},{17,16},{21,20},{25,24},{29,28}} | collective-permute-start | bytes 786440 | tf_op jit(solution)/shard_map/ppermute | solution.py:382
  43.0 3.1 %collective-permute-done.8.refs_0_ = bf16[2,256,256]{2,1,0:T(8,128)(2,1)S(1)} collective-permute-done((bf16[2,256,256]{2,1,0:T(8,128)(2,1)S(1)}, bf16[2,256,256]{2,1,0:T(8,128)(2,1)S(1)}, u32[]{:S(2)}, u32[]{:S(2)}) %collective-permute-start.8) | collective-permute-done | bytes 262176 | tf_op jit(solution)/shard_map/ppermute | solution.py:382
  46.1 0.8 %step.10 = (bf16[2,256,256]{2,1,0:T(8,128)(2,1)S(1)}, bf16[2,32,256]{2,1,0:T(8,128)(2,1)S(1)}, bf16[2,32,256]{2,1,0:T(8,128)(2,1)S(1)}, bf16[2,256,256]{2,1,0:T(8,128)(2,1)S(1)}, bf16[2,256,256]{2,1,0:T(8,128)(2,1)S(1)}) custom-call(s32[1]{0:T(128)} %bitcast.info_ref, bf16[2,256,256]{2,1,0:T(8,128)(2,1)S(1)} %collective-permute-done.8.refs_0_, ...), custom_call_target="tpu_custom_call" | custom-call | flops 99999997952 | bytes 1048576 | tf_op jit(solution)/shard_map/step/pallas_call | solution.py:395
  47.6 2.5 %collective-permute-done.18.refs_1_ = bf16[2,32,256]{2,1,0:T(8,128)(2,1)S(1)} collective-permute-done((bf16[2,32,256]{2,1,0:T(8,128)(2,1)S(1)}, bf16[2,32,256]{2,1,0:T(8,128)(2,1)S(1)}, u32[]{:S(2)}, u32[]{:S(2)}) %collective-permute-start.18) | collective-permute-done | bytes 32800 | tf_op jit(solution)/shard_map/ppermute | solution.py:382
  50.0 4.2 %collective-permute-done.17.refs_0_ = bf16[2,256,256]{2,1,0:T(8,128)(2,1)S(1)} collective-permute-done((bf16[2,256,256]{2,1,0:T(8,128)(2,1)S(1)}, bf16[2,256,256]{2,1,0:T(8,128)(2,1)S(1)}, u32[]{:S(2)}, u32[]{:S(2)}) %collective-permute-start.17) | collective-permute-done | bytes 262176 | tf_op jit(solution)/shard_map/ppermute | solution.py:382
  54.2 0.8 %step_last.1 = (bf16[2,256,256]{2,1,0:T(8,128)(2,1)S(1)}, bf16[2,256,256]{2,1,0:T(8,128)(2,1)S(1)}, bf16[2,256,256]{2,1,0:T(8,128)(2,1)S(1)}, bf16[4,32,256]{2,1,0:T(8,128)(2,1)S(1)}, bf16[4,32,256]{2,1,0:T(8,128)(2,1)S(1)}) custom-call(s32[1]{0:T(128)} %bitcast.info_ref, bf16[2,256,256]{2,1,0:T(8,128)(2,1)S(1)} %collective-permute-done.17.refs_0_, ...), custom_call_target="tpu_custom_call" | custom-call | flops 99999997952 | bytes 1048576 | tf_op jit(solution)/shard_map/step_last/pallas_call | solution.py:419
  55.9 1.3 %collective-permute-done.20.came_ref = bf16[640,256]{1,0:T(8,128)(2,1)S(1)} collective-permute-done((bf16[640,256]{1,0:T(8,128)(2,1)S(1)}, bf16[640,256]{1,0:T(8,128)(2,1)S(1)}, u32[]{:S(2)}, u32[]{:S(2)}) %collective-permute-start.20) | collective-permute-done | bytes 327712 | tf_op jit(solution)/shard_map/ppermute | solution.py:439
  57.2 2.6 %collective-permute-start.21 = (bf16[320,256]{1,0:T(8,128)(2,1)S(1)}, bf16[320,256]{1,0:T(8,128)(2,1)S(1)}, u32[]{:S(2)}, u32[]{:S(2)}) collective-permute-start(bf16[320,256]{1,0:T(8,128)(2,1)S(1)} %get-tuple-element.131.p_ref), channel_id=1, source_target_pairs={{0,8},{4,12},{8,0},{12,4},{16,24},{20,28},{24,16},{28,20},{1,9},{5... | collective-permute-start | bytes 491528 | tf_op jit(solution)/shard_map/ppermute | solution.py:439
  59.8 4.3 %collective-permute-done.21.other_ref.refs_2_ = bf16[320,256]{1,0:T(8,128)(2,1)S(1)} collective-permute-done((bf16[320,256]{1,0:T(8,128)(2,1)S(1)}, bf16[320,256]{1,0:T(8,128)(2,1)S(1)}, u32[]{:S(2)}, u32[]{:S(2)}) %collective-permute-start.21) | collective-permute-done | bytes 163872 | tf_op jit(solution)/shard_map/ppermute | solution.py:439
  64.3 1.2 %collective-permute-start.24 = (bf16[192,256]{1,0:T(8,128)(2,1)S(1)}, bf16[192,256]{1,0:T(8,128)(2,1)S(1)}, u32[]{:S(2)}, u32[]{:S(2)}) collective-permute-start(bf16[192,256]{1,0:T(8,128)(2,1)S(1)} %add_convert_fusion.q_ref), channel_id=1, source_target_pairs={{0,8},{4,12},{8,0},{12,4},{16,24},{20,28},{24,16},{28,20},{1,9},{5... | collective-permute-start | bytes 294920 | tf_op jit(solution)/shard_map/ppermute | solution.py:439
  65.5 2.4 %collective-permute-done.24.q_other_ref = bf16[192,256]{1,0:T(8,128)(2,1)S(1)} collective-permute-done((bf16[192,256]{1,0:T(8,128)(2,1)S(1)}, bf16[192,256]{1,0:T(8,128)(2,1)S(1)}, u32[]{:S(2)}, u32[]{:S(2)}) %collective-permute-start.24) | collective-permute-done | bytes 98336 | tf_op jit(solution)/shard_map/ppermute | solution.py:439
  67.8 1.2 %collective-permute-done.22.refs_3_.p_other_ref = bf16[320,256]{1,0:T(8,128)(2,1)S(1)} collective-permute-done((bf16[320,256]{1,0:T(8,128)(2,1)S(1)}, bf16[320,256]{1,0:T(8,128)(2,1)S(1)}, u32[]{:S(2)}, u32[]{:S(2)}) %collective-permute-start.22) | collective-permute-done | bytes 163872 | tf_op jit(solution)/shard_map/ppermute | solution.py:439
  69.1 1.8 %collective-permute-start.25 = (bf16[384,256]{1,0:T(8,128)(2,1)S(1)}, bf16[384,256]{1,0:T(8,128)(2,1)S(1)}, u32[]{:S(2)}, u32[]{:S(2)}) collective-permute-start(bf16[384,256]{1,0:T(8,128)(2,1)S(1)} %join.1.mine_ref), channel_id=1, source_target_pairs={{0,4},{4,0},{8,12},{12,8},{16,20},{20,16},{24,28},{28,24},{1,5},{5... | collective-permute-start | bytes 589832 | tf_op jit(solution)/shard_map/ppermute | solution.py:439
  70.9 1.1 %finish.1 = bf16[4,256,256]{2,1,0:T(8,128)(2,1)} custom-call(s32[1]{0:T(128)} %bitcast.info_ref, bf16[640,256]{1,0:T(8,128)(2,1)S(1)} %collective-permute-done.20.came_ref, bf16[256,64]{1,0:T(8,128)(2,1)S(1)} %get-tuple-element.87.refs_3_.place_ref, bf16[4,256,256]{2,1,0:T(8,128)(2,1)S(1)} %get-tuple-element.127.loc_ref, ...), custom_call_target="tpu_custom_call" | custom-call | tf_op jit(solution)/shard_map/finish/pallas_call | solution.py:475
  72.0 0.9 %split.1 = (f32[512,256]{1,0:T(8,128)}, f32[256,256]{1,0:T(8,128)}) custom-call(s32[1]{0:T(128)} %bitcast.info_ref, bf16[384,256]{1,0:T(8,128)(2,1)S(1)} %join.1.mine_ref, bf16[384,256]{1,0:T(8,128)(2,1)S(1)} %collective-permute-done.25.other_ref), custom_call_target="tpu_custom_call" | custom-call | tf_op jit(solution)/shard_map/split/pallas_call | solution.py:347
  (75 shorter events, 6.7 us)
Async XLA Ops:
  2.1 4.2 %collective-permute-start = (bf16[4,32,256]{2,1,0:T(8,128)(2,1)S(1)}, bf16[4,32,256]{2,1,0:T(8,128)(2,1)S(1)}, u32[]{:S(2)}, u32[]{:S(2)}) collective-permute-start(bf16[4,32,256]{2,1,0:T(8,128)(2,1)S(1)} %get-tuple-element.75), channel_id=1, source_target_pairs={{0,4},{4,0},{8,12},{12,8},{16,20},{20,16},{24,28},{28,24},{1,5},{5... | collective-permute-start | bytes 196616 | tf_op jit(solution)/shard_map/ppermute | solution.py:366
  2.2 4.9 %collective-permute-start.1 = (bf16[4,32,256]{2,1,0:T(8,128)(2,1)S(1)}, bf16[4,32,256]{2,1,0:T(8,128)(2,1)S(1)}, u32[]{:S(2)}, u32[]{:S(2)}) collective-permute-start(bf16[4,32,256]{2,1,0:T(8,128)(2,1)S(1)} %get-tuple-element.76), channel_id=1, source_target_pairs={{0,28},{4,8},{8,4},{12,16},{16,12},{20,24},{24,20},{28,0},{1,29},{... | collective-permute-start | bytes 196616 | tf_op jit(solution)/shard_map/ppermute | solution.py:366
  7.9 3.4 %collective-permute-start.3 = (bf16[2,32,256]{2,1,0:T(8,128)(2,1)S(1)}, bf16[2,32,256]{2,1,0:T(8,128)(2,1)S(1)}, u32[]{:S(2)}, u32[]{:S(2)}) collective-permute-start(bf16[2,32,256]{2,1,0:T(8,128)(2,1)S(1)} %get-tuple-element.85.refs_3_), channel_id=1, source_target_pairs={{7,2},{11,6},{15,10},{19,14},{23,18},{27,22},{31,26}} | collective-permute-start | bytes 98312 | tf_op jit(solution)/shard_map/ppermute | solution.py:382
  8.6 3.4 %collective-permute-start.4 = (bf16[2,32,256]{2,1,0:T(8,128)(2,1)S(1)}, bf16[2,32,256]{2,1,0:T(8,128)(2,1)S(1)}, u32[]{:S(2)}, u32[]{:S(2)}) collective-permute-start(bf16[2,32,256]{2,1,0:T(8,128)(2,1)S(1)} %get-tuple-element.86.refs_4_), channel_id=1, source_target_pairs={{3,6},{7,10},{11,14},{15,18},{19,22},{23,26},{27,30}} | collective-permute-start | bytes 98312 | tf_op jit(solution)/shard_map/ppermute | solution.py:382
  9.3 2.8 %collective-permute-start.2 = (bf16[2,256,256]{2,1,0:T(8,128)(2,1)S(1)}, bf16[2,256,256]{2,1,0:T(8,128)(2,1)S(1)}, u32[]{:S(2)}, u32[]{:S(2)}) collective-permute-start(bf16[2,256,256]{2,1,0:T(8,128)(2,1)S(1)} %get-tuple-element.84.refs_2_), channel_id=1, source_target_pairs={{3,2},{7,6},{11,10},{15,14},{19,18},{23,22},{27,26},{31,30}} | collective-permute-start | bytes 786440 | tf_op jit(solution)/shard_map/ppermute | solution.py:382
  10.0 3.5 %collective-permute-start.12 = (bf16[2,32,256]{2,1,0:T(8,128)(2,1)S(1)}, bf16[2,32,256]{2,1,0:T(8,128)(2,1)S(1)}, u32[]{:S(2)}, u32[]{:S(2)}) collective-permute-start(bf16[2,32,256]{2,1,0:T(8,128)(2,1)S(1)} %get-tuple-element.99.refs_8_), channel_id=1, source_target_pairs={{7,2},{11,6},{15,10},{19,14},{23,18},{27,22},{31,26}} | collective-permute-start | bytes 98312 | tf_op jit(solution)/shard_map/ppermute | solution.py:382
  10.7 3.5 %collective-permute-start.13 = (bf16[2,32,256]{2,1,0:T(8,128)(2,1)S(1)}, bf16[2,32,256]{2,1,0:T(8,128)(2,1)S(1)}, u32[]{:S(2)}, u32[]{:S(2)}) collective-permute-start(bf16[2,32,256]{2,1,0:T(8,128)(2,1)S(1)} %get-tuple-element.100.refs_9_), channel_id=1, source_target_pairs={{3,6},{7,10},{11,14},{15,18},{19,22},{23,26},{27,30}} | collective-permute-start | bytes 98312 | tf_op jit(solution)/shard_map/ppermute | solution.py:382
  11.4 2.8 %collective-permute-start.11 = (bf16[2,256,256]{2,1,0:T(8,128)(2,1)S(1)}, bf16[2,256,256]{2,1,0:T(8,128)(2,1)S(1)}, u32[]{:S(2)}, u32[]{:S(2)}) collective-permute-start(bf16[2,256,256]{2,1,0:T(8,128)(2,1)S(1)} %get-tuple-element.98.refs_7_), channel_id=1, source_target_pairs={{3,2},{7,6},{11,10},{15,14},{19,18},{23,22},{27,26},{31,30}} | collective-permute-start | bytes 786440 | tf_op jit(solution)/shard_map/ppermute | solution.py:382
  12.1 2.1 %copy-start.6 = (bf16[2,256,256]{2,1,0:T(8,128)(2,1)}, bf16[2,256,256]{2,1,0:T(8,128)(2,1)S(1)}, u32[]{:S(2)}) copy-start(bf16[2,256,256]{2,1,0:T(8,128)(2,1)S(1)} %get-tuple-element.88.refs_12_) | copy-start | bytes 786436
  12.1 3.5 %collective-permute-start.6 = (bf16[2,32,256]{2,1,0:T(8,128)(2,1)S(1)}, bf16[2,32,256]{2,1,0:T(8,128)(2,1)S(1)}, u32[]{:S(2)}, u32[]{:S(2)}) collective-permute-start(bf16[2,32,256]{2,1,0:T(8,128)(2,1)S(1)} %get-tuple-element.89.refs_13_), channel_id=1, source_target_pairs={{6,1},{10,5},{14,9},{18,13},{22,17},{26,21},{30,25}} | collective-permute-start | bytes 98312 | tf_op jit(solution)/shard_map/ppermute | solution.py:382
  12.8 3.5 %collective-permute-start.7 = (bf16[2,32,256]{2,1,0:T(8,128)(2,1)S(1)}, bf16[2,32,256]{2,1,0:T(8,128)(2,1)S(1)}, u32[]{:S(2)}, u32[]{:S(2)}) collective-permute-start(bf16[2,32,256]{2,1,0:T(8,128)(2,1)S(1)} %get-tuple-element.90.refs_14_), channel_id=1, source_target_pairs={{2,5},{6,9},{10,13},{14,17},{18,21},{22,25},{26,29}} | collective-permute-start | bytes 98312 | tf_op jit(solution)/shard_map/ppermute | solution.py:382
  13.5 2.8 %collective-permute-start.5 = (bf16[2,256,256]{2,1,0:T(8,128)(2,1)S(1)}, bf16[2,256,256]{2,1,0:T(8,128)(2,1)S(1)}, u32[]{:S(2)}, u32[]{:S(2)}) collective-permute-start(bf16[2,256,256]{2,1,0:T(8,128)(2,1)S(1)} %get-tuple-element.88.refs_12_), channel_id=1, source_target_pairs={{2,1},{6,5},{10,9},{14,13},{18,17},{22,21},{26,25},{30,29}} | collective-permute-start | bytes 786440 | tf_op jit(solution)/shard_map/ppermute | solution.py:382
  14.3 4.7 %collective-permute-start.15 = (bf16[2,32,256]{2,1,0:T(8,128)(2,1)S(1)}, bf16[2,32,256]{2,1,0:T(8,128)(2,1)S(1)}, u32[]{:S(2)}, u32[]{:S(2)}) collective-permute-start(bf16[2,32,256]{2,1,0:T(8,128)(2,1)S(1)} %get-tuple-element.106.refs_18_), channel_id=1, source_target_pairs={{6,1},{10,5},{14,9},{18,13},{22,17},{26,21},{30,25}} | collective-permute-start | bytes 98312 | tf_op jit(solution)/shard_map/ppermute | solution.py:382
  14.9 5.3 %collective-permute-start.16 = (bf16[2,32,256]{2,1,0:T(8,128)(2,1)S(1)}, bf16[2,32,256]{2,1,0:T(8,128)(2,1)S(1)}, u32[]{:S(2)}, u32[]{:S(2)}) collective-permute-start(bf16[2,32,256]{2,1,0:T(8,128)(2,1)S(1)} %get-tuple-element.107.refs_19_), channel_id=1, source_target_pairs={{2,5},{6,9},{10,13},{14,17},{18,21},{22,25},{26,29}} | collective-permute-start | bytes 98312 | tf_op jit(solution)/shard_map/ppermute | solution.py:382
  15.6 4.7 %collective-permute-start.14 = (bf16[2,256,256]{2,1,0:T(8,128)(2,1)S(1)}, bf16[2,256,256]{2,1,0:T(8,128)(2,1)S(1)}, u32[]{:S(2)}, u32[]{:S(2)}) collective-permute-start(bf16[2,256,256]{2,1,0:T(8,128)(2,1)S(1)} %get-tuple-element.105.refs_17_), channel_id=1, source_target_pairs={{2,1},{6,5},{10,9},{14,13},{18,17},{22,21},{26,25},{30,29}} | collective-permute-start | bytes 786440 | tf_op jit(solution)/shard_map/ppermute | solution.py:382
  16.4 25.2 %collective-permute-start.9 = (bf16[2,32,256]{2,1,0:T(8,128)(2,1)S(1)}, bf16[2,32,256]{2,1,0:T(8,128)(2,1)S(1)}, u32[]{:S(2)}, u32[]{:S(2)}) collective-permute-start(bf16[2,32,256]{2,1,0:T(8,128)(2,1)S(1)} %get-tuple-element.92.refs_23_), channel_id=1, source_target_pairs={{5,0},{9,4},{13,8},{17,12},{21,16},{25,20},{29,24}} | collective-permute-start | bytes 98312 | tf_op jit(solution)/shard_map/ppermute | solution.py:382
  17.7 25.3 %collective-permute-start.10 = (bf16[2,32,256]{2,1,0:T(8,128)(2,1)S(1)}, bf16[2,32,256]{2,1,0:T(8,128)(2,1)S(1)}, u32[]{:S(2)}, u32[]{:S(2)}) collective-permute-start(bf16[2,32,256]{2,1,0:T(8,128)(2,1)S(1)} %get-tuple-element.93.refs_24_), channel_id=1, source_target_pairs={{1,4},{5,8},{9,12},{13,16},{17,20},{21,24},{25,28}} | collective-permute-start | bytes 98312 | tf_op jit(solution)/shard_map/ppermute | solution.py:382
  19.0 27.1 %collective-permute-start.8 = (bf16[2,256,256]{2,1,0:T(8,128)(2,1)S(1)}, bf16[2,256,256]{2,1,0:T(8,128)(2,1)S(1)}, u32[]{:S(2)}, u32[]{:S(2)}) collective-permute-start(bf16[2,256,256]{2,1,0:T(8,128)(2,1)S(1)} %get-tuple-element.91.refs_22_), channel_id=1, source_target_pairs={{1,0},{5,4},{9,8},{13,12},{17,16},{21,20},{25,24},{29,28}} | collective-permute-start | bytes 786440 | tf_op jit(solution)/shard_map/ppermute | solution.py:382
  20.3 29.7 %collective-permute-start.18 = (bf16[2,32,256]{2,1,0:T(8,128)(2,1)S(1)}, bf16[2,32,256]{2,1,0:T(8,128)(2,1)S(1)}, u32[]{:S(2)}, u32[]{:S(2)}) collective-permute-start(bf16[2,32,256]{2,1,0:T(8,128)(2,1)S(1)} %get-tuple-element.113.refs_28_), channel_id=1, source_target_pairs={{5,0},{9,4},{13,8},{17,12},{21,16},{25,20},{29,24}} | collective-permute-start | bytes 98312 | tf_op jit(solution)/shard_map/ppermute | solution.py:382
  21.6 28.4 %collective-permute-start.19 = (bf16[2,32,256]{2,1,0:T(8,128)(2,1)S(1)}, bf16[2,32,256]{2,1,0:T(8,128)(2,1)S(1)}, u32[]{:S(2)}, u32[]{:S(2)}) collective-permute-start(bf16[2,32,256]{2,1,0:T(8,128)(2,1)S(1)} %get-tuple-element.114.refs_29_), channel_id=1, source_target_pairs={{1,4},{5,8},{9,12},{13,16},{17,20},{21,24},{25,28}} | collective-permute-start | bytes 98312 | tf_op jit(solution)/shard_map/ppermute | solution.py:382
  41.5 5.3 %copy-start.1 = (bf16[4,256,256]{2,1,0:T(8,128)(2,1)S(1)}, bf16[4,256,256]{2,1,0:T(8,128)(2,1)}, u32[]{:S(2)}) copy-start(bf16[4,256,256]{2,1,0:T(8,128)(2,1)} %copy-done) | copy-start | bytes 1572868
  41.5 5.4 %copy-start.3 = (bf16[2,256,256]{2,1,0:T(8,128)(2,1)S(1)}, bf16[2,256,256]{2,1,0:T(8,128)(2,1)}, u32[]{:S(2)}) copy-start(bf16[2,256,256]{2,1,0:T(8,128)(2,1)} %copy-done.2) | copy-start | bytes 786436
  41.5 5.4 %copy-start.5 = (bf16[2,256,256]{2,1,0:T(8,128)(2,1)S(1)}, bf16[2,256,256]{2,1,0:T(8,128)(2,1)}, u32[]{:S(2)}) copy-start(bf16[2,256,256]{2,1,0:T(8,128)(2,1)} %copy-done.4) | copy-start | bytes 786436
  41.5 5.4 %copy-start.7 = (bf16[2,256,256]{2,1,0:T(8,128)(2,1)S(1)}, bf16[2,256,256]{2,1,0:T(8,128)(2,1)}, u32[]{:S(2)}) copy-start(bf16[2,256,256]{2,1,0:T(8,128)(2,1)} %copy-done.6) | copy-start | bytes 786436
  41.6 5.4 %copy-start.9 = (bf16[2,256,256]{2,1,0:T(8,128)(2,1)S(1)}, bf16[2,256,256]{2,1,0:T(8,128)(2,1)}, u32[]{:S(2)}) copy-start(bf16[2,256,256]{2,1,0:T(8,128)(2,1)} %copy-done.8) | copy-start | bytes 786436
  41.6 12.6 %collective-permute-start.17 = (bf16[2,256,256]{2,1,0:T(8,128)(2,1)S(1)}, bf16[2,256,256]{2,1,0:T(8,128)(2,1)S(1)}, u32[]{:S(2)}, u32[]{:S(2)}) collective-permute-start(bf16[2,256,256]{2,1,0:T(8,128)(2,1)S(1)} %get-tuple-element.112.refs_27_), channel_id=1, source_target_pairs={{1,0},{5,4},{9,8},{13,12},{17,16},{21,20},{25,24},{29,28}} | collective-permute-start | bytes 786440 | tf_op jit(solution)/shard_map/ppermute | solution.py:382
  55.5 1.7 %collective-permute-start.20 = (bf16[640,256]{1,0:T(8,128)(2,1)S(1)}, bf16[640,256]{1,0:T(8,128)(2,1)S(1)}, u32[]{:S(2)}, u32[]{:S(2)}) collective-permute-start(bf16[640,256]{1,0:T(8,128)(2,1)S(1)} %get-tuple-element.126), channel_id=1, source_target_pairs={{0,4},{4,0},{8,12},{12,8},{16,20},{20,16},{24,28},{28,24},{1,5},{5... | collective-permute-start | bytes 983048 | tf_op jit(solution)/shard_map/ppermute | solution.py:439
  57.2 6.9 %collective-permute-start.21 = (bf16[320,256]{1,0:T(8,128)(2,1)S(1)}, bf16[320,256]{1,0:T(8,128)(2,1)S(1)}, u32[]{:S(2)}, u32[]{:S(2)}) collective-permute-start(bf16[320,256]{1,0:T(8,128)(2,1)S(1)} %get-tuple-element.131.p_ref), channel_id=1, source_target_pairs={{0,8},{4,12},{8,0},{12,4},{16,24},{20,28},{24,16},{28,20},{1,9},{5... | collective-permute-start | bytes 491528 | tf_op jit(solution)/shard_map/ppermute | solution.py:439
  59.8 4.4 %collective-permute-start.23 = (bf16[192,256]{1,0:T(8,128)(2,1)S(1)}, bf16[192,256]{1,0:T(8,128)(2,1)S(1)}, u32[]{:S(2)}, u32[]{:S(2)}) collective-permute-start(bf16[192,256]{1,0:T(8,128)(2,1)S(1)} %get-tuple-element.132), channel_id=1, source_target_pairs={{0,16},{4,20},{8,24},{12,28},{16,0},{20,4},{24,8},{28,12},{1,17},{... | collective-permute-start | bytes 294920 | tf_op jit(solution)/shard_map/ppermute | solution.py:439
  64.1 4.9 %collective-permute-start.22 = (bf16[320,256]{1,0:T(8,128)(2,1)S(1)}, bf16[320,256]{1,0:T(8,128)(2,1)S(1)}, u32[]{:S(2)}, u32[]{:S(2)}) collective-permute-start(bf16[320,256]{1,0:T(8,128)(2,1)S(1)} %forward_sum.1.p_ref), channel_id=1, source_target_pairs={{0,16},{4,20},{8,24},{12,28},{16,0},{20,4},{24,8},{28,12},{1,17},{... | collective-permute-start | bytes 491528 | tf_op jit(solution)/shard_map/ppermute | solution.py:439
  64.3 3.5 %collective-permute-start.24 = (bf16[192,256]{1,0:T(8,128)(2,1)S(1)}, bf16[192,256]{1,0:T(8,128)(2,1)S(1)}, u32[]{:S(2)}, u32[]{:S(2)}) collective-permute-start(bf16[192,256]{1,0:T(8,128)(2,1)S(1)} %add_convert_fusion.q_ref), channel_id=1, source_target_pairs={{0,8},{4,12},{8,0},{12,4},{16,24},{20,28},{24,16},{28,20},{1,9},{5... | collective-permute-start | bytes 294920 | tf_op jit(solution)/shard_map/ppermute | solution.py:439
  69.1 2.9 %collective-permute-start.25 = (bf16[384,256]{1,0:T(8,128)(2,1)S(1)}, bf16[384,256]{1,0:T(8,128)(2,1)S(1)}, u32[]{:S(2)}, u32[]{:S(2)}) collective-permute-start(bf16[384,256]{1,0:T(8,128)(2,1)S(1)} %join.1.mine_ref), channel_id=1, source_target_pairs={{0,4},{4,0},{8,12},{12,8},{16,20},{20,16},{24,28},{28,24},{1,5},{5... | collective-permute-start | bytes 589832 | tf_op jit(solution)/shard_map/ppermute | solution.py:439
  (12 other events, 18.8 us)

commit v8 on v7

--- a/solution.py
+++ b/solution.py
@@ -10,7 +10,7 @@
 F32 = jnp.float32
 BF16 = jnp.bfloat16
 CHUNKS = 2
-STEP_FLOPS = 10**11
+STEP_FLOPS = 2600 * 10**6
 
 
 def dot(a, b, dims=((1,), (0,))):
@@ -87,22 +87,26 @@
         base_ref[m] = dot(x, w_ref[:width])
 
 
-def forward_kernel(info_ref, base_ref, inner_ref, near_ref, far_ref, halo_ref, w_ref, slope_ref, act_ref, agg_ref):
-    batches, rows, width = base_ref.shape
-    slots = near_ref.shape[1]
-    odd = odd_of(info_ref) == 1
-    lower, upper = halo_ref[:slots].astype(F32), halo_ref[slots:].astype(F32)
-    near = jnp.where(odd, lower, upper)
-    far = jnp.where(end_of(info_ref) == 1, 0.0, jnp.where(odd, upper, lower))
-    halo_t = jnp.concatenate([near, far], axis=0).T.astype(BF16)
-    for m in range(batches):
-        edge = jnp.concatenate([near_ref[m], far_ref[m]], axis=0)
-        agg = (inner_ref[m] + dot(halo_t, edge)).astype(BF16)
-        z = base_ref[m] + dot(agg, w_ref[width:])
-        sig = 1.0 / (1.0 + jnp.exp(-z))
-        agg_ref[m] = agg
-        act_ref[m] = (z * sig).astype(BF16)
-        slope_ref[m] = sig * (1.0 + z * (1.0 - sig))
+def make_forward_kernel(first):
+    def body(info_ref, base_ref, inner_ref, near_ref, far_ref, halo_ref, w_ref, slope_ref, act_ref, agg_ref):
+        width = base_ref.shape[2]
+        slots = near_ref.shape[1]
+        odd = odd_of(info_ref) == 1
+        lower, upper = halo_ref[:slots].astype(F32), halo_ref[slots:].astype(F32)
+        near = jnp.where(odd, lower, upper)
+        far = jnp.where(end_of(info_ref) == 1, 0.0, jnp.where(odd, upper, lower))
+        halo_t = jnp.concatenate([near, far], axis=0).T.astype(BF16)
+        for j in range(slope_ref.shape[0]):
+            m = first + j
+            edge = jnp.concatenate([near_ref[m], far_ref[m]], axis=0)
+            agg = (inner_ref[m] + dot(halo_t, edge)).astype(BF16)
+            z = base_ref[m] + dot(agg, w_ref[width:])
+            sig = 1.0 / (1.0 + jnp.exp(-z))
+            agg_ref[j] = agg
+            act_ref[j] = (z * sig).astype(BF16)
+            slope_ref[j] = sig * (1.0 + z * (1.0 - sig))
+
+    return body
 
 
 def assemble(local, upper, lower, place):
@@ -110,12 +114,12 @@
     return (local.astype(F32) + dot(place, edge)).astype(BF16)
 
 
-def step(g, first, slope_ref, own_ref, halo_ref, w1_ref, w2_ref, local_ref, below_ref, above_ref, g_ref, dz_ref):
+def step(g, slope_ref, own_ref, halo_ref, w1_ref, w2_ref, local_ref, below_ref, above_ref, g_ref, dz_ref):
     rows, width = slope_ref.shape[1:]
     slots = halo_ref.shape[0] // 2
     count = len(g)
     d_act = dot(jnp.concatenate(g, axis=0), w2_ref[...], ((1,), (1,)))
-    dz = [(d_act[j * rows : (j + 1) * rows] * slope_ref[first + j]).astype(BF16) for j in range(count)]
+    dz = [(d_act[j * rows : (j + 1) * rows] * slope_ref[j]).astype(BF16) for j in range(count)]
     dj = dot(jnp.concatenate(dz, axis=0), w1_ref[...], ((1,), (1,)))
     for j in range(count):
         part = dj[j * rows : (j + 1) * rows]
@@ -142,64 +146,65 @@
 
         @pl.when(hop_of(info_ref) == hop)
         def _():
-            step(start_values(hop, first, count, inputs), first, *arrays)
+            step(start_values(hop, first, count, inputs), *arrays)
 
     return body
 
 
-def make_last_kernel(hop, first, count, earlier):
+def make_last_kernel(hop, first, count):
     def body(info_ref, *refs):
         (local_ref, g_ref, dz_ref, near_ref, far_ref, below_ref, above_ref) = refs[-7:]
-        kept_below, kept_above = refs[-9:-7]
-        edges = refs[-9 - 2 * earlier : -9]
-        arrays = refs[-14 - 2 * earlier : -9 - 2 * earlier]
-        inputs = refs[: -14 - 2 * earlier]
+        kept_below, kept_above, _ = refs[-10:-7]
+        arrays, inputs = refs[-15:-10], refs[:-15]
         odd = odd_of(info_ref) == 1
 
-        def sort(below, above, where):
-            near_ref[where] = jnp.where(odd, below, above)
-            far_ref[where] = jnp.where(odd, above, below)
+        def sort(below, above):
+            near_ref[...] = jnp.where(odd, below, above)
+            far_ref[...] = jnp.where(odd, above, below)
 
         @pl.when(hop_of(info_ref) == hop)
         def _():
-            step(start_values(hop, first, count, inputs), first, *arrays,
-                 local_ref, below_ref, above_ref, g_ref, dz_ref)
-            for c in range(earlier):
-                sort(edges[2 * c][...], edges[2 * c + 1][...], slice(c * count, (c + 1) * count))
-            sort(below_ref[...], above_ref[...], slice(first, first + count))
+            step(start_values(hop, first, count, inputs), *arrays, local_ref, below_ref, above_ref, g_ref, dz_ref)
+            sort(below_ref[...], above_ref[...])
 
         @pl.when(hop_of(info_ref) != hop)
         def _():
-            sort(kept_below[...], kept_above[...], slice(0, first + count))
+            sort(kept_below[first : first + count], kept_above[first : first + count])
 
     return body
 
 
-def gradients(sources, parts, out_ref, start=None):
-    width = out_ref.shape[1]
-    for n, source in enumerate(sources):
+def gradients(x_ref, parts, out_ref, start=None):
+    rows, width = x_ref.shape[1:]
+    for n in range(3):
         total = 0.0 if start is None else start[n * width : (n + 1) * width]
-        for first, size, g, dz in parts:
-            rows = source.shape[1]
-            left = source[first : first + size].reshape(size * rows, width)
-            right = (g if n == 2 else dz)[...].reshape(size * rows, width)
-            total = total + dot(left, right, ((0,), (0,)))
+        for first, size, agg, act, g, dz in parts:
+            left = (x_ref[first : first + size], agg[...] if n == 1 else None, act[...] if n == 2 else None)[n]
+            right = g() if n == 2 else dz()
+            total = total + dot(left.reshape(size * rows, width), right.reshape(size * rows, width), ((0,), (0,)))
         out_ref[n * width : (n + 1) * width] = total
 
 
 def make_partial_kernel(hops, chunks):
-    def body(info_ref, x_ref, agg_ref, act_ref, *refs):
-        part_ref, local_ref, below_ref, above_ref, g_ref, dz_ref, sems = refs[-7:]
-        here = [refs[2 * c : 2 * c + 2] for c in range(chunks - 1)]
-        pieces = refs[2 * chunks - 2 : -7]
+    def body(info_ref, x_ref, *refs):
+        (part_ref, local_ref, below_ref, above_ref, near_ref, far_ref, g_ref, dz_ref, sems) = refs[-9:]
+        early = chunks - 1
+        forward = [refs[2 * c : 2 * c + 2] for c in range(chunks)]
+        here = [refs[2 * chunks + 4 * c : 2 * chunks + 4 * c + 4] for c in range(early)]
+        pieces = refs[2 * chunks + 4 * early : -9]
         targets = (local_ref, below_ref, above_ref, g_ref, dz_ref)
         batches = x_ref.shape[0]
         count = batches // chunks
+        odd = odd_of(info_ref) == 1
 
         def copies(hop):
             return [pltpu.make_async_copy(pieces[(hop * chunks + c) * 5 + n],
                                           targets[n].at[pl.ds(c * count, count)], sems.at[n, c])
                     for n in range(5) for c in range(chunks)]
+
+        def sort(below, above, where):
+            near_ref[where] = jnp.where(odd, below, above)
+            far_ref[where] = jnp.where(odd, above, below)
 
         for hop in range(hops - 1):
             @pl.when(hop_of(info_ref) == hop)
@@ -207,14 +212,15 @@
                 for copy in copies(hop):
                     copy.start()
 
-        if chunks > 1:
-            @pl.when(hop_of(info_ref) == hops - 1)
-            def _():
-                parts = [(c * count, count, g, dz) for c, (g, dz) in enumerate(here)]
-                gradients((x_ref, agg_ref, act_ref), parts, part_ref)
-        else:
-            @pl.when(hop_of(info_ref) == hops - 1)
-            def _():
+        @pl.when(hop_of(info_ref) == hops - 1)
+        def _():
+            parts = []
+            for c, (below, above, g, dz) in enumerate(here):
+                sort(below[...], above[...], slice(c * count, (c + 1) * count))
+                parts.append((c * count, count, *forward[c], lambda g=g: g[...], lambda dz=dz: dz[...]))
+            if parts:
+                gradients(x_ref, parts, part_ref)
+            else:
                 part_ref[...] = jnp.zeros_like(part_ref)
 
         if hops > 1:
@@ -222,20 +228,28 @@
             def _():
                 for copy in copies(0):
                     copy.wait()
-                gradients((x_ref, agg_ref, act_ref), [(0, batches, g_ref, dz_ref)], part_ref)
+                if early:
+                    sort(below_ref[: early * count], above_ref[: early * count], slice(0, early * count))
+                parts = []
+                for c in range(chunks):
+                    where = slice(c * count, (c + 1) * count)
+                    parts.append((c * count, count, *forward[c], lambda w=where: g_ref[w], lambda w=where: dz_ref[w]))
+                gradients(x_ref, parts, part_ref)
 
     return body
 
 
 def make_weight_kernel(last, first, count):
-    def body(info_ref, x_ref, agg_ref, act_ref, part_ref, g_ref, dz_ref, near_ref, far_ref, keep_ref, give_ref, grad_ref):
+    def body(info_ref, x_ref, agg_ref, act_ref, part_ref, g_ref, dz_ref, near_early_ref, near_ref, far_ref,
+             keep_ref, give_ref, grad_ref):
         width = part_ref.shape[1]
         half = keep_ref.shape[0]
         odd = odd_of(info_ref)
 
         @pl.when(hop_of(info_ref) == last)
         def _():
-            gradients((x_ref, agg_ref, act_ref), [(first, count, g_ref, dz_ref)], grad_ref, part_ref)
+            parts = [(first, count, agg_ref, act_ref, lambda: g_ref[...], lambda: dz_ref[...])]
+            gradients(x_ref, parts, grad_ref, part_ref)
 
         @pl.when(hop_of(info_ref) != last)
         def _():
@@ -243,10 +257,12 @@
 
         keep_ref[...] = grad_ref[pl.ds(pl.multiple_of(odd * half, half), half)]
         give_ref[:half] = grad_ref[pl.ds(pl.multiple_of((1 - odd) * half, half), half)].astype(BF16)
-        size = near_ref.shape[0] * near_ref.shape[1]
-        give_ref[half : half + size] = near_ref[...].reshape(size, width)
-        if give_ref.shape[0] > half + size:
-            give_ref[half + size :] = far_ref[...].reshape(size, width)
+        start = half
+        for ref in (near_early_ref, near_ref, far_ref):
+            size = ref.shape[0] * ref.shape[1]
+            if start < give_ref.shape[0]:
+                give_ref[start : start + size] = ref[...].reshape(size, width)
+            start += size
 
     return body
 
@@ -275,34 +291,52 @@
     out_ref[quarter:] = add(q_ref[...], q_other_ref[...])
 
 
-def split_kernel(info_ref, mine_ref, other_ref, first_ref, second_ref):
-    half = mine_ref.shape[0]
+def half_copies(high, value_ref, first_ref, second_ref, sems):
+    half = value_ref.shape[0]
     size = first_ref.shape[0]
-    odd = odd_of(info_ref) == 1
-    mine, other = mine_ref[...].astype(F32), other_ref[...].astype(F32)
-    low = jnp.where(odd, other, mine)
-    high = jnp.where(odd, mine, other)
-    first_ref[:half] = low
-    first_ref[half:] = high[: size - half]
-    second_ref[...] = high[size - half :]
-
-
-def make_finish_kernel(last, half, slots, relay):
-    def body(info_ref, came_ref, place_ref, loc_ref, *refs):
-        here, halos, out_ref = refs[: -2 - relay], refs[-2 - relay : -1], refs[-1]
+    if not high:
+        return [pltpu.make_async_copy(value_ref, first_ref.at[pl.ds(0, half)], sems.at[0])]
+    return [pltpu.make_async_copy(value_ref.at[pl.ds(0, size - half)], first_ref.at[pl.ds(half, size - half)], sems.at[0]),
+            pltpu.make_async_copy(value_ref.at[pl.ds(size - half, 2 * half - size)], second_ref, sems.at[1])]
+
+
+def for_half(high, act, *refs):
+    for case in (0, 1):
+        @pl.when(high == case)
+        def _():
+            for copy in half_copies(case, *refs):
+                act(copy)
+
+
+def split_kernel(info_ref, other_ref, first_in, second_in, first_ref, second_ref, value_ref, sems):
+    value_ref[...] = other_ref[...].astype(F32)
+    refs = (1 - odd_of(info_ref), value_ref, first_ref, second_ref, sems)
+    for_half(refs[0], lambda copy: copy.start(), *refs[1:])
+    for_half(refs[0], lambda copy: copy.wait(), *refs[1:])
+
+
+def make_finish_kernel(last, start, slots, relay):
+    def body(info_ref, mine_ref, came_ref, place_ref, far_early_ref, loc_ref, *refs):
+        here, halos, (out_ref, first_ref, second_ref, value_ref, sems) = refs[: -6 - relay], refs[-6 - relay : -5], refs[-5:]
         odd, end = odd_of(info_ref) == 1, end_of(info_ref) == 1
         batches = loc_ref.shape[0]
         count = batches // len(here)
+        early = batches - count
+        value_ref[...] = mine_ref[...].astype(F32)
+        half_refs = (value_ref, first_ref, second_ref, sems)
+        for_half(odd_of(info_ref), lambda copy: copy.start(), *half_refs)
 
         def far_of(m):
+            if m < early:
+                return far_early_ref[m]
             if not relay:
-                return halos[0][m]
+                return halos[0][m - early]
             first, second = [halo[halo.shape[0] - (batches - m) * slots :][:slots] for halo in halos]
             return jnp.where(direct_of(info_ref) == 1, first, second)
 
         def write(local):
             for m in range(batches):
-                near = came_ref[half + m * slots : half + (m + 1) * slots]
+                near = came_ref[start + m * slots : start + (m + 1) * slots]
                 far = far_of(m)
                 far = jnp.where(end, jnp.zeros_like(far), far)
                 upper = jnp.where(odd, far, near)
@@ -316,6 +350,8 @@
         @pl.when(hop_of(info_ref) != last)
         def _():
             write(lambda m: loc_ref[m])
+
+        for_half(odd_of(info_ref), lambda copy: copy.wait(), *half_refs)
 
     return body
 
@@ -372,8 +408,12 @@
         out_shape=(wide_shape, wide_shape, sds((rows, rows), BF16), sds((2 * slots, rows), BF16)),
         compiler_params=params(), name="inner",
     )(x, neighbours, face_weight, w1)
-    slope, act, agg = call(
-        forward_kernel, (wide_shape, full_shape, full_shape), info, base, inner, near, far, halo, w1, name="forward")
+    forward = []
+    for c in range(chunks):
+        small = sds((count, rows, width), BF16)
+        forward.append(call(
+            make_forward_kernel(c * count), (sds(small.shape, F32), small, small),
+            info, base, inner, near, far, halo, w1, name="forward"))
 
     def move(value, hop, shift):
         source = sections - 1 - hop
@@ -385,7 +425,7 @@
     estimate = pl.CostEstimate(flops=STEP_FLOPS, bytes_accessed=1 << 20, transcendentals=0)
     pieces = []
     received = [None] * chunks
-    weights = (slope, own, halo, w1, w2)
+    weights = (own, halo, w1, w2)
     for hop in range(sections):
         sent = []
         for c in range(chunks):
@@ -397,7 +437,7 @@
                 in_specs=[smem] + [vmem()] * (len(inputs) + 5), out_specs=[vmem()] * 5,
                 out_shape=(piece, piece_edge, piece_edge, piece, piece),
                 cost_estimate=estimate, compiler_params=params(), name="step",
-            )(info, *inputs, *weights)
+            )(info, *inputs, forward[c][0], *weights)
             pieces.append((local, to_below, to_above, g, dz))
             if hop + 1 < sections:
                 sent.append((move(local, hop, 0), move(to_below, hop, -1), move(to_above, hop, 1)))
@@ -406,32 +446,34 @@
     early = chunks - 1
     here, others = pieces[len(pieces) - early :], pieces[: len(pieces) - early]
     last = sections - 1
-    part, local, kept_below, kept_above = pl.pallas_call(
+    early_shape = sds((max(early * count, 1), slots, width), BF16)
+    part, local, kept_below, kept_above, near_early, far_early = pl.pallas_call(
         make_partial_kernel(sections, chunks),
-        in_specs=[smem] + [vmem()] * (3 + 2 * early) + [any_spec] * (5 * len(others)),
-        out_specs=[vmem()] * 4,
-        out_shape=(sds((3 * width, width), F32), full_shape, edge_shape, edge_shape),
+        in_specs=[smem] + [vmem()] * (1 + 2 * chunks + 4 * early) + [any_spec] * (5 * len(others)),
+        out_specs=[vmem()] * 6,
+        out_shape=(sds((3 * width, width), F32), full_shape, edge_shape, edge_shape, early_shape, early_shape),
         scratch_shapes=[pltpu.VMEM(full_shape.shape, BF16)] * 2 + [pltpu.SemaphoreType.DMA((5, chunks))],
         compiler_params=params(), name="partial",
-    )(info, x, agg, act, *[value for outs in here for value in outs[3:]],
-      *[value for outs in others for value in outs])
-    edges = [value for outs in here for value in outs[1:3]]
+    )(info, x, *[value for _, act, agg in forward for value in (agg, act)],
+      *[value for outs in here for value in outs[1:]], *[value for outs in others for value in outs])
+    far_early = lax.ppermute(far_early, "dom", far_pairs)
     local_last, g, dz, near, far = pl.pallas_call(
-        make_last_kernel(last, early * count, count, early),
-        in_specs=[smem] + [vmem()] * (len(inputs) + 7 + 2 * early), out_specs=[vmem()] * 5,
-        out_shape=(piece, piece, piece, edge_shape, edge_shape),
+        make_last_kernel(last, early * count, count),
+        in_specs=[smem] + [vmem()] * (len(inputs) + 7) + [any_spec], out_specs=[vmem()] * 5,
+        out_shape=(piece, piece, piece, piece_edge, piece_edge),
         scratch_shapes=[pltpu.VMEM(piece_edge.shape, BF16)] * 2,
         cost_estimate=estimate, compiler_params=params(), name="step_last",
-    )(info, *inputs, *weights, *edges, kept_below, kept_above)
+    )(info, *inputs, forward[-1][0], *weights, kept_below, kept_above, far_early)
     relay = doms == 8
     half = 3 * width // 2
-    size = batches * slots
+    near_size, far_size = batches * slots, relay * count * slots
+    _, act, agg = forward[-1]
     keep, give = pl.pallas_call(
-        make_weight_kernel(last, early * count, count), in_specs=[smem] + [vmem()] * 8, out_specs=[vmem()] * 2,
-        out_shape=(sds((half, width), F32), sds((half + (1 + relay) * size, width), BF16)),
+        make_weight_kernel(last, early * count, count), in_specs=[smem] + [vmem()] * 9, out_specs=[vmem()] * 2,
+        out_shape=(sds((half, width), F32), sds((half + near_size + far_size, width), BF16)),
         scratch_shapes=[pltpu.VMEM((3 * width, width), F32)],
         cost_estimate=estimate, compiler_params=params(), name="weights",
-    )(info, x, agg, act, part, g, dz, near, far)
+    )(info, x, agg, act, part, g, dz, near_early, near, far)
     if not relay:
         far = lax.ppermute(far, "dom", far_pairs)
 
@@ -440,7 +482,7 @@
 
     came = swap(give, 1)
     quarter = sds((half // 2, width), BF16)
-    longer = sds((half // 2 + relay * size, width), BF16)
+    longer = sds((half // 2 + far_size, width), BF16)
     p, q = pl.pallas_call(
         take_kernel, in_specs=[vmem()] * 2 + [any_spec], out_specs=[vmem()] * 2, out_shape=(longer, quarter),
         compiler_params=params(), name="take",
@@ -472,12 +514,17 @@
         compiler_params=params(), name="join",
     )(p, p_other, q, q_other)
     other = swap(mine, 1)
-    grad_in = pl.pallas_call(
-        make_finish_kernel(last, half, slots, relay), in_specs=[smem] + [vmem()] * (3 + chunks + len(halos)),
-        out_specs=vmem(), out_shape=full_shape, compiler_params=params(), name="finish",
-    )(info, came, place, local, *[outs[0] for outs in here], local_last, *halos)
-    first, second = call(
-        split_kernel, (sds((2 * width, width), F32), sds((width, width), F32)), info, mine, other, name="split")
+    outs = (sds((2 * width, width), F32), sds((width, width), F32))
+    value = [pltpu.VMEM((half, width), F32), pltpu.SemaphoreType.DMA((2,))]
+    grad_in, first, second = pl.pallas_call(
+        make_finish_kernel(last, half, slots, relay),
+        in_specs=[smem] + [vmem()] * (5 + chunks + len(halos)), out_specs=[vmem()] + [any_spec] * 2,
+        out_shape=(full_shape, *outs), scratch_shapes=value, compiler_params=params(), name="finish",
+    )(info, mine, came, place, far_early, local, *[outs[0] for outs in here], local_last, *halos)
+    first, second = pl.pallas_call(
+        split_kernel, in_specs=[smem, vmem(), any_spec, any_spec], out_specs=[any_spec] * 2, out_shape=outs,
+        scratch_shapes=value, input_output_aliases={2: 0, 3: 1}, compiler_params=params(), name="split",
+    )(info, other, first, second)
     return grad_in[None], first[None], second[None]
 
 

time: 73.7 us -> 72.1 us (0.978)
  waiting for transfers between devices: 38.3 us -> 37 us
  local copies, waits for them, and re-layouts: 0.86 us -> 0 us
    ppermute x18, waiting for transfers between devices: 28.4 us -> 27.2 us  [move(): return lax.ppermute(value, ('dom', 'section'), pairs)]
    ppermute x6, waiting for transfers between devices: 9.09 us -> 8.2 us  [swap(): return lax.ppermute(value, 'dom', [(i, i ^ mask) for i in range(doms)])]
    unnamed x36 -> x0, local copies, waits for them, and re-layouts: 0.86 us -> none
    pallas_call x1 -> x2, Pallas kernels: 0.76 us -> 1.56 us  [the longest x1 0.79 us: per_device(): pl.pallas_call(split_kernel, in_specs=[smem, vmem(), any_spec, any_spec],...]
    ppermute x1, waiting for transfers between devices: 0.81 us -> 1.6 us  [per_device(): lax.ppermute(far, 'dom', far_pairs)]
  transfers between devices with their start and end apart: 26 -> 27, of which waited for: 9 -> 7; matrix products, arithmetic and copies ran while one was open for 0% -> 0% of each run, Pallas kernels for 4% -> 6%
where the time goes in v8:
time: 72.1 us; the launch traced here: 71.7 us
  waiting for transfers between devices  37 us (51%)
  starting transfers between devices  25.2 us (35%)
  Pallas kernels  8.36 us (12%)
  between operations  1.06 us (1%)
    ppermute x18, waiting for transfers between devices, move(): return lax.ppermute(value, ('dom', 'section'), pairs)  27.2 us
    ppermute x18, starting transfers between devices, move(): return lax.ppermute(value, ('dom', 'section'), pairs)  15.8 us
    ppermute x6, waiting for transfers between devices, swap(): return lax.ppermute(value, 'dom', [(i, i ^ mask) for i in range(doms)])  8.2 us
    ppermute x6, starting transfers between devices, swap(): return lax.ppermute(value, 'dom', [(i, i ^ mask) for i in range(doms)])  6.21 us
    ppermute x1, starting transfers between devices, per_device(): lax.ppermute(far, 'dom', far_pairs)  2.62 us
    ppermute x1, waiting for transfers between devices, per_device(): lax.ppermute(far, 'dom', far_pairs)  1.6 us
    pallas_call x1, Pallas kernels, per_device(): pl.pallas_call(make_finish_kernel(last, half, slots, relay), in_specs=[sm...  1.58 us
  transfers between devices with their start and end apart: 27, of which 7 were waited for; matrix products, arithmetic and copies ran while one was open for 0% of the time, Pallas kernels for 6%

profile of v8, /device:TPU:1, one launch (start us, length us, event | category | flops | bytes accessed | tf_op | source)
XLA Modules:
  0.0 71.7 jit_solution(413003827260533609)
XLA Ops:
  0.7 1.4 %load.1 = (bf16[4,256,256]{2,1,0:T(8,128)(2,1)S(1)}, bf16[4,256,256]{2,1,0:T(8,128)(2,1)S(1)}, bf16[512,256]{1,0:T(8,128)(2,1)S(1)}, bf16[256,256]{1,0:T(8,128)(...) custom-call(s32[1]{0:T(128)} %bitcast.info_ref, ...), custom_call_target="tpu_custom_call" | custom-call | tf_op jit(solution)/shard_map/load/pallas_call | solution.py:392
  2.2 2.6 %collective-permute-start.1 = (bf16[4,32,256]{2,1,0:T(8,128)(2,1)S(1)}, bf16[4,32,256]{2,1,0:T(8,128)(2,1)S(1)}, u32[]{:S(2)}, u32[]{:S(2)}) collective-permute-start(bf16[4,32,256]{2,1,0:T(8,128)(2,1)S(1)} %get-tuple-element.84), channel_id=1, source_target_pairs={{0,28},{4,8},{8,4},{12,16},{16,12},{20,24},{24,20},{28,0},{1,29},{... | collective-permute-start | bytes 196616 | tf_op jit(solution)/shard_map/ppermute | solution.py:402
  5.5 1.6 %collective-permute-done.1.far_ref = bf16[4,32,256]{2,1,0:T(8,128)(2,1)S(1)} collective-permute-done((bf16[4,32,256]{2,1,0:T(8,128)(2,1)S(1)}, bf16[4,32,256]{2,1,0:T(8,128)(2,1)S(1)}, u32[]{:S(2)}, u32[]{:S(2)}) %collective-permute-start.1) | collective-permute-done | bytes 65568 | tf_op jit(solution)/shard_map/ppermute | solution.py:402
  7.7 0.7 collective-permute-start.2
  8.4 0.7 collective-permute-start.3
  9.0 0.7 collective-permute-start.4
  10.3 0.7 collective-permute-start.11
  11.7 0.7 collective-permute-start.13
  12.4 0.7 collective-permute-start.5
  13.8 0.7 collective-permute-start.7
  14.5 0.7 collective-permute-start.14
  15.8 0.7 collective-permute-start.16
  16.6 1.3 %collective-permute-start.8 = (bf16[2,256,256]{2,1,0:T(8,128)(2,1)S(1)}, bf16[2,256,256]{2,1,0:T(8,128)(2,1)S(1)}, u32[]{:S(2)}, u32[]{:S(2)}) collective-permute-start(bf16[2,256,256]{2,1,0:T(8,128)(2,1)S(1)} %get-tuple-element.101.refs_28_), channel_id=1, source_target_pairs={{1,0},{5,4},{9,8},{13,12},{17,16},{21,20},{25,24},{29,28}} | collective-permute-start | bytes 786440 | tf_op jit(solution)/shard_map/ppermute | solution.py:422
  17.9 1.3 %collective-permute-start.10 = (bf16[2,32,256]{2,1,0:T(8,128)(2,1)S(1)}, bf16[2,32,256]{2,1,0:T(8,128)(2,1)S(1)}, u32[]{:S(2)}, u32[]{:S(2)}) collective-permute-start(bf16[2,32,256]{2,1,0:T(8,128)(2,1)S(1)} %get-tuple-element.103.refs_30_), channel_id=1, source_target_pairs={{1,4},{5,8},{9,12},{13,16},{17,20},{21,24},{25,28}} | collective-permute-start | bytes 98312 | tf_op jit(solution)/shard_map/ppermute | solution.py:422
  19.2 1.3 %collective-permute-start.9 = (bf16[2,32,256]{2,1,0:T(8,128)(2,1)S(1)}, bf16[2,32,256]{2,1,0:T(8,128)(2,1)S(1)}, u32[]{:S(2)}, u32[]{:S(2)}) collective-permute-start(bf16[2,32,256]{2,1,0:T(8,128)(2,1)S(1)} %get-tuple-element.102.refs_29_), channel_id=1, source_target_pairs={{5,0},{9,4},{13,8},{17,12},{21,16},{25,20},{29,24}} | collective-permute-start | bytes 98312 | tf_op jit(solution)/shard_map/ppermute | solution.py:422
  20.5 1.3 %collective-permute-start.17 = (bf16[2,256,256]{2,1,0:T(8,128)(2,1)S(1)}, bf16[2,256,256]{2,1,0:T(8,128)(2,1)S(1)}, u32[]{:S(2)}, u32[]{:S(2)}) collective-permute-start(bf16[2,256,256]{2,1,0:T(8,128)(2,1)S(1)} %get-tuple-element.125.refs_33_), channel_id=1, source_target_pairs={{1,0},{5,4},{9,8},{13,12},{17,16},{21,20},{25,24},{29,28}} | collective-permute-start | bytes 786440 | tf_op jit(solution)/shard_map/ppermute | solution.py:422
  21.8 1.3 %collective-permute-start.18 = (bf16[2,32,256]{2,1,0:T(8,128)(2,1)S(1)}, bf16[2,32,256]{2,1,0:T(8,128)(2,1)S(1)}, u32[]{:S(2)}, u32[]{:S(2)}) collective-permute-start(bf16[2,32,256]{2,1,0:T(8,128)(2,1)S(1)} %get-tuple-element.126.refs_34_), channel_id=1, source_target_pairs={{5,0},{9,4},{13,8},{17,12},{21,16},{25,20},{29,24}} | collective-permute-start | bytes 98312 | tf_op jit(solution)/shard_map/ppermute | solution.py:422
  23.1 18.0 %collective-permute-done.10.refs_2_ = bf16[2,32,256]{2,1,0:T(8,128)(2,1)S(1)} collective-permute-done((bf16[2,32,256]{2,1,0:T(8,128)(2,1)S(1)}, bf16[2,32,256]{2,1,0:T(8,128)(2,1)S(1)}, u32[]{:S(2)}, u32[]{:S(2)}) %collective-permute-start.10) | collective-permute-done | bytes 32800 | tf_op jit(solution)/shard_map/ppermute | solution.py:422
  41.1 1.3 %collective-permute-start.19 = (bf16[2,32,256]{2,1,0:T(8,128)(2,1)S(1)}, bf16[2,32,256]{2,1,0:T(8,128)(2,1)S(1)}, u32[]{:S(2)}, u32[]{:S(2)}) collective-permute-start(bf16[2,32,256]{2,1,0:T(8,128)(2,1)S(1)} %get-tuple-element.127.refs_35_), channel_id=1, source_target_pairs={{1,4},{5,8},{9,12},{13,16},{17,20},{21,24},{25,28}} | collective-permute-start | bytes 98312 | tf_op jit(solution)/shard_map/ppermute | solution.py:422
  42.4 4.7 %collective-permute-done.9.refs_1_ = bf16[2,32,256]{2,1,0:T(8,128)(2,1)S(1)} collective-permute-done((bf16[2,32,256]{2,1,0:T(8,128)(2,1)S(1)}, bf16[2,32,256]{2,1,0:T(8,128)(2,1)S(1)}, u32[]{:S(2)}, u32[]{:S(2)}) %collective-permute-start.9) | collective-permute-done | bytes 32800 | tf_op jit(solution)/shard_map/ppermute | solution.py:422
  47.1 0.8 %step.10 = (bf16[2,256,256]{2,1,0:T(8,128)(2,1)S(1)}, bf16[2,32,256]{2,1,0:T(8,128)(2,1)S(1)}, bf16[2,32,256]{2,1,0:T(8,128)(2,1)S(1)}, bf16[2,256,256]{2,1,0:T(8,128)(2,1)S(1)}, bf16[2,256,256]{2,1,0:T(8,128)(2,1)S(1)}) custom-call(s32[1]{0:T(128)} %bitcast.info_ref, bf16[2,256,256]{2,1,0:T(8,128)(2,1)S(1)} %collective-permute-done.8.refs_0_, ...), custom_call_target="tpu_custom_call" | custom-call | flops 2600000000 | bytes 1048576 | tf_op jit(solution)/shard_map/step/pallas_call | solution.py:435
  49.0 4.5 %collective-permute-done.18.refs_1_ = bf16[2,32,256]{2,1,0:T(8,128)(2,1)S(1)} collective-permute-done((bf16[2,32,256]{2,1,0:T(8,128)(2,1)S(1)}, bf16[2,32,256]{2,1,0:T(8,128)(2,1)S(1)}, u32[]{:S(2)}, u32[]{:S(2)}) %collective-permute-start.18) | collective-permute-done | bytes 32800 | tf_op jit(solution)/shard_map/ppermute | solution.py:422
  53.5 0.8 %step_last.1 = (bf16[2,256,256]{2,1,0:T(8,128)(2,1)S(1)}, bf16[2,256,256]{2,1,0:T(8,128)(2,1)S(1)}, bf16[2,256,256]{2,1,0:T(8,128)(2,1)S(1)}, bf16[2,32,256]{2,1,0:T(8,128)(2,1)S(1)}, bf16[2,32,256]{2,1,0:T(8,128)(2,1)S(1)}) custom-call(s32[1]{0:T(128)} %bitcast.info_ref, bf16[2,256,256]{2,1,0:T(8,128)(2,1)S(1)} %collective-permute-done.17.refs_0_, ...), custom_call_target="tpu_custom_call" | custom-call | flops 2600000000 | bytes 1048576 | tf_op jit(solution)/shard_map/step_last/pallas_call | solution.py:460
  54.8 1.6 %collective-permute-done.21.came_ref = bf16[576,256]{1,0:T(8,128)(2,1)S(1)} collective-permute-done((bf16[576,256]{1,0:T(8,128)(2,1)S(1)}, bf16[576,256]{1,0:T(8,128)(2,1)S(1)}, u32[]{:S(2)}, u32[]{:S(2)}) %collective-permute-start.21) | collective-permute-done | bytes 294944 | tf_op jit(solution)/shard_map/ppermute | solution.py:481
  56.5 0.7 %collective-permute-start.22 = (bf16[256,256]{1,0:T(8,128)(2,1)S(1)}, bf16[256,256]{1,0:T(8,128)(2,1)S(1)}, u32[]{:S(2)}, u32[]{:S(2)}) collective-permute-start(bf16[256,256]{1,0:T(8,128)(2,1)S(1)} %get-tuple-element.141.p_ref), channel_id=1, source_target_pairs={{0,8},{4,12},{8,0},{12,4},{16,24},{20,28},{24,16},{28,20},{1,9},{5... | collective-permute-start | bytes 393224 | tf_op jit(solution)/shard_map/ppermute | solution.py:481
  57.2 1.1 %collective-permute-start.24 = (bf16[192,256]{1,0:T(8,128)(2,1)S(1)}, bf16[192,256]{1,0:T(8,128)(2,1)S(1)}, u32[]{:S(2)}, u32[]{:S(2)}) collective-permute-start(bf16[192,256]{1,0:T(8,128)(2,1)S(1)} %get-tuple-element.142), channel_id=1, source_target_pairs={{0,16},{4,20},{8,24},{12,28},{16,0},{20,4},{24,8},{28,12},{1,17},{... | collective-permute-start | bytes 294920 | tf_op jit(solution)/shard_map/ppermute | solution.py:481
  58.3 3.2 %collective-permute-done.22.other_ref.refs_2_ = bf16[256,256]{1,0:T(8,128)(2,1)S(1)} collective-permute-done((bf16[256,256]{1,0:T(8,128)(2,1)S(1)}, bf16[256,256]{1,0:T(8,128)(2,1)S(1)}, u32[]{:S(2)}, u32[]{:S(2)}) %collective-permute-start.22) | collective-permute-done | bytes 131104 | tf_op jit(solution)/shard_map/ppermute | solution.py:481
  61.5 1.5 %collective-permute-start.23 = (bf16[256,256]{1,0:T(8,128)(2,1)S(1)}, bf16[256,256]{1,0:T(8,128)(2,1)S(1)}, u32[]{:S(2)}, u32[]{:S(2)}) collective-permute-start(bf16[256,256]{1,0:T(8,128)(2,1)S(1)} %forward_sum.1.p_ref), channel_id=1, source_target_pairs={{0,16},{4,20},{8,24},{12,28},{16,0},{20,4},{24,8},{28,12},{1,17},{... | collective-permute-start | bytes 393224 | tf_op jit(solution)/shard_map/ppermute | solution.py:481
  63.4 3.4 %collective-permute-done.25.q_other_ref = bf16[192,256]{1,0:T(8,128)(2,1)S(1)} collective-permute-done((bf16[192,256]{1,0:T(8,128)(2,1)S(1)}, bf16[192,256]{1,0:T(8,128)(2,1)S(1)}, u32[]{:S(2)}, u32[]{:S(2)}) %collective-permute-start.25) | collective-permute-done | bytes 98336 | tf_op jit(solution)/shard_map/ppermute | solution.py:481
  66.9 2.4 %collective-permute-start.26 = (bf16[384,256]{1,0:T(8,128)(2,1)S(1)}, bf16[384,256]{1,0:T(8,128)(2,1)S(1)}, u32[]{:S(2)}, u32[]{:S(2)}) collective-permute-start(bf16[384,256]{1,0:T(8,128)(2,1)S(1)} %join.1.mine_ref), channel_id=1, source_target_pairs={{0,4},{4,0},{8,12},{12,8},{16,20},{20,16},{24,28},{28,24},{1,5},{5... | collective-permute-start | bytes 589832 | tf_op jit(solution)/shard_map/ppermute | solution.py:481
  69.3 1.6 %finish.1 = (bf16[4,256,256]{2,1,0:T(8,128)(2,1)}, f32[512,256]{1,0:T(8,128)}, f32[256,256]{1,0:T(8,128)}) custom-call(s32[1]{0:T(128)} %bitcast.info_ref, bf16[384,256]{1,0:T(8,128)(2,1)S(1)} %join.1.mine_ref, bf16[576,256]{1,0:T(8,128)(2,1)S(1)} %collective-permute-done.21.came_ref, bf16[256,64]{1,0:T(8,128)(2,1)S(1)} %get-tuple-element.97.refs_3_.place_ref, ...), custom_call_target="tpu_custom_call" | custom-call | tf_op jit(solution)/shard_map/finish/pallas_call | solution.py:519
  70.9 0.8 %split.1 = (f32[512,256]{1,0:T(8,128)}, f32[256,256]{1,0:T(8,128)}) custom-call(s32[1]{0:T(128)} %bitcast.info_ref, bf16[384,256]{1,0:T(8,128)(2,1)S(1)} %collective-permute-done.26.other_ref, f32[512,256]{1,0:T(8,128)} %get-tuple-element.147.first_in, f32[256,256]{1,0:T(8,128)} %get-tuple-element.148.second_in), custom_call_target="tpu_custom_call", output_to_operand_aliasing={{0}: (2, {}), {1}: (3, {})} | custom-call | tf_op jit(solution)/shard_map/split/pallas_call | solution.py:524
  (42 shorter events, 6.2 us)
Async XLA Ops:
  2.1 3.4 %collective-permute-start = (bf16[4,32,256]{2,1,0:T(8,128)(2,1)S(1)}, bf16[4,32,256]{2,1,0:T(8,128)(2,1)S(1)}, u32[]{:S(2)}, u32[]{:S(2)}) collective-permute-start(bf16[4,32,256]{2,1,0:T(8,128)(2,1)S(1)} %get-tuple-element.83), channel_id=1, source_target_pairs={{0,4},{4,0},{8,12},{12,8},{16,20},{20,16},{24,28},{28,24},{1,5},{5... | collective-permute-start | bytes 196616 | tf_op jit(solution)/shard_map/ppermute | solution.py:402
  2.2 4.9 %collective-permute-start.1 = (bf16[4,32,256]{2,1,0:T(8,128)(2,1)S(1)}, bf16[4,32,256]{2,1,0:T(8,128)(2,1)S(1)}, u32[]{:S(2)}, u32[]{:S(2)}) collective-permute-start(bf16[4,32,256]{2,1,0:T(8,128)(2,1)S(1)} %get-tuple-element.84), channel_id=1, source_target_pairs={{0,28},{4,8},{8,4},{12,16},{16,12},{20,24},{24,20},{28,0},{1,29},{... | collective-permute-start | bytes 196616 | tf_op jit(solution)/shard_map/ppermute | solution.py:402
  7.7 4.7 %collective-permute-start.2 = (bf16[2,256,256]{2,1,0:T(8,128)(2,1)S(1)}, bf16[2,256,256]{2,1,0:T(8,128)(2,1)S(1)}, u32[]{:S(2)}, u32[]{:S(2)}) collective-permute-start(bf16[2,256,256]{2,1,0:T(8,128)(2,1)S(1)} %get-tuple-element.94.refs_8_), channel_id=1, source_target_pairs={{3,2},{7,6},{11,10},{15,14},{19,18},{23,22},{27,26},{31,30}} | collective-permute-start | bytes 786440 | tf_op jit(solution)/shard_map/ppermute | solution.py:422
  8.4 3.3 %collective-permute-start.3 = (bf16[2,32,256]{2,1,0:T(8,128)(2,1)S(1)}, bf16[2,32,256]{2,1,0:T(8,128)(2,1)S(1)}, u32[]{:S(2)}, u32[]{:S(2)}) collective-permute-start(bf16[2,32,256]{2,1,0:T(8,128)(2,1)S(1)} %get-tuple-element.95.refs_9_), channel_id=1, source_target_pairs={{7,2},{11,6},{15,10},{19,14},{23,18},{27,22},{31,26}} | collective-permute-start | bytes 98312 | tf_op jit(solution)/shard_map/ppermute | solution.py:422
  9.0 3.3 %collective-permute-start.4 = (bf16[2,32,256]{2,1,0:T(8,128)(2,1)S(1)}, bf16[2,32,256]{2,1,0:T(8,128)(2,1)S(1)}, u32[]{:S(2)}, u32[]{:S(2)}) collective-permute-start(bf16[2,32,256]{2,1,0:T(8,128)(2,1)S(1)} %get-tuple-element.96.refs_10_), channel_id=1, source_target_pairs={{3,6},{7,10},{11,14},{15,18},{19,22},{23,26},{27,30}} | collective-permute-start | bytes 98312 | tf_op jit(solution)/shard_map/ppermute | solution.py:422
  10.3 4.1 %collective-permute-start.11 = (bf16[2,256,256]{2,1,0:T(8,128)(2,1)S(1)}, bf16[2,256,256]{2,1,0:T(8,128)(2,1)S(1)}, u32[]{:S(2)}, u32[]{:S(2)}) collective-permute-start(bf16[2,256,256]{2,1,0:T(8,128)(2,1)S(1)} %get-tuple-element.111.refs_13_), channel_id=1, source_target_pairs={{3,2},{7,6},{11,10},{15,14},{19,18},{23,22},{27,26},{31,30}} | collective-permute-start | bytes 786440 | tf_op jit(solution)/shard_map/ppermute | solution.py:422
  11.0 2.8 %collective-permute-start.12 = (bf16[2,32,256]{2,1,0:T(8,128)(2,1)S(1)}, bf16[2,32,256]{2,1,0:T(8,128)(2,1)S(1)}, u32[]{:S(2)}, u32[]{:S(2)}) collective-permute-start(bf16[2,32,256]{2,1,0:T(8,128)(2,1)S(1)} %get-tuple-element.112.refs_14_), channel_id=1, source_target_pairs={{7,2},{11,6},{15,10},{19,14},{23,18},{27,22},{31,26}} | collective-permute-start | bytes 98312 | tf_op jit(solution)/shard_map/ppermute | solution.py:422
  11.7 2.8 %collective-permute-start.13 = (bf16[2,32,256]{2,1,0:T(8,128)(2,1)S(1)}, bf16[2,32,256]{2,1,0:T(8,128)(2,1)S(1)}, u32[]{:S(2)}, u32[]{:S(2)}) collective-permute-start(bf16[2,32,256]{2,1,0:T(8,128)(2,1)S(1)} %get-tuple-element.113.refs_15_), channel_id=1, source_target_pairs={{3,6},{7,10},{11,14},{15,18},{19,22},{23,26},{27,30}} | collective-permute-start | bytes 98312 | tf_op jit(solution)/shard_map/ppermute | solution.py:422
  12.4 4.1 %collective-permute-start.5 = (bf16[2,256,256]{2,1,0:T(8,128)(2,1)S(1)}, bf16[2,256,256]{2,1,0:T(8,128)(2,1)S(1)}, u32[]{:S(2)}, u32[]{:S(2)}) collective-permute-start(bf16[2,256,256]{2,1,0:T(8,128)(2,1)S(1)} %get-tuple-element.98.refs_18_), channel_id=1, source_target_pairs={{2,1},{6,5},{10,9},{14,13},{18,17},{22,21},{26,25},{30,29}} | collective-permute-start | bytes 786440 | tf_op jit(solution)/shard_map/ppermute | solution.py:422
  13.1 2.8 %collective-permute-start.6 = (bf16[2,32,256]{2,1,0:T(8,128)(2,1)S(1)}, bf16[2,32,256]{2,1,0:T(8,128)(2,1)S(1)}, u32[]{:S(2)}, u32[]{:S(2)}) collective-permute-start(bf16[2,32,256]{2,1,0:T(8,128)(2,1)S(1)} %get-tuple-element.99.refs_19_), channel_id=1, source_target_pairs={{6,1},{10,5},{14,9},{18,13},{22,17},{26,21},{30,25}} | collective-permute-start | bytes 98312 | tf_op jit(solution)/shard_map/ppermute | solution.py:422
  13.8 2.8 %collective-permute-start.7 = (bf16[2,32,256]{2,1,0:T(8,128)(2,1)S(1)}, bf16[2,32,256]{2,1,0:T(8,128)(2,1)S(1)}, u32[]{:S(2)}, u32[]{:S(2)}) collective-permute-start(bf16[2,32,256]{2,1,0:T(8,128)(2,1)S(1)} %get-tuple-element.100.refs_20_), channel_id=1, source_target_pairs={{2,5},{6,9},{10,13},{14,17},{18,21},{22,25},{26,29}} | collective-permute-start | bytes 98312 | tf_op jit(solution)/shard_map/ppermute | solution.py:422
  14.5 6.0 %collective-permute-start.14 = (bf16[2,256,256]{2,1,0:T(8,128)(2,1)S(1)}, bf16[2,256,256]{2,1,0:T(8,128)(2,1)S(1)}, u32[]{:S(2)}, u32[]{:S(2)}) collective-permute-start(bf16[2,256,256]{2,1,0:T(8,128)(2,1)S(1)} %get-tuple-element.118.refs_23_), channel_id=1, source_target_pairs={{2,1},{6,5},{10,9},{14,13},{18,17},{22,21},{26,25},{30,29}} | collective-permute-start | bytes 786440 | tf_op jit(solution)/shard_map/ppermute | solution.py:422
  15.2 4.0 %collective-permute-start.15 = (bf16[2,32,256]{2,1,0:T(8,128)(2,1)S(1)}, bf16[2,32,256]{2,1,0:T(8,128)(2,1)S(1)}, u32[]{:S(2)}, u32[]{:S(2)}) collective-permute-start(bf16[2,32,256]{2,1,0:T(8,128)(2,1)S(1)} %get-tuple-element.119.refs_24_), channel_id=1, source_target_pairs={{6,1},{10,5},{14,9},{18,13},{22,17},{26,21},{30,25}} | collective-permute-start | bytes 98312 | tf_op jit(solution)/shard_map/ppermute | solution.py:422
  15.8 4.6 %collective-permute-start.16 = (bf16[2,32,256]{2,1,0:T(8,128)(2,1)S(1)}, bf16[2,32,256]{2,1,0:T(8,128)(2,1)S(1)}, u32[]{:S(2)}, u32[]{:S(2)}) collective-permute-start(bf16[2,32,256]{2,1,0:T(8,128)(2,1)S(1)} %get-tuple-element.120.refs_25_), channel_id=1, source_target_pairs={{2,5},{6,9},{10,13},{14,17},{18,21},{22,25},{26,29}} | collective-permute-start | bytes 98312 | tf_op jit(solution)/shard_map/ppermute | solution.py:422
  16.6 30.5 %collective-permute-start.8 = (bf16[2,256,256]{2,1,0:T(8,128)(2,1)S(1)}, bf16[2,256,256]{2,1,0:T(8,128)(2,1)S(1)}, u32[]{:S(2)}, u32[]{:S(2)}) collective-permute-start(bf16[2,256,256]{2,1,0:T(8,128)(2,1)S(1)} %get-tuple-element.101.refs_28_), channel_id=1, source_target_pairs={{1,0},{5,4},{9,8},{13,12},{17,16},{21,20},{25,24},{29,28}} | collective-permute-start | bytes 786440 | tf_op jit(solution)/shard_map/ppermute | solution.py:422
  17.9 23.2 %collective-permute-start.10 = (bf16[2,32,256]{2,1,0:T(8,128)(2,1)S(1)}, bf16[2,32,256]{2,1,0:T(8,128)(2,1)S(1)}, u32[]{:S(2)}, u32[]{:S(2)}) collective-permute-start(bf16[2,32,256]{2,1,0:T(8,128)(2,1)S(1)} %get-tuple-element.103.refs_30_), channel_id=1, source_target_pairs={{1,4},{5,8},{9,12},{13,16},{17,20},{21,24},{25,28}} | collective-permute-start | bytes 98312 | tf_op jit(solution)/shard_map/ppermute | solution.py:422
  19.2 27.9 %collective-permute-start.9 = (bf16[2,32,256]{2,1,0:T(8,128)(2,1)S(1)}, bf16[2,32,256]{2,1,0:T(8,128)(2,1)S(1)}, u32[]{:S(2)}, u32[]{:S(2)}) collective-permute-start(bf16[2,32,256]{2,1,0:T(8,128)(2,1)S(1)} %get-tuple-element.102.refs_29_), channel_id=1, source_target_pairs={{5,0},{9,4},{13,8},{17,12},{21,16},{25,20},{29,24}} | collective-permute-start | bytes 98312 | tf_op jit(solution)/shard_map/ppermute | solution.py:422
  20.5 33.0 %collective-permute-start.17 = (bf16[2,256,256]{2,1,0:T(8,128)(2,1)S(1)}, bf16[2,256,256]{2,1,0:T(8,128)(2,1)S(1)}, u32[]{:S(2)}, u32[]{:S(2)}) collective-permute-start(bf16[2,256,256]{2,1,0:T(8,128)(2,1)S(1)} %get-tuple-element.125.refs_33_), channel_id=1, source_target_pairs={{1,0},{5,4},{9,8},{13,12},{17,16},{21,20},{25,24},{29,28}} | collective-permute-start | bytes 786440 | tf_op jit(solution)/shard_map/ppermute | solution.py:422
  21.8 31.7 %collective-permute-start.18 = (bf16[2,32,256]{2,1,0:T(8,128)(2,1)S(1)}, bf16[2,32,256]{2,1,0:T(8,128)(2,1)S(1)}, u32[]{:S(2)}, u32[]{:S(2)}) collective-permute-start(bf16[2,32,256]{2,1,0:T(8,128)(2,1)S(1)} %get-tuple-element.126.refs_34_), channel_id=1, source_target_pairs={{5,0},{9,4},{13,8},{17,12},{21,16},{25,20},{29,24}} | collective-permute-start | bytes 98312 | tf_op jit(solution)/shard_map/ppermute | solution.py:422
  41.1 12.4 %collective-permute-start.19 = (bf16[2,32,256]{2,1,0:T(8,128)(2,1)S(1)}, bf16[2,32,256]{2,1,0:T(8,128)(2,1)S(1)}, u32[]{:S(2)}, u32[]{:S(2)}) collective-permute-start(bf16[2,32,256]{2,1,0:T(8,128)(2,1)S(1)} %get-tuple-element.127.refs_35_), channel_id=1, source_target_pairs={{1,4},{5,8},{9,12},{13,16},{17,20},{21,24},{25,28}} | collective-permute-start | bytes 98312 | tf_op jit(solution)/shard_map/ppermute | solution.py:422
  48.4 5.1 %collective-permute-start.20 = (bf16[2,32,256]{2,1,0:T(8,128)(2,1)S(1)}, bf16[2,32,256]{2,1,0:T(8,128)(2,1)S(1)}, u32[]{:S(2)}, u32[]{:S(2)}) collective-permute-start(bf16[2,32,256]{2,1,0:T(8,128)(2,1)S(1)} %get-tuple-element.133), channel_id=1, source_target_pairs={{0,28},{4,8},{8,4},{12,16},{16,12},{20,24},{24,20},{28,0},{1,29},{... | collective-permute-start | bytes 98312 | tf_op jit(solution)/shard_map/ppermute | solution.py:459
  54.8 1.6 %collective-permute-start.21 = (bf16[576,256]{1,0:T(8,128)(2,1)S(1)}, bf16[576,256]{1,0:T(8,128)(2,1)S(1)}, u32[]{:S(2)}, u32[]{:S(2)}) collective-permute-start(bf16[576,256]{1,0:T(8,128)(2,1)S(1)} %get-tuple-element.140), channel_id=1, source_target_pairs={{0,4},{4,0},{8,12},{12,8},{16,20},{20,16},{24,28},{28,24},{1,5},{5... | collective-permute-start | bytes 884744 | tf_op jit(solution)/shard_map/ppermute | solution.py:481
  56.5 5.0 %collective-permute-start.22 = (bf16[256,256]{1,0:T(8,128)(2,1)S(1)}, bf16[256,256]{1,0:T(8,128)(2,1)S(1)}, u32[]{:S(2)}, u32[]{:S(2)}) collective-permute-start(bf16[256,256]{1,0:T(8,128)(2,1)S(1)} %get-tuple-element.141.p_ref), channel_id=1, source_target_pairs={{0,8},{4,12},{8,0},{12,4},{16,24},{20,28},{24,16},{28,20},{1,9},{5... | collective-permute-start | bytes 393224 | tf_op jit(solution)/shard_map/ppermute | solution.py:481
  57.2 5.8 %collective-permute-start.24 = (bf16[192,256]{1,0:T(8,128)(2,1)S(1)}, bf16[192,256]{1,0:T(8,128)(2,1)S(1)}, u32[]{:S(2)}, u32[]{:S(2)}) collective-permute-start(bf16[192,256]{1,0:T(8,128)(2,1)S(1)} %get-tuple-element.142), channel_id=1, source_target_pairs={{0,16},{4,20},{8,24},{12,28},{16,0},{20,4},{24,8},{28,12},{1,17},{... | collective-permute-start | bytes 294920 | tf_op jit(solution)/shard_map/ppermute | solution.py:481
  61.5 5.4 %collective-permute-start.23 = (bf16[256,256]{1,0:T(8,128)(2,1)S(1)}, bf16[256,256]{1,0:T(8,128)(2,1)S(1)}, u32[]{:S(2)}, u32[]{:S(2)}) collective-permute-start(bf16[256,256]{1,0:T(8,128)(2,1)S(1)} %forward_sum.1.p_ref), channel_id=1, source_target_pairs={{0,16},{4,20},{8,24},{12,28},{16,0},{20,4},{24,8},{28,12},{1,17},{... | collective-permute-start | bytes 393224 | tf_op jit(solution)/shard_map/ppermute | solution.py:481
  63.0 3.8 %collective-permute-start.25 = (bf16[192,256]{1,0:T(8,128)(2,1)S(1)}, bf16[192,256]{1,0:T(8,128)(2,1)S(1)}, u32[]{:S(2)}, u32[]{:S(2)}) collective-permute-start(bf16[192,256]{1,0:T(8,128)(2,1)S(1)} %add_convert_fusion.q_ref), channel_id=1, source_target_pairs={{0,8},{4,12},{8,0},{12,4},{16,24},{20,28},{24,16},{28,20},{1,9},{5... | collective-permute-start | bytes 294920 | tf_op jit(solution)/shard_map/ppermute | solution.py:481
  66.9 4.0 %collective-permute-start.26 = (bf16[384,256]{1,0:T(8,128)(2,1)S(1)}, bf16[384,256]{1,0:T(8,128)(2,1)S(1)}, u32[]{:S(2)}, u32[]{:S(2)}) collective-permute-start(bf16[384,256]{1,0:T(8,128)(2,1)S(1)} %join.1.mine_ref), channel_id=1, source_target_pairs={{0,4},{4,0},{8,12},{12,8},{16,20},{20,16},{24,28},{28,24},{1,5},{5... | collective-permute-start | bytes 589832 | tf_op jit(solution)/shard_map/ppermute | solution.py:481

commit v9 on v8

--- a/solution.py
+++ b/solution.py
@@ -272,12 +272,13 @@
 
 
 def take_kernel(keep_ref, came_ref, far_ref, p_ref, q_ref):
-    quarter = q_ref.shape[0]
+    quarter = keep_ref.shape[0] // 2
     p_ref[:quarter] = add(keep_ref[:quarter], came_ref[:quarter])
-    q_ref[...] = add(keep_ref[quarter:], came_ref[quarter : 2 * quarter])
+    q_ref[:quarter] = add(keep_ref[quarter:], came_ref[quarter : 2 * quarter])
     extra = p_ref.shape[0] - quarter
     if extra:
         p_ref[quarter:] = came_ref[came_ref.shape[0] - extra :]
+        q_ref[quarter:] = came_ref[came_ref.shape[0] - extra :]
 
 
 def forward_sum_kernel(p_ref, other_ref, out_ref, *, quarter):
@@ -286,9 +287,9 @@
 
 
 def join_kernel(p_ref, p_other_ref, q_ref, q_other_ref, out_ref):
-    quarter = q_ref.shape[0]
+    quarter = out_ref.shape[0] // 2
     out_ref[:quarter] = add(p_ref[:quarter], p_other_ref[:quarter])
-    out_ref[quarter:] = add(q_ref[...], q_other_ref[...])
+    out_ref[quarter:] = add(q_ref[:quarter], q_other_ref[:quarter])
 
 
 def half_copies(high, value_ref, first_ref, second_ref, sems):
@@ -317,7 +318,9 @@
 
 def make_finish_kernel(last, start, slots, relay):
     def body(info_ref, mine_ref, came_ref, place_ref, far_early_ref, loc_ref, *refs):
-        here, halos, (out_ref, first_ref, second_ref, value_ref, sems) = refs[: -6 - relay], refs[-6 - relay : -5], refs[-5:]
+        number = 4 if relay else 1
+        here, halos, refs = refs[: -5 - number], refs[-5 - number : -5], refs[-5:]
+        out_ref, first_ref, second_ref, value_ref, sems = refs
         odd, end = odd_of(info_ref) == 1, end_of(info_ref) == 1
         batches = loc_ref.shape[0]
         count = batches // len(here)
@@ -331,7 +334,8 @@
                 return far_early_ref[m]
             if not relay:
                 return halos[0][m - early]
-            first, second = [halo[halo.shape[0] - (batches - m) * slots :][:slots] for halo in halos]
+            rows = [halo[halo.shape[0] - (batches - m) * slots :][:slots] for halo in halos]
+            first, second = jnp.where(odd, rows[1], rows[0]), jnp.where(odd, rows[3], rows[2])
             return jnp.where(direct_of(info_ref) == 1, first, second)
 
         def write(local):
@@ -481,29 +485,34 @@
         return lax.ppermute(value, "dom", [(i, i ^ mask) for i in range(doms)])
 
     came = swap(give, 1)
-    quarter = sds((half // 2, width), BF16)
     longer = sds((half // 2 + far_size, width), BF16)
     p, q = pl.pallas_call(
-        take_kernel, in_specs=[vmem()] * 2 + [any_spec], out_specs=[vmem()] * 2, out_shape=(longer, quarter),
+        take_kernel, in_specs=[vmem()] * 2 + [any_spec], out_specs=[vmem()] * 2, out_shape=(longer, longer),
         compiler_params=params(), name="take",
     )(keep, came, far)
     halos = [] if relay else [far]
+
+    def cross(value, even, odd):
+        return lax.ppermute(value, "dom", [(i, i ^ (odd if i % 2 else even)) for i in range(doms)])
+
+    def forward_sum(value, other):
+        if not relay:
+            return add(value, other)
+        return pl.pallas_call(
+            functools.partial(forward_sum_kernel, quarter=half // 2), in_specs=[vmem()] * 2, out_specs=vmem(),
+            out_shape=longer, compiler_params=params(), name="forward_sum",
+        )(value, other)
+
     bit = 2
     while bit < doms:
         if bit * 2 < doms:
-            p_other, q_other = swap(p, bit), swap(q, 2 * bit)
+            p_other, q_other = cross(p, bit, 2 * bit), cross(q, 2 * bit, bit)
             if relay:
-                halos.append(p_other)
-                p = pl.pallas_call(
-                    functools.partial(forward_sum_kernel, quarter=half // 2), in_specs=[vmem()] * 2, out_specs=vmem(),
-                    out_shape=longer, compiler_params=params(), name="forward_sum",
-                )(p, p_other)
-            else:
-                p = add(p, p_other)
-            q = add(q, q_other)
-            p_other, q_other = swap(p, 2 * bit), swap(q, bit)
+                halos += [p_other, q_other]
+            p, q = forward_sum(p, p_other), forward_sum(q, q_other)
+            p_other, q_other = cross(p, 2 * bit, bit), cross(q, bit, 2 * bit)
             if relay:
-                halos.append(p_other)
+                halos += [p_other, q_other]
         else:
             p_other, q_other = swap(p, bit), swap(q, bit)
         bit *= 4

time: 72.1 us -> 71.8 us (level)
    ppermute x0 -> x4, waiting for transfers between devices: none -> 7.04 us  [cross(): lax.ppermute(value, 'dom', [(i, i ^ (odd if i % 2 else even)) for i in ra...]
    ppermute x6 -> x2, waiting for transfers between devices: 8.2 us -> 1.57 us  [swap(): return lax.ppermute(value, 'dom', [(i, i ^ mask) for i in range(doms)])]
    ppermute x6 -> x2, starting transfers between devices: 6.21 us -> 1.12 us  [swap(): return lax.ppermute(value, 'dom', [(i, i ^ mask) for i in range(doms)])]
    ppermute x0 -> x4, starting transfers between devices: none -> 4.4 us  [cross(): lax.ppermute(value, 'dom', [(i, i ^ (odd if i % 2 else even)) for i in ra...]
  transfers between devices with their start and end apart: 27 -> 27, of which waited for: 7 -> 8; matrix products, arithmetic and copies ran while one was open for 0% -> 0% of each run, Pallas kernels for 6% -> 6%
where the time goes in v9:
time: 71.8 us; the launch traced here: 71.4 us
  waiting for transfers between devices  37.4 us (52%)
  starting transfers between devices  24.6 us (34%)
  Pallas kernels  8.39 us (12%)
  between operations  1.06 us (1%)
    ppermute x18, waiting for transfers between devices, move(): return lax.ppermute(value, ('dom', 'section'), pairs)  27.2 us
    ppermute x18, starting transfers between devices, move(): return lax.ppermute(value, ('dom', 'section'), pairs)  15.8 us
    ppermute x4, waiting for transfers between devices, cross(): lax.ppermute(value, 'dom', [(i, i ^ (odd if i % 2 else even)) for i in ra...  7.04 us
    ppermute x4, starting transfers between devices, cross(): lax.ppermute(value, 'dom', [(i, i ^ (odd if i % 2 else even)) for i in ra...  4.4 us
    ppermute x1, starting transfers between devices, per_device(): lax.ppermute(far, 'dom', far_pairs)  2.62 us
    ppermute x1, waiting for transfers between devices, per_device(): lax.ppermute(far, 'dom', far_pairs)  1.6 us
    pallas_call x1, Pallas kernels, per_device(): pl.pallas_call(make_finish_kernel(last, half, slots, relay), in_specs=[sm...  1.58 us
    ppermute x2, waiting for transfers between devices, swap(): return lax.ppermute(value, 'dom', [(i, i ^ mask) for i in range(doms)])  1.57 us
  transfers between devices with their start and end apart: 27, of which 8 were waited for; matrix products, arithmetic and copies ran while one was open for 0% of the time, Pallas kernels for 6%

profile of v9, /device:TPU:1, one launch (start us, length us, event | category | flops | bytes accessed | tf_op | source)
XLA Modules:
  0.0 71.4 jit_solution(15748575796948348371)
XLA Ops:
  0.7 1.4 %load.1 = (bf16[4,256,256]{2,1,0:T(8,128)(2,1)S(1)}, bf16[4,256,256]{2,1,0:T(8,128)(2,1)S(1)}, bf16[512,256]{1,0:T(8,128)(2,1)S(1)}, bf16[256,256]{1,0:T(8,128)(...) custom-call(s32[1]{0:T(128)} %bitcast.info_ref, ...), custom_call_target="tpu_custom_call" | custom-call | tf_op jit(solution)/shard_map/load/pallas_call | solution.py:396
  2.2 2.6 %collective-permute-start.1 = (bf16[4,32,256]{2,1,0:T(8,128)(2,1)S(1)}, bf16[4,32,256]{2,1,0:T(8,128)(2,1)S(1)}, u32[]{:S(2)}, u32[]{:S(2)}) collective-permute-start(bf16[4,32,256]{2,1,0:T(8,128)(2,1)S(1)} %get-tuple-element.84), channel_id=1, source_target_pairs={{0,28},{4,8},{8,4},{12,16},{16,12},{20,24},{24,20},{28,0},{1,29},{... | collective-permute-start | bytes 196616 | tf_op jit(solution)/shard_map/ppermute | solution.py:406
  5.5 1.6 %collective-permute-done.1.far_ref = bf16[4,32,256]{2,1,0:T(8,128)(2,1)S(1)} collective-permute-done((bf16[4,32,256]{2,1,0:T(8,128)(2,1)S(1)}, bf16[4,32,256]{2,1,0:T(8,128)(2,1)S(1)}, u32[]{:S(2)}, u32[]{:S(2)}) %collective-permute-start.1) | collective-permute-done | bytes 65568 | tf_op jit(solution)/shard_map/ppermute | solution.py:406
  7.7 0.7 collective-permute-start.2
  8.4 0.7 collective-permute-start.3
  9.0 0.7 collective-permute-start.4
  10.3 0.7 collective-permute-start.11
  11.0 0.7 collective-permute-start.12
  11.7 0.7 collective-permute-start.13
  12.4 0.7 collective-permute-start.5
  14.5 0.7 collective-permute-start.14
  16.6 1.3 %collective-permute-start.8 = (bf16[2,256,256]{2,1,0:T(8,128)(2,1)S(1)}, bf16[2,256,256]{2,1,0:T(8,128)(2,1)S(1)}, u32[]{:S(2)}, u32[]{:S(2)}) collective-permute-start(bf16[2,256,256]{2,1,0:T(8,128)(2,1)S(1)} %get-tuple-element.101.refs_28_), channel_id=1, source_target_pairs={{1,0},{5,4},{9,8},{13,12},{17,16},{21,20},{25,24},{29,28}} | collective-permute-start | bytes 786440 | tf_op jit(solution)/shard_map/ppermute | solution.py:426
  17.9 1.3 %collective-permute-start.10 = (bf16[2,32,256]{2,1,0:T(8,128)(2,1)S(1)}, bf16[2,32,256]{2,1,0:T(8,128)(2,1)S(1)}, u32[]{:S(2)}, u32[]{:S(2)}) collective-permute-start(bf16[2,32,256]{2,1,0:T(8,128)(2,1)S(1)} %get-tuple-element.103.refs_30_), channel_id=1, source_target_pairs={{1,4},{5,8},{9,12},{13,16},{17,20},{21,24},{25,28}} | collective-permute-start | bytes 98312 | tf_op jit(solution)/shard_map/ppermute | solution.py:426
  19.2 1.3 %collective-permute-start.9 = (bf16[2,32,256]{2,1,0:T(8,128)(2,1)S(1)}, bf16[2,32,256]{2,1,0:T(8,128)(2,1)S(1)}, u32[]{:S(2)}, u32[]{:S(2)}) collective-permute-start(bf16[2,32,256]{2,1,0:T(8,128)(2,1)S(1)} %get-tuple-element.102.refs_29_), channel_id=1, source_target_pairs={{5,0},{9,4},{13,8},{17,12},{21,16},{25,20},{29,24}} | collective-permute-start | bytes 98312 | tf_op jit(solution)/shard_map/ppermute | solution.py:426
  20.5 1.3 %collective-permute-start.17 = (bf16[2,256,256]{2,1,0:T(8,128)(2,1)S(1)}, bf16[2,256,256]{2,1,0:T(8,128)(2,1)S(1)}, u32[]{:S(2)}, u32[]{:S(2)}) collective-permute-start(bf16[2,256,256]{2,1,0:T(8,128)(2,1)S(1)} %get-tuple-element.125.refs_33_), channel_id=1, source_target_pairs={{1,0},{5,4},{9,8},{13,12},{17,16},{21,20},{25,24},{29,28}} | collective-permute-start | bytes 786440 | tf_op jit(solution)/shard_map/ppermute | solution.py:426
  21.8 1.3 %collective-permute-start.18 = (bf16[2,32,256]{2,1,0:T(8,128)(2,1)S(1)}, bf16[2,32,256]{2,1,0:T(8,128)(2,1)S(1)}, u32[]{:S(2)}, u32[]{:S(2)}) collective-permute-start(bf16[2,32,256]{2,1,0:T(8,128)(2,1)S(1)} %get-tuple-element.126.refs_34_), channel_id=1, source_target_pairs={{5,0},{9,4},{13,8},{17,12},{21,16},{25,20},{29,24}} | collective-permute-start | bytes 98312 | tf_op jit(solution)/shard_map/ppermute | solution.py:426
  23.1 18.0 %collective-permute-done.10.refs_2_ = bf16[2,32,256]{2,1,0:T(8,128)(2,1)S(1)} collective-permute-done((bf16[2,32,256]{2,1,0:T(8,128)(2,1)S(1)}, bf16[2,32,256]{2,1,0:T(8,128)(2,1)S(1)}, u32[]{:S(2)}, u32[]{:S(2)}) %collective-permute-start.10) | collective-permute-done | bytes 32800 | tf_op jit(solution)/shard_map/ppermute | solution.py:426
  41.1 1.3 %collective-permute-start.19 = (bf16[2,32,256]{2,1,0:T(8,128)(2,1)S(1)}, bf16[2,32,256]{2,1,0:T(8,128)(2,1)S(1)}, u32[]{:S(2)}, u32[]{:S(2)}) collective-permute-start(bf16[2,32,256]{2,1,0:T(8,128)(2,1)S(1)} %get-tuple-element.127.refs_35_), channel_id=1, source_target_pairs={{1,4},{5,8},{9,12},{13,16},{17,20},{21,24},{25,28}} | collective-permute-start | bytes 98312 | tf_op jit(solution)/shard_map/ppermute | solution.py:426
  42.4 4.7 %collective-permute-done.9.refs_1_ = bf16[2,32,256]{2,1,0:T(8,128)(2,1)S(1)} collective-permute-done((bf16[2,32,256]{2,1,0:T(8,128)(2,1)S(1)}, bf16[2,32,256]{2,1,0:T(8,128)(2,1)S(1)}, u32[]{:S(2)}, u32[]{:S(2)}) %collective-permute-start.9) | collective-permute-done | bytes 32800 | tf_op jit(solution)/shard_map/ppermute | solution.py:426
  47.1 0.8 %step.10 = (bf16[2,256,256]{2,1,0:T(8,128)(2,1)S(1)}, bf16[2,32,256]{2,1,0:T(8,128)(2,1)S(1)}, bf16[2,32,256]{2,1,0:T(8,128)(2,1)S(1)}, bf16[2,256,256]{2,1,0:T(8,128)(2,1)S(1)}, bf16[2,256,256]{2,1,0:T(8,128)(2,1)S(1)}) custom-call(s32[1]{0:T(128)} %bitcast.info_ref, bf16[2,256,256]{2,1,0:T(8,128)(2,1)S(1)} %collective-permute-done.8.refs_0_, ...), custom_call_target="tpu_custom_call" | custom-call | flops 2600000000 | bytes 1048576 | tf_op jit(solution)/shard_map/step/pallas_call | solution.py:439
  49.0 4.5 %collective-permute-done.18.refs_1_ = bf16[2,32,256]{2,1,0:T(8,128)(2,1)S(1)} collective-permute-done((bf16[2,32,256]{2,1,0:T(8,128)(2,1)S(1)}, bf16[2,32,256]{2,1,0:T(8,128)(2,1)S(1)}, u32[]{:S(2)}, u32[]{:S(2)}) %collective-permute-start.18) | collective-permute-done | bytes 32800 | tf_op jit(solution)/shard_map/ppermute | solution.py:426
  53.5 0.8 %step_last.1 = (bf16[2,256,256]{2,1,0:T(8,128)(2,1)S(1)}, bf16[2,256,256]{2,1,0:T(8,128)(2,1)S(1)}, bf16[2,256,256]{2,1,0:T(8,128)(2,1)S(1)}, bf16[2,32,256]{2,1,0:T(8,128)(2,1)S(1)}, bf16[2,32,256]{2,1,0:T(8,128)(2,1)S(1)}) custom-call(s32[1]{0:T(128)} %bitcast.info_ref, bf16[2,256,256]{2,1,0:T(8,128)(2,1)S(1)} %collective-permute-done.17.refs_0_, ...), custom_call_target="tpu_custom_call" | custom-call | flops 2600000000 | bytes 1048576 | tf_op jit(solution)/shard_map/step_last/pallas_call | solution.py:464
  54.8 1.6 %collective-permute-done.21.came_ref = bf16[576,256]{1,0:T(8,128)(2,1)S(1)} collective-permute-done((bf16[576,256]{1,0:T(8,128)(2,1)S(1)}, bf16[576,256]{1,0:T(8,128)(2,1)S(1)}, u32[]{:S(2)}, u32[]{:S(2)}) %collective-permute-start.21) | collective-permute-done | bytes 294944 | tf_op jit(solution)/shard_map/ppermute | solution.py:485
  56.5 0.7 %collective-permute-start.24 = (bf16[256,256]{1,0:T(8,128)(2,1)S(1)}, bf16[256,256]{1,0:T(8,128)(2,1)S(1)}, u32[]{:S(2)}, u32[]{:S(2)}) collective-permute-start(bf16[256,256]{1,0:T(8,128)(2,1)S(1)} %get-tuple-element.142.p_ref), channel_id=1, source_target_pairs={{0,16},{4,12},{8,24},{12,4},{16,0},{20,28},{24,8},{28,20},{1,17},{... | collective-permute-start | bytes 393224 | tf_op jit(solution)/shard_map/ppermute | solution.py:496
  57.2 1.1 %collective-permute-start.22 = (bf16[256,256]{1,0:T(8,128)(2,1)S(1)}, bf16[256,256]{1,0:T(8,128)(2,1)S(1)}, u32[]{:S(2)}, u32[]{:S(2)}) collective-permute-start(bf16[256,256]{1,0:T(8,128)(2,1)S(1)} %get-tuple-element.141.p_ref), channel_id=1, source_target_pairs={{0,8},{4,20},{8,0},{12,28},{16,24},{20,4},{24,16},{28,12},{1,9},{5... | collective-permute-start | bytes 393224 | tf_op jit(solution)/shard_map/ppermute | solution.py:496
  58.3 2.3 %collective-permute-done.24.other_ref.refs_3_ = bf16[256,256]{1,0:T(8,128)(2,1)S(1)} collective-permute-done((bf16[256,256]{1,0:T(8,128)(2,1)S(1)}, bf16[256,256]{1,0:T(8,128)(2,1)S(1)}, u32[]{:S(2)}, u32[]{:S(2)}) %collective-permute-start.24) | collective-permute-done | bytes 131104 | tf_op jit(solution)/shard_map/ppermute | solution.py:496
  60.7 2.3 %collective-permute-start.25 = (bf16[256,256]{1,0:T(8,128)(2,1)S(1)}, bf16[256,256]{1,0:T(8,128)(2,1)S(1)}, u32[]{:S(2)}, u32[]{:S(2)}) collective-permute-start(bf16[256,256]{1,0:T(8,128)(2,1)S(1)} %forward_sum.3.q_ref), channel_id=1, source_target_pairs={{0,8},{4,20},{8,0},{12,28},{16,24},{20,4},{24,16},{28,12},{1,9},{5... | collective-permute-start | bytes 393224 | tf_op jit(solution)/shard_map/ppermute | solution.py:496
  63.3 2.0 %collective-permute-done.25.q_other_ref.refs_5_ = bf16[256,256]{1,0:T(8,128)(2,1)S(1)} collective-permute-done((bf16[256,256]{1,0:T(8,128)(2,1)S(1)}, bf16[256,256]{1,0:T(8,128)(2,1)S(1)}, u32[]{:S(2)}, u32[]{:S(2)}) %collective-permute-start.25) | collective-permute-done | bytes 131104 | tf_op jit(solution)/shard_map/ppermute | solution.py:496
  65.3 2.7 %collective-permute-done.23.p_other_ref.refs_4_ = bf16[256,256]{1,0:T(8,128)(2,1)S(1)} collective-permute-done((bf16[256,256]{1,0:T(8,128)(2,1)S(1)}, bf16[256,256]{1,0:T(8,128)(2,1)S(1)}, u32[]{:S(2)}, u32[]{:S(2)}) %collective-permute-start.23) | collective-permute-done | bytes 131104 | tf_op jit(solution)/shard_map/ppermute | solution.py:496
  68.0 1.1 %collective-permute-start.26 = (bf16[384,256]{1,0:T(8,128)(2,1)S(1)}, bf16[384,256]{1,0:T(8,128)(2,1)S(1)}, u32[]{:S(2)}, u32[]{:S(2)}) collective-permute-start(bf16[384,256]{1,0:T(8,128)(2,1)S(1)} %join.1.mine_ref), channel_id=1, source_target_pairs={{0,4},{4,0},{8,12},{12,8},{16,20},{20,16},{24,28},{28,24},{1,5},{5... | collective-permute-start | bytes 589832 | tf_op jit(solution)/shard_map/ppermute | solution.py:485
  69.1 1.6 %finish.1 = (bf16[4,256,256]{2,1,0:T(8,128)(2,1)}, f32[512,256]{1,0:T(8,128)}, f32[256,256]{1,0:T(8,128)}) custom-call(s32[1]{0:T(128)} %bitcast.info_ref, bf16[384,256]{1,0:T(8,128)(2,1)S(1)} %join.1.mine_ref, bf16[576,256]{1,0:T(8,128)(2,1)S(1)} %collective-permute-done.21.came_ref, bf16[256,64]{1,0:T(8,128)(2,1)S(1)} %get-tuple-element.97.refs_3_.place_ref, ...), custom_call_target="tpu_custom_call" | custom-call | tf_op jit(solution)/shard_map/finish/pallas_call | solution.py:528
  70.7 0.8 %split.1 = (f32[512,256]{1,0:T(8,128)}, f32[256,256]{1,0:T(8,128)}) custom-call(s32[1]{0:T(128)} %bitcast.info_ref, bf16[384,256]{1,0:T(8,128)(2,1)S(1)} %collective-permute-done.26.other_ref, f32[512,256]{1,0:T(8,128)} %get-tuple-element.147.first_in, f32[256,256]{1,0:T(8,128)} %get-tuple-element.148.second_in), custom_call_target="tpu_custom_call", output_to_operand_aliasing={{0}: (2, {}), {1}: (3, {})} | custom-call | tf_op jit(solution)/shard_map/split/pallas_call | solution.py:533
  (42 shorter events, 6.8 us)
Async XLA Ops:
  2.1 3.4 %collective-permute-start = (bf16[4,32,256]{2,1,0:T(8,128)(2,1)S(1)}, bf16[4,32,256]{2,1,0:T(8,128)(2,1)S(1)}, u32[]{:S(2)}, u32[]{:S(2)}) collective-permute-start(bf16[4,32,256]{2,1,0:T(8,128)(2,1)S(1)} %get-tuple-element.83), channel_id=1, source_target_pairs={{0,4},{4,0},{8,12},{12,8},{16,20},{20,16},{24,28},{28,24},{1,5},{5... | collective-permute-start | bytes 196616 | tf_op jit(solution)/shard_map/ppermute | solution.py:406
  2.2 4.9 %collective-permute-start.1 = (bf16[4,32,256]{2,1,0:T(8,128)(2,1)S(1)}, bf16[4,32,256]{2,1,0:T(8,128)(2,1)S(1)}, u32[]{:S(2)}, u32[]{:S(2)}) collective-permute-start(bf16[4,32,256]{2,1,0:T(8,128)(2,1)S(1)} %get-tuple-element.84), channel_id=1, source_target_pairs={{0,28},{4,8},{8,4},{12,16},{16,12},{20,24},{24,20},{28,0},{1,29},{... | collective-permute-start | bytes 196616 | tf_op jit(solution)/shard_map/ppermute | solution.py:406
  7.7 4.7 %collective-permute-start.2 = (bf16[2,256,256]{2,1,0:T(8,128)(2,1)S(1)}, bf16[2,256,256]{2,1,0:T(8,128)(2,1)S(1)}, u32[]{:S(2)}, u32[]{:S(2)}) collective-permute-start(bf16[2,256,256]{2,1,0:T(8,128)(2,1)S(1)} %get-tuple-element.94.refs_8_), channel_id=1, source_target_pairs={{3,2},{7,6},{11,10},{15,14},{19,18},{23,22},{27,26},{31,30}} | collective-permute-start | bytes 786440 | tf_op jit(solution)/shard_map/ppermute | solution.py:426
  8.4 3.3 %collective-permute-start.3 = (bf16[2,32,256]{2,1,0:T(8,128)(2,1)S(1)}, bf16[2,32,256]{2,1,0:T(8,128)(2,1)S(1)}, u32[]{:S(2)}, u32[]{:S(2)}) collective-permute-start(bf16[2,32,256]{2,1,0:T(8,128)(2,1)S(1)} %get-tuple-element.95.refs_9_), channel_id=1, source_target_pairs={{7,2},{11,6},{15,10},{19,14},{23,18},{27,22},{31,26}} | collective-permute-start | bytes 98312 | tf_op jit(solution)/shard_map/ppermute | solution.py:426
  9.0 3.3 %collective-permute-start.4 = (bf16[2,32,256]{2,1,0:T(8,128)(2,1)S(1)}, bf16[2,32,256]{2,1,0:T(8,128)(2,1)S(1)}, u32[]{:S(2)}, u32[]{:S(2)}) collective-permute-start(bf16[2,32,256]{2,1,0:T(8,128)(2,1)S(1)} %get-tuple-element.96.refs_10_), channel_id=1, source_target_pairs={{3,6},{7,10},{11,14},{15,18},{19,22},{23,26},{27,30}} | collective-permute-start | bytes 98312 | tf_op jit(solution)/shard_map/ppermute | solution.py:426
  10.3 4.1 %collective-permute-start.11 = (bf16[2,256,256]{2,1,0:T(8,128)(2,1)S(1)}, bf16[2,256,256]{2,1,0:T(8,128)(2,1)S(1)}, u32[]{:S(2)}, u32[]{:S(2)}) collective-permute-start(bf16[2,256,256]{2,1,0:T(8,128)(2,1)S(1)} %get-tuple-element.111.refs_13_), channel_id=1, source_target_pairs={{3,2},{7,6},{11,10},{15,14},{19,18},{23,22},{27,26},{31,30}} | collective-permute-start | bytes 786440 | tf_op jit(solution)/shard_map/ppermute | solution.py:426
  11.0 2.8 %collective-permute-start.12 = (bf16[2,32,256]{2,1,0:T(8,128)(2,1)S(1)}, bf16[2,32,256]{2,1,0:T(8,128)(2,1)S(1)}, u32[]{:S(2)}, u32[]{:S(2)}) collective-permute-start(bf16[2,32,256]{2,1,0:T(8,128)(2,1)S(1)} %get-tuple-element.112.refs_14_), channel_id=1, source_target_pairs={{7,2},{11,6},{15,10},{19,14},{23,18},{27,22},{31,26}} | collective-permute-start | bytes 98312 | tf_op jit(solution)/shard_map/ppermute | solution.py:426
  11.7 2.8 %collective-permute-start.13 = (bf16[2,32,256]{2,1,0:T(8,128)(2,1)S(1)}, bf16[2,32,256]{2,1,0:T(8,128)(2,1)S(1)}, u32[]{:S(2)}, u32[]{:S(2)}) collective-permute-start(bf16[2,32,256]{2,1,0:T(8,128)(2,1)S(1)} %get-tuple-element.113.refs_15_), channel_id=1, source_target_pairs={{3,6},{7,10},{11,14},{15,18},{19,22},{23,26},{27,30}} | collective-permute-start | bytes 98312 | tf_op jit(solution)/shard_map/ppermute | solution.py:426
  12.4 4.1 %collective-permute-start.5 = (bf16[2,256,256]{2,1,0:T(8,128)(2,1)S(1)}, bf16[2,256,256]{2,1,0:T(8,128)(2,1)S(1)}, u32[]{:S(2)}, u32[]{:S(2)}) collective-permute-start(bf16[2,256,256]{2,1,0:T(8,128)(2,1)S(1)} %get-tuple-element.98.refs_18_), channel_id=1, source_target_pairs={{2,1},{6,5},{10,9},{14,13},{18,17},{22,21},{26,25},{30,29}} | collective-permute-start | bytes 786440 | tf_op jit(solution)/shard_map/ppermute | solution.py:426
  13.1 2.8 %collective-permute-start.6 = (bf16[2,32,256]{2,1,0:T(8,128)(2,1)S(1)}, bf16[2,32,256]{2,1,0:T(8,128)(2,1)S(1)}, u32[]{:S(2)}, u32[]{:S(2)}) collective-permute-start(bf16[2,32,256]{2,1,0:T(8,128)(2,1)S(1)} %get-tuple-element.99.refs_19_), channel_id=1, source_target_pairs={{6,1},{10,5},{14,9},{18,13},{22,17},{26,21},{30,25}} | collective-permute-start | bytes 98312 | tf_op jit(solution)/shard_map/ppermute | solution.py:426
  13.8 2.8 %collective-permute-start.7 = (bf16[2,32,256]{2,1,0:T(8,128)(2,1)S(1)}, bf16[2,32,256]{2,1,0:T(8,128)(2,1)S(1)}, u32[]{:S(2)}, u32[]{:S(2)}) collective-permute-start(bf16[2,32,256]{2,1,0:T(8,128)(2,1)S(1)} %get-tuple-element.100.refs_20_), channel_id=1, source_target_pairs={{2,5},{6,9},{10,13},{14,17},{18,21},{22,25},{26,29}} | collective-permute-start | bytes 98312 | tf_op jit(solution)/shard_map/ppermute | solution.py:426
  14.5 6.0 %collective-permute-start.14 = (bf16[2,256,256]{2,1,0:T(8,128)(2,1)S(1)}, bf16[2,256,256]{2,1,0:T(8,128)(2,1)S(1)}, u32[]{:S(2)}, u32[]{:S(2)}) collective-permute-start(bf16[2,256,256]{2,1,0:T(8,128)(2,1)S(1)} %get-tuple-element.118.refs_23_), channel_id=1, source_target_pairs={{2,1},{6,5},{10,9},{14,13},{18,17},{22,21},{26,25},{30,29}} | collective-permute-start | bytes 786440 | tf_op jit(solution)/shard_map/ppermute | solution.py:426
  15.2 4.0 %collective-permute-start.15 = (bf16[2,32,256]{2,1,0:T(8,128)(2,1)S(1)}, bf16[2,32,256]{2,1,0:T(8,128)(2,1)S(1)}, u32[]{:S(2)}, u32[]{:S(2)}) collective-permute-start(bf16[2,32,256]{2,1,0:T(8,128)(2,1)S(1)} %get-tuple-element.119.refs_24_), channel_id=1, source_target_pairs={{6,1},{10,5},{14,9},{18,13},{22,17},{26,21},{30,25}} | collective-permute-start | bytes 98312 | tf_op jit(solution)/shard_map/ppermute | solution.py:426
  15.8 4.6 %collective-permute-start.16 = (bf16[2,32,256]{2,1,0:T(8,128)(2,1)S(1)}, bf16[2,32,256]{2,1,0:T(8,128)(2,1)S(1)}, u32[]{:S(2)}, u32[]{:S(2)}) collective-permute-start(bf16[2,32,256]{2,1,0:T(8,128)(2,1)S(1)} %get-tuple-element.120.refs_25_), channel_id=1, source_target_pairs={{2,5},{6,9},{10,13},{14,17},{18,21},{22,25},{26,29}} | collective-permute-start | bytes 98312 | tf_op jit(solution)/shard_map/ppermute | solution.py:426
  16.6 30.5 %collective-permute-start.8 = (bf16[2,256,256]{2,1,0:T(8,128)(2,1)S(1)}, bf16[2,256,256]{2,1,0:T(8,128)(2,1)S(1)}, u32[]{:S(2)}, u32[]{:S(2)}) collective-permute-start(bf16[2,256,256]{2,1,0:T(8,128)(2,1)S(1)} %get-tuple-element.101.refs_28_), channel_id=1, source_target_pairs={{1,0},{5,4},{9,8},{13,12},{17,16},{21,20},{25,24},{29,28}} | collective-permute-start | bytes 786440 | tf_op jit(solution)/shard_map/ppermute | solution.py:426
  17.9 23.2 %collective-permute-start.10 = (bf16[2,32,256]{2,1,0:T(8,128)(2,1)S(1)}, bf16[2,32,256]{2,1,0:T(8,128)(2,1)S(1)}, u32[]{:S(2)}, u32[]{:S(2)}) collective-permute-start(bf16[2,32,256]{2,1,0:T(8,128)(2,1)S(1)} %get-tuple-element.103.refs_30_), channel_id=1, source_target_pairs={{1,4},{5,8},{9,12},{13,16},{17,20},{21,24},{25,28}} | collective-permute-start | bytes 98312 | tf_op jit(solution)/shard_map/ppermute | solution.py:426
  19.2 27.9 %collective-permute-start.9 = (bf16[2,32,256]{2,1,0:T(8,128)(2,1)S(1)}, bf16[2,32,256]{2,1,0:T(8,128)(2,1)S(1)}, u32[]{:S(2)}, u32[]{:S(2)}) collective-permute-start(bf16[2,32,256]{2,1,0:T(8,128)(2,1)S(1)} %get-tuple-element.102.refs_29_), channel_id=1, source_target_pairs={{5,0},{9,4},{13,8},{17,12},{21,16},{25,20},{29,24}} | collective-permute-start | bytes 98312 | tf_op jit(solution)/shard_map/ppermute | solution.py:426
  20.5 33.0 %collective-permute-start.17 = (bf16[2,256,256]{2,1,0:T(8,128)(2,1)S(1)}, bf16[2,256,256]{2,1,0:T(8,128)(2,1)S(1)}, u32[]{:S(2)}, u32[]{:S(2)}) collective-permute-start(bf16[2,256,256]{2,1,0:T(8,128)(2,1)S(1)} %get-tuple-element.125.refs_33_), channel_id=1, source_target_pairs={{1,0},{5,4},{9,8},{13,12},{17,16},{21,20},{25,24},{29,28}} | collective-permute-start | bytes 786440 | tf_op jit(solution)/shard_map/ppermute | solution.py:426
  21.8 31.7 %collective-permute-start.18 = (bf16[2,32,256]{2,1,0:T(8,128)(2,1)S(1)}, bf16[2,32,256]{2,1,0:T(8,128)(2,1)S(1)}, u32[]{:S(2)}, u32[]{:S(2)}) collective-permute-start(bf16[2,32,256]{2,1,0:T(8,128)(2,1)S(1)} %get-tuple-element.126.refs_34_), channel_id=1, source_target_pairs={{5,0},{9,4},{13,8},{17,12},{21,16},{25,20},{29,24}} | collective-permute-start | bytes 98312 | tf_op jit(solution)/shard_map/ppermute | solution.py:426
  41.1 12.4 %collective-permute-start.19 = (bf16[2,32,256]{2,1,0:T(8,128)(2,1)S(1)}, bf16[2,32,256]{2,1,0:T(8,128)(2,1)S(1)}, u32[]{:S(2)}, u32[]{:S(2)}) collective-permute-start(bf16[2,32,256]{2,1,0:T(8,128)(2,1)S(1)} %get-tuple-element.127.refs_35_), channel_id=1, source_target_pairs={{1,4},{5,8},{9,12},{13,16},{17,20},{21,24},{25,28}} | collective-permute-start | bytes 98312 | tf_op jit(solution)/shard_map/ppermute | solution.py:426
  48.4 5.1 %collective-permute-start.20 = (bf16[2,32,256]{2,1,0:T(8,128)(2,1)S(1)}, bf16[2,32,256]{2,1,0:T(8,128)(2,1)S(1)}, u32[]{:S(2)}, u32[]{:S(2)}) collective-permute-start(bf16[2,32,256]{2,1,0:T(8,128)(2,1)S(1)} %get-tuple-element.133), channel_id=1, source_target_pairs={{0,28},{4,8},{8,4},{12,16},{16,12},{20,24},{24,20},{28,0},{1,29},{... | collective-permute-start | bytes 98312 | tf_op jit(solution)/shard_map/ppermute | solution.py:463
  54.8 1.6 %collective-permute-start.21 = (bf16[576,256]{1,0:T(8,128)(2,1)S(1)}, bf16[576,256]{1,0:T(8,128)(2,1)S(1)}, u32[]{:S(2)}, u32[]{:S(2)}) collective-permute-start(bf16[576,256]{1,0:T(8,128)(2,1)S(1)} %get-tuple-element.140), channel_id=1, source_target_pairs={{0,4},{4,0},{8,12},{12,8},{16,20},{20,16},{24,28},{28,24},{1,5},{5... | collective-permute-start | bytes 884744 | tf_op jit(solution)/shard_map/ppermute | solution.py:485
  56.5 4.2 %collective-permute-start.24 = (bf16[256,256]{1,0:T(8,128)(2,1)S(1)}, bf16[256,256]{1,0:T(8,128)(2,1)S(1)}, u32[]{:S(2)}, u32[]{:S(2)}) collective-permute-start(bf16[256,256]{1,0:T(8,128)(2,1)S(1)} %get-tuple-element.142.p_ref), channel_id=1, source_target_pairs={{0,16},{4,12},{8,24},{12,4},{16,0},{20,28},{24,8},{28,20},{1,17},{... | collective-permute-start | bytes 393224 | tf_op jit(solution)/shard_map/ppermute | solution.py:496
  57.2 5.7 %collective-permute-start.22 = (bf16[256,256]{1,0:T(8,128)(2,1)S(1)}, bf16[256,256]{1,0:T(8,128)(2,1)S(1)}, u32[]{:S(2)}, u32[]{:S(2)}) collective-permute-start(bf16[256,256]{1,0:T(8,128)(2,1)S(1)} %get-tuple-element.141.p_ref), channel_id=1, source_target_pairs={{0,8},{4,20},{8,0},{12,28},{16,24},{20,4},{24,16},{28,12},{1,9},{5... | collective-permute-start | bytes 393224 | tf_op jit(solution)/shard_map/ppermute | solution.py:496
  60.7 4.6 %collective-permute-start.25 = (bf16[256,256]{1,0:T(8,128)(2,1)S(1)}, bf16[256,256]{1,0:T(8,128)(2,1)S(1)}, u32[]{:S(2)}, u32[]{:S(2)}) collective-permute-start(bf16[256,256]{1,0:T(8,128)(2,1)S(1)} %forward_sum.3.q_ref), channel_id=1, source_target_pairs={{0,8},{4,20},{8,0},{12,28},{16,24},{20,4},{24,16},{28,12},{1,9},{5... | collective-permute-start | bytes 393224 | tf_op jit(solution)/shard_map/ppermute | solution.py:496
  63.0 5.0 %collective-permute-start.23 = (bf16[256,256]{1,0:T(8,128)(2,1)S(1)}, bf16[256,256]{1,0:T(8,128)(2,1)S(1)}, u32[]{:S(2)}, u32[]{:S(2)}) collective-permute-start(bf16[256,256]{1,0:T(8,128)(2,1)S(1)} %forward_sum.2.p_ref), channel_id=1, source_target_pairs={{0,16},{4,12},{8,24},{12,4},{16,0},{20,28},{24,8},{28,20},{1,17},{... | collective-permute-start | bytes 393224 | tf_op jit(solution)/shard_map/ppermute | solution.py:496
  68.0 2.6 %collective-permute-start.26 = (bf16[384,256]{1,0:T(8,128)(2,1)S(1)}, bf16[384,256]{1,0:T(8,128)(2,1)S(1)}, u32[]{:S(2)}, u32[]{:S(2)}) collective-permute-start(bf16[384,256]{1,0:T(8,128)(2,1)S(1)} %join.1.mine_ref), channel_id=1, source_target_pairs={{0,4},{4,0},{8,12},{12,8},{16,20},{20,16},{24,28},{28,24},{1,5},{5... | collective-permute-start | bytes 589832 | tf_op jit(solution)/shard_map/ppermute | solution.py:485

commit v10 on v9

--- a/solution.py
+++ b/solution.py
@@ -41,14 +41,16 @@
     return pltpu.CompilerParams(vmem_limit_bytes=16 * 1024 * 1024)
 
 
-def load_kernel(info_ref, x_hbm, g_hbm, w1_hbm, w2_hbm, nbr_hbm, coef_hbm, send_hbm,
-                x_ref, g_ref, w1_ref, w2_ref, nbr_ref, coef_ref, place_ref, near_ref, far_ref, send_ref, sems):
-    sources = (send_hbm, x_hbm, nbr_hbm, coef_hbm, w1_hbm, w2_hbm, g_hbm)
-    targets = (send_ref, x_ref, nbr_ref, coef_ref, w1_ref, w2_ref, g_ref)
+def start_all(sources, targets, sems):
     copies = [pltpu.make_async_copy(source, target, sems.at[n])
               for n, (source, target) in enumerate(zip(sources, targets))]
     for copy in copies:
         copy.start()
+    return copies
+
+
+def load_kernel(info_ref, x_hbm, send_hbm, x_ref, place_ref, near_ref, far_ref, send_ref, sems):
+    copies = start_all((send_hbm, x_hbm), (send_ref, x_ref), sems)
     batches, rows, _ = x_ref.shape
     slots = send_ref.shape[1]
     row = lax.broadcasted_iota(jnp.int32, (rows, slots), 0)
@@ -65,11 +67,13 @@
         up, down = sent[:slots], sent[slots:]
         near_ref[m] = jnp.where(odd, down, up).astype(BF16)
         far_ref[m] = jnp.where(odd, up, down).astype(BF16)
-    for copy in copies[2:]:
+
+
+def inner_kernel(x_ref, g_hbm, w1_hbm, w2_hbm, nbr_hbm, coef_hbm,
+                 base_ref, inner_ref, own_ref, halo_ref, g_ref, w_ref, w2_ref, nbr_ref, coef_ref, sems):
+    copies = start_all((nbr_hbm, coef_hbm, w1_hbm, w2_hbm, g_hbm), (nbr_ref, coef_ref, w_ref, w2_ref, g_ref), sems)
+    for copy in copies[:2]:
         copy.wait()
-
-
-def inner_kernel(x_ref, nbr_ref, coef_ref, w_ref, base_ref, inner_ref, own_ref, halo_ref):
     batches, rows, width = x_ref.shape
     slots = halo_ref.shape[0] // 2
     faces = nbr_ref.shape[0]
@@ -81,6 +85,8 @@
     halo_ref[...] = jnp.concatenate([spread[:slots], spread[slots + rows :]], axis=0).astype(BF16)
     own_ref[...] = own.astype(BF16)
     own_t = own.T.astype(BF16)
+    for copy in copies[2:]:
+        copy.wait()
     for m in range(batches):
         x = x_ref[m]
         inner_ref[m] = dot(own_t, x)
@@ -319,8 +325,8 @@
 def make_finish_kernel(last, start, slots, relay):
     def body(info_ref, mine_ref, came_ref, place_ref, far_early_ref, loc_ref, *refs):
         number = 4 if relay else 1
-        here, halos, refs = refs[: -5 - number], refs[-5 - number : -5], refs[-5:]
-        out_ref, first_ref, second_ref, value_ref, sems = refs
+        here, halos, refs = refs[: -7 - number], refs[-7 - number : -7], refs[-7:]
+        out_ref, first_ref, second_ref, value_ref, sems, rows_ref, row_sems = refs
         odd, end = odd_of(info_ref) == 1, end_of(info_ref) == 1
         batches = loc_ref.shape[0]
         count = batches // len(here)
@@ -345,7 +351,11 @@
                 far = jnp.where(end, jnp.zeros_like(far), far)
                 upper = jnp.where(odd, far, near)
                 lower = jnp.where(odd, near, far)
-                out_ref[m] = assemble(local(m), upper, lower, place_ref[...])
+                rows_ref[m] = assemble(local(m), upper, lower, place_ref[...])
+                row_copy(m).start()
+
+        def row_copy(m):
+            return pltpu.make_async_copy(rows_ref.at[m], out_ref.at[m], row_sems.at[m])
 
         @pl.when(hop_of(info_ref) == last)
         def _():
@@ -355,6 +365,8 @@
         def _():
             write(lambda m: loc_ref[m])
 
+        for m in range(batches):
+            row_copy(m).wait()
         for_half(odd_of(info_ref), lambda copy: copy.wait(), *half_refs)
 
     return body
@@ -393,25 +405,27 @@
     far_pairs = [(p, (p + 1 if p % 2 else p - 1) % doms) for p in range(doms)]
 
     edge_shape = sds((batches, slots, width), BF16)
-    x, grad_out, w1, w2, neighbours, face_weight, place, near, far = pl.pallas_call(
-        load_kernel,
-        in_specs=[smem] + [hbm_spec] * 7,
-        out_specs=[vmem()] * 9,
-        out_shape=(like(x), like(grad_out), like(w1), like(w2), like(neighbours), like(face_weight),
-                   sds((rows, 2 * slots), BF16), edge_shape, edge_shape),
-        scratch_shapes=[pltpu.VMEM(send_rows.shape, send_rows.dtype), pltpu.SemaphoreType.DMA((7,))],
+    def in_hbm(*values):
+        return [pltpu.with_memory_space_constraint(value, pltpu.HBM) for value in values]
+
+    x, place, near, far = pl.pallas_call(
+        load_kernel, in_specs=[smem] + [hbm_spec] * 2, out_specs=[vmem()] * 4,
+        out_shape=(like(x), sds((rows, 2 * slots), BF16), edge_shape, edge_shape),
+        scratch_shapes=[pltpu.VMEM(send_rows.shape, send_rows.dtype), pltpu.SemaphoreType.DMA((2,))],
         compiler_params=params(), name="load",
-    )(info, *[pltpu.with_memory_space_constraint(value, pltpu.HBM)
-             for value in (x, grad_out, w1, w2, neighbours, face_weight, send_rows)])
+    )(info, *in_hbm(x, send_rows))
     near, far = lax.ppermute(near, "dom", near_pairs), lax.ppermute(far, "dom", far_pairs)
 
     full_shape = sds((batches, rows, width), BF16)
     wide_shape = sds((batches, rows, width), F32)
-    base, inner, own, halo = pl.pallas_call(
-        inner_kernel, in_specs=[vmem()] * 4, out_specs=[vmem()] * 4,
-        out_shape=(wide_shape, wide_shape, sds((rows, rows), BF16), sds((2 * slots, rows), BF16)),
+    base, inner, own, halo, grad_out, w1, w2 = pl.pallas_call(
+        inner_kernel, in_specs=[vmem()] + [hbm_spec] * 5, out_specs=[vmem()] * 7,
+        out_shape=(wide_shape, wide_shape, sds((rows, rows), BF16), sds((2 * slots, rows), BF16),
+                   like(grad_out), like(w1), like(w2)),
+        scratch_shapes=[pltpu.VMEM(neighbours.shape, neighbours.dtype), pltpu.VMEM(face_weight.shape, face_weight.dtype),
+                        pltpu.SemaphoreType.DMA((5,))],
         compiler_params=params(), name="inner",
-    )(x, neighbours, face_weight, w1)
+    )(x, *in_hbm(grad_out, w1, w2, neighbours, face_weight))
     forward = []
     for c in range(chunks):
         small = sds((count, rows, width), BF16)
@@ -527,8 +541,9 @@
     value = [pltpu.VMEM((half, width), F32), pltpu.SemaphoreType.DMA((2,))]
     grad_in, first, second = pl.pallas_call(
         make_finish_kernel(last, half, slots, relay),
-        in_specs=[smem] + [vmem()] * (5 + chunks + len(halos)), out_specs=[vmem()] + [any_spec] * 2,
-        out_shape=(full_shape, *outs), scratch_shapes=value, compiler_params=params(), name="finish",
+        in_specs=[smem] + [vmem()] * (5 + chunks + len(halos)), out_specs=[any_spec] * 3,
+        out_shape=(full_shape, *outs),
+        scratch_shapes=value + [pltpu.VMEM(full_shape.shape, BF16), pltpu.SemaphoreType.DMA((batches,))], compiler_params=params(), name="finish",
     )(info, mine, came, place, far_early, local, *[outs[0] for outs in here], local_last, *halos)
     first, second = pl.pallas_call(
         split_kernel, in_specs=[smem, vmem(), any_spec, any_spec], out_specs=[any_spec] * 2, out_shape=outs,

time: 71.8 us -> 71.5 us (level)
  waiting for transfers between devices: 37.4 us -> 36.2 us
    ppermute x1, waiting for transfers between devices: 1.6 us -> 0.53 us  [per_device(): lax.ppermute(far, 'dom', far_pairs)]
    pallas_call x2, Pallas kernels: 2.06 us -> 2.98 us  [the longest x1 1.7 us: per_device(): pl.pallas_call(inner_kernel, in_specs=[vmem()] + [hbm_spec] * 5, out_spec...]
  transfers between devices with their start and end apart: 27 -> 27, of which waited for: 8 -> 8; matrix products, arithmetic and copies ran while one was open for 0% -> 0% of each run, Pallas kernels for 6% -> 7%
where the time goes in v10:
time: 71.5 us; the launch traced here: 70.8 us
  waiting for transfers between devices  36.2 us (51%)
  starting transfers between devices  24.8 us (35%)
  Pallas kernels  8.81 us (12%)
  between operations  1.07 us (1%)
    ppermute x18, waiting for transfers between devices, move(): return lax.ppermute(value, ('dom', 'section'), pairs)  27.1 us
    ppermute x18, starting transfers between devices, move(): return lax.ppermute(value, ('dom', 'section'), pairs)  15.8 us
    ppermute x4, waiting for transfers between devices, cross(): lax.ppermute(value, 'dom', [(i, i ^ (odd if i % 2 else even)) for i in ra...  6.96 us
    ppermute x4, starting transfers between devices, cross(): lax.ppermute(value, 'dom', [(i, i ^ (odd if i % 2 else even)) for i in ra...  4.6 us
    ppermute x1, starting transfers between devices, per_device(): lax.ppermute(far, 'dom', far_pairs)  2.62 us
    pallas_call x1, Pallas kernels, per_device(): pl.pallas_call(inner_kernel, in_specs=[vmem()] + [hbm_spec] * 5, out_spec...  1.7 us
    ppermute x2, waiting for transfers between devices, swap(): return lax.ppermute(value, 'dom', [(i, i ^ mask) for i in range(doms)])  1.57 us
  transfers between devices with their start and end apart: 27, of which 8 were waited for; matrix products, arithmetic and copies ran while one was open for 0% of the time, Pallas kernels for 7%

profile of v10, /device:TPU:1, one launch (start us, length us, event | category | flops | bytes accessed | tf_op | source)
XLA Modules:
  0.0 70.8 jit_solution(1781344893476159758)
XLA Ops:
  0.7 1.3 %load.1 = (bf16[4,256,256]{2,1,0:T(8,128)(2,1)S(1)}, bf16[256,64]{1,0:T(8,128)(2,1)S(1)}, bf16[4,32,256]{2,1,0:T(8,128)(2,1)S(1)}, bf16[4,32,256]{2,1,0:T(8,128)(2,1)S(1)}) custom-call(s32[1]{0:T(128)} %bitcast.info_ref, bf16[4,256,256]{2,1,0:T(8,128)(2,1)} %bitcast.8, s32[2,32]{1,0:T(2,128)} %send_hbm.1), custom_call_target="tpu_custom_call" | custom-call | tf_op jit(solution)/shard_map/load/pallas_call | solution.py:411
  2.1 2.6 %collective-permute-start.1 = (bf16[4,32,256]{2,1,0:T(8,128)(2,1)S(1)}, bf16[4,32,256]{2,1,0:T(8,128)(2,1)S(1)}, u32[]{:S(2)}, u32[]{:S(2)}) collective-permute-start(bf16[4,32,256]{2,1,0:T(8,128)(2,1)S(1)} %get-tuple-element.79), channel_id=1, source_target_pairs={{0,28},{4,8},{8,4},{12,16},{16,12},{20,24},{24,20},{28,0},{1,29},{... | collective-permute-start | bytes 196616 | tf_op jit(solution)/shard_map/ppermute | solution.py:417
  4.7 1.7 %inner.1 = (f32[4,256,256]{2,1,0:T(8,128)S(1)}, f32[4,256,256]{2,1,0:T(8,128)S(1)}, bf16[256,256]{1,0:T(8,128)(2,1)S(1)}, bf16[64,256]{1,0:T(8,128)(2,1)S(1)}, b...) custom-call(bf16[4,256,256]{2,1,0:T(8,128)(2,1)S(1)} %get-tuple-element.75.x_ref, ...), custom_call_target="tpu_custom_call" | custom-call | tf_op jit(solution)/shard_map/inner/pallas_call | solution.py:421
  7.5 0.7 collective-permute-start.2
  8.2 0.7 collective-permute-start.3
  8.9 0.7 collective-permute-start.4
  10.2 0.7 collective-permute-start.11
  10.8 0.7 collective-permute-start.12
  11.5 0.7 collective-permute-start.13
  12.2 0.7 collective-permute-start.5
  14.3 0.7 collective-permute-start.14
  16.4 1.3 %collective-permute-start.8 = (bf16[2,256,256]{2,1,0:T(8,128)(2,1)S(1)}, bf16[2,256,256]{2,1,0:T(8,128)(2,1)S(1)}, u32[]{:S(2)}, u32[]{:S(2)}) collective-permute-start(bf16[2,256,256]{2,1,0:T(8,128)(2,1)S(1)} %get-tuple-element.97.refs_28_), channel_id=1, source_target_pairs={{1,0},{5,4},{9,8},{13,12},{17,16},{21,20},{25,24},{29,28}} | collective-permute-start | bytes 786440 | tf_op jit(solution)/shard_map/ppermute | solution.py:440
  17.7 1.3 %collective-permute-start.10 = (bf16[2,32,256]{2,1,0:T(8,128)(2,1)S(1)}, bf16[2,32,256]{2,1,0:T(8,128)(2,1)S(1)}, u32[]{:S(2)}, u32[]{:S(2)}) collective-permute-start(bf16[2,32,256]{2,1,0:T(8,128)(2,1)S(1)} %get-tuple-element.99.refs_30_), channel_id=1, source_target_pairs={{1,4},{5,8},{9,12},{13,16},{17,20},{21,24},{25,28}} | collective-permute-start | bytes 98312 | tf_op jit(solution)/shard_map/ppermute | solution.py:440
  19.0 1.3 %collective-permute-start.9 = (bf16[2,32,256]{2,1,0:T(8,128)(2,1)S(1)}, bf16[2,32,256]{2,1,0:T(8,128)(2,1)S(1)}, u32[]{:S(2)}, u32[]{:S(2)}) collective-permute-start(bf16[2,32,256]{2,1,0:T(8,128)(2,1)S(1)} %get-tuple-element.98.refs_29_), channel_id=1, source_target_pairs={{5,0},{9,4},{13,8},{17,12},{21,16},{25,20},{29,24}} | collective-permute-start | bytes 98312 | tf_op jit(solution)/shard_map/ppermute | solution.py:440
  20.4 1.3 %collective-permute-start.17 = (bf16[2,256,256]{2,1,0:T(8,128)(2,1)S(1)}, bf16[2,256,256]{2,1,0:T(8,128)(2,1)S(1)}, u32[]{:S(2)}, u32[]{:S(2)}) collective-permute-start(bf16[2,256,256]{2,1,0:T(8,128)(2,1)S(1)} %get-tuple-element.121.refs_33_), channel_id=1, source_target_pairs={{1,0},{5,4},{9,8},{13,12},{17,16},{21,20},{25,24},{29,28}} | collective-permute-start | bytes 786440 | tf_op jit(solution)/shard_map/ppermute | solution.py:440
  21.7 1.3 %collective-permute-start.18 = (bf16[2,32,256]{2,1,0:T(8,128)(2,1)S(1)}, bf16[2,32,256]{2,1,0:T(8,128)(2,1)S(1)}, u32[]{:S(2)}, u32[]{:S(2)}) collective-permute-start(bf16[2,32,256]{2,1,0:T(8,128)(2,1)S(1)} %get-tuple-element.122.refs_34_), channel_id=1, source_target_pairs={{5,0},{9,4},{13,8},{17,12},{21,16},{25,20},{29,24}} | collective-permute-start | bytes 98312 | tf_op jit(solution)/shard_map/ppermute | solution.py:440
  23.0 18.0 %collective-permute-done.10.refs_2_ = bf16[2,32,256]{2,1,0:T(8,128)(2,1)S(1)} collective-permute-done((bf16[2,32,256]{2,1,0:T(8,128)(2,1)S(1)}, bf16[2,32,256]{2,1,0:T(8,128)(2,1)S(1)}, u32[]{:S(2)}, u32[]{:S(2)}) %collective-permute-start.10) | collective-permute-done | bytes 32800 | tf_op jit(solution)/shard_map/ppermute | solution.py:440
  40.9 1.3 %collective-permute-start.19 = (bf16[2,32,256]{2,1,0:T(8,128)(2,1)S(1)}, bf16[2,32,256]{2,1,0:T(8,128)(2,1)S(1)}, u32[]{:S(2)}, u32[]{:S(2)}) collective-permute-start(bf16[2,32,256]{2,1,0:T(8,128)(2,1)S(1)} %get-tuple-element.123.refs_35_), channel_id=1, source_target_pairs={{1,4},{5,8},{9,12},{13,16},{17,20},{21,24},{25,28}} | collective-permute-start | bytes 98312 | tf_op jit(solution)/shard_map/ppermute | solution.py:440
  42.2 4.7 %collective-permute-done.9.refs_1_ = bf16[2,32,256]{2,1,0:T(8,128)(2,1)S(1)} collective-permute-done((bf16[2,32,256]{2,1,0:T(8,128)(2,1)S(1)}, bf16[2,32,256]{2,1,0:T(8,128)(2,1)S(1)}, u32[]{:S(2)}, u32[]{:S(2)}) %collective-permute-start.9) | collective-permute-done | bytes 32800 | tf_op jit(solution)/shard_map/ppermute | solution.py:440
  46.9 0.8 %step.10 = (bf16[2,256,256]{2,1,0:T(8,128)(2,1)S(1)}, bf16[2,32,256]{2,1,0:T(8,128)(2,1)S(1)}, bf16[2,32,256]{2,1,0:T(8,128)(2,1)S(1)}, bf16[2,256,256]{2,1,0:T(8,128)(2,1)S(1)}, bf16[2,256,256]{2,1,0:T(8,128)(2,1)S(1)}) custom-call(s32[1]{0:T(128)} %bitcast.info_ref, bf16[2,256,256]{2,1,0:T(8,128)(2,1)S(1)} %collective-permute-done.8.refs_0_, ...), custom_call_target="tpu_custom_call" | custom-call | flops 2600000000 | bytes 1048576 | tf_op jit(solution)/shard_map/step/pallas_call | solution.py:453
  48.8 4.5 %collective-permute-done.18.refs_1_ = bf16[2,32,256]{2,1,0:T(8,128)(2,1)S(1)} collective-permute-done((bf16[2,32,256]{2,1,0:T(8,128)(2,1)S(1)}, bf16[2,32,256]{2,1,0:T(8,128)(2,1)S(1)}, u32[]{:S(2)}, u32[]{:S(2)}) %collective-permute-start.18) | collective-permute-done | bytes 32800 | tf_op jit(solution)/shard_map/ppermute | solution.py:440
  53.3 0.8 %step_last.1 = (bf16[2,256,256]{2,1,0:T(8,128)(2,1)S(1)}, bf16[2,256,256]{2,1,0:T(8,128)(2,1)S(1)}, bf16[2,256,256]{2,1,0:T(8,128)(2,1)S(1)}, bf16[2,32,256]{2,1,0:T(8,128)(2,1)S(1)}, bf16[2,32,256]{2,1,0:T(8,128)(2,1)S(1)}) custom-call(s32[1]{0:T(128)} %bitcast.info_ref, bf16[2,256,256]{2,1,0:T(8,128)(2,1)S(1)} %collective-permute-done.17.refs_0_, ...), custom_call_target="tpu_custom_call" | custom-call | flops 2600000000 | bytes 1048576 | tf_op jit(solution)/shard_map/step_last/pallas_call | solution.py:478
  54.6 1.6 %collective-permute-done.21.came_ref = bf16[576,256]{1,0:T(8,128)(2,1)S(1)} collective-permute-done((bf16[576,256]{1,0:T(8,128)(2,1)S(1)}, bf16[576,256]{1,0:T(8,128)(2,1)S(1)}, u32[]{:S(2)}, u32[]{:S(2)}) %collective-permute-start.21) | collective-permute-done | bytes 294944 | tf_op jit(solution)/shard_map/ppermute | solution.py:499
  56.3 0.8 %collective-permute-start.24 = (bf16[256,256]{1,0:T(8,128)(2,1)S(1)}, bf16[256,256]{1,0:T(8,128)(2,1)S(1)}, u32[]{:S(2)}, u32[]{:S(2)}) collective-permute-start(bf16[256,256]{1,0:T(8,128)(2,1)S(1)} %get-tuple-element.138.p_ref), channel_id=1, source_target_pairs={{0,16},{4,12},{8,24},{12,4},{16,0},{20,28},{24,8},{28,20},{1,17},{... | collective-permute-start | bytes 393224 | tf_op jit(solution)/shard_map/ppermute | solution.py:510
  57.0 1.1 %collective-permute-start.22 = (bf16[256,256]{1,0:T(8,128)(2,1)S(1)}, bf16[256,256]{1,0:T(8,128)(2,1)S(1)}, u32[]{:S(2)}, u32[]{:S(2)}) collective-permute-start(bf16[256,256]{1,0:T(8,128)(2,1)S(1)} %get-tuple-element.137.p_ref), channel_id=1, source_target_pairs={{0,8},{4,20},{8,0},{12,28},{16,24},{20,4},{24,16},{28,12},{1,9},{5... | collective-permute-start | bytes 393224 | tf_op jit(solution)/shard_map/ppermute | solution.py:510
  58.2 2.2 %collective-permute-done.24.other_ref.refs_3_ = bf16[256,256]{1,0:T(8,128)(2,1)S(1)} collective-permute-done((bf16[256,256]{1,0:T(8,128)(2,1)S(1)}, bf16[256,256]{1,0:T(8,128)(2,1)S(1)}, u32[]{:S(2)}, u32[]{:S(2)}) %collective-permute-start.24) | collective-permute-done | bytes 131104 | tf_op jit(solution)/shard_map/ppermute | solution.py:510
  60.5 2.4 %collective-permute-start.25 = (bf16[256,256]{1,0:T(8,128)(2,1)S(1)}, bf16[256,256]{1,0:T(8,128)(2,1)S(1)}, u32[]{:S(2)}, u32[]{:S(2)}) collective-permute-start(bf16[256,256]{1,0:T(8,128)(2,1)S(1)} %forward_sum.3.q_ref), channel_id=1, source_target_pairs={{0,8},{4,20},{8,0},{12,28},{16,24},{20,4},{24,16},{28,12},{1,9},{5... | collective-permute-start | bytes 393224 | tf_op jit(solution)/shard_map/ppermute | solution.py:510
  63.2 2.0 %collective-permute-done.25.q_other_ref.refs_5_ = bf16[256,256]{1,0:T(8,128)(2,1)S(1)} collective-permute-done((bf16[256,256]{1,0:T(8,128)(2,1)S(1)}, bf16[256,256]{1,0:T(8,128)(2,1)S(1)}, u32[]{:S(2)}, u32[]{:S(2)}) %collective-permute-start.25) | collective-permute-done | bytes 131104 | tf_op jit(solution)/shard_map/ppermute | solution.py:510
  65.2 2.7 %collective-permute-done.23.p_other_ref.refs_4_ = bf16[256,256]{1,0:T(8,128)(2,1)S(1)} collective-permute-done((bf16[256,256]{1,0:T(8,128)(2,1)S(1)}, bf16[256,256]{1,0:T(8,128)(2,1)S(1)}, u32[]{:S(2)}, u32[]{:S(2)}) %collective-permute-start.23) | collective-permute-done | bytes 131104 | tf_op jit(solution)/shard_map/ppermute | solution.py:510
  67.9 1.0 %collective-permute-start.26 = (bf16[384,256]{1,0:T(8,128)(2,1)S(1)}, bf16[384,256]{1,0:T(8,128)(2,1)S(1)}, u32[]{:S(2)}, u32[]{:S(2)}) collective-permute-start(bf16[384,256]{1,0:T(8,128)(2,1)S(1)} %join.1.mine_ref), channel_id=1, source_target_pairs={{0,4},{4,0},{8,12},{12,8},{16,20},{20,16},{24,28},{28,24},{1,5},{5... | collective-permute-start | bytes 589832 | tf_op jit(solution)/shard_map/ppermute | solution.py:499
  69.0 1.1 %finish.1 = (bf16[4,256,256]{2,1,0:T(8,128)(2,1)}, f32[512,256]{1,0:T(8,128)}, f32[256,256]{1,0:T(8,128)}) custom-call(s32[1]{0:T(128)} %bitcast.info_ref, bf16[384,256]{1,0:T(8,128)(2,1)S(1)} %join.1.mine_ref, bf16[576,256]{1,0:T(8,128)(2,1)S(1)} %collective-permute-done.21.came_ref, bf16[256,64]{1,0:T(8,128)(2,1)S(1)} %get-tuple-element.93.refs_3_.place_ref, ...), custom_call_target="tpu_custom_call" | custom-call | tf_op jit(solution)/shard_map/finish/pallas_call | solution.py:542
  70.0 0.8 %split.1 = (f32[512,256]{1,0:T(8,128)}, f32[256,256]{1,0:T(8,128)}) custom-call(s32[1]{0:T(128)} %bitcast.info_ref, bf16[384,256]{1,0:T(8,128)(2,1)S(1)} %collective-permute-done.26.other_ref, f32[512,256]{1,0:T(8,128)} %get-tuple-element.143.first_in, f32[256,256]{1,0:T(8,128)} %get-tuple-element.144.second_in), custom_call_target="tpu_custom_call", output_to_operand_aliasing={{0}: (2, {}), {1}: (3, {})} | custom-call | tf_op jit(solution)/shard_map/split/pallas_call | solution.py:548
  (42 shorter events, 6.7 us)
Async XLA Ops:
  2.0 4.5 %collective-permute-start = (bf16[4,32,256]{2,1,0:T(8,128)(2,1)S(1)}, bf16[4,32,256]{2,1,0:T(8,128)(2,1)S(1)}, u32[]{:S(2)}, u32[]{:S(2)}) collective-permute-start(bf16[4,32,256]{2,1,0:T(8,128)(2,1)S(1)} %get-tuple-element.78), channel_id=1, source_target_pairs={{0,4},{4,0},{8,12},{12,8},{16,20},{20,16},{24,28},{28,24},{1,5},{5... | collective-permute-start | bytes 196616 | tf_op jit(solution)/shard_map/ppermute | solution.py:417
  2.1 4.9 %collective-permute-start.1 = (bf16[4,32,256]{2,1,0:T(8,128)(2,1)S(1)}, bf16[4,32,256]{2,1,0:T(8,128)(2,1)S(1)}, u32[]{:S(2)}, u32[]{:S(2)}) collective-permute-start(bf16[4,32,256]{2,1,0:T(8,128)(2,1)S(1)} %get-tuple-element.79), channel_id=1, source_target_pairs={{0,28},{4,8},{8,4},{12,16},{16,12},{20,24},{24,20},{28,0},{1,29},{... | collective-permute-start | bytes 196616 | tf_op jit(solution)/shard_map/ppermute | solution.py:417
  7.5 4.7 %collective-permute-start.2 = (bf16[2,256,256]{2,1,0:T(8,128)(2,1)S(1)}, bf16[2,256,256]{2,1,0:T(8,128)(2,1)S(1)}, u32[]{:S(2)}, u32[]{:S(2)}) collective-permute-start(bf16[2,256,256]{2,1,0:T(8,128)(2,1)S(1)} %get-tuple-element.90.refs_8_), channel_id=1, source_target_pairs={{3,2},{7,6},{11,10},{15,14},{19,18},{23,22},{27,26},{31,30}} | collective-permute-start | bytes 786440 | tf_op jit(solution)/shard_map/ppermute | solution.py:440
  8.2 3.3 %collective-permute-start.3 = (bf16[2,32,256]{2,1,0:T(8,128)(2,1)S(1)}, bf16[2,32,256]{2,1,0:T(8,128)(2,1)S(1)}, u32[]{:S(2)}, u32[]{:S(2)}) collective-permute-start(bf16[2,32,256]{2,1,0:T(8,128)(2,1)S(1)} %get-tuple-element.91.refs_9_), channel_id=1, source_target_pairs={{7,2},{11,6},{15,10},{19,14},{23,18},{27,22},{31,26}} | collective-permute-start | bytes 98312 | tf_op jit(solution)/shard_map/ppermute | solution.py:440
  8.9 3.3 %collective-permute-start.4 = (bf16[2,32,256]{2,1,0:T(8,128)(2,1)S(1)}, bf16[2,32,256]{2,1,0:T(8,128)(2,1)S(1)}, u32[]{:S(2)}, u32[]{:S(2)}) collective-permute-start(bf16[2,32,256]{2,1,0:T(8,128)(2,1)S(1)} %get-tuple-element.92.refs_10_), channel_id=1, source_target_pairs={{3,6},{7,10},{11,14},{15,18},{19,22},{23,26},{27,30}} | collective-permute-start | bytes 98312 | tf_op jit(solution)/shard_map/ppermute | solution.py:440
  10.2 4.1 %collective-permute-start.11 = (bf16[2,256,256]{2,1,0:T(8,128)(2,1)S(1)}, bf16[2,256,256]{2,1,0:T(8,128)(2,1)S(1)}, u32[]{:S(2)}, u32[]{:S(2)}) collective-permute-start(bf16[2,256,256]{2,1,0:T(8,128)(2,1)S(1)} %get-tuple-element.107.refs_13_), channel_id=1, source_target_pairs={{3,2},{7,6},{11,10},{15,14},{19,18},{23,22},{27,26},{31,30}} | collective-permute-start | bytes 786440 | tf_op jit(solution)/shard_map/ppermute | solution.py:440
  10.8 2.8 %collective-permute-start.12 = (bf16[2,32,256]{2,1,0:T(8,128)(2,1)S(1)}, bf16[2,32,256]{2,1,0:T(8,128)(2,1)S(1)}, u32[]{:S(2)}, u32[]{:S(2)}) collective-permute-start(bf16[2,32,256]{2,1,0:T(8,128)(2,1)S(1)} %get-tuple-element.108.refs_14_), channel_id=1, source_target_pairs={{7,2},{11,6},{15,10},{19,14},{23,18},{27,22},{31,26}} | collective-permute-start | bytes 98312 | tf_op jit(solution)/shard_map/ppermute | solution.py:440
  11.5 2.8 %collective-permute-start.13 = (bf16[2,32,256]{2,1,0:T(8,128)(2,1)S(1)}, bf16[2,32,256]{2,1,0:T(8,128)(2,1)S(1)}, u32[]{:S(2)}, u32[]{:S(2)}) collective-permute-start(bf16[2,32,256]{2,1,0:T(8,128)(2,1)S(1)} %get-tuple-element.109.refs_15_), channel_id=1, source_target_pairs={{3,6},{7,10},{11,14},{15,18},{19,22},{23,26},{27,30}} | collective-permute-start | bytes 98312 | tf_op jit(solution)/shard_map/ppermute | solution.py:440
  12.2 4.1 %collective-permute-start.5 = (bf16[2,256,256]{2,1,0:T(8,128)(2,1)S(1)}, bf16[2,256,256]{2,1,0:T(8,128)(2,1)S(1)}, u32[]{:S(2)}, u32[]{:S(2)}) collective-permute-start(bf16[2,256,256]{2,1,0:T(8,128)(2,1)S(1)} %get-tuple-element.94.refs_18_), channel_id=1, source_target_pairs={{2,1},{6,5},{10,9},{14,13},{18,17},{22,21},{26,25},{30,29}} | collective-permute-start | bytes 786440 | tf_op jit(solution)/shard_map/ppermute | solution.py:440
  12.9 2.8 %collective-permute-start.6 = (bf16[2,32,256]{2,1,0:T(8,128)(2,1)S(1)}, bf16[2,32,256]{2,1,0:T(8,128)(2,1)S(1)}, u32[]{:S(2)}, u32[]{:S(2)}) collective-permute-start(bf16[2,32,256]{2,1,0:T(8,128)(2,1)S(1)} %get-tuple-element.95.refs_19_), channel_id=1, source_target_pairs={{6,1},{10,5},{14,9},{18,13},{22,17},{26,21},{30,25}} | collective-permute-start | bytes 98312 | tf_op jit(solution)/shard_map/ppermute | solution.py:440
  13.6 2.8 %collective-permute-start.7 = (bf16[2,32,256]{2,1,0:T(8,128)(2,1)S(1)}, bf16[2,32,256]{2,1,0:T(8,128)(2,1)S(1)}, u32[]{:S(2)}, u32[]{:S(2)}) collective-permute-start(bf16[2,32,256]{2,1,0:T(8,128)(2,1)S(1)} %get-tuple-element.96.refs_20_), channel_id=1, source_target_pairs={{2,5},{6,9},{10,13},{14,17},{18,21},{22,25},{26,29}} | collective-permute-start | bytes 98312 | tf_op jit(solution)/shard_map/ppermute | solution.py:440
  14.3 6.0 %collective-permute-start.14 = (bf16[2,256,256]{2,1,0:T(8,128)(2,1)S(1)}, bf16[2,256,256]{2,1,0:T(8,128)(2,1)S(1)}, u32[]{:S(2)}, u32[]{:S(2)}) collective-permute-start(bf16[2,256,256]{2,1,0:T(8,128)(2,1)S(1)} %get-tuple-element.114.refs_23_), channel_id=1, source_target_pairs={{2,1},{6,5},{10,9},{14,13},{18,17},{22,21},{26,25},{30,29}} | collective-permute-start | bytes 786440 | tf_op jit(solution)/shard_map/ppermute | solution.py:440
  15.0 4.0 %collective-permute-start.15 = (bf16[2,32,256]{2,1,0:T(8,128)(2,1)S(1)}, bf16[2,32,256]{2,1,0:T(8,128)(2,1)S(1)}, u32[]{:S(2)}, u32[]{:S(2)}) collective-permute-start(bf16[2,32,256]{2,1,0:T(8,128)(2,1)S(1)} %get-tuple-element.115.refs_24_), channel_id=1, source_target_pairs={{6,1},{10,5},{14,9},{18,13},{22,17},{26,21},{30,25}} | collective-permute-start | bytes 98312 | tf_op jit(solution)/shard_map/ppermute | solution.py:440
  15.7 4.6 %collective-permute-start.16 = (bf16[2,32,256]{2,1,0:T(8,128)(2,1)S(1)}, bf16[2,32,256]{2,1,0:T(8,128)(2,1)S(1)}, u32[]{:S(2)}, u32[]{:S(2)}) collective-permute-start(bf16[2,32,256]{2,1,0:T(8,128)(2,1)S(1)} %get-tuple-element.116.refs_25_), channel_id=1, source_target_pairs={{2,5},{6,9},{10,13},{14,17},{18,21},{22,25},{26,29}} | collective-permute-start | bytes 98312 | tf_op jit(solution)/shard_map/ppermute | solution.py:440
  16.4 30.5 %collective-permute-start.8 = (bf16[2,256,256]{2,1,0:T(8,128)(2,1)S(1)}, bf16[2,256,256]{2,1,0:T(8,128)(2,1)S(1)}, u32[]{:S(2)}, u32[]{:S(2)}) collective-permute-start(bf16[2,256,256]{2,1,0:T(8,128)(2,1)S(1)} %get-tuple-element.97.refs_28_), channel_id=1, source_target_pairs={{1,0},{5,4},{9,8},{13,12},{17,16},{21,20},{25,24},{29,28}} | collective-permute-start | bytes 786440 | tf_op jit(solution)/shard_map/ppermute | solution.py:440
  17.7 23.2 %collective-permute-start.10 = (bf16[2,32,256]{2,1,0:T(8,128)(2,1)S(1)}, bf16[2,32,256]{2,1,0:T(8,128)(2,1)S(1)}, u32[]{:S(2)}, u32[]{:S(2)}) collective-permute-start(bf16[2,32,256]{2,1,0:T(8,128)(2,1)S(1)} %get-tuple-element.99.refs_30_), channel_id=1, source_target_pairs={{1,4},{5,8},{9,12},{13,16},{17,20},{21,24},{25,28}} | collective-permute-start | bytes 98312 | tf_op jit(solution)/shard_map/ppermute | solution.py:440
  19.0 27.8 %collective-permute-start.9 = (bf16[2,32,256]{2,1,0:T(8,128)(2,1)S(1)}, bf16[2,32,256]{2,1,0:T(8,128)(2,1)S(1)}, u32[]{:S(2)}, u32[]{:S(2)}) collective-permute-start(bf16[2,32,256]{2,1,0:T(8,128)(2,1)S(1)} %get-tuple-element.98.refs_29_), channel_id=1, source_target_pairs={{5,0},{9,4},{13,8},{17,12},{21,16},{25,20},{29,24}} | collective-permute-start | bytes 98312 | tf_op jit(solution)/shard_map/ppermute | solution.py:440
  20.4 32.9 %collective-permute-start.17 = (bf16[2,256,256]{2,1,0:T(8,128)(2,1)S(1)}, bf16[2,256,256]{2,1,0:T(8,128)(2,1)S(1)}, u32[]{:S(2)}, u32[]{:S(2)}) collective-permute-start(bf16[2,256,256]{2,1,0:T(8,128)(2,1)S(1)} %get-tuple-element.121.refs_33_), channel_id=1, source_target_pairs={{1,0},{5,4},{9,8},{13,12},{17,16},{21,20},{25,24},{29,28}} | collective-permute-start | bytes 786440 | tf_op jit(solution)/shard_map/ppermute | solution.py:440
  21.7 31.6 %collective-permute-start.18 = (bf16[2,32,256]{2,1,0:T(8,128)(2,1)S(1)}, bf16[2,32,256]{2,1,0:T(8,128)(2,1)S(1)}, u32[]{:S(2)}, u32[]{:S(2)}) collective-permute-start(bf16[2,32,256]{2,1,0:T(8,128)(2,1)S(1)} %get-tuple-element.122.refs_34_), channel_id=1, source_target_pairs={{5,0},{9,4},{13,8},{17,12},{21,16},{25,20},{29,24}} | collective-permute-start | bytes 98312 | tf_op jit(solution)/shard_map/ppermute | solution.py:440
  40.9 12.4 %collective-permute-start.19 = (bf16[2,32,256]{2,1,0:T(8,128)(2,1)S(1)}, bf16[2,32,256]{2,1,0:T(8,128)(2,1)S(1)}, u32[]{:S(2)}, u32[]{:S(2)}) collective-permute-start(bf16[2,32,256]{2,1,0:T(8,128)(2,1)S(1)} %get-tuple-element.123.refs_35_), channel_id=1, source_target_pairs={{1,4},{5,8},{9,12},{13,16},{17,20},{21,24},{25,28}} | collective-permute-start | bytes 98312 | tf_op jit(solution)/shard_map/ppermute | solution.py:440
  48.2 5.1 %collective-permute-start.20 = (bf16[2,32,256]{2,1,0:T(8,128)(2,1)S(1)}, bf16[2,32,256]{2,1,0:T(8,128)(2,1)S(1)}, u32[]{:S(2)}, u32[]{:S(2)}) collective-permute-start(bf16[2,32,256]{2,1,0:T(8,128)(2,1)S(1)} %get-tuple-element.129), channel_id=1, source_target_pairs={{0,28},{4,8},{8,4},{12,16},{16,12},{20,24},{24,20},{28,0},{1,29},{... | collective-permute-start | bytes 98312 | tf_op jit(solution)/shard_map/ppermute | solution.py:477
  54.6 1.6 %collective-permute-start.21 = (bf16[576,256]{1,0:T(8,128)(2,1)S(1)}, bf16[576,256]{1,0:T(8,128)(2,1)S(1)}, u32[]{:S(2)}, u32[]{:S(2)}) collective-permute-start(bf16[576,256]{1,0:T(8,128)(2,1)S(1)} %get-tuple-element.136), channel_id=1, source_target_pairs={{0,4},{4,0},{8,12},{12,8},{16,20},{20,16},{24,28},{28,24},{1,5},{5... | collective-permute-start | bytes 884744 | tf_op jit(solution)/shard_map/ppermute | solution.py:499
  56.3 4.2 %collective-permute-start.24 = (bf16[256,256]{1,0:T(8,128)(2,1)S(1)}, bf16[256,256]{1,0:T(8,128)(2,1)S(1)}, u32[]{:S(2)}, u32[]{:S(2)}) collective-permute-start(bf16[256,256]{1,0:T(8,128)(2,1)S(1)} %get-tuple-element.138.p_ref), channel_id=1, source_target_pairs={{0,16},{4,12},{8,24},{12,4},{16,0},{20,28},{24,8},{28,20},{1,17},{... | collective-permute-start | bytes 393224 | tf_op jit(solution)/shard_map/ppermute | solution.py:510
  57.0 5.8 %collective-permute-start.22 = (bf16[256,256]{1,0:T(8,128)(2,1)S(1)}, bf16[256,256]{1,0:T(8,128)(2,1)S(1)}, u32[]{:S(2)}, u32[]{:S(2)}) collective-permute-start(bf16[256,256]{1,0:T(8,128)(2,1)S(1)} %get-tuple-element.137.p_ref), channel_id=1, source_target_pairs={{0,8},{4,20},{8,0},{12,28},{16,24},{20,4},{24,16},{28,12},{1,9},{5... | collective-permute-start | bytes 393224 | tf_op jit(solution)/shard_map/ppermute | solution.py:510
  60.5 4.7 %collective-permute-start.25 = (bf16[256,256]{1,0:T(8,128)(2,1)S(1)}, bf16[256,256]{1,0:T(8,128)(2,1)S(1)}, u32[]{:S(2)}, u32[]{:S(2)}) collective-permute-start(bf16[256,256]{1,0:T(8,128)(2,1)S(1)} %forward_sum.3.q_ref), channel_id=1, source_target_pairs={{0,8},{4,20},{8,0},{12,28},{16,24},{20,4},{24,16},{28,12},{1,9},{5... | collective-permute-start | bytes 393224 | tf_op jit(solution)/shard_map/ppermute | solution.py:510
  62.9 5.0 %collective-permute-start.23 = (bf16[256,256]{1,0:T(8,128)(2,1)S(1)}, bf16[256,256]{1,0:T(8,128)(2,1)S(1)}, u32[]{:S(2)}, u32[]{:S(2)}) collective-permute-start(bf16[256,256]{1,0:T(8,128)(2,1)S(1)} %forward_sum.2.p_ref), channel_id=1, source_target_pairs={{0,16},{4,12},{8,24},{12,4},{16,0},{20,28},{24,8},{28,20},{1,17},{... | collective-permute-start | bytes 393224 | tf_op jit(solution)/shard_map/ppermute | solution.py:510
  67.9 2.1 %collective-permute-start.26 = (bf16[384,256]{1,0:T(8,128)(2,1)S(1)}, bf16[384,256]{1,0:T(8,128)(2,1)S(1)}, u32[]{:S(2)}, u32[]{:S(2)}) collective-permute-start(bf16[384,256]{1,0:T(8,128)(2,1)S(1)} %join.1.mine_ref), channel_id=1, source_target_pairs={{0,4},{4,0},{8,12},{12,8},{16,20},{20,16},{24,28},{28,24},{1,5},{5... | collective-permute-start | bytes 589832 | tf_op jit(solution)/shard_map/ppermute | solution.py:499
